TPU v7x, 32 devices: a whole 2x2x4 slice. The times are simulated.
32 devices in a mesh: dp: 16 (over z, y, core), head: 2 (over x).
Axes of the slice: x: 2, y: 2, z: 4, core: 2. Of those that a mesh axis runs over, the one named last changes fastest.
Arguments:
- inputs: bfloat16 [49152, 1024], P(('dp', 'head')), may hold values from -6 to 6
- time_embed: bfloat16 [16, 1024], P('dp'), may hold values from -6 to 6
- segment_ids: int32 [16, 3072], P('dp'), may hold values from 0 to 7, never falling along the last dimension, each value on 1 to 1536 neighbouring positions
- modulator_weight: bfloat16 [1024, 6144], P(None, 'head'), may hold values from -0.1875 to 0.1875
- modulator_bias: bfloat16 [6144], P('head'), may hold values from -3 to 3
- projection_weight: bfloat16 [1024, 3, 1024], P(None, None, 'head'), may hold values from -0.1875 to 0.1875
- projection_bias: bfloat16 [3, 1024], P(None, 'head'), may hold values from -3 to 3
- output_weight: bfloat16 [1024, 1024], P('head'), may hold values from -3 to 3
- output_bias: bfloat16 [1024], replicated, may hold values from -3 to 3
- expand_weight: bfloat16 [1024, 2048], P(None, 'head'), may hold values from -0.1875 to 0.1875
- expand_bias: bfloat16 [2048], P('head'), may hold values from -3 to 3
- contract_weight: bfloat16 [2048, 1024], P('head'), may hold values from -0.125 to 0.125
- contract_bias: bfloat16 [1024], replicated, may hold values from -3 to 3
- cotangent: bfloat16 [49152, 1024], P(('dp', 'head')), may hold values from -6 to 6
Outputs:
- layer_output: bfloat16 [49152, 1024], P(('dp', 'head'))
- grad_inputs: float32 [49152, 1024], P(('dp', 'head'))
- grad_embed: float32 [16, 1024], P('dp')
- grad_modulator_weight: float32 [1024, 6144], P(None, 'head')
- grad_modulator_bias: float32 [6144], P('head')
- grad_projection_weight: float32 [1024, 3, 1024], P(None, None, 'head')
- grad_projection_bias: float32 [3, 1024], P(None, 'head')
- grad_output_weight: float32 [1024, 1024], P('head')
- grad_output_bias: float32 [1024], replicated
- grad_expand_weight: float32 [1024, 2048], P(None, 'head')
- grad_expand_bias: float32 [2048], P('head')
- grad_contract_weight: float32 [2048, 1024], P('head')
- grad_contract_bias: float32 [1024], replicated
Inputs may be any that keep to these rules, and one draw needn't show every extreme that they name: `segment_ids`: in each row the ids never fall, each of the 8 utterances takes 1 to 1536 frames.
All inputs are finite; a program needn't handle non-finite values.
Results may differ from a plain program's by a relative error of at most 0.018.
Values may be sent and summed in bfloat16 or wider, within the bound.
A program may use at most 512 MiB of HBM per device.

v0:
```python
import jax
import jax.numpy as jnp
from jax import lax
from jax.sharding import PartitionSpec as P

HDIM = 64
ROW_LEN = 3072


precise_setting = lax.Precision.HIGHEST


def layer_norm(values):
    centre = values - jnp.mean(values, axis=-1, keepdims=True)
    spread = jnp.mean(centre * centre, axis=-1, keepdims=True)
    return centre * lax.rsqrt(spread + 1e-06)


def modulate(values, scale_part, shift_part):
    return layer_norm(values) * (1.0 + scale_part) + shift_part


def gelu_tanh(values):
    return jax.nn.gelu(values, approximate=True)


def rotate(values, cosine, sine):
    half = values.shape[-1] // 2
    turned = jnp.concatenate([-values[..., half:], values[..., :half]], axis=-1)
    return values * cosine + turned * sine


def rotate_back(grads, cosine, sine):
    half = grads.shape[-1] // 2
    scaled = grads * sine
    return grads * cosine + jnp.concatenate([scaled[..., half:], -scaled[..., :half]], axis=-1)


def rotary_tables(positions, width):
    half = width // 2
    freqs = 10000.0 ** (-jnp.arange(half, dtype=jnp.float32) * 2.0 / width)
    angles = positions.astype(jnp.float32)[:, None] * freqs[None, :]
    angles = jnp.concatenate([angles, angles], axis=-1)
    return (jnp.cos(angles)[:, None, :], jnp.sin(angles)[:, None, :])


def on_device(
    inputs,
    time_embed,
    segment_ids,
    modulator_weight,
    modulator_bias,
    projection_weight,
    projection_bias,
    output_weight,
    output_bias,
    expand_weight,
    expand_bias,
    contract_weight,
    contract_bias,
    cotangent,
):
    local_frames = inputs.shape[0]
    width = inputs.shape[1]
    head_index = lax.axis_index("head")
    rows_here = time_embed.shape[0]
    total = rows_here * ROW_LEN
    local_inner = projection_weight.shape[2]
    heads_here = local_inner // HDIM
    local_hidden = expand_weight.shape[1]
    local_mod = modulator_weight.shape[1]
    block = min(512, ROW_LEN)
    count_blocks = ROW_LEN // block
    factor = HDIM ** (-0.5)
    frames = inputs.astype(jnp.float32)
    place = head_index * local_frames + jnp.arange(local_frames, dtype=jnp.int32)
    owner = place // ROW_LEN
    member = (owner[:, None] == jnp.arange(rows_here, dtype=jnp.int32)[None, :]).astype(jnp.float32)
    embeds = time_embed.astype(jnp.float32)
    silu_low = jax.nn.silu(embeds).astype(jnp.bfloat16)
    own_mod = jnp.dot(
        silu_low, modulator_weight, preferred_element_type=jnp.float32
    ) + modulator_bias.astype(jnp.float32)
    modulation = lax.all_gather(own_mod, "head", axis=1, tiled=True)
    per_frame = jnp.dot(member, modulation, precision=precise_setting)
    shift_a, scale_a, gate_a, shift_f, scale_f, gate_f = jnp.split(per_frame, 6, axis=1)
    normed_a_full, pull_a = jax.vjp(modulate, frames, scale_a, shift_a)
    attention_normed = normed_a_full.astype(jnp.bfloat16)
    positions = jnp.arange(total, dtype=jnp.int32) % ROW_LEN
    cosine, sine = rotary_tables(positions, HDIM)
    weight_proj = projection_weight.reshape(width, 3 * local_inner)
    gathered_a = lax.all_gather(attention_normed, "head", axis=0, tiled=True)
    projected_rows = jnp.dot(gathered_a, weight_proj, preferred_element_type=jnp.float32)
    projected_rows = (projected_rows + projection_bias.astype(jnp.float32).reshape(-1)).reshape(
        total, 3, heads_here, HDIM
    )
    queries = rotate(projected_rows[:, 0], cosine, sine).astype(jnp.bfloat16)
    keys = rotate(projected_rows[:, 1], cosine, sine).astype(jnp.bfloat16)
    values = projected_rows[:, 2].astype(jnp.bfloat16)
    query_rows = queries.reshape(rows_here, ROW_LEN, heads_here, HDIM)
    key_rows = keys.reshape(rows_here, ROW_LEN, heads_here, HDIM)
    value_rows = values.reshape(rows_here, ROW_LEN, heads_here, HDIM)
    block_ids = jnp.arange(count_blocks, dtype=jnp.int32)

    def block_scores(query_block, key_row, segment_block, segment_row):
        scores = (
            jnp.einsum("qhd,khd->hqk", query_block, key_row, preferred_element_type=jnp.float32)
            * factor
        )
        allowed = (segment_block[:, None] == segment_row[None, :])[None]
        return jnp.where(allowed, scores, -1e30)

    def attend_row(operands):
        query_row, key_row, value_row, segment_row = operands

        def attend_block(carry, index):
            start = index * block
            query_block = lax.dynamic_slice_in_dim(query_row, start, block, 0)
            segment_block = lax.dynamic_slice_in_dim(segment_row, start, block, 0)
            scores = block_scores(query_block, key_row, segment_block, segment_row)
            peak = jnp.max(scores, axis=-1, keepdims=True)
            expo = jnp.exp(scores - peak)
            mass = jnp.sum(expo, axis=-1, keepdims=True)
            weights = (expo / mass).astype(jnp.bfloat16)
            result = jnp.einsum(
                "hqk,khd->qhd", weights, value_row, preferred_element_type=jnp.float32
            )
            return (carry, (result, (peak + jnp.log(mass))[..., 0]))

        _, (results, log_mass) = lax.scan(attend_block, jnp.zeros((), jnp.float32), block_ids)
        return (results.reshape(ROW_LEN, heads_here, HDIM), log_mass)

    attended_rows, log_mass_rows = lax.map(
        attend_row, (query_rows, key_rows, value_rows, segment_ids)
    )
    attended = attended_rows.reshape(total, local_inner).astype(jnp.bfloat16)
    part = attended
    branch_a = lax.psum_scatter(
        jnp.dot(part, output_weight, preferred_element_type=jnp.float32),
        "head",
        scatter_dimension=0,
        tiled=True,
    ) + output_bias.astype(jnp.float32)
    middle = frames + gate_a * branch_a
    normed_f_full, pull_f = jax.vjp(modulate, middle, scale_f, shift_f)
    normed_f = normed_f_full.astype(jnp.bfloat16)
    full_expand, full_expand_bias, full_contract = (
        lax.all_gather(expand_weight, "head", axis=1, tiled=True),
        lax.all_gather(expand_bias, "head", axis=0, tiled=True),
        lax.all_gather(contract_weight, "head", axis=0, tiled=True),
    )
    hidden_pre = jnp.dot(
        normed_f, full_expand, preferred_element_type=jnp.float32
    ) + full_expand_bias.astype(jnp.float32)
    hidden_full, gelu_pull = jax.vjp(gelu_tanh, hidden_pre)
    hidden = hidden_full.astype(jnp.bfloat16)
    branch_f = jnp.dot(
        hidden, full_contract, preferred_element_type=jnp.float32
    ) + contract_bias.astype(jnp.float32)
    result = middle + gate_f * branch_f
    layer_output = result.astype(jnp.bfloat16)
    grad_out = cotangent.astype(jnp.float32)
    grad_gate_f = grad_out * branch_f
    grad_branch_f = (gate_f * grad_out).astype(jnp.bfloat16)
    bias_down = jnp.sum(grad_branch_f.astype(jnp.float32), axis=0)
    grad_hidden = jnp.einsum(
        "fd,hd->fh", grad_branch_f, full_contract, preferred_element_type=jnp.float32
    )
    contract_part = jnp.einsum(
        "fh,fd->hd", hidden, grad_branch_f, preferred_element_type=jnp.float32
    )
    grad_pre = gelu_pull(grad_hidden)[0].astype(jnp.bfloat16)
    expand_part = jnp.einsum("fd,fh->dh", normed_f, grad_pre, preferred_element_type=jnp.float32)
    expand_bias_slice = jnp.sum(grad_pre.astype(jnp.float32), axis=0)
    grad_normed_f = jnp.einsum(
        "fh,dh->fd", grad_pre, full_expand, preferred_element_type=jnp.float32
    )
    grad_expand, grad_expand_bias, grad_contract = (
        lax.psum_scatter(
            expand_part.astype(jnp.bfloat16), "head", scatter_dimension=1, tiled=True
        ).astype(jnp.float32),
        lax.psum_scatter(
            expand_bias_slice.astype(jnp.bfloat16), "head", scatter_dimension=0, tiled=True
        ).astype(jnp.float32),
        lax.psum_scatter(
            contract_part.astype(jnp.bfloat16), "head", scatter_dimension=0, tiled=True
        ).astype(jnp.float32),
    )
    grad_middle_part, grad_scale_f, grad_shift_f = pull_f(grad_normed_f)
    grad_middle = grad_out + grad_middle_part
    grad_gate_a = grad_middle * branch_a
    grad_branch_a = (gate_a * grad_middle).astype(jnp.bfloat16)
    bias_out = jnp.sum(grad_branch_a.astype(jnp.float32), axis=0)
    grad_branch_rows = lax.all_gather(grad_branch_a, "head", axis=0, tiled=True)
    grad_attended = jnp.einsum(
        "fd,id->fi", grad_branch_rows, output_weight, preferred_element_type=jnp.float32
    ).astype(jnp.bfloat16)
    grad_output = jnp.einsum(
        "fi,fd->id", attended, grad_branch_rows, preferred_element_type=jnp.float32
    )
    grad_attended_rows = grad_attended.reshape(rows_here, ROW_LEN, heads_here, HDIM)

    def attend_back(operands):
        query_row, key_row, value_row, segment_row, grad_row, log_mass = operands

        def back_block(carry, step_inputs):
            key_total, value_total = carry
            index, mass_block = step_inputs
            start = index * block
            query_block = lax.dynamic_slice_in_dim(query_row, start, block, 0)
            segment_block = lax.dynamic_slice_in_dim(segment_row, start, block, 0)
            grad_block = lax.dynamic_slice_in_dim(grad_row, start, block, 0)
            scores = block_scores(query_block, key_row, segment_block, segment_row)
            probs = jnp.exp(scores - mass_block[:, :, None])
            grad_probs = jnp.einsum(
                "qhd,khd->hqk", grad_block, value_row, preferred_element_type=jnp.float32
            )
            centre = jnp.sum(grad_probs * probs, axis=-1, keepdims=True)
            grad_scores = (probs * (grad_probs - centre)).astype(jnp.bfloat16)
            grad_query = (
                jnp.einsum("hqk,khd->qhd", grad_scores, key_row, preferred_element_type=jnp.float32)
                * factor
            )
            key_total = (
                key_total
                + jnp.einsum(
                    "hqk,qhd->khd", grad_scores, query_block, preferred_element_type=jnp.float32
                )
                * factor
            )
            value_total = value_total + jnp.einsum(
                "hqk,qhd->khd",
                probs.astype(jnp.bfloat16),
                grad_block,
                preferred_element_type=jnp.float32,
            )
            return ((key_total, value_total), grad_query)

        empty = jnp.zeros((ROW_LEN, heads_here, HDIM), jnp.float32)
        (grad_key_row, grad_value_row), grad_query_blocks = lax.scan(
            back_block, (empty, empty), (block_ids, log_mass)
        )
        return (grad_query_blocks.reshape(ROW_LEN, heads_here, HDIM), grad_key_row, grad_value_row)

    grad_query_rows, grad_key_rows, grad_value_rows = lax.map(
        attend_back,
        (query_rows, key_rows, value_rows, segment_ids, grad_attended_rows, log_mass_rows),
    )
    grad_query_pre = rotate_back(grad_query_rows.reshape(total, heads_here, HDIM), cosine, sine)
    grad_key_pre = rotate_back(grad_key_rows.reshape(total, heads_here, HDIM), cosine, sine)
    grad_value_pre = grad_value_rows.reshape(total, heads_here, HDIM)
    grad_projected = jnp.stack([grad_query_pre, grad_key_pre, grad_value_pre], axis=1).astype(
        jnp.bfloat16
    )
    inner_start = head_index * local_inner
    grad_projected = grad_projected.reshape(total, 3 * local_inner)
    grad_projection = jnp.einsum(
        "fd,fc->dc", gathered_a, grad_projected, preferred_element_type=jnp.float32
    )
    grad_projection = grad_projection.reshape(width, 3, local_inner)
    grad_projection_bias = jnp.sum(grad_projected.astype(jnp.float32), axis=0).reshape(
        3, local_inner
    )
    part = grad_projected
    grad_normed_a = lax.psum_scatter(
        jnp.einsum("fc,dc->fd", part, weight_proj, preferred_element_type=jnp.float32).astype(
            jnp.bfloat16
        ),
        "head",
        scatter_dimension=0,
        tiled=True,
    ).astype(jnp.float32)
    full_proj_bias = lax.dynamic_update_slice(
        jnp.zeros((3, local_inner * lax.axis_size("head")), jnp.float32),
        grad_projection_bias,
        (jnp.int32(0), inner_start),
    )
    grad_frames_part, grad_scale_a, grad_shift_a = pull_a(grad_normed_a)
    grad_inputs = grad_middle + grad_frames_part
    grad_per_frame = jnp.concatenate(
        [grad_shift_a, grad_scale_a, grad_gate_a, grad_shift_f, grad_scale_f, grad_gate_f], axis=1
    )
    grad_per_row = jnp.dot(member.T, grad_per_frame, precision=precise_setting)
    grad_mod = lax.psum_scatter(grad_per_row, "head", scatter_dimension=1, tiled=True)
    grad_mod_weight = jnp.dot(silu_low.astype(jnp.float32).T, grad_mod, precision=precise_setting)
    grad_mod_bias = jnp.sum(grad_mod, axis=0)
    grad_silu_part = jnp.dot(
        grad_mod, modulator_weight.astype(jnp.float32).T, precision=precise_setting
    )
    grad_silu = lax.psum(grad_silu_part, "head")
    _, silu_pull = jax.vjp(jax.nn.silu, embeds)
    grad_embed = silu_pull(grad_silu)[0]
    grad_mod_weight, grad_projection, grad_output, grad_expand, grad_contract = (
        lax.psum(grad_mod_weight.astype(jnp.bfloat16), "dp").astype(jnp.float32),
        lax.psum(grad_projection.astype(jnp.bfloat16), "dp").astype(jnp.float32),
        lax.psum(grad_output.astype(jnp.bfloat16), "dp").astype(jnp.float32),
        lax.psum(grad_expand.astype(jnp.bfloat16), "dp").astype(jnp.float32),
        lax.psum(grad_contract.astype(jnp.bfloat16), "dp").astype(jnp.float32),
    )
    mod_start = head_index * local_mod
    hidden_start = head_index * local_hidden
    full_mod_bias = lax.dynamic_update_slice(
        jnp.zeros((local_mod * lax.axis_size("head"),), jnp.float32), grad_mod_bias, (mod_start,)
    )
    full_hidden_bias = lax.dynamic_update_slice(
        jnp.zeros((local_hidden * lax.axis_size("head"),), jnp.float32),
        grad_expand_bias,
        (hidden_start,),
    )
    full_mod_bias, full_proj_bias, full_hidden_bias, bias_out, bias_down = lax.psum(
        (full_mod_bias, full_proj_bias, full_hidden_bias, bias_out, bias_down), ("dp", "head")
    )
    grad_mod_bias = lax.dynamic_slice_in_dim(full_mod_bias, mod_start, local_mod, 0)
    grad_projection_bias = lax.dynamic_slice_in_dim(full_proj_bias, inner_start, local_inner, 1)
    grad_expand_bias = lax.dynamic_slice_in_dim(full_hidden_bias, hidden_start, local_hidden, 0)
    return (
        layer_output,
        grad_inputs,
        grad_embed,
        grad_mod_weight,
        grad_mod_bias,
        grad_projection,
        grad_projection_bias,
        grad_output,
        bias_out,
        grad_expand,
        grad_expand_bias,
        grad_contract,
        bias_down,
    )


def solution(mesh):
    in_specs = (
        P(("dp", "head"), None),
        P("dp", None),
        P("dp", None),
        P(None, "head"),
        P("head"),
        P(None, None, "head"),
        P(None, "head"),
        P("head", None),
        P(),
        P(None, "head"),
        P("head"),
        P("head", None),
        P(),
        P(("dp", "head"), None),
    )
    out_specs = (
        P(("dp", "head"), None),
        P(("dp", "head"), None),
        P("dp", None),
        P(None, "head"),
        P("head"),
        P(None, None, "head"),
        P(None, "head"),
        P("head", None),
        P(),
        P(None, "head"),
        P("head"),
        P("head", None),
        P(),
    )
    return jax.shard_map(
        on_device, mesh=mesh, in_specs=in_specs, out_specs=out_specs, check_vma=False
    )
```

profile of v0, /device:TPU:0, one launch (start us, length us, event | category | flops | bytes accessed | tf_op | source)
XLA Modules:
  0.0 2761.1 jit_solution(12866396884245281831)
XLA Ops:
  47.7 74.4 %all-gather.6.cloned.1.call-done = bf16[3072,1024]{1,0:T(8,128)(2,1)} async-done(((bf16[1536,1024]{1,0:T(8,128)(2,1)}), bf16[3072,1024]{1,0:T(8,128)(2,1)}) %all-gather.6.cloned.1.call-update) | async-done | bytes 6291472 | tf_op jit(solution)/shard_map/all_gather | solution.py:92
  175.7 402.5 %while.47 = (s32[]{:T(128)}, bf16[6,512,8,64]{1,3,2,0:T(8,128)(2,1)}, f32[6,8,512]{2,1,0:T(8,128)S(1)}, s32[6]{0:T(128)S(1)}, s32[3072]{0:T(1024)S(1)}, /*index=...) while((s32[]{:T(128)}, ...), condition=%wide.region_5.6_spmd, body=%wide.region_2.5_spmd.sunk | while | flops 3373789184 | bytes 177883360 | solution.py:130
  178.4 21.8 fusion.136
  200.2 22.0 fusion.137
  222.2 20.9 fusion.138
  245.4 21.8 fusion.136
  267.2 22.0 fusion.137
  289.2 20.9 fusion.138
  312.4 21.8 fusion.136
  334.2 22.0 fusion.137
  356.2 20.9 fusion.138
  379.4 21.8 fusion.136
  401.2 22.0 fusion.137
  423.2 20.9 fusion.138
  446.4 21.8 fusion.136
  468.2 22.0 fusion.137
  490.2 20.9 fusion.138
  513.3 21.8 fusion.136
  535.2 22.0 fusion.137
  557.1 20.9 fusion.138
  598.1 138.9 %reduce-scatter.8.cloned.1.call-done = f32[1536,1024]{1,0:T(8,128)} async-done(((f32[3072,1024]{1,0:T(8,128)}), f32[1536,1024]{1,0:T(8,128)}) %reduce-scatter.8.cloned.1.call-update) | async-done | bytes 6291472 | tf_op jit(solution)/shard_map/reduce_scatter | solution.py:138
  759.6 35.7 %all-gather.8.cloned.1.call-done = bf16[1024,2048]{1,0:T(8,128)(2,1)} async-done(((bf16[1024,1024]{1,0:T(8,128)(2,1)}), bf16[1024,2048]{1,0:T(8,128)(2,1)}) %all-gather.8.cloned.1.call-update) | async-done | bytes 4194320 | tf_op jit(solution)/shard_map/all_gather | solution.py:148
  811.2 42.3 %all-gather.10.cloned.1.call-done = bf16[2048,1024]{1,0:T(8,128)(2,1)} async-done(((bf16[1024,1024]{1,0:T(8,128)(2,1)}), bf16[2048,1024]{1,0:T(8,128)(2,1)}) %all-gather.10.cloned.1.call-update) | async-done | bytes 4194320 | tf_op jit(solution)/shard_map/all_gather | solution.py:150
  853.5 21.8 fusion.75
  888.8 21.5 fusion.78
  919.0 80.4 %all-gather.12.cloned.1.call-done = bf16[3072,1024]{1,0:T(8,128)(2,1)} async-done(((bf16[1536,1024]{1,0:T(8,128)(2,1)}), bf16[3072,1024]{1,0:T(8,128)(2,1)}) %all-gather.12.cloned.1.call-update) | async-done | bytes 6291472 | tf_op jit(solution)/shard_map/all_gather | solution.py:194
  1007.0 1078.0 %while.48 = (s32[]{:T(128)}, f32[3072,8,64]{0,2,1:T(8,128)}, f32[3072,8,64]{0,2,1:T(8,128)}, f32[6,512,8,64]{1,0,3,2:T(8,128)}, s32[6]{0:T(128)S(1)}, /*index=5*...) while((s32[]{:T(128)}, f32[3072,8,64]{0,2,1:T(8,128)}, ...), condition=%wide.region_13.14_spmd.clone, body=%wide.region_11.13_spmd.clone.sunk | while | flops 8251502592 | bytes 425855200 | solution.py:240
  1009.5 21.0 fusion.148
  1030.4 23.5 bitcast_add_fusion.5
  1054.0 37.6 %multiply_reduce_fusion.4 = (f32[8,512]{1,0:T(8,128)S(1)}, f32[8,512,3072]{2,1,0:T(8,128)}) fusion(f32[8,512,3072]{2,1,0:T(8,128)} %fusion.148, f32[8,512]{1,0:T(8,128)S(1)} %dynamic-slice_bitcast_fusion.2, pred[512,3072]{1,0:T(8,128)(4,1)S(1)} %broadcast_compare_fusion.5, bf16[3072,8,64]{0,2,1:T(8,128)(2,1)} %get-tuple-element.509, ...), kind=kOutput, calls=%fused_computation.16.clone.1 | convolution fusion | flops 1673523200 | bytes 105938944 | tf_op jit(solution)/shard_map/while/body/eval_jaxpr/while/body/eval_jaxpr/qhd,khd->hqk/dot_general | solution.py:215
  1091.6 40.6 %multiply_convert_fusion.6 = bf16[8,512,3072]{2,1,0:T(8,128)(2,1)} fusion(f32[8,512,3072]{2,1,0:T(8,128)} %get-tuple-element.431, f32[8,512,3072]{2,1,0:T(8,128)} %fusion.148, f32[8,512]{1,0:T(8,128)S(1)} %get-tuple-element.432, f32[8,512]{1,0:T(8,128)S(1)} %dynamic-slice_bitcast_fusion.2, pred[512,3072]{1,0:T(8,128)(4,1)S(1)} %broadcast_compare_fusion.5), kind=kLoop, calls=%fused_computation.15.clone.1 | loop fusion | flops 75497472 | bytes 127434752 | tf_op jit(solution)/shard_map/while/body/eval_jaxpr/while/body/eval_jaxpr/convert_element_type | solution.py:219
  1162.3 21.8 dynamic_update_slice.45
  1186.3 21.0 fusion.148
  1207.3 25.0 bitcast_add_fusion.5
  1232.3 37.7 %multiply_reduce_fusion.4 = (f32[8,512]{1,0:T(8,128)S(1)}, f32[8,512,3072]{2,1,0:T(8,128)}) fusion(f32[8,512,3072]{2,1,0:T(8,128)} %fusion.148, f32[8,512]{1,0:T(8,128)S(1)} %dynamic-slice_bitcast_fusion.2, pred[512,3072]{1,0:T(8,128)(4,1)S(1)} %broadcast_compare_fusion.5, bf16[3072,8,64]{0,2,1:T(8,128)(2,1)} %get-tuple-element.509, ...), kind=kOutput, calls=%fused_computation.16.clone.1 | convolution fusion | flops 1673523200 | bytes 105938944 | tf_op jit(solution)/shard_map/while/body/eval_jaxpr/while/body/eval_jaxpr/qhd,khd->hqk/dot_general | solution.py:215
  1270.0 40.6 %multiply_convert_fusion.6 = bf16[8,512,3072]{2,1,0:T(8,128)(2,1)} fusion(f32[8,512,3072]{2,1,0:T(8,128)} %get-tuple-element.431, f32[8,512,3072]{2,1,0:T(8,128)} %fusion.148, f32[8,512]{1,0:T(8,128)S(1)} %get-tuple-element.432, f32[8,512]{1,0:T(8,128)S(1)} %dynamic-slice_bitcast_fusion.2, pred[512,3072]{1,0:T(8,128)(4,1)S(1)} %broadcast_compare_fusion.5), kind=kLoop, calls=%fused_computation.15.clone.1 | loop fusion | flops 75497472 | bytes 127434752 | tf_op jit(solution)/shard_map/while/body/eval_jaxpr/while/body/eval_jaxpr/convert_element_type | solution.py:219
  1342.5 21.8 dynamic_update_slice.45
  1366.5 21.0 fusion.148
  1387.5 24.9 bitcast_add_fusion.5
  1412.4 37.7 %multiply_reduce_fusion.4 = (f32[8,512]{1,0:T(8,128)S(1)}, f32[8,512,3072]{2,1,0:T(8,128)}) fusion(f32[8,512,3072]{2,1,0:T(8,128)} %fusion.148, f32[8,512]{1,0:T(8,128)S(1)} %dynamic-slice_bitcast_fusion.2, pred[512,3072]{1,0:T(8,128)(4,1)S(1)} %broadcast_compare_fusion.5, bf16[3072,8,64]{0,2,1:T(8,128)(2,1)} %get-tuple-element.509, ...), kind=kOutput, calls=%fused_computation.16.clone.1 | convolution fusion | flops 1673523200 | bytes 105938944 | tf_op jit(solution)/shard_map/while/body/eval_jaxpr/while/body/eval_jaxpr/qhd,khd->hqk/dot_general | solution.py:215
  1450.1 40.6 %multiply_convert_fusion.6 = bf16[8,512,3072]{2,1,0:T(8,128)(2,1)} fusion(f32[8,512,3072]{2,1,0:T(8,128)} %get-tuple-element.431, f32[8,512,3072]{2,1,0:T(8,128)} %fusion.148, f32[8,512]{1,0:T(8,128)S(1)} %get-tuple-element.432, f32[8,512]{1,0:T(8,128)S(1)} %dynamic-slice_bitcast_fusion.2, pred[512,3072]{1,0:T(8,128)(4,1)S(1)} %broadcast_compare_fusion.5), kind=kLoop, calls=%fused_computation.15.clone.1 | loop fusion | flops 75497472 | bytes 127434752 | tf_op jit(solution)/shard_map/while/body/eval_jaxpr/while/body/eval_jaxpr/convert_element_type | solution.py:219
  1522.6 21.8 dynamic_update_slice.45
  1546.6 21.0 fusion.148
  1567.6 24.9 bitcast_add_fusion.5
  1592.5 37.7 %multiply_reduce_fusion.4 = (f32[8,512]{1,0:T(8,128)S(1)}, f32[8,512,3072]{2,1,0:T(8,128)}) fusion(f32[8,512,3072]{2,1,0:T(8,128)} %fusion.148, f32[8,512]{1,0:T(8,128)S(1)} %dynamic-slice_bitcast_fusion.2, pred[512,3072]{1,0:T(8,128)(4,1)S(1)} %broadcast_compare_fusion.5, bf16[3072,8,64]{0,2,1:T(8,128)(2,1)} %get-tuple-element.509, ...), kind=kOutput, calls=%fused_computation.16.clone.1 | convolution fusion | flops 1673523200 | bytes 105938944 | tf_op jit(solution)/shard_map/while/body/eval_jaxpr/while/body/eval_jaxpr/qhd,khd->hqk/dot_general | solution.py:215
  1630.2 40.6 %multiply_convert_fusion.6 = bf16[8,512,3072]{2,1,0:T(8,128)(2,1)} fusion(f32[8,512,3072]{2,1,0:T(8,128)} %get-tuple-element.431, f32[8,512,3072]{2,1,0:T(8,128)} %fusion.148, f32[8,512]{1,0:T(8,128)S(1)} %get-tuple-element.432, f32[8,512]{1,0:T(8,128)S(1)} %dynamic-slice_bitcast_fusion.2, pred[512,3072]{1,0:T(8,128)(4,1)S(1)} %broadcast_compare_fusion.5), kind=kLoop, calls=%fused_computation.15.clone.1 | loop fusion | flops 75497472 | bytes 127434752 | tf_op jit(solution)/shard_map/while/body/eval_jaxpr/while/body/eval_jaxpr/convert_element_type | solution.py:219
  1684.1 17.4 bitcast_add_fusion.4
  1702.6 21.8 dynamic_update_slice.45
  1726.7 21.0 fusion.148
  1747.7 24.9 bitcast_add_fusion.5
  1772.6 37.7 %multiply_reduce_fusion.4 = (f32[8,512]{1,0:T(8,128)S(1)}, f32[8,512,3072]{2,1,0:T(8,128)}) fusion(f32[8,512,3072]{2,1,0:T(8,128)} %fusion.148, f32[8,512]{1,0:T(8,128)S(1)} %dynamic-slice_bitcast_fusion.2, pred[512,3072]{1,0:T(8,128)(4,1)S(1)} %broadcast_compare_fusion.5, bf16[3072,8,64]{0,2,1:T(8,128)(2,1)} %get-tuple-element.509, ...), kind=kOutput, calls=%fused_computation.16.clone.1 | convolution fusion | flops 1673523200 | bytes 105938944 | tf_op jit(solution)/shard_map/while/body/eval_jaxpr/while/body/eval_jaxpr/qhd,khd->hqk/dot_general | solution.py:215
  1810.3 40.6 %multiply_convert_fusion.6 = bf16[8,512,3072]{2,1,0:T(8,128)(2,1)} fusion(f32[8,512,3072]{2,1,0:T(8,128)} %get-tuple-element.431, f32[8,512,3072]{2,1,0:T(8,128)} %fusion.148, f32[8,512]{1,0:T(8,128)S(1)} %get-tuple-element.432, f32[8,512]{1,0:T(8,128)S(1)} %dynamic-slice_bitcast_fusion.2, pred[512,3072]{1,0:T(8,128)(4,1)S(1)} %broadcast_compare_fusion.5), kind=kLoop, calls=%fused_computation.15.clone.1 | loop fusion | flops 75497472 | bytes 127434752 | tf_op jit(solution)/shard_map/while/body/eval_jaxpr/while/body/eval_jaxpr/convert_element_type | solution.py:219
  1882.7 21.8 dynamic_update_slice.45
  1906.8 21.0 fusion.148
  1927.8 24.9 bitcast_add_fusion.5
  1952.7 37.6 %multiply_reduce_fusion.4 = (f32[8,512]{1,0:T(8,128)S(1)}, f32[8,512,3072]{2,1,0:T(8,128)}) fusion(f32[8,512,3072]{2,1,0:T(8,128)} %fusion.148, f32[8,512]{1,0:T(8,128)S(1)} %dynamic-slice_bitcast_fusion.2, pred[512,3072]{1,0:T(8,128)(4,1)S(1)} %broadcast_compare_fusion.5, bf16[3072,8,64]{0,2,1:T(8,128)(2,1)} %get-tuple-element.509, ...), kind=kOutput, calls=%fused_computation.16.clone.1 | convolution fusion | flops 1673523200 | bytes 105938944 | tf_op jit(solution)/shard_map/while/body/eval_jaxpr/while/body/eval_jaxpr/qhd,khd->hqk/dot_general | solution.py:215
  1990.3 40.6 %multiply_convert_fusion.6 = bf16[8,512,3072]{2,1,0:T(8,128)(2,1)} fusion(f32[8,512,3072]{2,1,0:T(8,128)} %get-tuple-element.431, f32[8,512,3072]{2,1,0:T(8,128)} %fusion.148, f32[8,512]{1,0:T(8,128)S(1)} %get-tuple-element.432, f32[8,512]{1,0:T(8,128)S(1)} %dynamic-slice_bitcast_fusion.2, pred[512,3072]{1,0:T(8,128)(4,1)S(1)} %broadcast_compare_fusion.5), kind=kLoop, calls=%fused_computation.15.clone.1 | loop fusion | flops 75497472 | bytes 127434752 | tf_op jit(solution)/shard_map/while/body/eval_jaxpr/while/body/eval_jaxpr/convert_element_type | solution.py:219
  2062.8 21.8 dynamic_update_slice.45
  2146.5 77.2 %reduce-scatter.10.cloned.1.call-done = bf16[1536,1024]{1,0:T(8,128)(2,1)} async-done(((bf16[3072,1024]{1,0:T(8,128)(2,1)}), bf16[1536,1024]{1,0:T(8,128)(2,1)}) %reduce-scatter.10.cloned.1.call-update) | async-done | bytes 3145744 | tf_op jit(solution)/shard_map/reduce_scatter | solution.py:265
  2269.2 35.1 %convolution_bitcast_fusion = f32[6144,1]{1,0:T(8,128)} fusion(pred[1536,1]{0,1:T(4,128)(4,1)S(1)} %reshape.351, f32[1536,6144]{1,0:T(8,128)} %fusion.46), kind=kOutput, calls=%fused_computation.69 | convolution fusion | flops 113246208 | bytes 37774848
  2354.9 50.2 %reduce-scatter.12.cloned.1.call-done = bf16[1024,1024]{1,0:T(8,128)(2,1)} async-done(((bf16[1024,2048]{1,0:T(8,128)(2,1)}), bf16[1024,1024]{1,0:T(8,128)(2,1)}) %reduce-scatter.12.cloned.1.call-update) | async-done | bytes 2097168 | tf_op jit(solution)/shard_map/reduce_scatter | solution.py:179
  2405.1 57.3 %reduce-scatter.14.cloned.1.call-done = bf16[1024,1024]{1,0:T(8,128)(2,1)} async-done(((bf16[2048,1024]{1,0:T(8,128)(2,1)}), bf16[1024,1024]{1,0:T(8,128)(2,1)}) %reduce-scatter.14.cloned.1.call-update) | async-done | bytes 2097168 | tf_op jit(solution)/shard_map/reduce_scatter | solution.py:185
  2469.7 42.2 %all-reduce.1 = (f32[6144]{0:T(1024)S(1)}, f32[3,1024]{1,0:T(4,128)S(1)}, f32[1024]{0:T(1024)}, f32[2048]{0:T(1024)S(1)}, f32[1024]{0:T(1024)}) all-reduce(f32[6144]{0:T(1024)S(1)} %dynamic_update_slice.32, f32[3,1024]{1,0:T(4,128)S(1)} %constant_dynamic-update-slice_fusion.1, ...), channel_id=1, replica_groups=mesh['dp'=16,'head'=2] {'dp','head'}, use_global_device_ids=true, to_apply=%region_20.21 | all-reduce | flops 13312 | bytes 106496 | tf_op jit(solution)/shard_map/psum | solution.py:310
  2526.7 207.5 %all-reduce.5.cloned.1.call-done = (bf16[1024,3072]{1,0:T(8,128)(2,1)}, bf16[1024,3,512]{2,0,1:T(8,128)(2,1)}, bf16[512,1024]{1,0:T(8,128)(2,1)}, bf16[1024,1024]{1,0:T(8,128)(2,1)}, bf16[1024,1024]{1,0:T(8,128)(2,1)}) async-done(((bf16[1024,3072]{1,0:T(8,128)(2,1)}, bf16[1024,3,512]{2,0,1:T(8,128)(2,1)}, bf16[512,1024]{1,0:T(8,128)(2,1)}, bf16[1024,1024]{1,0:T(8,128)(2,1)}, bf16[1024,1024]{1,0:T(8,128)(2,1)}), ...) | async-done | bytes 14680080 | tf_op jit(solution)/shard_map/psum | solution.py:294
  (335 shorter events, 571.2 us)
Async XLA Ops:
  7.2 578.4 %copy-start = (bf16[512,1024]{1,0:T(8,128)(2,1)S(1)}, bf16[512,1024]{1,0:T(8,128)(2,1)}, u32[]{:S(2)}) copy-start(bf16[512,1024]{1,0:T(8,128)(2,1)} %param.25) | copy-start | bytes 3145732
  7.2 7.1 copy-start.35
  7.2 115.0 %all-gather.6.cloned.1.call-start = ((), (), s32[]{:S(2)}) async-start(), calls=%async_computation.5 | async-start | bytes 9437184 | tf_op jit(solution)/shard_map/all_gather | solution.py:92
  8.6 6.6 copy-start.37
  8.6 5.7 copy-start.10
  8.6 6.6 copy-start.46
  11.2 22.0 copy-start.23
  14.3 18.9 copy-start.27
  20.6 12.6 copy-start.3
  33.2 7.0 copy-start.47
  39.9 697.1 %reduce-scatter.8.cloned.1.call-start = ((), (), s32[]{:S(2)}) async-start(), calls=%async_computation.6 | async-start | bytes 18874368 | tf_op jit(solution)/shard_map/reduce_scatter | solution.py:138
  47.7 116.1 %copy-start.12 = (f32[3072,64]{0,1:T(8,128)}, f32[3072,64]{0,1:T(8,128)S(1)}, u32[]{:S(2)}) copy-start(f32[3072,64]{0,1:T(8,128)S(1)} %get-tuple-element.300) | copy-start | bytes 2359300
  47.7 116.1 %copy-start.15 = (f32[3072,64]{0,1:T(8,128)}, f32[3072,64]{0,1:T(8,128)S(1)}, u32[]{:S(2)}) copy-start(f32[3072,64]{0,1:T(8,128)S(1)} %get-tuple-element.301) | copy-start | bytes 2359300
  135.3 6.4 copy-start.8
  163.8 11.9 copy-start.22
  200.2 22.0 copy-start.2
  267.2 22.0 copy-start.2
  334.2 22.0 copy-start.2
  401.2 22.0 copy-start.2
  468.2 22.0 copy-start.2
  535.1 22.0 copy-start.2
  592.3 203.0 %all-gather.8.cloned.1.call-start = ((), (), s32[]{:S(2)}) async-start(), calls=%async_computation.7 | async-start | bytes 6291456 | tf_op jit(solution)/shard_map/all_gather | solution.py:148
  593.0 260.4 %all-gather.10.cloned.1.call-start = ((), (), s32[]{:S(2)}) async-start(), calls=%async_computation.8 | async-start | bytes 6291456 | tf_op jit(solution)/shard_map/all_gather | solution.py:150
  593.6 405.8 %all-gather.12.cloned.1.call-start = ((), (), s32[]{:S(2)}) async-start(), calls=%async_computation.9 | async-start | bytes 9437184 | tf_op jit(solution)/shard_map/all_gather | solution.py:194
  593.7 149.9 %copy-start.39 = (f32[1024]{0:T(1024)}, f32[1024]{0:T(1024)S(1)}, u32[]{:S(2)}) copy-start(f32[1024]{0:T(1024)S(1)} %convert_element_type.167) | copy-start | bytes 12292
  593.7 295.1 %copy-start.43 = (f32[1024]{0:T(1024)}, f32[1024]{0:T(1024)S(1)}, u32[]{:S(2)}) copy-start(f32[1024]{0:T(1024)S(1)} %convert_element_type.171) | copy-start | bytes 12292
  743.7 145.1 %copy-start.25 = (f32[1536]{0:T(1024)}, f32[1536]{0:T(1024)S(1)}, u32[]{:S(2)}) copy-start(f32[1536]{0:T(1024)S(1)} %broadcast_multiply_fusion.4) | copy-start | bytes 18436
  748.0 140.8 %copy-start.31 = (f32[1536]{0:T(1024)}, f32[1536]{0:T(1024)S(1)}, u32[]{:S(2)}) copy-start(f32[1536]{0:T(1024)S(1)} %fusion.67) | copy-start | bytes 18436
  795.3 79.9 %slice-start.2 = ((s8[6291456]{0:T(1024)(128)(4,1)}), s8[2097152]{0:T(1024)(128)(4,1)S(1)}, s32[]{:S(2)}) async-start(s8[6291456]{0:T(1024)(128)(4,1)} %bitcast.141), calls=%async_computation.17 | async-start | bytes 4194304
  853.5 21.8 slice-start.3
  853.5 21.8 copy-start.52
  910.3 8.6 copy-start.33
  918.9 1304.8 %reduce-scatter.10.cloned.1.call-start = ((), (), s32[]{:S(2)}) async-start(), calls=%async_computation.10 | async-start | bytes 9437184 | tf_op jit(solution)/shard_map/reduce_scatter | solution.py:265
  2094.3 9.4 copy-start.16
  2115.5 5.9 slice-start
  2125.9 8.2 copy-start.19
  2146.4 77.3 %copy-start.24 = (f32[1536]{0:T(1024)S(1)}, f32[1536]{0:T(1024)}, u32[]{:S(2)}) copy-start(f32[1536]{0:T(1024)} %copy-done.23) | copy-start | bytes 18436
  2146.4 202.5 %reduce-scatter.16.cloned.1.call-start = ((), (), s32[]{:S(2)}) async-start(), calls=%async_computation.13 | async-start | bytes 4718592 | tf_op jit(solution)/shard_map/reshape.47
  2146.5 83.8 %copy-start.30 = (f32[1536]{0:T(1024)S(1)}, f32[1536]{0:T(1024)}, u32[]{:S(2)}) copy-start(f32[1536]{0:T(1024)} %copy-done.29) | copy-start | bytes 18436
  2223.7 6.6 copy-start.9
  2233.9 9.5 copy-start.7
  2233.9 9.5 copy-start.34
  2233.9 9.5 copy-start.40
  2233.9 21.5 slice-start.8
  2233.9 24.8 slice-start.4
  2243.4 12.0 slice-start.9
  2243.4 15.3 slice-start.5
  2304.3 100.9 %reduce-scatter.12.cloned.1.call-start = ((), (), s32[]{:S(2)}) async-start(), calls=%async_computation.11 | async-start | bytes 6291456 | tf_op jit(solution)/shard_map/reduce_scatter | solution.py:179
  2315.7 11.3 copy-start.45
  2315.7 146.7 %reduce-scatter.14.cloned.1.call-start = ((), (), s32[]{:S(2)}) async-start(), calls=%async_computation.12 | async-start | bytes 6291456 | tf_op jit(solution)/shard_map/reduce_scatter | solution.py:185
  2327.0 8.4 slice-start.10
  2327.0 407.2 %all-reduce.5.cloned.1.call-start = ((), (), s32[]{:S(2)}) async-start(), calls=%async_computation.14 | async-start | bytes 29360128 | tf_op jit(solution)/shard_map/psum | solution.py:294
  2327.1 8.3 slice-start.11
  2327.1 8.3 slice-start.12
  2462.4 7.3 copy-start.41
  2462.4 7.3 copy-start.42
  2462.4 50.8 %copy-start.17 = (f32[3072,1]{1,0:T(8,128)S(1)}, f32[3072,1]{1,0:T(8,128)}, u32[]{:S(2)}) copy-start(f32[3072,1]{1,0:T(8,128)} %reduce-scatter.16.cloned.1.call-done) | copy-start | bytes 36868
  2462.5 63.6 %copy-start.36 = (bf16[1,1024]{1,0:T(2,128)(2,1)S(1)}, bf16[1,1024]{1,0:T(2,128)(2,1)}, u32[]{:S(2)}) copy-start(bf16[1,1024]{1,0:T(2,128)(2,1)} %param.19) | copy-start | bytes 6148
  2462.5 63.6 %copy-start.38 = (f32[1,1024]{1,0:T(1,128)S(1)}, f32[1,1024]{1,0:T(1,128)}, u32[]{:S(2)}) copy-start(f32[1,1024]{1,0:T(1,128)} %copy-done.37) | copy-start | bytes 12292
  2734.2 7.2 copy-start.21
  2734.2 9.6 slice-start.13
  2737.1 6.7 slice-start.14
  2743.8 6.5 copy-start.20
  2743.8 10.1 copy-start.1
  (20 other events, 52.7 us)
Sparse Core Ops, SparseCore 0:
  40.0 82.1 all-gather.5
  592.4 144.5 reduce-scatter.7
  738.5 56.7 all-gather.7
  796.7 56.7 all-gather.9
  919.0 80.3 all-gather.11
  2146.5 77.1 reduce-scatter.9
  2304.4 43.4 reduce-scatter.15
  2350.7 54.3 reduce-scatter.11
  2408.0 54.3 reduce-scatter.13
  2467.8 266.3 all-reduce.4
where the time goes:
time: 2770 us; the launch traced here: 2760 us
  matrix products  1140 us (41%)
  waiting for transfers between devices  765 us (28%)
  other arithmetic  554 us (20%)
  local copies, waits for them, and re-layouts  215 us (8%)
  blocking collectives  62 us (2%)
    dot_general x12, matrix products, block_scores(): jnp.einsum('qhd,khd->hqk', query_block, key_row, preferred_element_type=j...  257 us
    convert_element_type x6, other arithmetic, back_block(): grad_scores = (probs * (grad_probs - centre)).astype(jnp.bfloat16)  244 us
    dot_general x6, matrix products, back_block(): jnp.einsum('qhd,khd->hqk', grad_block, value_row, preferred_element_type=...  226 us
    psum x1, waiting for transfers between devices, on_device(): lax.psum(grad_mod_weight.astype(jnp.bfloat16), 'dp').astype(jnp.float32)  208 us
    dot_general x6, matrix products, back_block(): jnp.einsum('hqk,qhd->khd', probs.astype(jnp.bfloat16), grad_block, prefer...  148 us
    reduce_scatter x1, waiting for transfers between devices, on_device(): lax.psum_scatter(jnp.dot(part, output_weight, preferred_element_type=jnp....  139 us
    dynamic_update_slice x12, local copies, waits for them, and re-layouts, attend_row(): lax.scan(attend_block, jnp.zeros((), jnp.float32), block_ids)  137 us
    reduce_sum x6, other arithmetic, attend_block(): mass = jnp.sum(expo, axis=-1, keepdims=True)  132 us
  transfers between devices with their start and end apart: 10, of which 9 were waited for; matrix products, arithmetic and copies ran while one was open for 4% of the time, Pallas kernels for 0%

commit v1 on v0

v1 whole, which is shorter than its diff:
```python
import math
import jax
import jax.numpy as jnp
from jax import lax
from jax.experimental import pallas as pl
from jax.experimental.pallas import tpu as pltpu
from jax.sharding import PartitionSpec as P

HDIM = 64
QB = 256
CK = 512
CT = 256
BIG = 1e30
SCALE = HDIM ** -0.5
TWO = SCALE * math.log2(math.e)
NT = (((1,), (1,)), ((), ()))
NN = (((1,), (0,)), ((), ()))

def mm(a, b, dims):
    return lax.dot_general(a, b, dims, preferred_element_type=jnp.float32)

def low_half(rows):
    return lax.broadcasted_iota(jnp.int32, (rows, 128), 1) < HDIM

def span_table(seg, seq):
    nq = seq // QB
    ids = jnp.arange(8, dtype=jnp.int32)
    begin = jnp.sum(seg[None, :] < ids[:, None], axis=1)
    end = jnp.sum(seg[None, :] <= ids[:, None], axis=1)
    blocks = seg.reshape(nq, QB)
    first = (blocks[:, :1] == ids[None, :])
    last = (blocks[:, QB - 1:] == ids[None, :])
    lo = jnp.sum(jnp.where(first, begin[None, :], 0), axis=1)
    hi = jnp.sum(jnp.where(last, end[None, :], 0), axis=1)
    lo = lo // 16 * 16
    total = hi - lo
    full = (total + (CK - CT - 1)) // CK
    tail = (total > full * CK).astype(jnp.int32)
    return jnp.concatenate([lo, full, tail]).astype(jnp.int32)

def features(seg):
    lane = jnp.arange(128, dtype=jnp.int32) % HDIM
    same = seg[:, None] == lane[None, :]
    used = (lane < 8)[None, :]
    fq = jnp.where(same & used, 1.0, 0.0).astype(jnp.bfloat16)
    fk = jnp.where(used & ~same, -BIG, 0.0).astype(jnp.bfloat16)
    return fq, fk

def split_keys(k_ref, fk_ref, ka, kb, seq):
    lowm = low_half(QB)
    def one(i, _):
        rows = pl.ds(pl.multiple_of(i * QB, QB), QB)
        k = k_ref[0, rows, :]
        f = fk_ref[rows, :]
        ka[rows, :] = jnp.where(lowm, k, f)
        kb[rows, :] = jnp.where(lowm, f, k)
        return 0
    lax.fori_loop(0, seq // QB, one, 0)

def pad_fill(ka, kb, seq):
    lane = lax.broadcasted_iota(jnp.int32, (CK, 128), 1)
    ka[seq:, :] = jnp.where((lane >= HDIM) & (lane < HDIM + 8), -BIG, 0.0).astype(jnp.bfloat16)
    kb[seq:, :] = jnp.where(lane < 8, -BIG, 0.0).astype(jnp.bfloat16)

def fwd_kernel(tab, q_ref, k_ref, v_ref, fq_ref, fk_ref, o_ref, lse_ref, ka, kb, vs):
    seq = q_ref.shape[1]
    nq = seq // QB
    lowm = low_half(QB)
    @pl.when(pl.program_id(0) == 0)
    def _():
        pad_fill(ka, kb, seq)
        vs[seq:, :] = jnp.zeros((CK, 128), jnp.bfloat16)
    split_keys(k_ref, fk_ref, ka, kb, seq)
    vs[:seq, :] = v_ref[0]

    def block(i, _):
        rows = pl.ds(pl.multiple_of(i * QB, QB), QB)
        q = q_ref[0, rows, :]
        f = fq_ref[rows, :]
        qa = jnp.where(lowm, q, f)
        qb = jnp.where(lowm, f, q)
        lo = tab[i]
        full = tab[nq + i]
        tail = tab[2 * nq + i]

        def chunk(start, size, carry):
            ma, la, oa, mb, lb, ob = carry
            keys = pl.ds(pl.multiple_of(start, 16), size)
            vt = vs[keys, :].T
            sa = mm(ka[keys, :], qa, NT)
            sb = mm(kb[keys, :], qb, NT)
            def half(s, m, l, o, vh):
                new = jnp.maximum(m, jnp.max(s, axis=0, keepdims=True) * TWO)
                p = jnp.exp2(s * TWO - new)
                fade = jnp.exp2(m - new)
                l = l * fade + jnp.sum(p, axis=0, keepdims=True)
                o = o * fade + mm(vh, p.astype(jnp.bfloat16), NN)
                return new, l, o
            return half(sa, ma, la, oa, vt[:HDIM]) + half(sb, mb, lb, ob, vt[HDIM:])

        m0 = jnp.full((1, QB), -1e38, jnp.float32)
        l0 = jnp.zeros((1, QB), jnp.float32)
        o0 = jnp.zeros((HDIM, QB), jnp.float32)
        carry = lax.fori_loop(0, full, lambda j, c: chunk(lo + j * CK, CK, c), (m0, l0, o0, m0, l0, o0))
        carry = lax.fori_loop(0, tail, lambda j, c: chunk(lo + full * CK, CT, c), carry)
        ma, la, oa, mb, lb, ob = carry
        o = jnp.concatenate([oa / la, ob / lb], axis=0)
        o_ref[rows, :] = o.T.astype(jnp.bfloat16)
        cols = rows
        lse_ref[0, 0:1, cols] = ma + jnp.log2(la)
        lse_ref[0, 1:2, cols] = mb + jnp.log2(lb)
        return 0
    lax.fori_loop(0, nq, block, 0)

def attend_fwd(tab, qkv, fq, fk, first=0, pairs=None):
    _, seq, inner = qkv.shape
    pairs = pairs or inner // 128
    part = lambda t: pl.BlockSpec((1, seq, 128), lambda p, tab: (t, 0, first + p))
    whole = pl.BlockSpec((seq, 128), lambda p, tab: (0, 0))
    return pl.pallas_call(
        fwd_kernel,
        grid_spec=pltpu.PrefetchScalarGridSpec(
            num_scalar_prefetch=1, grid=(pairs,),
            in_specs=[part(0), part(1), part(2), whole, whole],
            out_specs=[pl.BlockSpec((seq, 128), lambda p, tab: (0, p)), pl.BlockSpec((1, 8, seq), lambda p, tab: (p, 0, 0))],
            scratch_shapes=[pltpu.VMEM((seq + CK, 128), jnp.bfloat16)] * 3),
        out_shape=[jax.ShapeDtypeStruct((seq, pairs * 128), jnp.bfloat16), jax.ShapeDtypeStruct((pairs, 8, seq), jnp.float32)],
        compiler_params=pltpu.CompilerParams(vmem_limit_bytes=60 << 20),
        name="attend_fwd",
    )(tab, qkv, qkv, qkv, fq, fk)

def turn_back(g, cos, sin):
    u = g * sin
    lane = lax.broadcasted_iota(jnp.int32, g.shape, 1) % HDIM
    return g * cos + jnp.where(lane < HDIM // 2, pltpu.roll(u, 96, 1), -pltpu.roll(u, 32, 1))

def bwd_kernel(tab, q_ref, k_ref, v_ref, fq_ref, fk_ref, o_ref, do_ref, lse_ref, cos_ref, sin_ref, g_ref, ka, kb, ks, vs, dk, dv):
    seq = q_ref.shape[1]
    nq = seq // QB
    lowm = low_half(QB)
    @pl.when(pl.program_id(0) == 0)
    def _():
        pad_fill(ka, kb, seq)
        vs[seq:, :] = jnp.zeros((CK, 128), jnp.bfloat16)
        ks[seq:, :] = jnp.zeros((CK, 128), jnp.bfloat16)
    split_keys(k_ref, fk_ref, ka, kb, seq)
    vs[:seq, :] = v_ref[0]
    ks[:seq, :] = k_ref[0]
    dk[...] = jnp.zeros_like(dk)
    dv[...] = jnp.zeros_like(dv)

    def block(i, _):
        rows = pl.ds(pl.multiple_of(i * QB, QB), QB)
        q = q_ref[0, rows, :]
        f = fq_ref[rows, :]
        qa = jnp.where(lowm, q, f)
        qb = jnp.where(lowm, f, q)
        none = jnp.zeros_like(q)
        g = do_ref[rows, :]
        ga = jnp.where(lowm, g, none)
        gb = jnp.where(lowm, none, g)
        gcat = jnp.concatenate([ga, gb], axis=0)
        qcat = jnp.concatenate([jnp.where(lowm, q, none), jnp.where(lowm, none, q)], axis=0)
        prod = (g.astype(jnp.float32) * o_ref[rows, :].astype(jnp.float32)).T
        da = jnp.sum(prod[:HDIM], axis=0, keepdims=True)
        db = jnp.sum(prod[HDIM:], axis=0, keepdims=True)
        lsa = lse_ref[0, 0:1, rows]
        lsb = lse_ref[0, 1:2, rows]
        lo = tab[i]
        full = tab[nq + i]
        tail = tab[2 * nq + i]

        def chunk(start, size, carry):
            dqa, dqb = carry
            keys = pl.ds(pl.multiple_of(start, 16), size)
            v = vs[keys, :]
            kt = ks[keys, :].T
            def half(kx, qx, gx, ls, dl):
                s = mm(kx[keys, :], qx, NT)
                dp = mm(v, gx, NT)
                p = jnp.exp2(s * TWO - ls)
                ds = (p * (dp - dl)).astype(jnp.bfloat16)
                return p.astype(jnp.bfloat16), ds
            pa, dsa = half(ka, qa, ga, lsa, da)
            pb, dsb = half(kb, qb, gb, lsb, db)
            dv[keys, :] += mm(jnp.concatenate([pa, pb], axis=1), gcat, NN)
            dk[keys, :] += mm(jnp.concatenate([dsa, dsb], axis=1), qcat, NN)
            return dqa + mm(kt[:HDIM], dsa, NN), dqb + mm(kt[HDIM:], dsb, NN)

        z = jnp.zeros((HDIM, QB), jnp.float32)
        carry = lax.fori_loop(0, full, lambda j, c: chunk(lo + j * CK, CK, c), (z, z))
        carry = lax.fori_loop(0, tail, lambda j, c: chunk(lo + full * CK, CT, c), carry)
        dq = jnp.concatenate(carry, axis=0).T * SCALE
        g_ref[0, rows, :] = turn_back(dq, cos_ref[rows, :], sin_ref[rows, :]).astype(jnp.bfloat16)
        return 0
    lax.fori_loop(0, nq, block, 0)

    def finish(i, _):
        rows = pl.ds(pl.multiple_of(i * QB, QB), QB)
        g_ref[1, rows, :] = turn_back(dk[rows, :] * SCALE, cos_ref[rows, :], sin_ref[rows, :]).astype(jnp.bfloat16)
        g_ref[2, rows, :] = dv[rows, :].astype(jnp.bfloat16)
        return 0
    lax.fori_loop(0, nq, finish, 0)

def attend_bwd(tab, qkv, fq, fk, o, do, lse, cos, sin, first=0, pairs=None):
    _, seq, inner = qkv.shape
    pairs = pairs or inner // 128
    part = lambda t: pl.BlockSpec((1, seq, 128), lambda p, tab: (t, 0, first + p))
    whole = pl.BlockSpec((seq, 128), lambda p, tab: (0, 0))
    cols = pl.BlockSpec((seq, 128), lambda p, tab: (0, p))
    return pl.pallas_call(
        bwd_kernel,
        grid_spec=pltpu.PrefetchScalarGridSpec(
            num_scalar_prefetch=1, grid=(pairs,),
            in_specs=[part(0), part(1), part(2), whole, whole, cols, cols, pl.BlockSpec((1, 8, seq), lambda p, tab: (p, 0, 0)), whole, whole],
            out_specs=pl.BlockSpec((3, seq, 128), lambda p, tab: (0, 0, p)),
            scratch_shapes=[pltpu.VMEM((seq + CK, 128), jnp.bfloat16)] * 4 + [pltpu.VMEM((seq + CK, 128), jnp.float32)] * 2),
        out_shape=jax.ShapeDtypeStruct((3, seq, pairs * 128), jnp.bfloat16),
        compiler_params=pltpu.CompilerParams(vmem_limit_bytes=60 << 20),
        name="attend_bwd",
    )(tab, qkv, qkv, qkv, fq, fk, o, do, lse, cos, sin)

def normalize(x):
    mean = jnp.mean(x, axis=-1, keepdims=True)
    centre = x - mean
    var = jnp.mean(centre * centre, axis=-1, keepdims=True)
    rstd = lax.rsqrt(var + 1e-06)
    return centre * rstd, rstd

def turn(v, cos, sin):
    lane = lax.broadcasted_iota(jnp.int32, v.shape, 1) % HDIM
    return v * cos + jnp.where(lane < HDIM // 2, -pltpu.roll(v, 96, 1), pltpu.roll(v, 32, 1)) * sin

def qkv_kernel(x_ref, scale_ref, shift_ref, w_ref, b_ref, cos_ref, sin_ref, qkv_ref, n_ref):
    inner = qkv_ref.shape[2]
    unit, _ = normalize(x_ref[...].astype(jnp.float32))
    low = (unit * (1.0 + scale_ref[...]) + shift_ref[...]).astype(jnp.bfloat16)
    n_ref[...] = low
    cos, sin = cos_ref[...], sin_ref[...]
    for t in range(3):
        part = slice(t * inner, (t + 1) * inner)
        out = mm(low, w_ref[:, part], NN) + b_ref[:, part]
        for c in range(inner // 128):
            v = out[:, c * 128:(c + 1) * 128]
            if t < 2:
                v = turn(v, cos, sin)
            qkv_ref[t, :, c * 128:(c + 1) * 128] = v.astype(jnp.bfloat16)

def project(x, scale, shift, w, b, cos, sin):
    seq, width = x.shape
    inner = w.shape[1] // 3
    step = 256
    row = pl.BlockSpec((step, width), lambda i: (i, 0))
    table = pl.BlockSpec((step, 128), lambda i: (i, 0))
    const = lambda a: pl.BlockSpec(a.shape, lambda i: (0, 0))
    return pl.pallas_call(
        qkv_kernel,
        grid=(seq // step,),
        in_specs=[row, const(scale), const(shift), const(w), const(b), table, table],
        out_specs=[pl.BlockSpec((3, step, inner), lambda i: (0, i, 0)), row],
        out_shape=[jax.ShapeDtypeStruct((3, seq, inner), jnp.bfloat16), jax.ShapeDtypeStruct((seq, width), jnp.bfloat16)],
        compiler_params=pltpu.CompilerParams(vmem_limit_bytes=60 << 20),
        name="project",
    )(x, scale, shift, w, b, cos, sin)

def relative(axis, size):
    return lambda x, r: x if r % size == 0 else lax.ppermute(x, axis, [(i, (i + r) % size) for i in range(size)])

def on_device(
    inputs,
    time_embed,
    segment_ids,
    modulator_weight,
    modulator_bias,
    projection_weight,
    projection_bias,
    output_weight,
    output_bias,
    expand_weight,
    expand_bias,
    contract_weight,
    contract_bias,
    cotangent,
):
    f32, bf16 = jnp.float32, jnp.bfloat16
    n = lax.axis_size("head")
    ndp = lax.axis_size("dp")
    me = lax.axis_index("head")
    mine = lax.axis_index("dp")
    move = relative("head", n)
    frames_here, width = inputs.shape
    seq = frames_here * n
    inner = projection_weight.shape[2]
    hidden_here = expand_weight.shape[1]
    local_mod = modulator_weight.shape[1]
    groups = inner // 128
    owner = [lax.rem(me - r + n, n) for r in range(n)]
    source = [lax.rem(me + r, n) for r in range(n)]

    gathered = lax.all_gather(inputs, "head", axis=0, tiled=True)

    def whole_weight(w):
        rows = w.shape[0] // ndp
        cut = lax.dynamic_slice_in_dim(w, mine * rows, rows, 0)
        return [w] + [lax.all_gather(move(cut, r), "dp", axis=0, tiled=True) for r in range(1, n)]

    def total_grad(parts):
        cut = [lax.psum_scatter(p.astype(bf16), "dp", scatter_dimension=0, tiled=True) for p in parts]
        own = cut[0].astype(f32)
        for r in range(1, n):
            own = own + move(cut[r], -r).astype(f32)
        return lax.all_gather(own.astype(bf16), "dp", axis=0, tiled=True).astype(f32)

    embeds = time_embed.astype(f32)
    silu_low = jax.nn.silu(embeds).astype(bf16)
    own_mod = jnp.dot(silu_low, modulator_weight, preferred_element_type=f32) + modulator_bias.astype(f32)
    modulation = lax.all_gather(own_mod, "head", axis=1, tiled=True)
    shift_a, scale_a, gate_a, shift_f, scale_f, gate_f = jnp.split(modulation, 6, axis=1)
    embeds_all = lax.all_gather(time_embed, "dp", axis=0, tiled=True).astype(f32)
    silu_all = jax.nn.silu(embeds_all).astype(bf16).astype(f32)

    seg = segment_ids[0]
    tab = span_table(seg, seq)
    fq, fk = features(seg)
    half = HDIM // 2
    freqs = 10000.0 ** (-jnp.arange(half, dtype=f32) * 2.0 / HDIM)
    angles = jnp.arange(seq, dtype=f32)[:, None] * freqs[None, :]
    cosine = jnp.tile(jnp.cos(angles), (1, 4))
    sine = jnp.tile(jnp.sin(angles), (1, 4))

    out_all = whole_weight(output_weight)
    expand_all = whole_weight(expand_weight)
    contract_all = whole_weight(contract_weight)
    expand_bias_all = [move(expand_bias, r) for r in range(n)]

    weight_proj = projection_weight.reshape(width, 3 * inner)
    bias_proj = projection_bias.astype(f32).reshape(1, 3 * inner)
    qkv, normed_a = project(gathered, scale_a, shift_a, weight_proj, bias_proj, cosine, sine)

    attended, log_mass, attended_here = [], [], []
    for g in range(groups):
        o, lse = attend_fwd(tab, qkv, fq, fk, g, 1)
        attended.append(o)
        log_mass.append(lse)
        attended_here.append([
            move(lax.dynamic_slice_in_dim(o, source[r] * frames_here, frames_here, 0), r) for r in range(n)
        ])
    att_rel = [jnp.concatenate([attended_here[g][r] for g in range(groups)], axis=1) for r in range(n)]

    att_cat = jnp.concatenate(att_rel, axis=1)
    out_cat = jnp.concatenate(out_all, axis=0)
    expand_cat = jnp.concatenate(expand_all, axis=1)
    contract_cat = jnp.concatenate(contract_all, axis=0)
    expand_bias_cat = jnp.concatenate(expand_bias_all, axis=0).astype(f32)

    frames = inputs.astype(f32)
    grad_out = cotangent.astype(f32)
    branch_a = jnp.dot(att_cat, out_cat, preferred_element_type=f32) + output_bias.astype(f32)
    middle = frames + gate_a * branch_a
    unit_f, rstd_f = normalize(middle)
    normed_f = (unit_f * (1.0 + scale_f) + shift_f).astype(bf16)
    hidden_pre = jnp.dot(normed_f, expand_cat, preferred_element_type=f32) + expand_bias_cat
    hidden_full, gelu_pull = jax.vjp(lambda v: jax.nn.gelu(v, approximate=True), hidden_pre)
    hidden = hidden_full.astype(bf16)
    branch_f = jnp.dot(hidden, contract_cat, preferred_element_type=f32) + contract_bias.astype(f32)
    layer_output = (middle + gate_f * branch_f).astype(bf16)
    row_gate_f = jnp.sum(grad_out * branch_f, axis=0)
    grad_branch_f = (gate_f * grad_out).astype(bf16)
    bias_down = jnp.sum(grad_branch_f.astype(f32), axis=0)
    grad_hidden = jnp.einsum("fd,hd->fh", grad_branch_f, contract_cat, preferred_element_type=f32)
    grad_pre = gelu_pull(grad_hidden)[0].astype(bf16)
    contract_part = jnp.einsum("fh,fd->hd", hidden, grad_branch_f, preferred_element_type=f32)
    expand_part = jnp.einsum("fd,fh->dh", normed_f, grad_pre, preferred_element_type=f32)
    bias_up = jnp.sum(grad_pre.astype(f32), axis=0)
    grad_normed_f = jnp.einsum("fh,dh->fd", grad_pre, expand_cat, preferred_element_type=f32)

    def norm_back(g, unit, rstd, scale):
        u = g * (1.0 + scale)
        return rstd * (u - jnp.mean(u, axis=-1, keepdims=True) - unit * jnp.mean(u * unit, axis=-1, keepdims=True))

    grad_middle = grad_out + norm_back(grad_normed_f, unit_f, rstd_f, scale_f)
    row_shift_f = jnp.sum(grad_normed_f, axis=0)
    row_scale_f = jnp.sum(grad_normed_f * unit_f, axis=0)
    row_gate_a = jnp.sum(grad_middle * branch_a, axis=0)
    grad_branch_a = (gate_a * grad_middle).astype(bf16)
    bias_out = jnp.sum(grad_branch_a.astype(f32), axis=0)
    grad_att = jnp.einsum("fd,id->fi", grad_branch_a, out_cat, preferred_element_type=f32).astype(bf16)
    output_part = jnp.einsum("fi,fd->id", att_cat, grad_branch_a, preferred_element_type=f32)

    grad_projected = []
    for g in range(groups):
        whole = jnp.zeros((seq, 128), bf16)
        for r in range(n):
            piece = move(grad_att[:, r * inner + g * 128:r * inner + (g + 1) * 128], -r)
            whole = lax.dynamic_update_slice_in_dim(whole, piece, source[r] * frames_here, 0)
        grad_projected.append(attend_bwd(tab, qkv, fq, fk, attended[g], whole, log_mass[g], cosine, sine, g, 1))

    grad_output = total_grad([output_part[r * inner:(r + 1) * inner] for r in range(n)])
    grad_expand = total_grad([expand_part[:, r * hidden_here:(r + 1) * hidden_here] for r in range(n)])
    grad_contract = total_grad([contract_part[r * hidden_here:(r + 1) * hidden_here] for r in range(n)])

    g_all = jnp.concatenate(grad_projected, axis=2)
    flat = jnp.concatenate([g_all[0], g_all[1], g_all[2]], axis=1)
    grad_projection = jnp.einsum("fd,fc->dc", normed_a, flat, preferred_element_type=f32)
    bias_proj_grad = jnp.sum(flat.astype(f32), axis=0)
    grad_normed_a = lax.psum_scatter(
        jnp.einsum("fc,dc->fd", flat, weight_proj, preferred_element_type=f32).astype(bf16),
        "head", scatter_dimension=0, tiled=True,
    ).astype(f32)
    grad_projection = lax.psum(grad_projection.astype(bf16), "dp").astype(f32).reshape(width, 3, inner)
    unit_a, rstd_a = normalize(frames)
    grad_inputs = grad_middle + norm_back(grad_normed_a, unit_a, rstd_a, scale_a)
    row_shift_a = jnp.sum(grad_normed_a, axis=0)
    row_scale_a = jnp.sum(grad_normed_a * unit_a, axis=0)

    early = jnp.concatenate([bias_proj_grad, bias_out, bias_down, bias_up, row_shift_a, row_scale_a, row_gate_a, row_shift_f, row_scale_f, row_gate_f])
    table = lax.all_gather(early, ("dp", "head"), axis=0)
    table = table.reshape(ndp, n, early.shape[0])
    base = 3 * inner
    own_col = lax.dynamic_index_in_dim(table, me, 1, keepdims=False)
    grad_projection_bias = jnp.sum(own_col[:, :base], axis=0).reshape(3, inner)
    both = jnp.sum(table[:, :, base:base + 2 * width], axis=(0, 1))
    grad_output_bias, grad_contract_bias = both[:width], both[width:]
    base = base + 2 * width
    up = jnp.sum(table[:, :, base:base + n * hidden_here], axis=0).reshape(n, n, hidden_here)
    grad_expand_bias = sum(
        lax.dynamic_slice(up, (source[r], r, 0), (1, 1, hidden_here)).reshape(hidden_here) for r in range(n)
    )
    base = base + n * hidden_here
    grad_mod = jnp.sum(lax.dynamic_slice_in_dim(table[:, :, base:], me * local_mod, local_mod, 2), axis=1)
    grad_mod_weight = jnp.dot(silu_all.T, grad_mod, precision=lax.Precision.HIGHEST)
    grad_mod_bias = jnp.sum(grad_mod, axis=0)
    own_row = lax.dynamic_slice_in_dim(grad_mod, mine, 1, 0)
    grad_silu = lax.psum(jnp.sum(modulator_weight.astype(f32) * own_row, axis=1), "head")[None, :]
    _, silu_pull = jax.vjp(jax.nn.silu, embeds)
    grad_embed = silu_pull(grad_silu)[0]
    return (
        layer_output,
        grad_inputs,
        grad_embed,
        grad_mod_weight,
        grad_mod_bias,
        grad_projection,
        grad_projection_bias,
        grad_output,
        grad_output_bias,
        grad_expand,
        grad_expand_bias,
        grad_contract,
        grad_contract_bias,
    )


def solution(mesh):
    in_specs = (
        P(("dp", "head"), None),
        P("dp", None),
        P("dp", None),
        P(None, "head"),
        P("head"),
        P(None, None, "head"),
        P(None, "head"),
        P("head", None),
        P(),
        P(None, "head"),
        P("head"),
        P("head", None),
        P(),
        P(("dp", "head"), None),
    )
    out_specs = (
        P(("dp", "head"), None),
        P(("dp", "head"), None),
        P("dp", None),
        P(None, "head"),
        P("head"),
        P(None, None, "head"),
        P(None, "head"),
        P("head", None),
        P(),
        P(None, "head"),
        P("head"),
        P("head", None),
        P(),
    )
    return jax.shard_map(
        on_device, mesh=mesh, in_specs=in_specs, out_specs=out_specs, check_vma=False
    )
```

time: 2770 us -> 1270 us (0.46)
  matrix products: 1140 us -> 141 us
  other arithmetic: 554 us -> 62.3 us
  Pallas kernels: 0 us -> 283 us
  waiting for transfers between devices: 765 us -> 622 us
  local copies, waits for them, and re-layouts: 215 us -> 84.4 us
  blocking collectives: 62 us -> 31.5 us
    dot_general x56 -> x13, matrix products: 1100 us -> 141 us  [the longest x1 20.5 us: on_device(): jnp.einsum('fd,hd->fh', grad_branch_f, contract_cat, preferred_element_ty...]
    pallas_call x0 -> x9, Pallas kernels: none -> 283 us  [the longest x4 146 us: attend_bwd(): pl.pallas_call(bwd_kernel, grid_spec=pltpu.PrefetchScalarGridSpec(num_sca...]
    convert_element_type x19 -> x12, other arithmetic: 287 us -> 20.7 us  [the longest x3 11.1 us: total_grad(): lax.all_gather(own.astype(bf16), 'dp', axis=0, tiled=True).astype(f32)]
    reduce_sum x15 -> x11, other arithmetic: 185 us -> 18.6 us  [the longest x1 5.54 us: on_device(): bias_proj_grad = jnp.sum(flat.astype(f32), axis=0)]
    dynamic_update_slice x14 -> x7, local copies, waits for them, and re-layouts: 138 us -> 4.58 us  [on_device(): lax.dynamic_update_slice_in_dim(whole, piece, source[r] * frames_here, 0)]
    psum x1, waiting for transfers between devices: 208 us -> 80.2 us  [on_device(): lax.psum(grad_projection.astype(bf16), 'dp').astype(f32)]
    reduce_scatter x4 -> x7, waiting for transfers between devices: 324 us -> 219 us  [the longest x6 147 us: total_grad(): lax.psum_scatter(p.astype(bf16), 'dp', scatter_dimension=0, tiled=True)]
    all_gather x4 -> x8, waiting for transfers between devices: 233 us -> 294 us  [the longest x3 112 us: total_grad(): lax.all_gather(own.astype(bf16), 'dp', axis=0, tiled=True).astype(f32)]
  transfers between devices with their start and end apart: 10 -> 31, of which waited for: 9 -> 20; matrix products, arithmetic and copies ran while one was open for 4% -> 14% of each run, Pallas kernels for 0% -> 12%
where the time goes in v1:
time: 1270 us; the launch traced here: 1260 us
  waiting for transfers between devices  622 us (49%)
  Pallas kernels  283 us (22%)
  matrix products  141 us (11%)
  local copies, waits for them, and re-layouts  84.4 us (7%)
  other arithmetic  62.3 us (5%)
  blocking collectives  31.5 us (2%)
  starting transfers between devices  20.8 us (2%)
  between operations  15 us (1%)
    reduce_scatter x6, waiting for transfers between devices, total_grad(): lax.psum_scatter(p.astype(bf16), 'dp', scatter_dimension=0, tiled=True)  147 us
    pallas_call x4, Pallas kernels, attend_bwd(): pl.pallas_call(bwd_kernel, grid_spec=pltpu.PrefetchScalarGridSpec(num_sca...  146 us
    pallas_call x4, Pallas kernels, attend_fwd(): pl.pallas_call(fwd_kernel, grid_spec=pltpu.PrefetchScalarGridSpec(num_sca...  116 us
    all_gather x3, waiting for transfers between devices, total_grad(): lax.all_gather(own.astype(bf16), 'dp', axis=0, tiled=True).astype(f32)  112 us
    psum x1, waiting for transfers between devices, on_device(): lax.psum(grad_projection.astype(bf16), 'dp').astype(f32)  80.2 us
    all_gather x1, waiting for transfers between devices, on_device(): gathered = lax.all_gather(inputs, 'head', axis=0, tiled=True)  77.4 us
    reduce_scatter x1, waiting for transfers between devices, on_device(): lax.psum_scatter(jnp.einsum('fc,dc->fd', flat, weight_proj, preferred_ele...  71.6 us
    all_gather x3, waiting for transfers between devices, whole_weight(): lax.all_gather(move(cut, r), 'dp', axis=0, tiled=True)  57.7 us
  transfers between devices with their start and end apart: 31, of which 20 were waited for; matrix products, arithmetic and copies ran while one was open for 14% of the time, Pallas kernels for 12%

profile of v1, /device:TPU:0, one launch (start us, length us, event | category | flops | bytes accessed | tf_op | source)
XLA Modules:
  0.0 1259.5 jit_solution(10852829542972796670)
XLA Ops:
  8.1 3.0 collective-permute-start.4
  17.0 2.9 collective-permute-done.5
  23.7 2.9 collective-permute-done.7
  32.2 3.9 fusion.39
  36.1 4.5 all-gather
  42.6 3.1 constant_dynamic-update-slice_fusion.7
  56.0 4.7 copy.65
  60.7 4.6 copy.66.w_ref
  68.2 3.0 copy.67.cos_ref
  72.5 3.1 copy.68.sin_ref
  78.5 18.4 %all-gather.17.cloned.1.call-done = bf16[1024,1024]{1,0:T(8,128)(2,1)} async-done(((bf16[64,1024]{1,0:T(8,128)(2,1)}), bf16[1024,1024]{1,0:T(8,128)(2,1)}) %all-gather.17.cloned.1.call-update) | async-done | bytes 2097168 | tf_op jit(solution)/shard_map/all_gather | solution.py:305
  97.0 3.1 constant_dynamic-update-slice_fusion.6
  100.0 39.3 %all-gather.19.cloned.1.call-done = bf16[1024,1024]{1,0:T(8,128)(2,1)} async-done(((bf16[64,1024]{1,0:T(8,128)(2,1)}), bf16[1024,1024]{1,0:T(8,128)(2,1)}) %all-gather.19.cloned.1.call-update) | async-done | bytes 2097168 | tf_op jit(solution)/shard_map/all_gather | solution.py:305
  139.3 3.1 constant_dynamic-update-slice_fusion.8
  142.4 77.4 %all-gather.13.cloned.1.call-done.x_ref = bf16[3072,1024]{1,0:T(8,128)(2,1)} async-done(((bf16[1536,1024]{1,0:T(8,128)(2,1)}), bf16[3072,1024]{1,0:T(8,128)(2,1)}) %all-gather.13.cloned.1.call-update) | async-done | bytes 6291472 | tf_op jit(solution)/shard_map/all_gather | solution.py:300
  219.8 20.4 %project.1 = (bf16[3,3072,512]{2,1,0:T(8,128)(2,1)}, bf16[3072,1024]{1,0:T(8,128)(2,1)}) custom-call(bf16[3072,1024]{1,0:T(8,128)(2,1)} %all-gather.13.cloned.1.call-done.x_ref, f32[1,1024]{1,0:T(1,128)} %get-tuple-element.129.scale_ref, f32[1,1024]{1,0:T(1,128)} %get-tuple-element.128.shift_ref, bf16[1024,1536]{1,0:T(8,128)(2,1)} %copy.66.w_ref, ...), custom_call_target="tpu_custom_call" | custom-call | tf_op jit(solution)/shard_map/project/pallas_call | solution.py:256
  240.2 29.0 %attend_fwd.7 = (bf16[3072,128]{1,0:T(8,128)(2,1)}, f32[1,8,3072]{2,1,0:T(8,128)}) custom-call(s32[36]{0:T(128)} %pad_add_fusion.tab, bf16[3,3072,512]{2,1,0:T(8,128)(2,1)} %get-tuple-element.23.q_ref.k_ref.v_ref, bf16[3,3072,512]{2,1,0:T(8,128)(2,1)} %get-tuple-element.23.q_ref.k_ref.v_ref, bf16[3,3072,512]{2,1,0:T(8,128)(2,1)} %get-tuple-element.23.q_ref.k_ref.v_ref, ...), custom_call_target="tpu_custom_call" | custom-call | tf_op jit(solution)/shard_map/attend_fwd/pallas_call | solution.py:120
  269.2 29.0 %attend_fwd.6 = (bf16[3072,128]{1,0:T(8,128)(2,1)}, f32[1,8,3072]{2,1,0:T(8,128)}) custom-call(s32[36]{0:T(128)} %pad_add_fusion.tab, bf16[3,3072,512]{2,1,0:T(8,128)(2,1)} %get-tuple-element.23.q_ref.k_ref.v_ref, bf16[3,3072,512]{2,1,0:T(8,128)(2,1)} %get-tuple-element.23.q_ref.k_ref.v_ref, bf16[3,3072,512]{2,1,0:T(8,128)(2,1)} %get-tuple-element.23.q_ref.k_ref.v_ref, ...), custom_call_target="tpu_custom_call" | custom-call | tf_op jit(solution)/shard_map/attend_fwd/pallas_call | solution.py:120
  298.3 29.0 %attend_fwd.5 = (bf16[3072,128]{1,0:T(8,128)(2,1)}, f32[1,8,3072]{2,1,0:T(8,128)}) custom-call(s32[36]{0:T(128)} %pad_add_fusion.tab, bf16[3,3072,512]{2,1,0:T(8,128)(2,1)} %get-tuple-element.23.q_ref.k_ref.v_ref, bf16[3,3072,512]{2,1,0:T(8,128)(2,1)} %get-tuple-element.23.q_ref.k_ref.v_ref, bf16[3,3072,512]{2,1,0:T(8,128)(2,1)} %get-tuple-element.23.q_ref.k_ref.v_ref, ...), custom_call_target="tpu_custom_call" | custom-call | tf_op jit(solution)/shard_map/attend_fwd/pallas_call | solution.py:120
  327.3 29.0 %attend_fwd.4 = (bf16[3072,128]{1,0:T(8,128)(2,1)}, f32[1,8,3072]{2,1,0:T(8,128)}) custom-call(s32[36]{0:T(128)} %pad_add_fusion.tab, bf16[3,3072,512]{2,1,0:T(8,128)(2,1)} %get-tuple-element.23.q_ref.k_ref.v_ref, bf16[3,3072,512]{2,1,0:T(8,128)(2,1)} %get-tuple-element.23.q_ref.k_ref.v_ref, bf16[3,3072,512]{2,1,0:T(8,128)(2,1)} %get-tuple-element.23.q_ref.k_ref.v_ref, ...), custom_call_target="tpu_custom_call" | custom-call | tf_op jit(solution)/shard_map/attend_fwd/pallas_call | solution.py:120
  366.0 3.8 collective-permute-done.1
  369.9 4.1 collective-permute-done.2
  374.1 4.1 collective-permute-done.3
  378.4 7.3 fusion.47
  386.5 3.6 copy-done.17
  390.2 13.2 %multiply_convert_fusion = (bf16[1536,2048]{1,0:T(8,128)(2,1)}, f32[1536,2048]{1,0:T(8,128)}) fusion(f32[2048]{0:T(1024)S(1)} %maximum_convert_fusion, bf16[1024,2048]{1,0:T(8,128)(2,1)S(1)} %copy-done.17, f32[1536,1024]{1,0:T(8,128)S(1)} %get-tuple-element.93, f32[1024]{0:T(1024)S(1)} %bitcast.88, f32[1024]{0:T(1024)S(1)} %bitcast.90, ...), kind=kOutput, calls=%fused_computation.12 | convolution fusion | flops 6481772544 | bytes 29388800 | tf_op jit(solution)/shard_map/dot_general | solution.py:362
  403.4 20.5 %convert_reduce_fusion.1 = (f32[2048]{0:T(1024)}, bf16[1536,2048]{1,0:T(8,128)(2,1)}) fusion(f32[1536,2048]{1,0:T(8,128)} %get-tuple-element.141, f32[2048]{0:T(1024)S(1)} %maximum_convert_fusion, bf16[2048,1024]{1,0:T(8,128)(2,1)S(1)} %copy-done.16, bf16[1536,1024]{1,0:T(8,128)(2,1)} %param.27, f32[1024]{0:T(1024)S(1)} %bitcast.85), kind=kOutput, calls=%fused_computation.11 | convolution fusion | flops 6519519232 | bytes 26234880 | tf_op jit(solution)/shard_map/fd,hd->fh/dot_general | solution.py:370
  424.0 12.9 %multiply_reduce_fusion.1 = (f32[1024]{0:T(1024)}, f32[1536]{0:T(1024)S(1)}, f32[1536]{0:T(1024)S(1)}, f32[1024]{0:T(1024)}, f32[1536,1024]{1,0:T(8,128)}) fusion(f32[1536,1024]{1,0:T(8,128)S(1)} %get-tuple-element.93, f32[1536]{0:T(1024)S(1)} %add_rsqrt_fusion.1, f32[1536]{0:T(1024)S(1)} %broadcast_multiply_fusion.5, f32[1024]{0:T(1024)S(1)} %bitcast.91, ...), kind=kOutput, calls=%fused_computation.38 | convolution fusion | flops 6456601600 | bytes 23105536 | tf_op jit(solution)/shard_map/fh,dh->fd/dot_general | solution.py:375
  436.8 16.5 %fusion.19 = (f32[1024]{0:T(1024)}, f32[1024]{0:T(1024)}, bf16[1536,1024]{1,0:T(8,128)(2,1)}, f32[1024]{0:T(1024)}, f32[1536,1024]{1,0:T(8,128)S(1)}) fusion(bf16[1536,1024]{1,0:T(8,128)(2,1)} %param.27, f32[1024]{0:T(1024)S(1)} %convert_element_type.152, f32[1024]{0:T(1024)S(1)} %bitcast.86, f32[1536,1024]{1,0:T(8,128)} %copy-done.9, ...), kind=kOutput, calls=%fused_computation.36 | convolution fusion | flops 6477050880 | bytes 41996288 | tf_op jit(solution)/shard_map/dot_general | solution.py:365
  457.5 3.7 convolution_convert_fusion.5
  463.3 11.3 convolution_convert_fusion.3
  477.9 9.9 convolution_convert_fusion.2
  490.3 5.3 convolution_convert_fusion.4
  502.0 3.2 collective-permute-done.11
  507.1 36.6 %attend_bwd.7 = bf16[3,3072,128]{2,1,0:T(8,128)(2,1)} custom-call(s32[36]{0:T(128)} %pad_add_fusion.tab, bf16[3,3072,512]{2,1,0:T(8,128)(2,1)} %get-tuple-element.23.q_ref.k_ref.v_ref, bf16[3,3072,512]{2,1,0:T(8,128)(2,1)} %get-tuple-element.23.q_ref.k_ref.v_ref, bf16[3,3072,512]{2,1,0:T(8,128)(2,1)} %get-tuple-element.23.q_ref.k_ref.v_ref, ...), custom_call_target="tpu_custom_call" | custom-call | tf_op jit(solution)/shard_map/attend_bwd/pallas_call | solution.py:211
  545.7 36.5 %attend_bwd.6 = bf16[3,3072,128]{2,1,0:T(8,128)(2,1)} custom-call(s32[36]{0:T(128)} %pad_add_fusion.tab, bf16[3,3072,512]{2,1,0:T(8,128)(2,1)} %get-tuple-element.23.q_ref.k_ref.v_ref, bf16[3,3072,512]{2,1,0:T(8,128)(2,1)} %get-tuple-element.23.q_ref.k_ref.v_ref, bf16[3,3072,512]{2,1,0:T(8,128)(2,1)} %get-tuple-element.23.q_ref.k_ref.v_ref, ...), custom_call_target="tpu_custom_call" | custom-call | tf_op jit(solution)/shard_map/attend_bwd/pallas_call | solution.py:211
  584.2 36.5 %attend_bwd.5 = bf16[3,3072,128]{2,1,0:T(8,128)(2,1)} custom-call(s32[36]{0:T(128)} %pad_add_fusion.tab, bf16[3,3072,512]{2,1,0:T(8,128)(2,1)} %get-tuple-element.23.q_ref.k_ref.v_ref, bf16[3,3072,512]{2,1,0:T(8,128)(2,1)} %get-tuple-element.23.q_ref.k_ref.v_ref, bf16[3,3072,512]{2,1,0:T(8,128)(2,1)} %get-tuple-element.23.q_ref.k_ref.v_ref, ...), custom_call_target="tpu_custom_call" | custom-call | tf_op jit(solution)/shard_map/attend_bwd/pallas_call | solution.py:211
  622.6 36.5 %attend_bwd.4 = bf16[3,3072,128]{2,1,0:T(8,128)(2,1)} custom-call(s32[36]{0:T(128)} %pad_add_fusion.tab, bf16[3,3072,512]{2,1,0:T(8,128)(2,1)} %get-tuple-element.23.q_ref.k_ref.v_ref, bf16[3,3072,512]{2,1,0:T(8,128)(2,1)} %get-tuple-element.23.q_ref.k_ref.v_ref, bf16[3,3072,512]{2,1,0:T(8,128)(2,1)} %get-tuple-element.23.q_ref.k_ref.v_ref, ...), custom_call_target="tpu_custom_call" | custom-call | tf_op jit(solution)/shard_map/attend_bwd/pallas_call | solution.py:211
  659.1 4.8 pad_maximum_fusion
  667.3 11.6 convolution_convert_fusion
  679.0 16.3 %convolution_convert_fusion.1 = bf16[1024,1536]{1,0:T(8,128)(2,1)} fusion(bf16[3072,1024]{1,0:T(8,128)(2,1)} %get-tuple-element.32, bf16[3072,512]{1,0:T(8,128)(2,1)} %copy-done.5, bf16[3072,512]{1,0:T(8,128)(2,1)} %copy-done.6, bf16[3072,512]{1,0:T(8,128)(2,1)S(1)} %get-tuple-element.98), kind=kOutput, calls=%fused_computation.50 | convolution fusion | flops 9693560832 | bytes 18874368 | tf_op jit(solution)/shard_map/fd,fc->dc/dot_general | solution.py:404
  695.3 4.6 copy.77
  700.6 4.0 collective-permute-done.12
  706.7 21.3 %reduce-scatter.14.cloned.1.call-done = bf16[64,1024]{1,0:T(8,128)(2,1)} async-done(((bf16[1024,1024]{1,0:T(8,128)(2,1)}), bf16[64,1024]{1,0:T(8,128)(2,1)}) %reduce-scatter.14.cloned.1.call-update) | async-done | bytes 131088 | tf_op jit(solution)/shard_map/reduce_scatter | solution.py:308
  729.7 62.9 %reduce-scatter.20.cloned.1.call-done = bf16[64,1024]{1,0:T(8,128)(2,1)} async-done(((bf16[1024,1024]{1,0:T(8,128)(2,1)}), bf16[64,1024]{1,0:T(8,128)(2,1)}) %reduce-scatter.20.cloned.1.call-update) | async-done | bytes 131088 | tf_op jit(solution)/shard_map/reduce_scatter | solution.py:308
  794.0 62.9 %reduce-scatter.18.cloned.1.call-done = bf16[64,1024]{1,0:T(8,128)(2,1)} async-done(((bf16[1024,1024]{1,0:T(8,128)(2,1)}), bf16[64,1024]{1,0:T(8,128)(2,1)}) %reduce-scatter.18.cloned.1.call-update) | async-done | bytes 131088 | tf_op jit(solution)/shard_map/reduce_scatter | solution.py:308
  858.7 5.5 convert_reduce_fusion
  864.3 71.6 %reduce-scatter.8.cloned.1.call-done = bf16[1536,1024]{1,0:T(8,128)(2,1)} async-done(((bf16[3072,1024]{1,0:T(8,128)(2,1)}), bf16[1536,1024]{1,0:T(8,128)(2,1)}) %reduce-scatter.8.cloned.1.call-update) | async-done | bytes 3145744 | tf_op jit(solution)/shard_map/reduce_scatter | solution.py:406
  935.9 4.9 fusion.20
  941.7 22.0 %all-gather.3 = bf16[16,1,1024]{2,1,0:T(2,128)(2,1)S(1)} all-gather(bf16[1,1,1024]{2,1,0:T(2,128)(2,1)S(1)} %bitcast.77), channel_id=1, replica_groups=mesh['dp'=16,'head'=2] {'dp'}, dimensions={0}, use_global_device_ids=true | all-gather | bytes 34816 | tf_op jit(solution)/shard_map/all_gather | solution.py:319
  963.8 80.2 %all-reduce.2.cloned.1.call-done = bf16[1024,3,512]{0,2,1:T(8,128)(2,1)} async-done(((bf16[1024,3,512]{0,2,1:T(8,128)(2,1)}), bf16[1024,3,512]{0,2,1:T(8,128)(2,1)}) %all-reduce.2.cloned.1.call-update) | async-done | bytes 3145744 | tf_op jit(solution)/shard_map/psum | solution.py:410
  1044.0 5.5 copy.78
  1049.5 34.3 %all-gather.21.cloned.1.call-done = bf16[512,1024]{1,0:T(8,128)(2,1)} async-done(((bf16[32,1024]{1,0:T(8,128)(2,1)}), bf16[512,1024]{1,0:T(8,128)(2,1)}) %all-gather.21.cloned.1.call-update) | async-done | bytes 1048592 | tf_op jit(solution)/shard_map/all_gather | solution.py:312
  1083.8 2.8 convert_element_type.172
  1086.6 39.7 %all-gather.23.cloned.1.call-done = bf16[1024,1024]{1,0:T(8,128)(2,1)} async-done(((bf16[64,1024]{1,0:T(8,128)(2,1)}), bf16[1024,1024]{1,0:T(8,128)(2,1)}) %all-gather.23.cloned.1.call-update) | async-done | bytes 2097168 | tf_op jit(solution)/shard_map/all_gather | solution.py:312
  1126.3 4.1 convert_element_type.176
  1130.3 38.1 %all-gather.25.cloned.1.call-done = bf16[1024,1024]{1,0:T(8,128)(2,1)} async-done(((bf16[64,1024]{1,0:T(8,128)(2,1)}), bf16[1024,1024]{1,0:T(8,128)(2,1)}) %all-gather.25.cloned.1.call-update) | async-done | bytes 2097168 | tf_op jit(solution)/shard_map/all_gather | solution.py:312
  1168.5 4.2 convert_element_type.180
  1172.7 5.9 fusion.15
  1178.6 46.8 %all-gather.27.cloned.1.call-done = f32[32,1,11776]{2,1,0:T(1,128)} async-done(((f32[1,1,11776]{2,1,0:T(1,128)}), f32[32,1,11776]{2,1,0:T(1,128)}) %all-gather.27.cloned.1.call-update) | async-done | bytes 1507344 | tf_op jit(solution)/shard_map/all_gather | solution.py:417
  1225.4 5.0 reduce.2
  1232.3 4.1 multiply_reduce_fusion
  1236.3 4.9 psum.14
  1241.9 8.3 fusion.33
  (242 shorter events, 89.1 us)
Async XLA Ops:
  7.2 33.5 %copy-start.21 = (s32[1,3072]{1,0:T(1,128)S(1)}, s32[1,3072]{1,0:T(1,128)}, u32[]{:S(2)}) copy-start(s32[1,3072]{1,0:T(1,128)} %param.16) | copy-start | bytes 36868
  7.2 28.9 %copy-start.33 = (bf16[3072]{0:T(1024)(128)(2,1)S(1)}, bf16[3072]{0:T(1024)(128)(2,1)}, u32[]{:S(2)}) copy-start(bf16[3072]{0:T(1024)(128)(2,1)} %param.18) | copy-start | bytes 18436
  7.2 69.0 %all-gather.15.cloned.1.call-start = ((), (), s32[]{:S(2)}) async-start(), calls=%async_computation.8 | async-start | bytes 1114112 | tf_op jit(solution)/shard_map/all_gather | solution.py:305
  8.1 5.2 collective-permute-start.4
  14.0 83.0 %all-gather.17.cloned.1.call-start = ((), (), s32[]{:S(2)}) async-start(), calls=%async_computation.9 | async-start | bytes 2228224 | tf_op jit(solution)/shard_map/all_gather | solution.py:305
  14.9 5.0 collective-permute-start.5
  20.6 118.7 %all-gather.19.cloned.1.call-start = ((), (), s32[]{:S(2)}) async-start(), calls=%async_computation.10 | async-start | bytes 2228224 | tf_op jit(solution)/shard_map/all_gather | solution.py:305
  21.6 5.0 collective-permute-start.7
  27.3 192.5 %all-gather.13.cloned.1.call-start = ((), (), s32[]{:S(2)}) async-start(), calls=%async_computation.7 | async-start | bytes 9437184 | tf_op jit(solution)/shard_map/all_gather | solution.py:300
  27.9 672.2 %reduce-scatter.12.cloned.1.call-start = ((), (), s32[]{:S(2)}) async-start(), calls=%async_computation.14 | async-start | bytes 1114112 | tf_op jit(solution)/shard_map/reduce_scatter | solution.py:308
  27.9 47.7 %collective-permute-start.6 = (bf16[1024]{0:T(1024)(128)(2,1)}, bf16[1024]{0:T(1024)(128)(2,1)}, u32[]{:S(2)}, u32[]{:S(2)}) collective-permute-start(bf16[1024]{0:T(1024)(128)(2,1)} %param.24), channel_id=1, source_target_pairs={{0,1},{1,0},{2,3},{3,2},{4,5},{5,4},{6,7},{7,6},{8,9},{9,8},{10,11... | collective-permute-start | bytes 6152 | tf_op jit(solution)/shard_map/ppermute | solution.py:267
  32.2 9.3 copy-start.15
  32.2 13.5 %copy-start.14 = (bf16[1024,1024]{1,0:T(8,128)(2,1)S(1)}, bf16[1024,1024]{1,0:T(8,128)(2,1)}, u32[]{:S(2)}) copy-start(bf16[1024,1024]{1,0:T(8,128)(2,1)} %param.25) | copy-start | bytes 6291460
  36.1 11.1 copy-start.34
  36.1 11.7 copy-start
  56.0 9.3 copy-start.29
  65.9 9.7 copy-start.44
  356.3 22.0 %copy-start.18 = (bf16[1024,1024]{1,0:T(8,128)(2,1)S(1)}, bf16[1024,1024]{1,0:T(8,128)(2,1)}, u32[]{:S(2)}) copy-start(bf16[1024,1024]{1,0:T(8,128)(2,1)} %constant_dynamic-update-slice_fusion.4) | copy-start | bytes 6291460
  356.3 22.0 %copy-start.22 = (f32[1536]{0:T(1024)S(1)}, f32[1536]{0:T(1024)}, u32[]{:S(2)}) copy-start(f32[1536]{0:T(1024)} %broadcast_multiply_fusion.2) | copy-start | bytes 18436
  356.3 22.1 %copy-start.35 = (f32[1024]{0:T(1024)S(1)}, f32[1024]{0:T(1024)}, u32[]{:S(2)}) copy-start(f32[1024]{0:T(1024)} %convert_element_type.148) | copy-start | bytes 12292
  357.7 8.1 collective-permute-start
  359.4 10.4 collective-permute-start.1
  362.4 11.6 collective-permute-start.2
  364.1 14.1 %collective-permute-start.3 = (bf16[1536,128]{1,0:T(8,128)(2,1)S(1)}, bf16[1536,128]{1,0:T(8,128)(2,1)S(1)}, u32[]{:S(2)}, u32[]{:S(2)}) collective-permute-start(bf16[1536,128]{1,0:T(8,128)(2,1)S(1)} %get-tuple-element.116), channel_id=1, source_target_pairs={{0,1},{1,0},{2,3},{3,2},{4,5},{5,4},{6,7},{7,6},{8,9},{9,8},{10,11... | collective-permute-start | bytes 1179656 | tf_op jit(solution)/shard_map/ppermute | solution.py:267
  378.3 7.4 copy-start.25
  385.7 38.3 %copy-start.9 = (f32[1536,1024]{1,0:T(8,128)}, f32[1536,1024]{1,0:T(8,128)S(1)}, u32[]{:S(2)}) copy-start(f32[1536,1024]{1,0:T(8,128)S(1)} %get-tuple-element.93) | copy-start | bytes 18874372
  385.7 4.5 copy-start.17
  385.7 4.5 copy-start.42
  385.7 4.5 copy-start.43
  390.2 13.2 %copy-start.16 = (bf16[2048,1024]{1,0:T(8,128)(2,1)S(1)}, bf16[2048,1024]{1,0:T(8,128)(2,1)}, u32[]{:S(2)}) copy-start(bf16[2048,1024]{1,0:T(8,128)(2,1)} %constant_dynamic-update-slice_fusion.8) | copy-start | bytes 12582916
  390.2 13.2 %copy-start.41 = (f32[1,1024]{1,0:T(1,128)S(1)}, f32[1,1024]{1,0:T(1,128)}, u32[]{:S(2)}) copy-start(f32[1,1024]{1,0:T(1,128)} %get-tuple-element.127) | copy-start | bytes 12292
  453.3 7.8 copy-start.2
  462.7 237.9 %reduce-scatter.10.cloned.1.call-start = ((), (), s32[]{:S(2)}) async-start(), calls=%async_computation.13 | async-start | bytes 1114112 | tf_op jit(solution)/shard_map/reduce_scatter | solution.py:308
  463.3 242.9 %reduce-scatter.16.cloned.1.call-start = ((), (), s32[]{:S(2)}) async-start(), calls=%async_computation.17 | async-start | bytes 2228224 | tf_op jit(solution)/shard_map/reduce_scatter | solution.py:308
  477.1 250.9 %reduce-scatter.14.cloned.1.call-start = ((), (), s32[]{:S(2)}) async-start(), calls=%async_computation.16 | async-start | bytes 2228224 | tf_op jit(solution)/shard_map/reduce_scatter | solution.py:308
  477.8 314.7 %reduce-scatter.20.cloned.1.call-start = ((), (), s32[]{:S(2)}) async-start(), calls=%async_computation.20 | async-start | bytes 2228224 | tf_op jit(solution)/shard_map/reduce_scatter | solution.py:308
  490.2 366.7 %reduce-scatter.18.cloned.1.call-start = ((), (), s32[]{:S(2)}) async-start(), calls=%async_computation.19 | async-start | bytes 2228224 | tf_op jit(solution)/shard_map/reduce_scatter | solution.py:308
  497.1 8.1 collective-permute-start.11
  497.4 46.3 %collective-permute-start.10 = (bf16[1536,128]{1,0:T(8,128)(2,1)}, bf16[1536,128]{1,0:T(8,128)(2,1)}, u32[]{:S(2)}, u32[]{:S(2)}) collective-permute-start(bf16[1536,128]{1,0:T(8,128)(2,1)} %get-tuple-element.112), channel_id=1, source_target_pairs={{0,1},{1,0},{2,3},{3,2},{4,5},{5,4},{6,7},{7,6},{8,9},{9,8},{10,11... | collective-permute-start | bytes 1179656 | tf_op jit(solution)/shard_map/ppermute | solution.py:267
  499.1 83.1 %collective-permute-start.9 = (bf16[1536,128]{1,0:T(8,128)(2,1)}, bf16[1536,128]{1,0:T(8,128)(2,1)}, u32[]{:S(2)}, u32[]{:S(2)}) collective-permute-start(bf16[1536,128]{1,0:T(8,128)(2,1)} %get-tuple-element.113), channel_id=1, source_target_pairs={{0,1},{1,0},{2,3},{3,2},{4,5},{5,4},{6,7},{7,6},{8,9},{9,8},{10,11... | collective-permute-start | bytes 1179656 | tf_op jit(solution)/shard_map/ppermute | solution.py:267
  500.2 120.4 %collective-permute-start.8 = (bf16[1536,128]{1,0:T(8,128)(2,1)}, bf16[1536,128]{1,0:T(8,128)(2,1)}, u32[]{:S(2)}, u32[]{:S(2)}) collective-permute-start(bf16[1536,128]{1,0:T(8,128)(2,1)} %get-tuple-element.109), channel_id=1, source_target_pairs={{0,1},{1,0},{2,3},{3,2},{4,5},{5,4},{6,7},{7,6},{8,9},{9,8},{10,11... | collective-permute-start | bytes 1179656 | tf_op jit(solution)/shard_map/ppermute | solution.py:267
  502.0 433.9 %reduce-scatter.8.cloned.1.call-start = ((), (), s32[]{:S(2)}) async-start(), calls=%async_computation.11 | async-start | bytes 9437184 | tf_op jit(solution)/shard_map/reduce_scatter | solution.py:406
  622.6 36.5 %copy-start.8 = (bf16[3,3072,128]{2,1,0:T(8,128)(2,1)S(1)}, bf16[3,3072,128]{2,1,0:T(8,128)(2,1)}, u32[]{:S(2)}) copy-start(bf16[3,3072,128]{2,1,0:T(8,128)(2,1)} %attend_bwd.7) | copy-start | bytes 7077892
  664.6 14.4 %copy-start.4 = (bf16[3072,512]{1,0:T(8,128)(2,1)}, bf16[3072,512]{1,0:T(8,128)(2,1)S(1)}, u32[]{:S(2)}) copy-start(bf16[3072,512]{1,0:T(8,128)(2,1)S(1)} %get-tuple-element.98) | copy-start | bytes 9437188
  678.9 365.1 %all-reduce.2.cloned.1.call-start = ((), (), s32[]{:S(2)}) async-start(), calls=%async_computation.12 | async-start | bytes 6291456 | tf_op jit(solution)/shard_map/psum | solution.py:410
  695.3 163.3 %copy-start.32 = (f32[1536]{0:T(1024)S(1)}, f32[1536]{0:T(1024)}, u32[]{:S(2)}) copy-start(f32[1536]{0:T(1024)} %get-tuple-element.108) | copy-start | bytes 18436
  699.9 164.3 %copy-start.30 = (f32[1024]{0:T(1024)S(1)}, f32[1024]{0:T(1024)}, u32[]{:S(2)}) copy-start(f32[1024]{0:T(1024)} %get-tuple-element.90) | copy-start | bytes 12292
  699.9 164.3 %copy-start.40 = (f32[1024]{0:T(1024)S(1)}, f32[1024]{0:T(1024)}, u32[]{:S(2)}) copy-start(f32[1024]{0:T(1024)} %get-tuple-element.80) | copy-start | bytes 12292
  699.9 164.3 %copy-start.31 = (f32[2048]{0:T(1024)S(1)}, f32[2048]{0:T(1024)}, u32[]{:S(2)}) copy-start(f32[2048]{0:T(1024)} %get-tuple-element.143) | copy-start | bytes 24580
  700.0 236.0 %copy-start.1 = (bf16[1536,1024]{1,0:T(8,128)(2,1)S(1)}, bf16[1536,1024]{1,0:T(8,128)(2,1)}, u32[]{:S(2)}) copy-start(bf16[1536,1024]{1,0:T(8,128)(2,1)} %param.14) | copy-start | bytes 9437188
  700.0 236.0 %copy-start.23 = (f32[1536]{0:T(1024)S(1)}, f32[1536]{0:T(1024)}, u32[]{:S(2)}) copy-start(f32[1536]{0:T(1024)} %broadcast_multiply_fusion.2) | copy-start | bytes 18436
  700.0 236.0 %copy-start.28 = (f32[1,1024]{1,0:T(1,128)S(1)}, f32[1,1024]{1,0:T(1,128)}, u32[]{:S(2)}) copy-start(f32[1,1024]{1,0:T(1,128)} %get-tuple-element.124) | copy-start | bytes 12292
  700.0 383.8 %all-gather.21.cloned.1.call-start = ((), (), s32[]{:S(2)}) async-start(), calls=%async_computation.15 | async-start | bytes 1114112 | tf_op jit(solution)/shard_map/all_gather | solution.py:312
  700.1 4.5 collective-permute-start.12
  706.1 420.1 %all-gather.23.cloned.1.call-start = ((), (), s32[]{:S(2)}) async-start(), calls=%async_computation.18 | async-start | bytes 2228224 | tf_op jit(solution)/shard_map/all_gather | solution.py:312
  706.2 21.8 %collective-permute-start.13 = (bf16[64,1024]{1,0:T(8,128)(2,1)}, bf16[64,1024]{1,0:T(8,128)(2,1)S(1)}, u32[]{:S(2)}, u32[]{:S(2)}) collective-permute-start(bf16[64,1024]{1,0:T(8,128)(2,1)} %reduce-scatter.16.cloned.1.call-done), channel_id=1, source_target_pairs={{0,1},{1,0},{2,3},{3,2},{4,5},{5,4},{6,7},{7,6},{8,9},{9,8},{10,11... | collective-permute-start | bytes 393224 | tf_op jit(solution)/shard_map/ppermute | solution.py:267
  729.6 438.9 %all-gather.25.cloned.1.call-start = ((), (), s32[]{:S(2)}) async-start(), calls=%async_computation.21 | async-start | bytes 2228224 | tf_op jit(solution)/shard_map/all_gather | solution.py:312
  792.5 64.4 %collective-permute-start.14 = (bf16[64,1024]{1,0:T(8,128)(2,1)}, bf16[64,1024]{1,0:T(8,128)(2,1)S(1)}, u32[]{:S(2)}, u32[]{:S(2)}) collective-permute-start(bf16[64,1024]{1,0:T(8,128)(2,1)} %reduce-scatter.20.cloned.1.call-done), channel_id=1, source_target_pairs={{0,1},{1,0},{2,3},{3,2},{4,5},{5,4},{6,7},{7,6},{8,9},{9,8},{10,11... | collective-permute-start | bytes 393224 | tf_op jit(solution)/shard_map/ppermute | solution.py:267
  858.5 366.9 %all-gather.27.cloned.1.call-start = ((), (), s32[]{:S(2)}) async-start(), calls=%async_computation.22 | async-start | bytes 1554432 | tf_op jit(solution)/shard_map/all_gather | solution.py:417
  858.6 82.3 %copy-start.39 = (f32[1024]{0:T(1024)S(1)}, f32[1024]{0:T(1024)}, u32[]{:S(2)}) copy-start(f32[1024]{0:T(1024)} %get-tuple-element.102) | copy-start | bytes 12292
  858.6 82.3 %copy-start.37 = (f32[1024]{0:T(1024)S(1)}, f32[1024]{0:T(1024)}, u32[]{:S(2)}) copy-start(f32[1024]{0:T(1024)} %get-tuple-element.77) | copy-start | bytes 12292
  858.6 82.3 %copy-start.36 = (f32[1024]{0:T(1024)S(1)}, f32[1024]{0:T(1024)}, u32[]{:S(2)}) copy-start(f32[1024]{0:T(1024)} %get-tuple-element.72) | copy-start | bytes 12292
  858.7 82.3 %copy-start.38 = (f32[1024]{0:T(1024)S(1)}, f32[1024]{0:T(1024)}, u32[]{:S(2)}) copy-start(f32[1024]{0:T(1024)} %get-tuple-element.79) | copy-start | bytes 12292
  858.7 83.0 %copy-start.27 = (bf16[1,1024]{1,0:T(2,128)(2,1)S(1)}, bf16[1,1024]{1,0:T(2,128)(2,1)}, u32[]{:S(2)}) copy-start(bf16[1,1024]{1,0:T(2,128)(2,1)} %param.15) | copy-start | bytes 6148
  (12 other events, 21.6 us)
Sparse Core Ops, SparseCore 0:
  14.1 39.6 all-gather.14
  56.5 40.4 all-gather.16
  99.1 40.1 all-gather.18
  140.7 79.0 all-gather.12
  462.8 75.8 reduce-scatter.11
  542.1 56.6 reduce-scatter.9
  602.5 60.8 reduce-scatter.15
  667.2 60.7 reduce-scatter.13
  731.7 60.7 reduce-scatter.19
  796.1 60.7 reduce-scatter.17
  859.8 76.0 reduce-scatter.7
  939.9 104.0 all-reduce.1
  1046.7 37.0 all-gather.20
  1085.8 40.4 all-gather.22
  1128.3 40.1 all-gather.24
  1171.7 53.6 all-gather.26

commit v2 on v1

--- a/solution.py
+++ b/solution.py
@@ -231,11 +231,12 @@
     lane = lax.broadcasted_iota(jnp.int32, v.shape, 1) % HDIM
     return v * cos + jnp.where(lane < HDIM // 2, -pltpu.roll(v, 96, 1), pltpu.roll(v, 32, 1)) * sin
 
-def qkv_kernel(x_ref, scale_ref, shift_ref, w_ref, b_ref, cos_ref, sin_ref, qkv_ref, n_ref):
+def qkv_kernel(base, x_ref, scale_ref, shift_ref, w_ref, b_ref, cos_ref, sin_ref, *rest):
+    qkv_ref, nt_ref = rest[-2:]
     inner = qkv_ref.shape[2]
     unit, _ = normalize(x_ref[...].astype(jnp.float32))
     low = (unit * (1.0 + scale_ref[...]) + shift_ref[...]).astype(jnp.bfloat16)
-    n_ref[...] = low
+    nt_ref[...] = low.T
     cos, sin = cos_ref[...], sin_ref[...]
     for t in range(3):
         part = slice(t * inner, (t + 1) * inner)
@@ -246,22 +247,93 @@
                 v = turn(v, cos, sin)
             qkv_ref[t, :, c * 128:(c + 1) * 128] = v.astype(jnp.bfloat16)
 
-def project(x, scale, shift, w, b, cos, sin):
-    seq, width = x.shape
+def project(base, seq, x, scale, shift, w, b, cos, sin, before=None):
+    frames, width = x.shape
     inner = w.shape[1] // 3
-    step = 256
-    row = pl.BlockSpec((step, width), lambda i: (i, 0))
-    table = pl.BlockSpec((step, 128), lambda i: (i, 0))
-    const = lambda a: pl.BlockSpec(a.shape, lambda i: (0, 0))
+    step = math.gcd(256, frames)
+    row = pl.BlockSpec((step, width), lambda i, s: (i, 0))
+    table = pl.BlockSpec((step, 128), lambda i, s: (s[0] + i, 0))
+    const = lambda a: pl.BlockSpec(a.shape, lambda i, s: (0, 0))
+    keep = [pl.BlockSpec(memory_space=pl.ANY)] * 2 if before else []
     return pl.pallas_call(
         qkv_kernel,
+        grid_spec=pltpu.PrefetchScalarGridSpec(
+            num_scalar_prefetch=1, grid=(frames // step,),
+            in_specs=[row, const(scale), const(shift), const(w), const(b), table, table] + keep,
+            out_specs=[pl.BlockSpec((3, step, inner), lambda i, s: (0, s[0] + i, 0)), pl.BlockSpec((width, step), lambda i, s: (0, s[0] + i))]),
+        out_shape=[jax.ShapeDtypeStruct((3, seq, inner), jnp.bfloat16), jax.ShapeDtypeStruct((width, seq), jnp.bfloat16)],
+        input_output_aliases={8: 0, 9: 1} if before else {},
+        compiler_params=pltpu.CompilerParams(vmem_limit_bytes=60 << 20),
+        cost_estimate=pl.CostEstimate(flops=6 * frames * width * inner, bytes_accessed=2 * frames * (2 * width + 3 * inner), transcendentals=0),
+        name="project",
+    )(base * (frames // step), x, scale, shift, w, b, cos, sin, *(before or ()))
+
+def wgrad_kernel(nt_ref, g_ref, w_ref, b_ref, acc):
+    i = pl.program_id(0)
+    g = jnp.concatenate([g_ref[0], g_ref[1], g_ref[2]], axis=1)
+    part = mm(nt_ref[...], g, NN)
+    sums = jnp.broadcast_to(jnp.sum(g.astype(jnp.float32), axis=0, keepdims=True), b_ref.shape)
+    @pl.when(i == 0)
+    def _():
+        acc[...] = part
+        b_ref[...] = sums
+    @pl.when(i > 0)
+    def _():
+        acc[...] += part
+        b_ref[...] += sums
+    @pl.when(i == pl.num_programs(0) - 1)
+    def _():
+        w_ref[...] = acc[...].astype(jnp.bfloat16)
+
+def weight_grad(nt, g):
+    width, seq = nt.shape
+    step = math.gcd(512, seq)
+    return pl.pallas_call(
+        wgrad_kernel,
         grid=(seq // step,),
-        in_specs=[row, const(scale), const(shift), const(w), const(b), table, table],
-        out_specs=[pl.BlockSpec((3, step, inner), lambda i: (0, i, 0)), row],
-        out_shape=[jax.ShapeDtypeStruct((3, seq, inner), jnp.bfloat16), jax.ShapeDtypeStruct((seq, width), jnp.bfloat16)],
+        in_specs=[pl.BlockSpec((width, step), lambda i: (0, i)), pl.BlockSpec((3, step, 128), lambda i: (0, i, 0))],
+        out_specs=[pl.BlockSpec((width, 384), lambda i: (0, 0)), pl.BlockSpec((8, 384), lambda i: (0, 0))],
+        out_shape=[jax.ShapeDtypeStruct((width, 384), jnp.bfloat16), jax.ShapeDtypeStruct((8, 384), jnp.float32)],
+        scratch_shapes=[pltpu.VMEM((width, 384), jnp.float32)],
         compiler_params=pltpu.CompilerParams(vmem_limit_bytes=60 << 20),
-        name="project",
-    )(x, scale, shift, w, b, cos, sin)
+        cost_estimate=pl.CostEstimate(flops=2 * seq * width * 384, bytes_accessed=2 * seq * (width + 384), transcendentals=0),
+        name="weight_grad",
+    )(nt, g)
+
+def last_kernel(base, x_ref, gm_ref, scale_ref, w_ref, *rest):
+    gi_ref, rows_ref = rest[-2:]
+    flat = jnp.concatenate([p[t] for p in rest[:-2] for t in range(3)], axis=1)
+    g = mm(flat, w_ref[...], NT)
+    unit, rstd = normalize(x_ref[...].astype(jnp.float32))
+    u = g * (1.0 + scale_ref[...])
+    back = rstd * (u - jnp.mean(u, axis=-1, keepdims=True) - unit * jnp.mean(u * unit, axis=-1, keepdims=True))
+    gi_ref[...] = gm_ref[...] + back
+    shift = jnp.sum(g, axis=0, keepdims=True)
+    scale = jnp.sum(g * unit, axis=0, keepdims=True)
+    @pl.when(pl.program_id(0) == 0)
+    def _():
+        rows_ref[...] = jnp.zeros_like(rows_ref)
+    rows_ref[0:1, :] += shift
+    rows_ref[1:2, :] += scale
+
+def input_grad(base, own, others, x, grad_middle, scale, w):
+    frames, width = x.shape
+    step = math.gcd(256, frames)
+    row = pl.BlockSpec((step, width), lambda i, s: (i, 0))
+    const = lambda a: pl.BlockSpec(a.shape, lambda i, s: (0, 0))
+    return pl.pallas_call(
+        last_kernel,
+        grid_spec=pltpu.PrefetchScalarGridSpec(
+            num_scalar_prefetch=1, grid=(frames // step,),
+            in_specs=[row, row, const(scale), const(w)]
+            + [pl.BlockSpec((3, step, 128), lambda i, s: (0, s[0] + i, 0))] * len(own)
+            + [pl.BlockSpec((3, step, 128), lambda i, s: (0, i, 0))] * len(others),
+            out_specs=[row, pl.BlockSpec((8, width), lambda i, s: (0, 0))]),
+        out_shape=[jax.ShapeDtypeStruct((frames, width), jnp.float32), jax.ShapeDtypeStruct((8, width), jnp.float32)],
+        compiler_params=pltpu.CompilerParams(vmem_limit_bytes=60 << 20),
+        cost_estimate=pl.CostEstimate(flops=2 * frames * width * w.shape[1], bytes_accessed=frames * (10 * width + 2 * w.shape[1]), transcendentals=0),
+        name="input_grad",
+    )(base * (frames // step), x, grad_middle, scale, w, *own, *others)
 
 def relative(axis, size):
     return lambda x, r: x if r % size == 0 else lax.ppermute(x, axis, [(i, (i + r) % size) for i in range(size)])
@@ -297,27 +369,22 @@
     owner = [lax.rem(me - r + n, n) for r in range(n)]
     source = [lax.rem(me + r, n) for r in range(n)]
 
-    gathered = lax.all_gather(inputs, "head", axis=0, tiled=True)
-
-    def whole_weight(w):
-        rows = w.shape[0] // ndp
-        cut = lax.dynamic_slice_in_dim(w, mine * rows, rows, 0)
-        return [w] + [lax.all_gather(move(cut, r), "dp", axis=0, tiled=True) for r in range(1, n)]
-
-    def total_grad(parts):
-        cut = [lax.psum_scatter(p.astype(bf16), "dp", scatter_dimension=0, tiled=True) for p in parts]
-        own = cut[0].astype(f32)
-        for r in range(1, n):
-            own = own + move(cut[r], -r).astype(f32)
-        return lax.all_gather(own.astype(bf16), "dp", axis=0, tiled=True).astype(f32)
+    elsewhere = [move(inputs, r) for r in range(1, n)]
+
+    shards = [("out", output_weight), ("expand", expand_weight), ("contract", contract_weight), ("proj", projection_weight.reshape(width, 3 * inner))]
+    heights = {name: w.size // (ndp * width) for name, w in shards}
+    cut = [lax.dynamic_slice_in_dim(w, mine * (w.shape[0] // ndp), w.shape[0] // ndp, 0).reshape(heights[name], width) for name, w in shards]
+    bias_rows = jnp.pad(expand_bias[None, :], ((0, 15), (0, width - hidden_here)))
+    pack = jnp.concatenate(cut + [bias_rows], axis=0)
+    embed_rows = jnp.pad(time_embed, ((0, 15), (0, 0)))
+    packs = jnp.concatenate([move(pack, r) for r in range(1, n)] + [embed_rows], axis=0)
+    packed = lax.all_gather(packs, "dp", axis=0)
 
     embeds = time_embed.astype(f32)
     silu_low = jax.nn.silu(embeds).astype(bf16)
     own_mod = jnp.dot(silu_low, modulator_weight, preferred_element_type=f32) + modulator_bias.astype(f32)
     modulation = lax.all_gather(own_mod, "head", axis=1, tiled=True)
     shift_a, scale_a, gate_a, shift_f, scale_f, gate_f = jnp.split(modulation, 6, axis=1)
-    embeds_all = lax.all_gather(time_embed, "dp", axis=0, tiled=True).astype(f32)
-    silu_all = jax.nn.silu(embeds_all).astype(bf16).astype(f32)
 
     seg = segment_ids[0]
     tab = span_table(seg, seq)
@@ -328,14 +395,13 @@
     cosine = jnp.tile(jnp.cos(angles), (1, 4))
     sine = jnp.tile(jnp.sin(angles), (1, 4))
 
-    out_all = whole_weight(output_weight)
-    expand_all = whole_weight(expand_weight)
-    contract_all = whole_weight(contract_weight)
-    expand_bias_all = [move(expand_bias, r) for r in range(n)]
-
     weight_proj = projection_weight.reshape(width, 3 * inner)
     bias_proj = projection_bias.astype(f32).reshape(1, 3 * inner)
-    qkv, normed_a = project(gathered, scale_a, shift_a, weight_proj, bias_proj, cosine, sine)
+    place = lambda r: owner[r].astype(jnp.int32).reshape(1)
+    into = project(place(0), seq, inputs, scale_a, shift_a, weight_proj, bias_proj, cosine, sine)
+    for r in range(1, n):
+        into = project(place(r), seq, elsewhere[r - 1], scale_a, shift_a, weight_proj, bias_proj, cosine, sine, into)
+    qkv, normed_t = into
 
     attended, log_mass, attended_here = [], [], []
     for g in range(groups):
@@ -345,7 +411,22 @@
         attended_here.append([
             move(lax.dynamic_slice_in_dim(o, source[r] * frames_here, frames_here, 0), r) for r in range(n)
         ])
+    packed, _ = lax.optimization_barrier((packed, log_mass[min(1, groups - 1)]))
     att_rel = [jnp.concatenate([attended_here[g][r] for g in range(groups)], axis=1) for r in range(n)]
+
+    own_w = dict(shards)
+    whole_w = {name: [w] for name, w in shards}
+    expand_bias_all = [expand_bias]
+    at = 0
+    for r in range(1, n):
+        for name, w in shards:
+            whole_w[name].append(packed[:, at:at + heights[name]].reshape(w.shape))
+            at += heights[name]
+        expand_bias_all.append(packed[0, at, :hidden_here])
+        at += 16
+    out_all, expand_all, contract_all = whole_w["out"], whole_w["expand"], whole_w["contract"]
+    proj_cat = jnp.concatenate([w.reshape(width, 3, groups, 128).transpose(0, 2, 1, 3).reshape(width, 3 * inner) for w in whole_w["proj"]], axis=1)
+    silu_all = jax.nn.silu(packed[:, at].astype(f32)).astype(bf16).astype(f32)
 
     att_cat = jnp.concatenate(att_rel, axis=1)
     out_cat = jnp.concatenate(out_all, axis=0)
@@ -387,31 +468,48 @@
     grad_att = jnp.einsum("fd,id->fi", grad_branch_a, out_cat, preferred_element_type=f32).astype(bf16)
     output_part = jnp.einsum("fi,fd->id", att_cat, grad_branch_a, preferred_element_type=f32)
 
-    grad_projected = []
+    def slots(part):
+        return part.astype(bf16).reshape(ndp, part.size // (ndp * width), width)
+
+    sent = jnp.concatenate([
+        slots(p) for r in range(n) for p in (
+            output_part[r * inner:(r + 1) * inner],
+            expand_part[:, r * hidden_here:(r + 1) * hidden_here],
+            contract_part[r * hidden_here:(r + 1) * hidden_here])], axis=1)
+    reduced = lax.psum_scatter(sent, "dp", scatter_dimension=0, tiled=False)
+    tall = reduced.shape[0] // n
+    own_grads = reduced[:tall].astype(f32)
+    for r in range(1, n):
+        own_grads = own_grads + move(reduced[r * tall:(r + 1) * tall], -r).astype(f32)
+
+    flat, flat_far, wgrads, bias_sums = [], [[] for _ in range(1, n)], [], []
     for g in range(groups):
         whole = jnp.zeros((seq, 128), bf16)
         for r in range(n):
             piece = move(grad_att[:, r * inner + g * 128:r * inner + (g + 1) * 128], -r)
             whole = lax.dynamic_update_slice_in_dim(whole, piece, source[r] * frames_here, 0)
-        grad_projected.append(attend_bwd(tab, qkv, fq, fk, attended[g], whole, log_mass[g], cosine, sine, g, 1))
-
-    grad_output = total_grad([output_part[r * inner:(r + 1) * inner] for r in range(n)])
-    grad_expand = total_grad([expand_part[:, r * hidden_here:(r + 1) * hidden_here] for r in range(n)])
-    grad_contract = total_grad([contract_part[r * hidden_here:(r + 1) * hidden_here] for r in range(n)])
-
-    g_all = jnp.concatenate(grad_projected, axis=2)
-    flat = jnp.concatenate([g_all[0], g_all[1], g_all[2]], axis=1)
-    grad_projection = jnp.einsum("fd,fc->dc", normed_a, flat, preferred_element_type=f32)
-    bias_proj_grad = jnp.sum(flat.astype(f32), axis=0)
-    grad_normed_a = lax.psum_scatter(
-        jnp.einsum("fc,dc->fd", flat, weight_proj, preferred_element_type=f32).astype(bf16),
-        "head", scatter_dimension=0, tiled=True,
-    ).astype(f32)
-    grad_projection = lax.psum(grad_projection.astype(bf16), "dp").astype(f32).reshape(width, 3, inner)
-    unit_a, rstd_a = normalize(frames)
-    grad_inputs = grad_middle + norm_back(grad_normed_a, unit_a, rstd_a, scale_a)
-    row_shift_a = jnp.sum(grad_normed_a, axis=0)
-    row_scale_a = jnp.sum(grad_normed_a * unit_a, axis=0)
+        back = attend_bwd(tab, qkv, fq, fk, attended[g], whole, log_mass[g], cosine, sine, g, 1)
+        flat.append(back)
+        for r in range(1, n):
+            flat_far[r - 1].append(move(lax.dynamic_slice_in_dim(back, source[r] * frames_here, frames_here, 1), r))
+        w, b = weight_grad(normed_t, back)
+        wgrads.append(w)
+        bias_sums.append(b[0].reshape(3, 128))
+
+    proj_part = jnp.stack([w.reshape(width, 3, 128) for w in wgrads], axis=2)
+    proj_own = lax.psum_scatter(proj_part.reshape(ndp, width // ndp, 3 * inner), "dp", scatter_dimension=0, tiled=False)
+    all_own = jnp.concatenate([own_grads.astype(bf16), proj_own.reshape(heights["proj"], width)], axis=0)
+    totals = lax.all_gather(all_own, "dp", axis=0)
+    at, grads = 0, {}
+    for name, w in shards:
+        grads[name] = totals[:, at:at + heights[name]].astype(f32).reshape(w.shape)
+        at += heights[name]
+    grad_output, grad_expand, grad_contract = grads["out"], grads["expand"], grads["contract"]
+    grad_projection = grads["proj"].reshape(width, 3, inner)
+    bias_proj_grad = jnp.stack(bias_sums, axis=1).reshape(3 * inner)
+
+    grad_inputs, row_sums = input_grad(place(0), flat, [p for far in flat_far for p in far], inputs, grad_middle, scale_a, proj_cat)
+    row_shift_a, row_scale_a = row_sums[0], row_sums[1]
 
     early = jnp.concatenate([bias_proj_grad, bias_out, bias_down, bias_up, row_shift_a, row_scale_a, row_gate_a, row_shift_f, row_scale_f, row_gate_f])
     table = lax.all_gather(early, ("dp", "head"), axis=0)

time: 1270 us -> 975 us (0.77)
  waiting for transfers between devices: 622 us -> 233 us
  Pallas kernels: 283 us -> 350 us
  local copies, waits for them, and re-layouts: 84.4 us -> 134 us
  blocking collectives: 31.5 us -> 52.4 us
  other arithmetic: 62.3 us -> 46.7 us
  matrix products: 141 us -> 126 us
    reduce_scatter x7 -> x2, waiting for transfers between devices: 219 us -> 0.02 us  [the longest x1 0.02 us: on_device(): reduced = lax.psum_scatter(sent, 'dp', scatter_dimension=0, tiled=False)]
    all_gather x7 -> x2, waiting for transfers between devices: 247 us -> 48.1 us  [the longest x1 48.1 us: on_device(): totals = lax.all_gather(all_own, 'dp', axis=0)]
    psum x1 -> x0, waiting for transfers between devices: 80.2 us -> none  [on_device(): lax.psum(grad_projection.astype(bf16), 'dp').astype(f32)]
    all_gather x1, waiting for transfers between devices: 46.8 us -> 107 us  [on_device(): table = lax.all_gather(early, ('dp', 'head'), axis=0)]
    pallas_call x1 -> x7, Pallas kernels: 20.4 us -> 77.2 us  [the longest x4 34.5 us: weight_grad(): pl.pallas_call(wgrad_kernel, grid=(seq // step,), in_specs=[pl.BlockSpec(...]
    ppermute x15, waiting for transfers between devices: 27.3 us -> 77.2 us  [relative(): lax.ppermute(x, axis, [(i, (i + r) % size) for i in range(size)])]
    all_gather x1, blocking collectives: 4.52 us -> 47.3 us  [on_device(): modulation = lax.all_gather(own_mod, 'head', axis=1, tiled=True)]
    dot_general x2 -> x0, matrix products: 28 us -> none  [the longest x1 16.3 us: on_device(): jnp.einsum('fd,fc->dc', normed_a, flat, preferred_element_type=f32)]
  transfers between devices with their start and end apart: 31 -> 20, of which waited for: 20 -> 13; matrix products, arithmetic and copies ran while one was open for 14% -> 13% of each run, Pallas kernels for 12% -> 36%
where the time goes in v2:
time: 975 us
  Pallas kernels  350 us (36%)
  waiting for transfers between devices  233 us (24%)
  local copies, waits for them, and re-layouts  134 us (14%)
  matrix products  126 us (13%)
  blocking collectives  52.4 us (5%)
  other arithmetic  46.7 us (5%)
  starting transfers between devices  18.8 us (2%)
  between operations  14.8 us (2%)
    pallas_call x4, Pallas kernels, attend_bwd(): pl.pallas_call(bwd_kernel, grid_spec=pltpu.PrefetchScalarGridSpec(num_sca...  151 us
    pallas_call x4, Pallas kernels, attend_fwd(): pl.pallas_call(fwd_kernel, grid_spec=pltpu.PrefetchScalarGridSpec(num_sca...  121 us
    all_gather x1, waiting for transfers between devices, on_device(): table = lax.all_gather(early, ('dp', 'head'), axis=0)  107 us
    ppermute x15, waiting for transfers between devices, relative(): lax.ppermute(x, axis, [(i, (i + r) % size) for i in range(size)])  77.2 us
    all_gather x1, waiting for transfers between devices, on_device(): totals = lax.all_gather(all_own, 'dp', axis=0)  48.1 us
    all_gather x1, blocking collectives, on_device(): modulation = lax.all_gather(own_mod, 'head', axis=1, tiled=True)  47.3 us
    pallas_call x4, Pallas kernels, weight_grad(): pl.pallas_call(wgrad_kernel, grid=(seq // step,), in_specs=[pl.BlockSpec(...  34.5 us
    unnamed x95, local copies, waits for them, and re-layouts  29.9 us
  transfers between devices with their start and end apart: 20, of which 13 were waited for; matrix products, arithmetic and copies ran while one was open for 13% of the time, Pallas kernels for 36%

profile of v2, /device:TPU:0, one launch (start us, length us, event | category | flops | bytes accessed | tf_op | source)
XLA Modules:
  0.0 974.8 jit_solution(14106744623126161869)
XLA Ops:
  7.2 3.2 copy.122
  16.3 3.0 collective-permute-start.5
  19.3 12.6 %collective-permute-done.5 = bf16[272,1024]{1,0:T(8,128)(2,1)S(1)} collective-permute-done((bf16[272,1024]{1,0:T(8,128)(2,1)S(1)}, bf16[272,1024]{1,0:T(8,128)(2,1)S(1)}, u32[]{:S(2)}, u32[]{:S(2)}) %collective-permute-start.5) | collective-permute-done | bytes 557088 | tf_op jit(solution)/shard_map/ppermute | solution.py:339
  40.1 2.9 copy.126.w_ref
  43.0 2.4 tile.58
  45.4 3.1 copy.127.cos_ref
  51.7 3.7 fusion.32
  55.4 47.3 %all-gather = f32[6144]{0:T(1024)S(1)} all-gather(f32[3072]{0:T(1024)S(1)} %convert_add_fusion.2), channel_id=2, replica_groups=mesh['dp'=16,'head'=2] {'head'}, dimensions={0}, use_global_device_ids=true | all-gather | bytes 36864 | tf_op jit(solution)/shard_map/all_gather | solution.py:386
  104.2 11.8 %project.2 = (bf16[3,3072,512]{2,1,0:T(8,128)(2,1)}, bf16[1024,3072]{1,0:T(8,128)(2,1)}) custom-call(s32[1]{0:T(128)} %bitcast.10.base, bf16[1536,1024]{1,0:T(8,128)(2,1)} %x_ref.3, f32[1,1024]{1,0:T(1,128)} %get-tuple-element.165.scale_ref, f32[1,1024]{1,0:T(1,128)} %get-tuple-element.164.shift_ref, bf16[1024,1536]{1,0:T(8,128)(2,1)} %copy.126.w_ref, ...), custom_call_target="tpu_custom_call" | custom-call | flops 4831838208 | bytes 11010048 | tf_op jit(solution)/shard_map/project/pallas_call | solution.py:258
  118.3 11.7 %project.3 = (bf16[3,3072,512]{2,1,0:T(8,128)(2,1)}, bf16[1024,3072]{1,0:T(8,128)(2,1)}) custom-call(s32[1]{0:T(128)} %bitcast.6.base, bf16[1536,1024]{1,0:T(8,128)(2,1)} %collective-permute-done.x_ref, f32[1,1024]{1,0:T(1,128)} %get-tuple-element.165.scale_ref, ...), custom_call_target="tpu_custom_call", output_to_operand_aliasing={{0}: (8, {}), {1}: (9, {})} | custom-call | flops 4831838208 | bytes 11010048 | tf_op jit(solution)/shard_map/project/pallas_call | solution.py:258
  130.0 30.3 %attend_fwd.4 = (bf16[3072,128]{1,0:T(8,128)(2,1)}, f32[1,8,3072]{2,1,0:T(8,128)}) custom-call(s32[36]{0:T(128)} %pad_add_fusion.tab, bf16[3,3072,512]{2,1,0:T(8,128)(2,1)} %get-tuple-element.38.q_ref.k_ref.v_ref, bf16[3,3072,512]{2,1,0:T(8,128)(2,1)} %get-tuple-element.38.q_ref.k_ref.v_ref, bf16[3,3072,512]{2,1,0:T(8,128)(2,1)} %get-tuple-element.38.q_ref.k_ref.v_ref, ...), custom_call_target="tpu_custom_call" | custom-call | tf_op jit(solution)/shard_map/attend_fwd/pallas_call | solution.py:120
  160.3 30.3 %attend_fwd.5 = (bf16[3072,128]{1,0:T(8,128)(2,1)}, f32[1,8,3072]{2,1,0:T(8,128)}) custom-call(s32[36]{0:T(128)} %pad_add_fusion.tab, bf16[3,3072,512]{2,1,0:T(8,128)(2,1)} %get-tuple-element.38.q_ref.k_ref.v_ref, bf16[3,3072,512]{2,1,0:T(8,128)(2,1)} %get-tuple-element.38.q_ref.k_ref.v_ref, bf16[3,3072,512]{2,1,0:T(8,128)(2,1)} %get-tuple-element.38.q_ref.k_ref.v_ref, ...), custom_call_target="tpu_custom_call" | custom-call | tf_op jit(solution)/shard_map/attend_fwd/pallas_call | solution.py:120
  190.6 30.3 %attend_fwd.6 = (bf16[3072,128]{1,0:T(8,128)(2,1)}, f32[1,8,3072]{2,1,0:T(8,128)}) custom-call(s32[36]{0:T(128)} %pad_add_fusion.tab, bf16[3,3072,512]{2,1,0:T(8,128)(2,1)} %get-tuple-element.38.q_ref.k_ref.v_ref, bf16[3,3072,512]{2,1,0:T(8,128)(2,1)} %get-tuple-element.38.q_ref.k_ref.v_ref, bf16[3,3072,512]{2,1,0:T(8,128)(2,1)} %get-tuple-element.38.q_ref.k_ref.v_ref, ...), custom_call_target="tpu_custom_call" | custom-call | tf_op jit(solution)/shard_map/attend_fwd/pallas_call | solution.py:120
  220.8 30.6 %attend_fwd.7 = (bf16[3072,128]{1,0:T(8,128)(2,1)}, f32[1,8,3072]{2,1,0:T(8,128)}) custom-call(s32[36]{0:T(128)} %pad_add_fusion.tab, bf16[3,3072,512]{2,1,0:T(8,128)(2,1)} %get-tuple-element.38.q_ref.k_ref.v_ref, bf16[3,3072,512]{2,1,0:T(8,128)(2,1)} %get-tuple-element.38.q_ref.k_ref.v_ref, bf16[3,3072,512]{2,1,0:T(8,128)(2,1)} %get-tuple-element.38.q_ref.k_ref.v_ref, ...), custom_call_target="tpu_custom_call" | custom-call | tf_op jit(solution)/shard_map/attend_fwd/pallas_call | solution.py:120
  260.8 3.4 collective-permute-done.2
  265.0 3.4 collective-permute-done.3
  269.2 3.4 collective-permute-done.4
  274.8 3.3 fusion.48
  278.8 9.9 %fusion.45 = (f32[1536]{0:T(1024)S(1)}, f32[1536,1024]{1,0:T(8,128)S(1)}, f32[1536,1024]{1,0:T(8,128)}) fusion(f32[1024]{0:T(1024)S(1)} %convert_element_type.121, f32[1024]{0:T(1024)S(1)} %bitcast.134, bf16[1536,1024]{1,0:T(8,128)(2,1)} %x_ref.3, bf16[1536,1024]{1,0:T(8,128)(2,1)} %constant_dynamic-update-slice_fusion, ...), kind=kOutput, calls=%fused_computation.181 | convolution fusion | flops 3233282560 | bytes 20985856 | tf_op jit(solution)/shard_map/dot_general | solution.py:439
  290.3 10.1 %fusion.12 = f32[1536,2048]{1,0:T(8,128)} fusion(bf16[1024,1024]{1,0:T(8,128)(2,1)S(1)} %bitcast.122, bf16[1024,1024]{1,0:T(8,128)(2,1)S(1)} %copy-done.21, f32[1536,1024]{1,0:T(8,128)S(1)} %get-tuple-element.128, f32[1024]{0:T(1024)S(1)} %bitcast.150, f32[1024]{0:T(1024)S(1)} %bitcast.146, f32[1536]{0:T(1024)S(1)} %add_rsqrt_fusion, ...), kind=kOutput, calls=%fused_computation.40 | convolution fusion | flops 6458703872 | bytes 23089152 | tf_op jit(solution)/shard_map/dot_general | solution.py:443
  300.4 22.8 %convert_reduce_fusion = (f32[2048]{0:T(1024)}, bf16[1536,2048]{1,0:T(8,128)(2,1)}) fusion(f32[1536,2048]{1,0:T(8,128)} %fusion.12, f32[2048]{0:T(1024)S(1)} %maximum_convert_fusion, bf16[1024,1024]{1,0:T(8,128)(2,1)S(1)} %bitcast.120, bf16[1024,1024]{1,0:T(8,128)(2,1)S(1)} %copy-done.23, bf16[1536,1024]{1,0:T(8,128)(2,1)} %param.27, f32[1024]{0:T(1024)S(1)} %bitcast.143), kind=kOutput, calls=%fused_computation.10 | convolution fusion | flops 6527907840 | bytes 26234880 | tf_op jit(solution)/shard_map/fd,hd->fh/dot_general | solution.py:451
  323.3 10.3 %convolution_convert_fusion.1 = bf16[1024,2048]{1,0:T(8,128)(2,1)S(1)} fusion(bf16[1536,2048]{1,0:T(8,128)(2,1)} %get-tuple-element.178, f32[1536,1024]{1,0:T(8,128)S(1)} %get-tuple-element.128, f32[1024]{0:T(1024)S(1)} %bitcast.151, f32[1024]{0:T(1024)S(1)} %bitcast.147, f32[1536]{0:T(1024)S(1)} %add_rsqrt_fusion, f32[1536]{0:T(1024)S(1)} %broadcast_multiply_fusion.2), kind=kOutput, calls=%fused_computation.33 | convolution fusion | flops 6452412416 | bytes 16797696 | tf_op jit(solution)/shard_map/fd,fh->dh/dot_general | solution.py:454
  333.6 14.3 %multiply_reduce_fusion.1 = (f32[1024]{0:T(1024)}, f32[1536]{0:T(1024)S(1)}, f32[1536]{0:T(1024)S(1)}, f32[1024]{0:T(1024)}, f32[1536,1024]{1,0:T(8,128)}) fusion(f32[1536,1024]{1,0:T(8,128)S(1)} %get-tuple-element.128, f32[1536]{0:T(1024)S(1)} %add_rsqrt_fusion, f32[1536]{0:T(1024)S(1)} %broadcast_multiply_fusion.2, f32[1024]{0:T(1024)S(1)} %bitcast.148, ...), kind=kOutput, calls=%fused_computation.18 | convolution fusion | flops 6464990208 | bytes 23105536 | tf_op jit(solution)/shard_map/fh,dh->fd/dot_general | solution.py:456
  347.9 14.4 %convolution_convert_fusion = bf16[2048,1024]{1,0:T(8,128)(2,1)} fusion(bf16[1536,1024]{1,0:T(8,128)(2,1)S(1)} %copy-done.32, f32[1024]{0:T(1024)S(1)} %bitcast.144, f32[1536,2048]{1,0:T(8,128)} %fusion.12, f32[2048]{0:T(1024)S(1)} %maximum_convert_fusion), kind=kOutput, calls=%fused_computation.32 | convolution fusion | flops 6480723968 | bytes 19935232 | tf_op jit(solution)/shard_map/fh,fd->hd/dot_general | solution.py:453
  363.0 21.0 %fusion.8 = (f32[1024]{0:T(1024)S(1)}, f32[1024]{0:T(1024)S(1)}, bf16[1536,1024]{1,0:T(8,128)(2,1)}, f32[1024]{0:T(1024)S(1)}, f32[1536,1024]{1,0:T(8,128)}) fusion(bf16[1536,1024]{1,0:T(8,128)(2,1)} %param.27, f32[1024]{0:T(1024)S(1)} %copy-done.27, f32[1024]{0:T(1024)S(1)} %bitcast.145, f32[1536,1024]{1,0:T(8,128)S(1)} %get-tuple-element.128, ...), kind=kOutput, calls=%fused_computation.16 | convolution fusion | flops 6516896768 | bytes 48295936 | tf_op jit(solution)/shard_map/dot_general | solution.py:446
  384.0 3.8 convert_reduce_fusion.2
  387.8 5.7 convolution_convert_fusion.3
  402.6 5.7 convolution_convert_fusion.2
  414.3 3.0 collective-permute-done.6
  418.3 37.8 %attend_bwd.4.rest_0_.g_ref = bf16[3,3072,128]{2,1,0:T(8,128)(2,1)} custom-call(s32[36]{0:T(128)} %pad_add_fusion.tab, bf16[3,3072,512]{2,1,0:T(8,128)(2,1)} %get-tuple-element.38.q_ref.k_ref.v_ref, bf16[3,3072,512]{2,1,0:T(8,128)(2,1)} %get-tuple-element.38.q_ref.k_ref.v_ref, bf16[3,3072,512]{2,1,0:T(8,128)(2,1)} %get-tuple-element.38.q_ref.k_ref.v_ref, ...), custom_call_target="tpu_custom_call" | custom-call | tf_op jit(solution)/shard_map/attend_bwd/pallas_call | solution.py:211
  456.1 8.6 weight_grad.4
  468.9 37.7 %attend_bwd.5.rest_1_.g_ref = bf16[3,3072,128]{2,1,0:T(8,128)(2,1)} custom-call(s32[36]{0:T(128)} %pad_add_fusion.tab, bf16[3,3072,512]{2,1,0:T(8,128)(2,1)} %get-tuple-element.38.q_ref.k_ref.v_ref, bf16[3,3072,512]{2,1,0:T(8,128)(2,1)} %get-tuple-element.38.q_ref.k_ref.v_ref, bf16[3,3072,512]{2,1,0:T(8,128)(2,1)} %get-tuple-element.38.q_ref.k_ref.v_ref, ...), custom_call_target="tpu_custom_call" | custom-call | tf_op jit(solution)/shard_map/attend_bwd/pallas_call | solution.py:211
  506.6 8.6 weight_grad.5
  519.5 37.7 %attend_bwd.6.rest_2_.g_ref = bf16[3,3072,128]{2,1,0:T(8,128)(2,1)} custom-call(s32[36]{0:T(128)} %pad_add_fusion.tab, bf16[3,3072,512]{2,1,0:T(8,128)(2,1)} %get-tuple-element.38.q_ref.k_ref.v_ref, bf16[3,3072,512]{2,1,0:T(8,128)(2,1)} %get-tuple-element.38.q_ref.k_ref.v_ref, bf16[3,3072,512]{2,1,0:T(8,128)(2,1)} %get-tuple-element.38.q_ref.k_ref.v_ref, ...), custom_call_target="tpu_custom_call" | custom-call | tf_op jit(solution)/shard_map/attend_bwd/pallas_call | solution.py:211
  557.2 8.7 weight_grad.6
  570.1 37.6 %attend_bwd.7.rest_3_.g_ref = bf16[3,3072,128]{2,1,0:T(8,128)(2,1)} custom-call(s32[36]{0:T(128)} %pad_add_fusion.tab, bf16[3,3072,512]{2,1,0:T(8,128)(2,1)} %get-tuple-element.38.q_ref.k_ref.v_ref, bf16[3,3072,512]{2,1,0:T(8,128)(2,1)} %get-tuple-element.38.q_ref.k_ref.v_ref, bf16[3,3072,512]{2,1,0:T(8,128)(2,1)} %get-tuple-element.38.q_ref.k_ref.v_ref, ...), custom_call_target="tpu_custom_call" | custom-call | tf_op jit(solution)/shard_map/attend_bwd/pallas_call | solution.py:211
  607.8 8.6 weight_grad.7
  620.7 3.6 copy.148
  624.3 6.3 reshape.248
  632.9 4.6 copy.133
  637.5 4.0 slice.136
  641.5 4.7 reshape_reshape.13
  646.2 4.3 copy.132
  650.5 3.2 copy.134
  653.7 2.5 constant_dynamic-slice_fusion.4
  660.6 2.5 constant_dynamic-slice_fusion.6
  666.2 3.7 pad_maximum_fusion.w_ref
  672.9 5.0 collective-permute-done.13.rest_7_
  677.9 12.6 %collective-permute-done.12.rest_6_ = bf16[3,1536,128]{2,1,0:T(8,128)(2,1)} collective-permute-done((bf16[3,1536,128]{2,1,0:T(8,128)(2,1)}, bf16[3,1536,128]{2,1,0:T(8,128)(2,1)}, u32[]{:S(2)}, u32[]{:S(2)}) %collective-permute-start.12) | collective-permute-done | bytes 1179680 | tf_op jit(solution)/shard_map/ppermute | solution.py:339
  690.5 16.2 %collective-permute-done.11.rest_5_ = bf16[3,1536,128]{2,1,0:T(8,128)(2,1)} collective-permute-done((bf16[3,1536,128]{2,1,0:T(8,128)(2,1)}, bf16[3,1536,128]{2,1,0:T(8,128)(2,1)}, u32[]{:S(2)}, u32[]{:S(2)}) %collective-permute-start.11) | collective-permute-done | bytes 1179680 | tf_op jit(solution)/shard_map/ppermute | solution.py:339
  706.7 12.6 %collective-permute-done.10.rest_4_ = bf16[3,1536,128]{2,1,0:T(8,128)(2,1)} collective-permute-done((bf16[3,1536,128]{2,1,0:T(8,128)(2,1)}, bf16[3,1536,128]{2,1,0:T(8,128)(2,1)}, u32[]{:S(2)}, u32[]{:S(2)}) %collective-permute-start.10) | collective-permute-done | bytes 1179680 | tf_op jit(solution)/shard_map/ppermute | solution.py:339
  719.3 19.2 %input_grad.1 = (f32[1536,1024]{1,0:T(8,128)}, f32[8,1024]{1,0:T(8,128)}) custom-call(s32[1]{0:T(128)} %bitcast.10.base, bf16[1536,1024]{1,0:T(8,128)(2,1)} %x_ref.3, f32[1536,1024]{1,0:T(8,128)} %get-tuple-element.139.gm_ref, f32[1,1024]{1,0:T(1,128)} %get-tuple-element.165.scale_ref, bf16[1024,3072]{1,0:T(8,128)(2,1)} %pad_maximum_fusion.w_ref, ...), custom_call_target="tpu_custom_call" | custom-call | flops 9663676416 | bytes 25165824 | tf_op jit(solution)/shard_map/input_grad/pallas_call | solution.py:324
  743.9 4.6 collective-permute-done.14
  751.5 107.4 %all-gather.13.cloned.1.call-done = f32[32,1,11776]{2,1,0:T(1,128)} async-done(((f32[1,1,11776]{2,1,0:T(1,128)}), f32[32,1,11776]{2,1,0:T(1,128)}) %all-gather.13.cloned.1.call-update) | async-done | bytes 1507344 | tf_op jit(solution)/shard_map/all_gather | solution.py:515
  858.9 5.0 reduce.7
  867.2 4.5 multiply_reduce_fusion
  871.7 5.2 psum.7
  878.7 8.1 fusion.26
  886.7 48.1 %all-gather.11.cloned.1.call-done = bf16[4096,1024]{1,0:T(8,128)(2,1)} async-done(((bf16[256,1024]{1,0:T(8,128)(2,1)}), bf16[4096,1024]{1,0:T(8,128)(2,1)}) %all-gather.11.cloned.1.call-update) | async-done | bytes 8388624 | tf_op jit(solution)/shard_map/all_gather | solution.py:502
  934.8 5.5 slice_convert_fusion
  942.3 10.6 %reshape.261 = f32[1024,3,512]{2,1,0:T(4,128)} reshape(f32[16,96,1024]{2,1,0:T(8,128)} %slice_convert_fusion) | data formatting | bytes 12582912 | tf_op jit(solution)/shard_map/reshape;reshape | solution.py:508
  952.9 8.3 copy.149
  961.1 2.6 bitcast_convert_fusion
  963.8 2.6 bitcast_convert_fusion.1
  (218 shorter events, 99.6 us)
Async XLA Ops:
  7.2 24.8 %copy-start.16 = (bf16[1,1024]{1,0:T(2,128)(2,1)S(1)}, bf16[1,1024]{1,0:T(2,128)(2,1)}, u32[]{:S(2)}) copy-start(bf16[1,1024]{1,0:T(2,128)(2,1)} %param.15) | copy-start | bytes 6148
  7.2 28.0 %copy-start.15 = (s32[1,3072]{1,0:T(1,128)S(1)}, s32[1,3072]{1,0:T(1,128)}, u32[]{:S(2)}) copy-start(s32[1,3072]{1,0:T(1,128)} %param.16) | copy-start | bytes 36868
  7.2 266.2 %all-gather.9.cloned.1.call-start = ((), (), s32[]{:S(2)}) async-start(), calls=%async_computation.4 | async-start | bytes 10027008 | tf_op jit(solution)/shard_map/all_gather | solution.py:381
  10.4 35.0 %copy-start = (bf16[1024,3,512]{0,2,1:T(8,128)(2,1)}, bf16[1024,3,512]{0,2,1:T(8,128)(2,1)S(1)}, u32[]{:S(2)}) copy-start(bf16[1024,3,512]{0,2,1:T(8,128)(2,1)S(1)} %copy.122) | copy-start | bytes 9437188
  16.3 15.7 %collective-permute-start.5 = (bf16[272,1024]{1,0:T(8,128)(2,1)S(1)}, bf16[272,1024]{1,0:T(8,128)(2,1)S(1)}, u32[]{:S(2)}, u32[]{:S(2)}) collective-permute-start(bf16[272,1024]{1,0:T(8,128)(2,1)S(1)} %constant_dynamic-update-slice_fusion.4), channel_id=1, source_target_pairs={{0,1},{1,0},{2,3},{3,2},{4,5},{5,4},{6,7},{7,6},{8,9},{9,8},{10,11... | collective-permute-start | bytes 1671176 | tf_op jit(solution)/shard_map/ppermute | solution.py:339
  32.8 707.6 %reduce-scatter.3.cloned.1.call-start = ((), (), s32[]{:S(2)}) async-start(), calls=%async_computation.2 | async-start | bytes 11141120 | tf_op jit(solution)/shard_map/reduce_scatter | solution.py:479
  32.9 85.4 %collective-permute-start = (bf16[1536,1024]{1,0:T(8,128)(2,1)}, bf16[1536,1024]{1,0:T(8,128)(2,1)}, u32[]{:S(2)}, u32[]{:S(2)}) collective-permute-start(bf16[1536,1024]{1,0:T(8,128)(2,1)} %x_ref.3), channel_id=1, source_target_pairs={{0,1},{1,0},{2,3},{3,2},{4,5},{5,4},{6,7},{7,6},{8,9},{9,8},{10,11... | collective-permute-start | bytes 9437192 | tf_op jit(solution)/shard_map/ppermute | solution.py:339
  45.4 4.9 copy-start.18
  45.4 5.5 copy-start.20
  45.4 5.6 copy-start.19
  45.4 5.7 copy-start.30
  45.4 5.7 copy-start.31
  48.5 6.9 copy-start.26
  220.8 30.6 %copy-start.9 = (bf16[3072,128]{1,0:T(8,128)(2,1)S(1)}, bf16[3072,128]{1,0:T(8,128)(2,1)}, u32[]{:S(2)}) copy-start(bf16[3072,128]{1,0:T(8,128)(2,1)} %get-tuple-element.39.o_ref) | copy-start | bytes 2359300
  220.8 32.9 %copy-start.8 = (bf16[3072,128]{1,0:T(8,128)(2,1)S(1)}, bf16[3072,128]{1,0:T(8,128)(2,1)}, u32[]{:S(2)}) copy-start(bf16[3072,128]{1,0:T(8,128)(2,1)} %get-tuple-element.40.o_ref) | copy-start | bytes 2359300
  220.8 34.2 %copy-start.7 = (bf16[3072,128]{1,0:T(8,128)(2,1)S(1)}, bf16[3072,128]{1,0:T(8,128)(2,1)}, u32[]{:S(2)}) copy-start(bf16[3072,128]{1,0:T(8,128)(2,1)} %get-tuple-element.41.o_ref) | copy-start | bytes 2359300
  252.3 7.8 collective-permute-start.1
  254.5 9.7 collective-permute-start.2
  255.9 12.6 %collective-permute-start.3 = (bf16[1536,128]{1,0:T(8,128)(2,1)S(1)}, bf16[1536,128]{1,0:T(8,128)(2,1)S(1)}, u32[]{:S(2)}, u32[]{:S(2)}) collective-permute-start(bf16[1536,128]{1,0:T(8,128)(2,1)S(1)} %get-tuple-element.153), channel_id=1, source_target_pairs={{0,1},{1,0},{2,3},{3,2},{4,5},{5,4},{6,7},{7,6},{8,9},{9,8},{10,11... | collective-permute-start | bytes 1179656 | tf_op jit(solution)/shard_map/ppermute | solution.py:339
  259.2 13.4 %collective-permute-start.4 = (bf16[1536,128]{1,0:T(8,128)(2,1)S(1)}, bf16[1536,128]{1,0:T(8,128)(2,1)S(1)}, u32[]{:S(2)}, u32[]{:S(2)}) collective-permute-start(bf16[1536,128]{1,0:T(8,128)(2,1)S(1)} %get-tuple-element.151), channel_id=1, source_target_pairs={{0,1},{1,0},{2,3},{3,2},{4,5},{5,4},{6,7},{7,6},{8,9},{9,8},{10,11... | collective-permute-start | bytes 1179656 | tf_op jit(solution)/shard_map/ppermute | solution.py:339
  274.8 14.0 %copy-start.14 = (bf16[16,32,1024]{2,1,0:T(8,128)(2,1)}, bf16[16,32,1024]{2,1,0:T(8,128)(2,1)S(1)}, u32[]{:S(2)}) copy-start(bf16[16,32,1024]{2,1,0:T(8,128)(2,1)S(1)} %slice.132) | copy-start | bytes 3145732
  288.7 0.8 copy-start.25
  288.7 1.6 copy-start.21
  290.3 10.1 %copy-start.23 = (bf16[1024,1024]{1,0:T(8,128)(2,1)S(1)}, bf16[1024,1024]{1,0:T(8,128)(2,1)}, u32[]{:S(2)}) copy-start(bf16[1024,1024]{1,0:T(8,128)(2,1)} %param.25) | copy-start | bytes 6291460
  323.3 10.3 %copy-start.22 = (bf16[1024,1024]{1,0:T(8,128)(2,1)S(1)}, bf16[1024,1024]{1,0:T(8,128)(2,1)}, u32[]{:S(2)}) copy-start(bf16[1024,1024]{1,0:T(8,128)(2,1)} %param.23) | copy-start | bytes 6291460
  333.6 14.3 %copy-start.32 = (bf16[1536,1024]{1,0:T(8,128)(2,1)S(1)}, bf16[1536,1024]{1,0:T(8,128)(2,1)}, u32[]{:S(2)}) copy-start(bf16[1536,1024]{1,0:T(8,128)(2,1)} %param.27) | copy-start | bytes 9437188
  362.3 0.7 copy-start.27
  387.8 7.0 copy-start.6
  402.5 340.4 %reduce-scatter.5.cloned.1.call-start = ((), (), s32[]{:S(2)}) async-start(), calls=%async_computation.3 | async-start | bytes 3342336 | tf_op jit(solution)/shard_map/reduce_scatter | solution.py:500
  409.6 7.8 collective-permute-start.6
  411.0 56.0 %collective-permute-start.7 = (bf16[1536,128]{1,0:T(8,128)(2,1)}, bf16[1536,128]{1,0:T(8,128)(2,1)}, u32[]{:S(2)}, u32[]{:S(2)}) collective-permute-start(bf16[1536,128]{1,0:T(8,128)(2,1)} %get-tuple-element.147), channel_id=1, source_target_pairs={{0,1},{1,0},{2,3},{3,2},{4,5},{5,4},{6,7},{7,6},{8,9},{9,8},{10,11... | collective-permute-start | bytes 1179656 | tf_op jit(solution)/shard_map/ppermute | solution.py:339
  411.6 106.0 %collective-permute-start.8 = (bf16[1536,128]{1,0:T(8,128)(2,1)}, bf16[1536,128]{1,0:T(8,128)(2,1)}, u32[]{:S(2)}, u32[]{:S(2)}) collective-permute-start(bf16[1536,128]{1,0:T(8,128)(2,1)} %get-tuple-element.146), channel_id=1, source_target_pairs={{0,1},{1,0},{2,3},{3,2},{4,5},{5,4},{6,7},{7,6},{8,9},{9,8},{10,11... | collective-permute-start | bytes 1179656 | tf_op jit(solution)/shard_map/ppermute | solution.py:339
  413.0 155.2 %collective-permute-start.9 = (bf16[1536,128]{1,0:T(8,128)(2,1)S(1)}, bf16[1536,128]{1,0:T(8,128)(2,1)}, u32[]{:S(2)}, u32[]{:S(2)}) collective-permute-start(bf16[1536,128]{1,0:T(8,128)(2,1)S(1)} %get-tuple-element.144), channel_id=1, source_target_pairs={{0,1},{1,0},{2,3},{3,2},{4,5},{5,4},{6,7},{7,6},{8,9},{9,8},{10,11... | collective-permute-start | bytes 1179656 | tf_op jit(solution)/shard_map/ppermute | solution.py:339
  417.4 0.9 copy-start.12
  468.0 0.9 copy-start.13
  518.6 0.9 copy-start.11
  569.2 0.9 copy-start.10
  624.3 6.4 copy-start.1
  630.6 228.3 %all-gather.13.cloned.1.call-start = ((), (), s32[]{:S(2)}) async-start(), calls=%async_computation.6 | async-start | bytes 1554432 | tf_op jit(solution)/shard_map/all_gather | solution.py:515
  653.6 10.8 %copy-start.5 = (bf16[3,3072,128]{2,1,0:T(8,128)(2,1)S(1)}, bf16[3,3072,128]{2,1,0:T(8,128)(2,1)}, u32[]{:S(2)}) copy-start(bf16[3,3072,128]{2,1,0:T(8,128)(2,1)} %attend_bwd.4.rest_0_.g_ref) | copy-start | bytes 7077892
  653.7 12.5 %copy-start.2 = (bf16[1024,1536]{1,0:T(8,128)(2,1)S(1)}, bf16[1024,1536]{1,0:T(8,128)(2,1)}, u32[]{:S(2)}) copy-start(bf16[1024,1536]{1,0:T(8,128)(2,1)} %copy.133) | copy-start | bytes 9437188
  656.2 21.7 %collective-permute-start.13 = (bf16[3,1536,128]{2,1,0:T(8,128)(2,1)}, bf16[3,1536,128]{2,1,0:T(8,128)(2,1)}, u32[]{:S(2)}, u32[]{:S(2)}) collective-permute-start(bf16[3,1536,128]{2,1,0:T(8,128)(2,1)} %constant_dynamic-slice_fusion.4), channel_id=1, source_target_pairs={{0,1},{1,0},{2,3},{3,2},{4,5},{5,4},{6,7},{7,6},{8,9},{9,8},{10,11... | collective-permute-start | bytes 3538952 | tf_op jit(solution)/shard_map/ppermute | solution.py:339
  660.0 30.5 %collective-permute-start.12 = (bf16[3,1536,128]{2,1,0:T(8,128)(2,1)}, bf16[3,1536,128]{2,1,0:T(8,128)(2,1)}, u32[]{:S(2)}, u32[]{:S(2)}) collective-permute-start(bf16[3,1536,128]{2,1,0:T(8,128)(2,1)} %constant_dynamic-slice_fusion.5), channel_id=1, source_target_pairs={{0,1},{1,0},{2,3},{3,2},{4,5},{5,4},{6,7},{7,6},{8,9},{9,8},{10,11... | collective-permute-start | bytes 3538952 | tf_op jit(solution)/shard_map/ppermute | solution.py:339
  663.1 43.6 %collective-permute-start.11 = (bf16[3,1536,128]{2,1,0:T(8,128)(2,1)}, bf16[3,1536,128]{2,1,0:T(8,128)(2,1)}, u32[]{:S(2)}, u32[]{:S(2)}) collective-permute-start(bf16[3,1536,128]{2,1,0:T(8,128)(2,1)} %constant_dynamic-slice_fusion.6), channel_id=1, source_target_pairs={{0,1},{1,0},{2,3},{3,2},{4,5},{5,4},{6,7},{7,6},{8,9},{9,8},{10,11... | collective-permute-start | bytes 3538952 | tf_op jit(solution)/shard_map/ppermute | solution.py:339
  665.5 7.3 copy-start.24
  665.5 53.8 %collective-permute-start.10 = (bf16[3,1536,128]{2,1,0:T(8,128)(2,1)}, bf16[3,1536,128]{2,1,0:T(8,128)(2,1)}, u32[]{:S(2)}, u32[]{:S(2)}) collective-permute-start(bf16[3,1536,128]{2,1,0:T(8,128)(2,1)} %constant_dynamic-slice_fusion.7), channel_id=1, source_target_pairs={{0,1},{1,0},{2,3},{3,2},{4,5},{5,4},{6,7},{7,6},{8,9},{9,8},{10,11... | collective-permute-start | bytes 3538952 | tf_op jit(solution)/shard_map/ppermute | solution.py:339
  672.9 66.5 %copy-start.29 = (f32[1024]{0:T(1024)S(1)}, f32[1024]{0:T(1024)}, u32[]{:S(2)}) copy-start(f32[1024]{0:T(1024)} %get-tuple-element.114) | copy-start | bytes 12292
  672.9 66.6 %copy-start.28 = (f32[1024]{0:T(1024)S(1)}, f32[1024]{0:T(1024)}, u32[]{:S(2)}) copy-start(f32[1024]{0:T(1024)} %get-tuple-element.111) | copy-start | bytes 12292
  740.1 194.7 %all-gather.11.cloned.1.call-start = ((), (), s32[]{:S(2)}) async-start(), calls=%async_computation.5 | async-start | bytes 8912896 | tf_op jit(solution)/shard_map/all_gather | solution.py:502
  741.4 7.1 collective-permute-start.14
  864.8 12.7 %copy-start.17 = (bf16[1,1024]{1,0:T(2,128)(2,1)S(1)}, bf16[1,1024]{1,0:T(2,128)(2,1)}, u32[]{:S(2)}) copy-start(bf16[1,1024]{1,0:T(2,128)(2,1)} %param.15) | copy-start | bytes 6148
  934.8 5.6 copy-start.3
  952.9 8.3 copy-start.4
Sparse Core Ops, SparseCore 0:
  32.9 82.3 all-gather.8
  402.6 135.3 reduce-scatter.2
  630.7 91.7 reduce-scatter.4
  740.3 118.5 all-gather.12
  861.5 73.2 all-gather.10

commit v3 on v2

--- a/solution.py
+++ b/solution.py
@@ -126,6 +126,7 @@
             scratch_shapes=[pltpu.VMEM((seq + CK, 128), jnp.bfloat16)] * 3),
         out_shape=[jax.ShapeDtypeStruct((seq, pairs * 128), jnp.bfloat16), jax.ShapeDtypeStruct((pairs, 8, seq), jnp.float32)],
         compiler_params=pltpu.CompilerParams(vmem_limit_bytes=60 << 20),
+        cost_estimate=pl.CostEstimate(flops=3072 * pairs * seq * seq, bytes_accessed=8 * pairs * seq * 128, transcendentals=0),
         name="attend_fwd",
     )(tab, qkv, qkv, qkv, fq, fk)
 
@@ -217,6 +218,7 @@
             scratch_shapes=[pltpu.VMEM((seq + CK, 128), jnp.bfloat16)] * 4 + [pltpu.VMEM((seq + CK, 128), jnp.float32)] * 2),
         out_shape=jax.ShapeDtypeStruct((3, seq, pairs * 128), jnp.bfloat16),
         compiler_params=pltpu.CompilerParams(vmem_limit_bytes=60 << 20),
+        cost_estimate=pl.CostEstimate(flops=4096 * pairs * seq * seq, bytes_accessed=16 * pairs * seq * 128, transcendentals=0),
         name="attend_bwd",
     )(tab, qkv, qkv, qkv, fq, fk, o, do, lse, cos, sin)
 
@@ -268,7 +270,8 @@
         name="project",
     )(base * (frames // step), x, scale, shift, w, b, cos, sin, *(before or ()))
 
-def wgrad_kernel(nt_ref, g_ref, w_ref, b_ref, acc):
+def wgrad_kernel(nt_ref, g_ref, *rest):
+    w_ref, b_ref, acc = rest[-3:]
     i = pl.program_id(0)
     g = jnp.concatenate([g_ref[0], g_ref[1], g_ref[2]], axis=1)
     part = mm(nt_ref[...], g, NN)
@@ -285,20 +288,41 @@
     def _():
         w_ref[...] = acc[...].astype(jnp.bfloat16)
 
-def weight_grad(nt, g):
+def weight_grad(nt, g, index, groups, before=None):
     width, seq = nt.shape
     step = math.gcd(512, seq)
     return pl.pallas_call(
         wgrad_kernel,
         grid=(seq // step,),
-        in_specs=[pl.BlockSpec((width, step), lambda i: (0, i)), pl.BlockSpec((3, step, 128), lambda i: (0, i, 0))],
-        out_specs=[pl.BlockSpec((width, 384), lambda i: (0, 0)), pl.BlockSpec((8, 384), lambda i: (0, 0))],
-        out_shape=[jax.ShapeDtypeStruct((width, 384), jnp.bfloat16), jax.ShapeDtypeStruct((8, 384), jnp.float32)],
+        in_specs=[pl.BlockSpec((width, step), lambda i: (0, i)), pl.BlockSpec((3, step, 128), lambda i: (0, i, 0))]
+        + ([] if before is None else [pl.BlockSpec(memory_space=pl.ANY)]),
+        out_specs=[pl.BlockSpec((width, 384), lambda i: (0, index)), pl.BlockSpec((8, 384), lambda i: (0, 0))],
+        out_shape=[jax.ShapeDtypeStruct((width, 384 * groups), jnp.bfloat16), jax.ShapeDtypeStruct((8, 384), jnp.float32)],
         scratch_shapes=[pltpu.VMEM((width, 384), jnp.float32)],
+        input_output_aliases={} if before is None else {2: 0},
         compiler_params=pltpu.CompilerParams(vmem_limit_bytes=60 << 20),
         cost_estimate=pl.CostEstimate(flops=2 * seq * width * 384, bytes_accessed=2 * seq * (width + 384), transcendentals=0),
         name="weight_grad",
-    )(nt, g)
+    )(nt, g, *(() if before is None else (before,)))
+
+def unpack_kernel(g_ref, o_ref):
+    for t in range(3):
+        for g in range(o_ref.shape[2] // 128):
+            at = g * 384 + t * 128
+            o_ref[:, t, g * 128:(g + 1) * 128] = g_ref[:, at:at + 128].astype(jnp.float32)
+
+def unpack(g):
+    width, cols = g.shape
+    step = math.gcd(128, width)
+    return pl.pallas_call(
+        unpack_kernel,
+        grid=(width // step,),
+        in_specs=[pl.BlockSpec((step, cols), lambda i: (i, 0))],
+        out_specs=pl.BlockSpec((step, 3, cols // 3), lambda i: (i, 0, 0)),
+        out_shape=jax.ShapeDtypeStruct((width, 3, cols // 3), jnp.float32),
+        compiler_params=pltpu.CompilerParams(vmem_limit_bytes=60 << 20),
+        name="unpack",
+    )(g)
 
 def last_kernel(base, x_ref, gm_ref, scale_ref, w_ref, *rest):
     gi_ref, rows_ref = rest[-2:]
@@ -369,33 +393,30 @@
     owner = [lax.rem(me - r + n, n) for r in range(n)]
     source = [lax.rem(me + r, n) for r in range(n)]
 
-    elsewhere = [move(inputs, r) for r in range(1, n)]
+    embeds = time_embed.astype(f32)
+    silu_low = jax.nn.silu(embeds).astype(bf16)
+    own_mod = jnp.dot(silu_low, modulator_weight, preferred_element_type=f32) + modulator_bias.astype(f32)
+    modulation = jnp.zeros((1, n * local_mod), f32)
+    far_mod = [move(own_mod, r) for r in range(n)]
+    for r in range(n):
+        modulation = lax.dynamic_update_slice_in_dim(modulation, far_mod[r], owner[r] * local_mod, 1)
+    shift_a, scale_a, gate_a, shift_f, scale_f, gate_f = jnp.split(modulation, 6, axis=1)
+    half = HDIM // 2
+    freqs = 10000.0 ** (-jnp.arange(half, dtype=f32) * 2.0 / HDIM)
+    ahead, _, seg, freqs, weight_proj = lax.optimization_barrier((inputs, far_mod, segment_ids[0], freqs, projection_weight))
+    elsewhere = [move(ahead, r) for r in range(1, n)]
 
     shards = [("out", output_weight), ("expand", expand_weight), ("contract", contract_weight), ("proj", projection_weight.reshape(width, 3 * inner))]
     heights = {name: w.size // (ndp * width) for name, w in shards}
     cut = [lax.dynamic_slice_in_dim(w, mine * (w.shape[0] // ndp), w.shape[0] // ndp, 0).reshape(heights[name], width) for name, w in shards]
     bias_rows = jnp.pad(expand_bias[None, :], ((0, 15), (0, width - hidden_here)))
-    pack = jnp.concatenate(cut + [bias_rows], axis=0)
-    embed_rows = jnp.pad(time_embed, ((0, 15), (0, 0)))
-    packs = jnp.concatenate([move(pack, r) for r in range(1, n)] + [embed_rows], axis=0)
-    packed = lax.all_gather(packs, "dp", axis=0)
-
-    embeds = time_embed.astype(f32)
-    silu_low = jax.nn.silu(embeds).astype(bf16)
-    own_mod = jnp.dot(silu_low, modulator_weight, preferred_element_type=f32) + modulator_bias.astype(f32)
-    modulation = lax.all_gather(own_mod, "head", axis=1, tiled=True)
-    shift_a, scale_a, gate_a, shift_f, scale_f, gate_f = jnp.split(modulation, 6, axis=1)
-
-    seg = segment_ids[0]
     tab = span_table(seg, seq)
     fq, fk = features(seg)
-    half = HDIM // 2
-    freqs = 10000.0 ** (-jnp.arange(half, dtype=f32) * 2.0 / HDIM)
     angles = jnp.arange(seq, dtype=f32)[:, None] * freqs[None, :]
     cosine = jnp.tile(jnp.cos(angles), (1, 4))
     sine = jnp.tile(jnp.sin(angles), (1, 4))
 
-    weight_proj = projection_weight.reshape(width, 3 * inner)
+    weight_proj = weight_proj.reshape(width, 3 * inner)
     bias_proj = projection_bias.astype(f32).reshape(1, 3 * inner)
     place = lambda r: owner[r].astype(jnp.int32).reshape(1)
     into = project(place(0), seq, inputs, scale_a, shift_a, weight_proj, bias_proj, cosine, sine)
@@ -403,15 +424,25 @@
         into = project(place(r), seq, elsewhere[r - 1], scale_a, shift_a, weight_proj, bias_proj, cosine, sine, into)
     qkv, normed_t = into
 
+    pack = jnp.concatenate(cut + [bias_rows], axis=0)
+    pack, qkv = lax.optimization_barrier((pack, qkv))
+    moved = [move(pack, r) for r in range(1, n)]
+    embed_rows = jnp.pad(time_embed, ((0, 15), (0, 0)))
+
     attended, log_mass, attended_here = [], [], []
     for g in range(groups):
         o, lse = attend_fwd(tab, qkv, fq, fk, g, 1)
         attended.append(o)
         log_mass.append(lse)
-        attended_here.append([
-            move(lax.dynamic_slice_in_dim(o, source[r] * frames_here, frames_here, 0), r) for r in range(n)
-        ])
-    packed, _ = lax.optimization_barrier((packed, log_mass[min(1, groups - 1)]))
+        halves = [lax.dynamic_slice_in_dim(o, source[r] * frames_here, frames_here, 0) for r in range(n)]
+        halves, tab = lax.optimization_barrier((halves, tab))
+        attended_here.append([move(halves[r], r) for r in range(n)])
+        if g == 0:
+            moved, tab = lax.optimization_barrier((moved, tab))
+            packed = lax.all_gather(jnp.concatenate(moved + [embed_rows], axis=0), "dp", axis=0)
+        else:
+            attended_here[g - 1], tab = lax.optimization_barrier((attended_here[g - 1], tab))
+    packed, _ = lax.optimization_barrier((packed, log_mass[-1]))
     att_rel = [jnp.concatenate([attended_here[g][r] for g in range(groups)], axis=1) for r in range(n)]
 
     own_w = dict(shards)
@@ -478,11 +509,7 @@
             contract_part[r * hidden_here:(r + 1) * hidden_here])], axis=1)
     reduced = lax.psum_scatter(sent, "dp", scatter_dimension=0, tiled=False)
     tall = reduced.shape[0] // n
-    own_grads = reduced[:tall].astype(f32)
-    for r in range(1, n):
-        own_grads = own_grads + move(reduced[r * tall:(r + 1) * tall], -r).astype(f32)
-
-    flat, flat_far, wgrads, bias_sums = [], [[] for _ in range(1, n)], [], []
+    flat, flat_far, wgrads, bias_sums = [], [[] for _ in range(1, n)], None, []
     for g in range(groups):
         whole = jnp.zeros((seq, 128), bf16)
         for r in range(n):
@@ -490,22 +517,32 @@
             whole = lax.dynamic_update_slice_in_dim(whole, piece, source[r] * frames_here, 0)
         back = attend_bwd(tab, qkv, fq, fk, attended[g], whole, log_mass[g], cosine, sine, g, 1)
         flat.append(back)
+        parts = [lax.dynamic_slice_in_dim(back, source[r] * frames_here, frames_here, 1) for r in range(1, n)]
+        arrived = [far[-1] for far in flat_far if far]
+        parts, arrived, back = lax.optimization_barrier((parts, arrived, back))
         for r in range(1, n):
-            flat_far[r - 1].append(move(lax.dynamic_slice_in_dim(back, source[r] * frames_here, frames_here, 1), r))
-        w, b = weight_grad(normed_t, back)
-        wgrads.append(w)
+            if arrived:
+                flat_far[r - 1][-1] = arrived[r - 1]
+            flat_far[r - 1].append(move(parts[r - 1], r))
+        wgrads, b = weight_grad(normed_t, back, g, groups, wgrads)
+        wgrads, tab = lax.optimization_barrier((wgrads, tab))
+        if g == max(groups - 2, 0):
+            reduced, tab = lax.optimization_barrier((reduced, tab))
+            own_grads = reduced[:tall].astype(f32)
+            for r in range(1, n):
+                own_grads = own_grads + move(reduced[r * tall:(r + 1) * tall], -r).astype(f32)
+            own_grads, tab = lax.optimization_barrier((own_grads.astype(bf16), tab))
+            own_grads = lax.all_gather(own_grads, "dp", axis=0)
         bias_sums.append(b[0].reshape(3, 128))
 
-    proj_part = jnp.stack([w.reshape(width, 3, 128) for w in wgrads], axis=2)
-    proj_own = lax.psum_scatter(proj_part.reshape(ndp, width // ndp, 3 * inner), "dp", scatter_dimension=0, tiled=False)
-    all_own = jnp.concatenate([own_grads.astype(bf16), proj_own.reshape(heights["proj"], width)], axis=0)
-    totals = lax.all_gather(all_own, "dp", axis=0)
+    wgrads, own_grads = lax.optimization_barrier((wgrads, own_grads))
+    proj_own = lax.psum_scatter(wgrads.reshape(ndp, width // ndp, 3 * inner), "dp", scatter_dimension=0, tiled=False)
+    grad_projection = unpack(lax.all_gather(proj_own, "dp", axis=0, tiled=True))
     at, grads = 0, {}
-    for name, w in shards:
-        grads[name] = totals[:, at:at + heights[name]].astype(f32).reshape(w.shape)
+    for name, w in shards[:3]:
+        grads[name] = own_grads[:, at:at + heights[name]].astype(f32).reshape(w.shape)
         at += heights[name]
     grad_output, grad_expand, grad_contract = grads["out"], grads["expand"], grads["contract"]
-    grad_projection = grads["proj"].reshape(width, 3, inner)
     bias_proj_grad = jnp.stack(bias_sums, axis=1).reshape(3 * inner)
 
     grad_inputs, row_sums = input_grad(place(0), flat, [p for far in flat_far for p in far], inputs, grad_middle, scale_a, proj_cat)

time: 975 us -> 856 us (0.88); the launches traced: 975 us -> 845 us
  waiting for transfers between devices: 233 us -> 158 us
  blocking collectives: 52.4 us -> 5.21 us
  local copies, waits for them, and re-layouts: 134 us -> 115 us
  Pallas kernels: 350 us -> 363 us
    all_gather x1, waiting for transfers between devices: 107 us -> 55.6 us  [on_device(): table = lax.all_gather(early, ('dp', 'head'), axis=0)]
    all_gather x1 -> x0, blocking collectives: 47.3 us -> none  [on_device(): modulation = lax.all_gather(own_mod, 'head', axis=1, tiled=True)]
    all_gather x2 -> x3, waiting for transfers between devices: 48.1 us -> 11.5 us  [the longest x1 11.5 us: on_device(): grad_projection = unpack(lax.all_gather(proj_own, 'dp', axis=0, tiled=True))]
    another operation x8 -> x4, local copies, waits for them, and re-layouts: 15.7 us -> 0.42 us  [the longest x1 10.6 us: on_device(): grad_projection = grads['proj'].reshape(width, 3, inner)]
    ppermute x15 -> x16, waiting for transfers between devices: 77.2 us -> 91 us  [relative(): lax.ppermute(x, axis, [(i, (i + r) % size) for i in range(size)])]
    unnamed x95 -> x120, local copies, waits for them, and re-layouts: 29.9 us -> 34.3 us
  transfers between devices with their start and end apart: 20 -> 22, of which waited for: 13 -> 8; matrix products, arithmetic and copies ran while one was open for 13% -> 15% of each run, Pallas kernels for 36% -> 40%
where the time goes in v3:
time: 856 us; the launch traced here: 845 us
  Pallas kernels  363 us (42%)
  waiting for transfers between devices  158 us (18%)
  matrix products  129 us (15%)
  local copies, waits for them, and re-layouts  115 us (13%)
  other arithmetic  41.3 us (5%)
  starting transfers between devices  17.4 us (2%)
  between operations  15.5 us (2%)
    pallas_call x4, Pallas kernels, attend_bwd(): pl.pallas_call(bwd_kernel, grid_spec=pltpu.PrefetchScalarGridSpec(num_sca...  153 us
    pallas_call x4, Pallas kernels, attend_fwd(): pl.pallas_call(fwd_kernel, grid_spec=pltpu.PrefetchScalarGridSpec(num_sca...  123 us
    ppermute x16, waiting for transfers between devices, relative(): lax.ppermute(x, axis, [(i, (i + r) % size) for i in range(size)])  91 us
    all_gather x1, waiting for transfers between devices, on_device(): table = lax.all_gather(early, ('dp', 'head'), axis=0)  55.6 us
    pallas_call x4, Pallas kernels, weight_grad(): pl.pallas_call(wgrad_kernel, grid=(seq // step,), in_specs=[pl.BlockSpec(...  34.9 us
    unnamed x120, local copies, waits for them, and re-layouts  34.3 us
    dot_general x1, matrix products, on_device(): jnp.einsum('fd,hd->fh', grad_branch_f, contract_cat, preferred_element_ty...  31.1 us
    pallas_call x2, Pallas kernels, project(): pl.pallas_call(qkv_kernel, grid_spec=pltpu.PrefetchScalarGridSpec(num_sca...  23.4 us
  transfers between devices with their start and end apart: 22, of which 8 were waited for; matrix products, arithmetic and copies ran while one was open for 15% of the time, Pallas kernels for 40%

profile of v3, /device:TPU:0, one launch (start us, length us, event | category | flops | bytes accessed | tf_op | source)
XLA Modules:
  0.0 845.4 jit_solution(16615406889125455985)
XLA Ops:
  7.3 3.7 fusion.31
  11.6 3.0 collective-permute-start
  16.2 3.2 copy.104
  28.0 2.1 fusion.19
  31.5 3.1 copy.112.sin_ref
  35.8 3.1 copy.111.cos_ref
  38.9 4.7 copy.106
  43.6 4.6 copy.110.w_ref
  50.7 11.7 %project.2 = (bf16[3,3072,512]{2,1,0:T(8,128)(2,1)}, bf16[1024,3072]{1,0:T(8,128)(2,1)}) custom-call(s32[1]{0:T(128)} %bitcast.9.base, bf16[1536,1024]{1,0:T(8,128)(2,1)} %x_ref.3, f32[1,1024]{1,0:T(1,128)} %get-tuple-element.286.scale_ref, f32[1,1024]{1,0:T(1,128)} %get-tuple-element.285.shift_ref, bf16[1024,1536]{1,0:T(8,128)(2,1)} %copy.110.w_ref, ...), custom_call_target="tpu_custom_call" | custom-call | flops 4831838208 | bytes 11010048 | tf_op jit(solution)/shard_map/project/pallas_call | solution.py:260
  62.4 2.3 select_convert_fusion
  64.7 33.2 %collective-permute-done.1.x_ref = bf16[1536,1024]{1,0:T(8,128)(2,1)} collective-permute-done((bf16[1536,1024]{1,0:T(8,128)(2,1)}, bf16[1536,1024]{1,0:T(8,128)(2,1)}, u32[]{:S(2)}, u32[]{:S(2)}) %collective-permute-start.1) | collective-permute-done | bytes 3145760 | tf_op jit(solution)/shard_map/ppermute | solution.py:363
  97.9 11.7 %project.3 = (bf16[3,3072,512]{2,1,0:T(8,128)(2,1)}, bf16[1024,3072]{1,0:T(8,128)(2,1)}) custom-call(s32[1]{0:T(128)} %bitcast.5.base, bf16[1536,1024]{1,0:T(8,128)(2,1)} %collective-permute-done.1.x_ref, f32[1,1024]{1,0:T(1,128)} %get-tuple-element.286.scale_ref, ...), custom_call_target="tpu_custom_call", output_to_operand_aliasing={{0}: (8, {}), {1}: (9, {})} | custom-call | flops 4831838208 | bytes 11010048 | tf_op jit(solution)/shard_map/project/pallas_call | solution.py:260
  110.0 30.8 %attend_fwd.4 = (bf16[3072,128]{1,0:T(8,128)(2,1)}, f32[1,8,3072]{2,1,0:T(8,128)}) custom-call(s32[36]{0:T(128)} %pad_add_fusion.tab, bf16[3,3072,512]{2,1,0:T(8,128)(2,1)} %get-tuple-element.96.q_ref.k_ref.v_ref, bf16[3,3072,512]{2,1,0:T(8,128)(2,1)} %get-tuple-element.96.q_ref.k_ref.v_ref, bf16[3,3072,512]{2,1,0:T(8,128)(2,1)} %get-tuple-element.96.q_ref.k_ref.v_ref, ...), custom_call_target="tpu_custom_call" | custom-call | flops 28991029248 | bytes 3145728 | tf_op jit(solution)/shard_map/attend_fwd/pallas_call | solution.py:120
  143.8 1.7 collective-permute-start.2
  145.5 30.6 %attend_fwd.5 = (bf16[3072,128]{1,0:T(8,128)(2,1)}, f32[1,8,3072]{2,1,0:T(8,128)}) custom-call(s32[36]{0:T(128)} %pad_add_fusion.tab, bf16[3,3072,512]{2,1,0:T(8,128)(2,1)} %get-tuple-element.96.q_ref.k_ref.v_ref, bf16[3,3072,512]{2,1,0:T(8,128)(2,1)} %get-tuple-element.96.q_ref.k_ref.v_ref, bf16[3,3072,512]{2,1,0:T(8,128)(2,1)} %get-tuple-element.96.q_ref.k_ref.v_ref, ...), custom_call_target="tpu_custom_call" | custom-call | flops 28991029248 | bytes 3145728 | tf_op jit(solution)/shard_map/attend_fwd/pallas_call | solution.py:120
  177.7 31.1 %attend_fwd.6 = (bf16[3072,128]{1,0:T(8,128)(2,1)}, f32[1,8,3072]{2,1,0:T(8,128)}) custom-call(s32[36]{0:T(128)} %pad_add_fusion.tab, bf16[3,3072,512]{2,1,0:T(8,128)(2,1)} %get-tuple-element.96.q_ref.k_ref.v_ref, bf16[3,3072,512]{2,1,0:T(8,128)(2,1)} %get-tuple-element.96.q_ref.k_ref.v_ref, bf16[3,3072,512]{2,1,0:T(8,128)(2,1)} %get-tuple-element.96.q_ref.k_ref.v_ref, ...), custom_call_target="tpu_custom_call" | custom-call | flops 28991029248 | bytes 3145728 | tf_op jit(solution)/shard_map/attend_fwd/pallas_call | solution.py:120
  210.0 1.7 collective-permute-start.5
  212.5 30.7 %attend_fwd.7 = (bf16[3072,128]{1,0:T(8,128)(2,1)}, f32[1,8,3072]{2,1,0:T(8,128)}) custom-call(s32[36]{0:T(128)} %pad_add_fusion.tab, bf16[3,3072,512]{2,1,0:T(8,128)(2,1)} %get-tuple-element.96.q_ref.k_ref.v_ref, bf16[3,3072,512]{2,1,0:T(8,128)(2,1)} %get-tuple-element.96.q_ref.k_ref.v_ref, bf16[3,3072,512]{2,1,0:T(8,128)(2,1)} %get-tuple-element.96.q_ref.k_ref.v_ref, ...), custom_call_target="tpu_custom_call" | custom-call | flops 28991029248 | bytes 3145728 | tf_op jit(solution)/shard_map/attend_fwd/pallas_call | solution.py:120
  249.4 4.8 collective-permute-done.6
  257.3 3.3 fusion.47
  260.6 8.1 fusion.44
  269.6 2.3 copy-done.21
  271.9 10.1 %fusion.12 = f32[1536,2048]{1,0:T(8,128)} fusion(bf16[1024,1024]{1,0:T(8,128)(2,1)S(1)} %bitcast.112, bf16[1024,1024]{1,0:T(8,128)(2,1)S(1)} %copy-done.21, f32[1536,1024]{1,0:T(8,128)S(1)} %get-tuple-element.249, f32[1024]{0:T(1024)S(1)} %bitcast.142, f32[1024]{0:T(1024)S(1)} %bitcast.138, f32[1536]{0:T(1024)S(1)} %add_rsqrt_fusion, ...), kind=kOutput, calls=%fused_computation.38 | convolution fusion | flops 6458703872 | bytes 23089152 | tf_op jit(solution)/shard_map/dot_general | solution.py:474
  282.1 12.9 %convolution_convert_fusion = bf16[2048,1024]{1,0:T(8,128)(2,1)S(1)} fusion(bf16[1536,1024]{1,0:T(8,128)(2,1)S(1)} %copy-done.42, f32[1024]{0:T(1024)S(1)} %bitcast.135, f32[1536,2048]{1,0:T(8,128)} %fusion.12, f32[2048]{0:T(1024)S(1)} %maximum_convert_fusion), kind=kOutput, calls=%fused_computation.32 | convolution fusion | flops 6480723968 | bytes 19935232 | tf_op jit(solution)/shard_map/fh,fd->hd/dot_general | solution.py:484
  294.9 31.1 %convert_reduce_fusion = (f32[2048]{0:T(1024)}, bf16[1536,2048]{1,0:T(8,128)(2,1)}) fusion(f32[1536,2048]{1,0:T(8,128)} %fusion.12, f32[2048]{0:T(1024)S(1)} %maximum_convert_fusion, bf16[1024,1024]{1,0:T(8,128)(2,1)S(1)} %bitcast.110, bf16[1024,1024]{1,0:T(8,128)(2,1)} %param.25, bf16[1536,1024]{1,0:T(8,128)(2,1)} %param.27, f32[1024]{0:T(1024)S(1)} %bitcast.136), kind=kOutput, calls=%fused_computation.10 | convolution fusion | flops 6527907840 | bytes 26234880 | tf_op jit(solution)/shard_map/fd,hd->fh/dot_general | solution.py:482
  326.1 10.6 %convolution_convert_fusion.1 = bf16[1024,2048]{1,0:T(8,128)(2,1)S(1)} fusion(bf16[1536,2048]{1,0:T(8,128)(2,1)} %get-tuple-element.297, f32[1536,1024]{1,0:T(8,128)S(1)} %get-tuple-element.249, f32[1024]{0:T(1024)S(1)} %bitcast.143, f32[1024]{0:T(1024)S(1)} %bitcast.139, f32[1536]{0:T(1024)S(1)} %add_rsqrt_fusion, f32[1536]{0:T(1024)S(1)} %broadcast_multiply_fusion.2), kind=kOutput, calls=%fused_computation.33 | convolution fusion | flops 6452412416 | bytes 16797696 | tf_op jit(solution)/shard_map/fd,fh->dh/dot_general | solution.py:485
  336.7 14.8 %multiply_reduce_fusion.1 = (f32[1024]{0:T(1024)}, f32[1536]{0:T(1024)S(1)}, f32[1536]{0:T(1024)S(1)}, f32[1024]{0:T(1024)}, f32[1536,1024]{1,0:T(8,128)}) fusion(f32[1536,1024]{1,0:T(8,128)S(1)} %get-tuple-element.249, f32[1536]{0:T(1024)S(1)} %add_rsqrt_fusion, f32[1536]{0:T(1024)S(1)} %broadcast_multiply_fusion.2, f32[1024]{0:T(1024)S(1)} %bitcast.140, ...), kind=kOutput, calls=%fused_computation.18 | convolution fusion | flops 6464990208 | bytes 23105536 | tf_op jit(solution)/shard_map/fh,dh->fd/dot_general | solution.py:487
  353.6 20.9 %fusion.8 = (f32[1024]{0:T(1024)}, f32[1024]{0:T(1024)}, bf16[1536,1024]{1,0:T(8,128)(2,1)}, f32[1024]{0:T(1024)}, f32[1536,1024]{1,0:T(8,128)}) fusion(bf16[1536,1024]{1,0:T(8,128)(2,1)} %param.27, f32[1024]{0:T(1024)S(1)} %copy-done.33, f32[1024]{0:T(1024)S(1)} %bitcast.137, f32[1536,1024]{1,0:T(8,128)} %copy-done.3, ...), kind=kOutput, calls=%fused_computation.16 | convolution fusion | flops 6516896768 | bytes 48295936 | tf_op jit(solution)/shard_map/dot_general | solution.py:477
  374.5 4.6 convert_reduce_fusion.2
  379.1 3.7 convolution_convert_fusion.3
  391.3 5.4 convolution_convert_fusion.2
  401.4 22.5 %collective-permute-done.7 = bf16[1536,128]{1,0:T(8,128)(2,1)S(1)} collective-permute-done((bf16[1536,128]{1,0:T(8,128)(2,1)S(1)}, bf16[1536,128]{1,0:T(8,128)(2,1)S(1)}, u32[]{:S(2)}, u32[]{:S(2)}) %collective-permute-start.7) | collective-permute-done | bytes 393248 | tf_op jit(solution)/shard_map/ppermute | solution.py:363
  424.8 38.2 %attend_bwd.4.g_ref.rest_0_ = bf16[3,3072,128]{2,1,0:T(8,128)(2,1)} custom-call(s32[36]{0:T(128)} %pad_add_fusion.tab, bf16[3,3072,512]{2,1,0:T(8,128)(2,1)} %get-tuple-element.96.q_ref.k_ref.v_ref, bf16[3,3072,512]{2,1,0:T(8,128)(2,1)} %get-tuple-element.96.q_ref.k_ref.v_ref, bf16[3,3072,512]{2,1,0:T(8,128)(2,1)} %get-tuple-element.96.q_ref.k_ref.v_ref, ...), custom_call_target="tpu_custom_call" | custom-call | flops 38654705664 | bytes 6291456 | tf_op jit(solution)/shard_map/attend_bwd/pallas_call | solution.py:212
  465.2 8.7 %weight_grad.4 = (bf16[1024,1536]{1,0:T(8,128)(2,1)}, f32[8,384]{1,0:T(8,128)}) custom-call(bf16[1024,3072]{1,0:T(8,128)(2,1)} %get-tuple-element.128.nt_ref, bf16[3,3072,128]{2,1,0:T(8,128)(2,1)} %attend_bwd.4.g_ref.rest_0_), custom_call_target="tpu_custom_call" | custom-call | flops 2415919104 | bytes 8650752 | tf_op jit(solution)/shard_map/weight_grad/pallas_call | solution.py:294
  475.8 38.4 %attend_bwd.5.g_ref.rest_1_ = bf16[3,3072,128]{2,1,0:T(8,128)(2,1)} custom-call(s32[36]{0:T(128)} %pad_add_fusion.tab, bf16[3,3072,512]{2,1,0:T(8,128)(2,1)} %get-tuple-element.96.q_ref.k_ref.v_ref, bf16[3,3072,512]{2,1,0:T(8,128)(2,1)} %get-tuple-element.96.q_ref.k_ref.v_ref, bf16[3,3072,512]{2,1,0:T(8,128)(2,1)} %get-tuple-element.96.q_ref.k_ref.v_ref, ...), custom_call_target="tpu_custom_call" | custom-call | flops 38654705664 | bytes 6291456 | tf_op jit(solution)/shard_map/attend_bwd/pallas_call | solution.py:212
  517.0 8.6 %weight_grad.5 = (bf16[1024,1536]{1,0:T(8,128)(2,1)}, f32[8,384]{1,0:T(8,128)}) custom-call(bf16[1024,3072]{1,0:T(8,128)(2,1)} %get-tuple-element.128.nt_ref, bf16[3,3072,128]{2,1,0:T(8,128)(2,1)} %attend_bwd.5.g_ref.rest_1_, bf16[1024,1536]{1,0:T(8,128)(2,1)} %get-tuple-element.135.rest_0_), custom_call_target="tpu_custom_call", output_to_operand_aliasing={{0}: (2, {})} | custom-call | flops 2415919104 | bytes 8650752 | tf_op jit(solution)/shard_map/weight_grad/pallas_call | solution.py:294
  526.9 38.1 %attend_bwd.6.g_ref.rest_2_ = bf16[3,3072,128]{2,1,0:T(8,128)(2,1)} custom-call(s32[36]{0:T(128)} %pad_add_fusion.tab, bf16[3,3072,512]{2,1,0:T(8,128)(2,1)} %get-tuple-element.96.q_ref.k_ref.v_ref, bf16[3,3072,512]{2,1,0:T(8,128)(2,1)} %get-tuple-element.96.q_ref.k_ref.v_ref, bf16[3,3072,512]{2,1,0:T(8,128)(2,1)} %get-tuple-element.96.q_ref.k_ref.v_ref, ...), custom_call_target="tpu_custom_call" | custom-call | flops 38654705664 | bytes 6291456 | tf_op jit(solution)/shard_map/attend_bwd/pallas_call | solution.py:212
  565.1 2.4 constant_dynamic-slice_fusion.5
  567.4 8.7 %weight_grad.6 = (bf16[1024,1536]{1,0:T(8,128)(2,1)}, f32[8,384]{1,0:T(8,128)}) custom-call(bf16[1024,3072]{1,0:T(8,128)(2,1)} %get-tuple-element.128.nt_ref, bf16[3,3072,128]{2,1,0:T(8,128)(2,1)} %attend_bwd.6.g_ref.rest_2_, bf16[1024,1536]{1,0:T(8,128)(2,1)} %get-tuple-element.141.rest_0_), custom_call_target="tpu_custom_call", output_to_operand_aliasing={{0}: (2, {})} | custom-call | flops 2415919104 | bytes 8650752 | tf_op jit(solution)/shard_map/weight_grad/pallas_call | solution.py:294
  578.0 7.0 collective-permute-done.12
  585.0 1.8 add_convert_fusion.2
  588.1 7.9 collective-permute-done.13
  597.2 38.2 %attend_bwd.7.rest_3_.g_ref = bf16[3,3072,128]{2,1,0:T(8,128)(2,1)} custom-call(s32[36]{0:T(128)} %pad_add_fusion.tab, bf16[3,3072,512]{2,1,0:T(8,128)(2,1)} %get-tuple-element.96.q_ref.k_ref.v_ref, bf16[3,3072,512]{2,1,0:T(8,128)(2,1)} %get-tuple-element.96.q_ref.k_ref.v_ref, bf16[3,3072,512]{2,1,0:T(8,128)(2,1)} %get-tuple-element.96.q_ref.k_ref.v_ref, ...), custom_call_target="tpu_custom_call" | custom-call | flops 38654705664 | bytes 6291456 | tf_op jit(solution)/shard_map/attend_bwd/pallas_call | solution.py:212
  635.4 2.4 constant_dynamic-slice_fusion.4
  637.7 8.8 %weight_grad.7 = (bf16[1024,1536]{1,0:T(8,128)(2,1)}, f32[8,384]{1,0:T(8,128)}) custom-call(bf16[1024,3072]{1,0:T(8,128)(2,1)} %get-tuple-element.128.nt_ref, bf16[3,3072,128]{2,1,0:T(8,128)(2,1)} %attend_bwd.7.rest_3_.g_ref, bf16[1024,1536]{1,0:T(8,128)(2,1)} %get-tuple-element.157.rest_0_), custom_call_target="tpu_custom_call", output_to_operand_aliasing={{0}: (2, {})} | custom-call | flops 2415919104 | bytes 8650752 | tf_op jit(solution)/shard_map/weight_grad/pallas_call | solution.py:294
  646.7 2.2 copy.114
  648.9 4.6 copy.116
  653.6 4.0 slice.129
  657.5 4.7 reshape_reshape.7
  662.3 4.3 copy.115
  666.5 4.9 copy.117
  672.5 5.3 pad_maximum_fusion.w_ref
  680.9 15.5 %collective-permute-done.15.rest_7_ = bf16[3,1536,128]{2,1,0:T(8,128)(2,1)} collective-permute-done((bf16[3,1536,128]{2,1,0:T(8,128)(2,1)}, bf16[3,1536,128]{2,1,0:T(8,128)(2,1)}, u32[]{:S(2)}, u32[]{:S(2)}) %collective-permute-start.15) | collective-permute-done | bytes 1179680 | tf_op jit(solution)/shard_map/ppermute | solution.py:363
  696.5 19.3 %input_grad.1 = (f32[1536,1024]{1,0:T(8,128)}, f32[8,1024]{1,0:T(8,128)}) custom-call(s32[1]{0:T(128)} %bitcast.9.base, bf16[1536,1024]{1,0:T(8,128)(2,1)} %x_ref.3, f32[1536,1024]{1,0:T(8,128)} %get-tuple-element.258.gm_ref, f32[1,1024]{1,0:T(1,128)} %get-tuple-element.286.scale_ref, bf16[1024,3072]{1,0:T(8,128)(2,1)} %pad_maximum_fusion.w_ref, ...), custom_call_target="tpu_custom_call" | custom-call | flops 9663676416 | bytes 25165824 | tf_op jit(solution)/shard_map/input_grad/pallas_call | solution.py:348
  718.9 55.6 %all-gather.16.cloned.1.call-done = f32[32,1,11776]{2,1,0:T(1,128)} async-done(((f32[1,1,11776]{2,1,0:T(1,128)}), f32[32,1,11776]{2,1,0:T(1,128)}) %all-gather.16.cloned.1.call-update) | async-done | bytes 1507344 | tf_op jit(solution)/shard_map/all_gather | solution.py:552
  774.5 5.0 reduce.8
  782.8 4.3 multiply_reduce_fusion
  787.1 5.2 psum.7
  794.1 8.1 fusion.25
  804.4 2.6 bitcast_convert_fusion
  807.0 2.6 bitcast_convert_fusion.1
  809.6 11.5 %all-gather.14.cloned.1.call-done = bf16[1,1024,1536]{2,1,0:T(8,128)(2,1)} async-done(((bf16[1,64,1536]{2,1,0:T(8,128)(2,1)}), bf16[1,1024,1536]{2,1,0:T(8,128)(2,1)}) %all-gather.14.cloned.1.call-update) | async-done | bytes 3145744 | tf_op jit(solution)/shard_map/all_gather | solution.py:540
  821.1 8.8 %unpack.1 = f32[1024,3,512]{2,1,0:T(4,128)} custom-call(bf16[1024,1536]{1,0:T(8,128)(2,1)} %bitcast.109), custom_call_target="tpu_custom_call" | custom-call | tf_op jit(solution)/shard_map/unpack/pallas_call | solution.py:317
  830.0 8.1 copy.127
  (241 shorter events, 75.9 us)
Async XLA Ops:
  7.2 3.8 copy-start.28
  7.2 8.4 copy-start.24
  7.2 8.4 copy-start.29
  7.2 20.2 %copy-start.12 = (s32[1,3072]{1,0:T(1,128)S(1)}, s32[1,3072]{1,0:T(1,128)}, u32[]{:S(2)}) copy-start(s32[1,3072]{1,0:T(1,128)} %param.16) | copy-start | bytes 36868
  7.2 247.8 %all-gather.10.cloned.1.call-start = ((), (), s32[]{:S(2)}) async-start(), calls=%async_computation.4 | async-start | bytes 10027008 | tf_op jit(solution)/shard_map/all_gather | solution.py:442
  11.6 15.8 %collective-permute-start = (f32[1,3072]{1,0:T(1,128)}, f32[1,3072]{1,0:T(1,128)}, u32[]{:S(2)}, u32[]{:S(2)}) collective-permute-start(f32[1,3072]{1,0:T(1,128)} %bitcast.1), channel_id=1, source_target_pairs={{0,1},{1,0},{2,3},{3,2},{4,5},{5,4},{6,7},{7,6},{8,9},{9,8},{10,11... | collective-permute-start | bytes 36872 | tf_op jit(solution)/shard_map/ppermute | solution.py:363
  19.4 19.5 %copy-start = (bf16[1024,3,512]{0,2,1:T(8,128)(2,1)}, bf16[1024,3,512]{0,2,1:T(8,128)(2,1)S(1)}, u32[]{:S(2)}) copy-start(bf16[1024,3,512]{0,2,1:T(8,128)(2,1)S(1)} %copy.104) | copy-start | bytes 9437188
  22.6 5.5 copy-start.13
  28.0 69.9 %collective-permute-start.1 = (bf16[1536,1024]{1,0:T(8,128)(2,1)}, bf16[1536,1024]{1,0:T(8,128)(2,1)}, u32[]{:S(2)}, u32[]{:S(2)}) collective-permute-start(bf16[1536,1024]{1,0:T(8,128)(2,1)} %x_ref.3), channel_id=1, source_target_pairs={{0,1},{1,0},{2,3},{3,2},{4,5},{5,4},{6,7},{7,6},{8,9},{9,8},{10,11... | collective-permute-start | bytes 9437192 | tf_op jit(solution)/shard_map/ppermute | solution.py:363
  38.9 9.3 %copy-start.15 = (s32[12,256]{1,0:T(8,128)S(1)}, s32[12,256]{1,0:T(8,128)}, u32[]{:S(2)}) copy-start(s32[12,256]{1,0:T(8,128)} %reshape.225) | copy-start | bytes 36868
  38.9 10.4 %copy-start.14 = (f32[1,6144]{1,0:T(1,128)S(1)}, f32[1,6144]{1,0:T(1,128)}, u32[]{:S(2)}) copy-start(f32[1,6144]{1,0:T(1,128)} %copy-done.13) | copy-start | bytes 73732
  50.7 11.7 %copy-start.41 = (pred[128]{0:T(512)(128)(4,1)S(1)}, pred[128]{0:T(512)(128)(4,1)}, u32[]{:S(2)}) copy-start(pred[128]{0:T(512)(128)(4,1)} %broadcast_compare_fusion) | copy-start | bytes 388
  97.9 11.7 %copy-start.27 = (bf16[272,1024]{1,0:T(8,128)(2,1)S(1)}, bf16[272,1024]{1,0:T(8,128)(2,1)}, u32[]{:S(2)}) copy-start(bf16[272,1024]{1,0:T(8,128)(2,1)} %copy-done.26) | copy-start | bytes 1671172
  109.7 32.3 %collective-permute-start.3 = (bf16[272,1024]{1,0:T(8,128)(2,1)S(1)}, bf16[272,1024]{1,0:T(8,128)(2,1)S(1)}, u32[]{:S(2)}, u32[]{:S(2)}) collective-permute-start(bf16[272,1024]{1,0:T(8,128)(2,1)S(1)} %copy-done.27), channel_id=1, source_target_pairs={{0,1},{1,0},{2,3},{3,2},{4,5},{5,4},{6,7},{7,6},{8,9},{9,8},{10,11... | collective-permute-start | bytes 1671176 | tf_op jit(solution)/shard_map/ppermute | solution.py:363
  110.0 31.9 %copy-start.18 = (bf16[1,1024]{1,0:T(2,128)(2,1)S(1)}, bf16[1,1024]{1,0:T(2,128)(2,1)}, u32[]{:S(2)}) copy-start(bf16[1,1024]{1,0:T(2,128)(2,1)} %param.15) | copy-start | bytes 6148
  110.0 33.1 %copy-start.39 = (bf16[1024]{0:T(1024)(128)(2,1)S(1)}, bf16[1024]{0:T(1024)(128)(2,1)}, u32[]{:S(2)}) copy-start(bf16[1024]{0:T(1024)(128)(2,1)} %param.22) | copy-start | bytes 6148
  110.0 33.2 %copy-start.40 = (bf16[1024]{0:T(1024)(128)(2,1)S(1)}, bf16[1024]{0:T(1024)(128)(2,1)}, u32[]{:S(2)}) copy-start(bf16[1024]{0:T(1024)(128)(2,1)} %param.26) | copy-start | bytes 6148
  142.9 433.3 %reduce-scatter.3.cloned.1.call-start = ((), (), s32[]{:S(2)}) async-start(), calls=%async_computation.2 | async-start | bytes 11141120 | tf_op jit(solution)/shard_map/reduce_scatter | solution.py:510
  143.8 33.5 %collective-permute-start.2 = (bf16[1536,128]{1,0:T(8,128)(2,1)S(1)}, bf16[1536,128]{1,0:T(8,128)(2,1)S(1)}, u32[]{:S(2)}, u32[]{:S(2)}) collective-permute-start(bf16[1536,128]{1,0:T(8,128)(2,1)S(1)} %get-tuple-element.99), channel_id=1, source_target_pairs={{0,1},{1,0},{2,3},{3,2},{4,5},{5,4},{6,7},{7,6},{8,9},{9,8},{10,11... | collective-permute-start | bytes 1179656 | tf_op jit(solution)/shard_map/ppermute | solution.py:363
  177.3 35.1 %collective-permute-start.4 = (bf16[1536,128]{1,0:T(8,128)(2,1)S(1)}, bf16[1536,128]{1,0:T(8,128)(2,1)S(1)}, u32[]{:S(2)}, u32[]{:S(2)}) collective-permute-start(bf16[1536,128]{1,0:T(8,128)(2,1)S(1)} %get-tuple-element.107), channel_id=1, source_target_pairs={{0,1},{1,0},{2,3},{3,2},{4,5},{5,4},{6,7},{7,6},{8,9},{9,8},{10,11... | collective-permute-start | bytes 1179656 | tf_op jit(solution)/shard_map/ppermute | solution.py:363
  210.0 34.3 %collective-permute-start.5 = (bf16[1536,128]{1,0:T(8,128)(2,1)S(1)}, bf16[1536,128]{1,0:T(8,128)(2,1)S(1)}, u32[]{:S(2)}, u32[]{:S(2)}) collective-permute-start(bf16[1536,128]{1,0:T(8,128)(2,1)S(1)} %get-tuple-element.113), channel_id=1, source_target_pairs={{0,1},{1,0},{2,3},{3,2},{4,5},{5,4},{6,7},{7,6},{8,9},{9,8},{10,11... | collective-permute-start | bytes 1179656 | tf_op jit(solution)/shard_map/ppermute | solution.py:363
  244.3 9.9 %collective-permute-start.6 = (bf16[1536,128]{1,0:T(8,128)(2,1)S(1)}, bf16[1536,128]{1,0:T(8,128)(2,1)S(1)}, u32[]{:S(2)}, u32[]{:S(2)}) collective-permute-start(bf16[1536,128]{1,0:T(8,128)(2,1)S(1)} %get-tuple-element.122), channel_id=1, source_target_pairs={{0,1},{1,0},{2,3},{3,2},{4,5},{5,4},{6,7},{7,6},{8,9},{9,8},{10,11... | collective-permute-start | bytes 1179656 | tf_op jit(solution)/shard_map/ppermute | solution.py:363
  247.9 12.7 %copy-start.25 = (bf16[1024]{0:T(1024)(128)(2,1)S(1)}, bf16[1024]{0:T(1024)(128)(2,1)}, u32[]{:S(2)}) copy-start(bf16[1024]{0:T(1024)(128)(2,1)} %param.24) | copy-start | bytes 6148
  255.0 5.6 copy-start.16
  257.3 11.5 %copy-start.6 = (bf16[16,32,1024]{2,1,0:T(8,128)(2,1)}, bf16[16,32,1024]{2,1,0:T(8,128)(2,1)S(1)}, u32[]{:S(2)}) copy-start(bf16[16,32,1024]{2,1,0:T(8,128)(2,1)S(1)} %slice.125) | copy-start | bytes 3145732
  260.6 9.0 %copy-start.4 = (bf16[16,64,1024]{2,1,0:T(8,128)(2,1)}, bf16[16,64,1024]{2,1,0:T(8,128)(2,1)S(1)}, u32[]{:S(2)}) copy-start(bf16[16,64,1024]{2,1,0:T(8,128)(2,1)S(1)} %get-tuple-element.254) | copy-start | bytes 6291460
  268.8 67.9 %copy-start.3 = (f32[1536,1024]{1,0:T(8,128)}, f32[1536,1024]{1,0:T(8,128)S(1)}, u32[]{:S(2)}) copy-start(f32[1536,1024]{1,0:T(8,128)S(1)} %get-tuple-element.249) | copy-start | bytes 18874372
  268.8 3.1 copy-start.21
  268.8 3.1 copy-start.31
  268.8 3.1 copy-start.32
  271.9 10.2 %copy-start.30 = (f32[1,1024]{1,0:T(1,128)S(1)}, f32[1,1024]{1,0:T(1,128)}, u32[]{:S(2)}) copy-start(f32[1,1024]{1,0:T(1,128)} %get-tuple-element.282) | copy-start | bytes 12292
  271.9 10.2 %copy-start.42 = (bf16[1536,1024]{1,0:T(8,128)(2,1)S(1)}, bf16[1536,1024]{1,0:T(8,128)(2,1)}, u32[]{:S(2)}) copy-start(bf16[1536,1024]{1,0:T(8,128)(2,1)} %param.27) | copy-start | bytes 9437188
  326.1 10.6 %copy-start.5 = (bf16[16,64,1024]{2,1,0:T(8,128)(2,1)S(1)}, bf16[16,64,1024]{2,1,0:T(8,128)(2,1)}, u32[]{:S(2)}) copy-start(bf16[16,64,1024]{2,1,0:T(8,128)(2,1)} %copy-done.4) | copy-start | bytes 6291460
  352.0 1.6 copy-start.22
  352.0 1.6 copy-start.33
  374.5 4.6 copy-start.17
  391.2 255.4 %all-gather.12.cloned.1.call-start = ((), (), s32[]{:S(2)}) async-start(), calls=%async_computation.5 | async-start | bytes 5570560 | tf_op jit(solution)/shard_map/all_gather | solution.py:535
  398.0 116.2 %collective-permute-start.10 = (bf16[1536,128]{1,0:T(8,128)(2,1)S(1)}, bf16[1536,128]{1,0:T(8,128)(2,1)}, u32[]{:S(2)}, u32[]{:S(2)}) collective-permute-start(bf16[1536,128]{1,0:T(8,128)(2,1)S(1)} %get-tuple-element.267), channel_id=1, source_target_pairs={{0,1},{1,0},{2,3},{3,2},{4,5},{5,4},{6,7},{7,6},{8,9},{9,8},{10,11... | collective-permute-start | bytes 1179656 | tf_op jit(solution)/shard_map/ppermute | solution.py:363
  398.6 75.3 %collective-permute-start.8 = (bf16[1536,128]{1,0:T(8,128)(2,1)}, bf16[1536,128]{1,0:T(8,128)(2,1)}, u32[]{:S(2)}, u32[]{:S(2)}) collective-permute-start(bf16[1536,128]{1,0:T(8,128)(2,1)} %get-tuple-element.268), channel_id=1, source_target_pairs={{0,1},{1,0},{2,3},{3,2},{4,5},{5,4},{6,7},{7,6},{8,9},{9,8},{10,11... | collective-permute-start | bytes 1179656 | tf_op jit(solution)/shard_map/ppermute | solution.py:363
  400.1 23.8 %collective-permute-start.7 = (bf16[1536,128]{1,0:T(8,128)(2,1)S(1)}, bf16[1536,128]{1,0:T(8,128)(2,1)S(1)}, u32[]{:S(2)}, u32[]{:S(2)}) collective-permute-start(bf16[1536,128]{1,0:T(8,128)(2,1)S(1)} %get-tuple-element.269), channel_id=1, source_target_pairs={{0,1},{1,0},{2,3},{3,2},{4,5},{5,4},{6,7},{7,6},{8,9},{9,8},{10,11... | collective-permute-start | bytes 1179656 | tf_op jit(solution)/shard_map/ppermute | solution.py:363
  464.3 52.7 %collective-permute-start.9 = (bf16[3,1536,128]{2,1,0:T(8,128)(2,1)S(1)}, bf16[3,1536,128]{2,1,0:T(8,128)(2,1)}, u32[]{:S(2)}, u32[]{:S(2)}) collective-permute-start(bf16[3,1536,128]{2,1,0:T(8,128)(2,1)S(1)} %constant_dynamic-slice_fusion.7), channel_id=1, source_target_pairs={{0,1},{1,0},{2,3},{3,2},{4,5},{5,4},{6,7},{7,6},{8,9},{9,8},{10,11... | collective-permute-start | bytes 3538952 | tf_op jit(solution)/shard_map/ppermute | solution.py:363
  515.3 10.3 %copy-start.10 = (bf16[3072,128]{1,0:T(8,128)(2,1)}, bf16[3072,128]{1,0:T(8,128)(2,1)S(1)}, u32[]{:S(2)}) copy-start(bf16[3072,128]{1,0:T(8,128)(2,1)S(1)} %constant_dynamic-update-slice_fusion.18.do_ref) | copy-start | bytes 2359300
  525.7 41.8 %collective-permute-start.11 = (bf16[3,1536,128]{2,1,0:T(8,128)(2,1)S(1)}, bf16[3,1536,128]{2,1,0:T(8,128)(2,1)}, u32[]{:S(2)}, u32[]{:S(2)}) collective-permute-start(bf16[3,1536,128]{2,1,0:T(8,128)(2,1)S(1)} %constant_dynamic-slice_fusion.6), channel_id=1, source_target_pairs={{0,1},{1,0},{2,3},{3,2},{4,5},{5,4},{6,7},{7,6},{8,9},{9,8},{10,11... | collective-permute-start | bytes 3538952 | tf_op jit(solution)/shard_map/ppermute | solution.py:363
  567.4 19.6 %copy-start.11 = (bf16[1536,128]{1,0:T(8,128)(2,1)S(1)}, bf16[1536,128]{1,0:T(8,128)(2,1)}, u32[]{:S(2)}) copy-start(bf16[1536,128]{1,0:T(8,128)(2,1)} %get-tuple-element.265) | copy-start | bytes 1179652
  577.1 7.8 collective-permute-start.12
  586.8 130.9 %reduce-scatter.5.cloned.1.call-start = ((), (), s32[]{:S(2)}) async-start(), calls=%async_computation.3 | async-start | bytes 3342336 | tf_op jit(solution)/shard_map/reduce_scatter | solution.py:539
  587.1 9.0 %collective-permute-start.13 = (bf16[1536,128]{1,0:T(8,128)(2,1)S(1)}, bf16[1536,128]{1,0:T(8,128)(2,1)S(1)}, u32[]{:S(2)}, u32[]{:S(2)}) collective-permute-start(bf16[1536,128]{1,0:T(8,128)(2,1)S(1)} %copy-done.11), channel_id=1, source_target_pairs={{0,1},{1,0},{2,3},{3,2},{4,5},{5,4},{6,7},{7,6},{8,9},{9,8},{10,11... | collective-permute-start | bytes 1179656 | tf_op jit(solution)/shard_map/ppermute | solution.py:363
  596.1 1.1 copy-start.7
  596.1 41.6 %collective-permute-start.14 = (bf16[3,1536,128]{2,1,0:T(8,128)(2,1)}, bf16[3,1536,128]{2,1,0:T(8,128)(2,1)}, u32[]{:S(2)}, u32[]{:S(2)}) collective-permute-start(bf16[3,1536,128]{2,1,0:T(8,128)(2,1)} %constant_dynamic-slice_fusion.5), channel_id=1, source_target_pairs={{0,1},{1,0},{2,3},{3,2},{4,5},{5,4},{6,7},{7,6},{8,9},{9,8},{10,11... | collective-permute-start | bytes 3538952 | tf_op jit(solution)/shard_map/ppermute | solution.py:363
  637.7 8.9 %copy-start.1 = (bf16[1024,3,512]{0,2,1:T(8,128)(2,1)S(1)}, bf16[1024,3,512]{0,2,1:T(8,128)(2,1)}, u32[]{:S(2)}) copy-start(bf16[1024,3,512]{0,2,1:T(8,128)(2,1)} %copy-done) | copy-start | bytes 9437188
  646.6 127.9 %all-gather.16.cloned.1.call-start = ((), (), s32[]{:S(2)}) async-start(), calls=%async_computation.7 | async-start | bytes 1554432 | tf_op jit(solution)/shard_map/all_gather | solution.py:552
  666.5 6.0 copy-start.2
  671.4 9.4 %copy-start.20 = (f32[1024]{0:T(1024)S(1)}, f32[1024]{0:T(1024)}, u32[]{:S(2)}) copy-start(f32[1024]{0:T(1024)} %get-tuple-element.246) | copy-start | bytes 12292
  671.4 9.4 %copy-start.38 = (f32[1024]{0:T(1024)S(1)}, f32[1024]{0:T(1024)}, u32[]{:S(2)}) copy-start(f32[1024]{0:T(1024)} %get-tuple-element.235) | copy-start | bytes 12292
  671.4 9.4 %copy-start.23 = (f32[2048]{0:T(1024)S(1)}, f32[2048]{0:T(1024)}, u32[]{:S(2)}) copy-start(f32[2048]{0:T(1024)} %get-tuple-element.296) | copy-start | bytes 24580
  671.4 25.1 %collective-permute-start.15 = (bf16[3,1536,128]{2,1,0:T(8,128)(2,1)}, bf16[3,1536,128]{2,1,0:T(8,128)(2,1)}, u32[]{:S(2)}, u32[]{:S(2)}) collective-permute-start(bf16[3,1536,128]{2,1,0:T(8,128)(2,1)} %constant_dynamic-slice_fusion.4), channel_id=1, source_target_pairs={{0,1},{1,0},{2,3},{3,2},{4,5},{5,4},{6,7},{7,6},{8,9},{9,8},{10,11... | collective-permute-start | bytes 3538952 | tf_op jit(solution)/shard_map/ppermute | solution.py:363
  680.9 35.7 %copy-start.37 = (f32[1024]{0:T(1024)S(1)}, f32[1024]{0:T(1024)}, u32[]{:S(2)}) copy-start(f32[1024]{0:T(1024)} %get-tuple-element.257) | copy-start | bytes 12292
  680.9 35.7 %copy-start.35 = (f32[1024]{0:T(1024)S(1)}, f32[1024]{0:T(1024)}, u32[]{:S(2)}) copy-start(f32[1024]{0:T(1024)} %get-tuple-element.233) | copy-start | bytes 12292
  680.9 35.7 %copy-start.34 = (f32[1024]{0:T(1024)S(1)}, f32[1024]{0:T(1024)}, u32[]{:S(2)}) copy-start(f32[1024]{0:T(1024)} %get-tuple-element.230) | copy-start | bytes 12292
  680.9 35.8 %copy-start.36 = (f32[1024]{0:T(1024)S(1)}, f32[1024]{0:T(1024)}, u32[]{:S(2)}) copy-start(f32[1024]{0:T(1024)} %get-tuple-element.234) | copy-start | bytes 12292
  717.3 103.8 %all-gather.14.cloned.1.call-start = ((), (), s32[]{:S(2)}) async-start(), calls=%async_computation.6 | async-start | bytes 3342336 | tf_op jit(solution)/shard_map/all_gather | solution.py:540
  780.4 13.1 %copy-start.19 = (bf16[1,1024]{1,0:T(2,128)(2,1)S(1)}, bf16[1,1024]{1,0:T(2,128)(2,1)}, u32[]{:S(2)}) copy-start(bf16[1,1024]{1,0:T(2,128)(2,1)} %param.15) | copy-start | bytes 6148
  782.8 19.4 %slice-start = ((s8[5242880]{0:T(1024)(128)(4,1)}), s8[1048576]{0:T(1024)(128)(4,1)S(1)}, s32[]{:S(2)}) async-start(s8[5242880]{0:T(1024)(128)(4,1)} %bitcast.103), calls=%async_computation.8 | async-start | bytes 2097152
  794.1 8.1 slice-start.1
  (3 other events, 2.6 us)
Sparse Core Ops, SparseCore 0:
  143.0 82.0 all-gather.9
  391.4 118.6 reduce-scatter.2
  586.9 56.1 all-gather.11
  646.8 70.7 reduce-scatter.4
  720.8 53.6 all-gather.15
  776.7 44.4 all-gather.13

commit v4 on v3

--- a/solution.py
+++ b/solution.py
@@ -1,3 +1,4 @@
+import functools
 import math
 import jax
 import jax.numpy as jnp
@@ -62,6 +63,23 @@
     ka[seq:, :] = jnp.where((lane >= HDIM) & (lane < HDIM + 8), -BIG, 0.0).astype(jnp.bfloat16)
     kb[seq:, :] = jnp.where(lane < 8, -BIG, 0.0).astype(jnp.bfloat16)
 
+LIMIT = 90.0
+
+def sweep(chunk, lo, full, carry):
+    two = lax.div(full, 2)
+    carry = lax.fori_loop(0, two, lambda j, c: chunk(lo + (2 * j + 1) * CK, CK, chunk(lo + 2 * j * CK, CK, c)), carry)
+    return lax.fori_loop(2 * two, full, lambda j, c: chunk(lo + j * CK, CK, c), carry)
+
+def largest(ref, seq):
+    lane = lax.broadcasted_iota(jnp.int32, (128, 128), 0) // HDIM
+    same = lane == lax.broadcasted_iota(jnp.int32, (128, 128), 1) // HDIM
+    ones = jnp.where(same, 1.0, 0.0).astype(jnp.bfloat16)
+    def one(i, top):
+        v = ref[0, pl.ds(pl.multiple_of(i * QB, QB), QB), :].astype(jnp.float32)
+        size = mm((v * v).astype(jnp.bfloat16), ones, NN)
+        return jnp.maximum(top, jnp.max(size, axis=0, keepdims=True))
+    return lax.fori_loop(0, seq // QB, one, jnp.zeros((1, 128), jnp.float32)) * 1.02
+
 def fwd_kernel(tab, q_ref, k_ref, v_ref, fq_ref, fk_ref, o_ref, lse_ref, ka, kb, vs):
     seq = q_ref.shape[1]
     nq = seq // QB
@@ -72,6 +90,39 @@
         vs[seq:, :] = jnp.zeros((CK, 128), jnp.bfloat16)
     split_keys(k_ref, fk_ref, ka, kb, seq)
     vs[:seq, :] = v_ref[0]
+    room = jnp.max(largest(q_ref, seq) * largest(k_ref, seq))
+    small = room < (LIMIT / TWO) ** 2
+
+    def direct(i, _):
+        rows = pl.ds(pl.multiple_of(i * QB, QB), QB)
+        q = q_ref[0, rows, :]
+        f = fq_ref[rows, :]
+        qa = jnp.where(lowm, q, f)
+        qb = jnp.where(lowm, f, q)
+        lo = tab[i]
+        full = tab[nq + i]
+        tail = tab[2 * nq + i]
+
+        def chunk(start, size, carry):
+            oa, ob = carry
+            keys = pl.ds(pl.multiple_of(start, 16), size)
+            vt = vs[keys, :].T
+            ones = jnp.ones((16, size), jnp.bfloat16)
+            pa = jnp.exp2(mm(ka[keys, :], qa, NT) * TWO).astype(jnp.bfloat16)
+            pb = jnp.exp2(mm(kb[keys, :], qb, NT) * TWO).astype(jnp.bfloat16)
+            oa = oa + mm(jnp.concatenate([vt[:HDIM], ones], axis=0), pa, NN)
+            ob = ob + mm(jnp.concatenate([vt[HDIM:], ones], axis=0), pb, NN)
+            return oa, ob
+
+        z = jnp.zeros((HDIM + 16, QB), jnp.float32)
+        carry = sweep(chunk, lo, full, (z, z))
+        oa, ob = lax.fori_loop(0, tail, lambda j, c: chunk(lo + full * CK, CT, c), carry)
+        la, lb = oa[HDIM:HDIM + 1], ob[HDIM:HDIM + 1]
+        o = jnp.concatenate([oa[:HDIM] / la, ob[:HDIM] / lb], axis=0)
+        o_ref[rows, :] = o.T.astype(jnp.bfloat16)
+        lse_ref[0, 0:1, rows] = jnp.log2(la)
+        lse_ref[0, 1:2, rows] = jnp.log2(lb)
+        return 0
 
     def block(i, _):
         rows = pl.ds(pl.multiple_of(i * QB, QB), QB)
@@ -101,7 +152,7 @@
         m0 = jnp.full((1, QB), -1e38, jnp.float32)
         l0 = jnp.zeros((1, QB), jnp.float32)
         o0 = jnp.zeros((HDIM, QB), jnp.float32)
-        carry = lax.fori_loop(0, full, lambda j, c: chunk(lo + j * CK, CK, c), (m0, l0, o0, m0, l0, o0))
+        carry = sweep(chunk, lo, full, (m0, l0, o0, m0, l0, o0))
         carry = lax.fori_loop(0, tail, lambda j, c: chunk(lo + full * CK, CT, c), carry)
         ma, la, oa, mb, lb, ob = carry
         o = jnp.concatenate([oa / la, ob / lb], axis=0)
@@ -110,7 +161,13 @@
         lse_ref[0, 0:1, cols] = ma + jnp.log2(la)
         lse_ref[0, 1:2, cols] = mb + jnp.log2(lb)
         return 0
-    lax.fori_loop(0, nq, block, 0)
+
+    @pl.when(small)
+    def _():
+        lax.fori_loop(0, nq, direct, 0)
+    @pl.when(jnp.logical_not(small))
+    def _():
+        lax.fori_loop(0, nq, block, 0)
 
 def attend_fwd(tab, qkv, fq, fk, first=0, pairs=None):
     _, seq, inner = qkv.shape
@@ -189,7 +246,7 @@
             return dqa + mm(kt[:HDIM], dsa, NN), dqb + mm(kt[HDIM:], dsb, NN)
 
         z = jnp.zeros((HDIM, QB), jnp.float32)
-        carry = lax.fori_loop(0, full, lambda j, c: chunk(lo + j * CK, CK, c), (z, z))
+        carry = sweep(chunk, lo, full, (z, z))
         carry = lax.fori_loop(0, tail, lambda j, c: chunk(lo + full * CK, CT, c), carry)
         dq = jnp.concatenate(carry, axis=0).T * SCALE
         g_ref[0, rows, :] = turn_back(dq, cos_ref[rows, :], sin_ref[rows, :]).astype(jnp.bfloat16)
@@ -306,28 +363,32 @@
     )(nt, g, *(() if before is None else (before,)))
 
 def unpack_kernel(g_ref, o_ref):
+    rows = o_ref.shape[1]
     for t in range(3):
         for g in range(o_ref.shape[2] // 128):
             at = g * 384 + t * 128
-            o_ref[:, t, g * 128:(g + 1) * 128] = g_ref[:, at:at + 128].astype(jnp.float32)
-
-def unpack(g):
-    width, cols = g.shape
-    step = math.gcd(128, width)
+            o_ref[t, :, g * 128:(g + 1) * 128] = g_ref[0, :rows, at:at + 128].astype(jnp.float32)
+
+def unpack(g, rows):
+    parts, tall, cols = g.shape
     return pl.pallas_call(
         unpack_kernel,
-        grid=(width // step,),
-        in_specs=[pl.BlockSpec((step, cols), lambda i: (i, 0))],
-        out_specs=pl.BlockSpec((step, 3, cols // 3), lambda i: (i, 0, 0)),
-        out_shape=jax.ShapeDtypeStruct((width, 3, cols // 3), jnp.float32),
+        grid=(parts,),
+        in_specs=[pl.BlockSpec((1, tall, cols), lambda i: (i, 0, 0))],
+        out_specs=pl.BlockSpec((3, rows, cols // 3), lambda i: (0, i, 0)),
+        out_shape=jax.ShapeDtypeStruct((3, parts * rows, cols // 3), jnp.float32),
         compiler_params=pltpu.CompilerParams(vmem_limit_bytes=60 << 20),
         name="unpack",
-    )(g)
-
-def last_kernel(base, x_ref, gm_ref, scale_ref, w_ref, *rest):
+    )(g).transpose(1, 0, 2)
+
+def side_by_side(pieces):
+    return jnp.concatenate([p[t] for t in range(3) for p in pieces], axis=1)
+
+def last_kernel(n, base, x_ref, gm_ref, scale_ref, *rest):
     gi_ref, rows_ref = rest[-2:]
-    flat = jnp.concatenate([p[t] for p in rest[:-2] for t in range(3)], axis=1)
-    g = mm(flat, w_ref[...], NT)
+    pieces = rest[n:-2]
+    groups = len(pieces) // n
+    g = sum(mm(side_by_side(pieces[r * groups:(r + 1) * groups]), rest[r][...], NT) for r in range(n))
     unit, rstd = normalize(x_ref[...].astype(jnp.float32))
     u = g * (1.0 + scale_ref[...])
     back = rstd * (u - jnp.mean(u, axis=-1, keepdims=True) - unit * jnp.mean(u * unit, axis=-1, keepdims=True))
@@ -340,24 +401,109 @@
     rows_ref[0:1, :] += shift
     rows_ref[1:2, :] += scale
 
-def input_grad(base, own, others, x, grad_middle, scale, w):
+def input_grad(base, own, others, x, grad_middle, scale, weights):
     frames, width = x.shape
     step = math.gcd(256, frames)
     row = pl.BlockSpec((step, width), lambda i, s: (i, 0))
     const = lambda a: pl.BlockSpec(a.shape, lambda i, s: (0, 0))
     return pl.pallas_call(
-        last_kernel,
+        functools.partial(last_kernel, len(weights)),
         grid_spec=pltpu.PrefetchScalarGridSpec(
             num_scalar_prefetch=1, grid=(frames // step,),
-            in_specs=[row, row, const(scale), const(w)]
+            in_specs=[row, row, const(scale)] + [const(w) for w in weights]
             + [pl.BlockSpec((3, step, 128), lambda i, s: (0, s[0] + i, 0))] * len(own)
             + [pl.BlockSpec((3, step, 128), lambda i, s: (0, i, 0))] * len(others),
             out_specs=[row, pl.BlockSpec((8, width), lambda i, s: (0, 0))]),
         out_shape=[jax.ShapeDtypeStruct((frames, width), jnp.float32), jax.ShapeDtypeStruct((8, width), jnp.float32)],
         compiler_params=pltpu.CompilerParams(vmem_limit_bytes=60 << 20),
-        cost_estimate=pl.CostEstimate(flops=2 * frames * width * w.shape[1], bytes_accessed=frames * (10 * width + 2 * w.shape[1]), transcendentals=0),
+        cost_estimate=pl.CostEstimate(flops=2 * frames * width * sum(w.shape[1] for w in weights), bytes_accessed=16 * frames * width, transcendentals=0),
         name="input_grad",
-    )(base * (frames // step), x, grad_middle, scale, w, *own, *others)
+    )(base * (frames // step), x, grad_middle, scale, *weights, *own, *others)
+
+ROOT = math.sqrt(2.0 / math.pi)
+CUBE = 0.044715
+
+def middle_kernel(n, groups, base, *refs):
+    f32, bf16 = jnp.float32, jnp.bfloat16
+    x_ref, cot_ref, gate_a_ref, shift_ref, scale_ref, gate_f_ref, ob_ref, cb_ref = refs[:8]
+    at = 8
+    eb, ow, ew, cw = (refs[at + k * n:at + (k + 1) * n] for k in range(4))
+    at += 4 * n
+    pieces = refs[at:at + n * groups]
+    at += n * groups
+    lo_ref, gm_ref, nf_ref, hid_ref, gp_ref, gbf_ref, gba_ref, att_ref, rows_ref, up_ref = refs[at:at + 10]
+    ga = refs[at + 10:]
+    inner, hid = groups * 128, cw[0].shape[0]
+    gate_a, gate_f, scale_f = gate_a_ref[...], gate_f_ref[...], scale_ref[...]
+    branch = ob_ref[...]
+    for r in range(n):
+        att = jnp.concatenate([p[...] for p in pieces[r * groups:(r + 1) * groups]], axis=1)
+        att_ref[:, r * inner:(r + 1) * inner] = att
+        branch = branch + mm(att, ow[r][...], NN)
+    middle = x_ref[...].astype(f32) + gate_a * branch
+    unit, rstd = normalize(middle)
+    nf = (unit * (1.0 + scale_f) + shift_ref[...]).astype(bf16)
+    nf_ref[...] = nf
+    cot = cot_ref[...].astype(f32)
+    gbf = (gate_f * cot).astype(bf16)
+    gbf_ref[...] = gbf
+    low = cb_ref[...]
+    gn = jnp.zeros(branch.shape, f32)
+    @pl.when(pl.program_id(0) == 0)
+    def _():
+        rows_ref[...] = jnp.zeros_like(rows_ref)
+        up_ref[...] = jnp.zeros_like(up_ref)
+    for r in range(n):
+        cols = slice(r * hid, (r + 1) * hid)
+        pre = mm(nf, ew[r][...], NN) + eb[r][...]
+        square = pre * pre
+        turn_over = jnp.tanh(ROOT * pre * (1.0 + CUBE * square))
+        share = 0.5 + 0.5 * turn_over
+        hidden = (pre * share).astype(bf16)
+        hid_ref[:, cols] = hidden
+        low = low + mm(hidden, cw[r][...], NN)
+        slope = share + pre * (1.0 - turn_over * turn_over) * (0.5 * ROOT + 1.5 * ROOT * CUBE * square)
+        gp = (mm(gbf, cw[r][...], NT) * slope).astype(bf16)
+        gp_ref[:, cols] = gp
+        up_ref[0:1, cols] += jnp.sum(gp.astype(f32), axis=0, keepdims=True)
+        gn = gn + mm(gp, ew[r][...], NT)
+    lo_ref[...] = (middle + gate_f * low).astype(bf16)
+    u = gn * (1.0 + scale_f)
+    gm = cot + rstd * (u - jnp.mean(u, axis=-1, keepdims=True) - unit * jnp.mean(u * unit, axis=-1, keepdims=True))
+    gm_ref[...] = gm
+    gba = (gate_a * gm).astype(bf16)
+    gba_ref[...] = gba
+    for r in range(n):
+        back = mm(gba, ow[r][...], NT).astype(bf16)
+        for g in range(groups):
+            ga[r * groups + g][...] = back[:, g * 128:(g + 1) * 128]
+    for k, v in enumerate((gba.astype(f32), gbf.astype(f32), gm * branch, gn, gn * unit, cot * low)):
+        rows_ref[k:k + 1, :] += jnp.sum(v, axis=0, keepdims=True)
+
+def feed_forward(base, own, others, x, cot, vectors, expand_bias, out_w, expand_w, contract_w):
+    frames, width = x.shape
+    n, groups = len(out_w), len(own)
+    step = math.gcd(256, frames)
+    hid = contract_w[0].shape[0]
+    row = pl.BlockSpec((step, width), lambda i, s: (i, 0))
+    wide = lambda cols: pl.BlockSpec((step, cols), lambda i, s: (i, 0))
+    const = lambda a: pl.BlockSpec(a.shape, lambda i, s: (0, 0))
+    shape = lambda cols, kind=jnp.bfloat16: jax.ShapeDtypeStruct((frames, cols), kind)
+    sums = lambda cols: pl.BlockSpec((8, cols), lambda i, s: (0, 0))
+    consts = list(vectors) + list(expand_bias) + list(out_w) + list(expand_w) + list(contract_w)
+    return pl.pallas_call(
+        functools.partial(middle_kernel, n, groups),
+        grid_spec=pltpu.PrefetchScalarGridSpec(
+            num_scalar_prefetch=1, grid=(frames // step,),
+            in_specs=[row, row] + [const(c) for c in consts]
+            + [pl.BlockSpec((step, 128), lambda i, s: (s[0] + i, 0))] * groups + [wide(128)] * len(others),
+            out_specs=[row, row, row, wide(n * hid), wide(n * hid), row, row, wide(n * groups * 128), sums(width), sums(n * hid)] + [wide(128)] * (n * groups)),
+        out_shape=[shape(width), shape(width, jnp.float32), shape(width), shape(n * hid), shape(n * hid), shape(width), shape(width), shape(n * groups * 128),
+                   jax.ShapeDtypeStruct((8, width), jnp.float32), jax.ShapeDtypeStruct((8, n * hid), jnp.float32)] + [shape(128)] * (n * groups),
+        compiler_params=pltpu.CompilerParams(vmem_limit_bytes=63 << 20),
+        cost_estimate=pl.CostEstimate(flops=4 * frames * width * n * (groups * 128 + 2 * hid), bytes_accessed=24 * frames * width, transcendentals=frames * n * hid),
+        name="feed_forward",
+    )(base * (frames // step), x, cot, *consts, *own, *others)
 
 def relative(axis, size):
     return lambda x, r: x if r % size == 0 else lax.ppermute(x, axis, [(i, (i + r) % size) for i in range(size)])
@@ -406,7 +552,7 @@
     ahead, _, seg, freqs, weight_proj = lax.optimization_barrier((inputs, far_mod, segment_ids[0], freqs, projection_weight))
     elsewhere = [move(ahead, r) for r in range(1, n)]
 
-    shards = [("out", output_weight), ("expand", expand_weight), ("contract", contract_weight), ("proj", projection_weight.reshape(width, 3 * inner))]
+    shards = [("out", output_weight), ("expand", expand_weight), ("contract", contract_weight)]
     heights = {name: w.size // (ndp * width) for name, w in shards}
     cut = [lax.dynamic_slice_in_dim(w, mine * (w.shape[0] // ndp), w.shape[0] // ndp, 0).reshape(heights[name], width) for name, w in shards]
     bias_rows = jnp.pad(expand_bias[None, :], ((0, 15), (0, width - hidden_here)))
@@ -425,8 +571,11 @@
     qkv, normed_t = into
 
     pack = jnp.concatenate(cut + [bias_rows], axis=0)
-    pack, qkv = lax.optimization_barrier((pack, qkv))
+    rows_here = width // ndp
+    proj_cut = lax.dynamic_slice_in_dim(weight_proj, mine * rows_here, rows_here, 0)
+    pack, proj_cut, qkv = lax.optimization_barrier((pack, proj_cut, qkv))
     moved = [move(pack, r) for r in range(1, n)]
+    moved_proj = [move(proj_cut, r) for r in range(1, n)]
     embed_rows = jnp.pad(time_embed, ((0, 15), (0, 0)))
 
     attended, log_mass, attended_here = [], [], []
@@ -434,18 +583,18 @@
         o, lse = attend_fwd(tab, qkv, fq, fk, g, 1)
         attended.append(o)
         log_mass.append(lse)
-        halves = [lax.dynamic_slice_in_dim(o, source[r] * frames_here, frames_here, 0) for r in range(n)]
+        halves = [lax.dynamic_slice_in_dim(o, source[r] * frames_here, frames_here, 0) for r in range(1, n)]
         halves, tab = lax.optimization_barrier((halves, tab))
-        attended_here.append([move(halves[r], r) for r in range(n)])
+        attended_here.append([move(halves[r - 1], r) for r in range(1, n)])
         if g == 0:
-            moved, tab = lax.optimization_barrier((moved, tab))
+            moved, moved_proj, tab = lax.optimization_barrier((moved, moved_proj, tab))
             packed = lax.all_gather(jnp.concatenate(moved + [embed_rows], axis=0), "dp", axis=0)
+            proj_rows, _ = lax.optimization_barrier((jnp.concatenate(moved_proj, axis=0), packed))
+            proj_all = lax.all_gather(proj_rows, "dp", axis=0)
         else:
             attended_here[g - 1], tab = lax.optimization_barrier((attended_here[g - 1], tab))
     packed, _ = lax.optimization_barrier((packed, log_mass[-1]))
-    att_rel = [jnp.concatenate([attended_here[g][r] for g in range(groups)], axis=1) for r in range(n)]
-
-    own_w = dict(shards)
+
     whole_w = {name: [w] for name, w in shards}
     expand_bias_all = [expand_bias]
     at = 0
@@ -456,48 +605,19 @@
         expand_bias_all.append(packed[0, at, :hidden_here])
         at += 16
     out_all, expand_all, contract_all = whole_w["out"], whole_w["expand"], whole_w["contract"]
-    proj_cat = jnp.concatenate([w.reshape(width, 3, groups, 128).transpose(0, 2, 1, 3).reshape(width, 3 * inner) for w in whole_w["proj"]], axis=1)
     silu_all = jax.nn.silu(packed[:, at].astype(f32)).astype(bf16).astype(f32)
 
-    att_cat = jnp.concatenate(att_rel, axis=1)
-    out_cat = jnp.concatenate(out_all, axis=0)
-    expand_cat = jnp.concatenate(expand_all, axis=1)
-    contract_cat = jnp.concatenate(contract_all, axis=0)
-    expand_bias_cat = jnp.concatenate(expand_bias_all, axis=0).astype(f32)
-
-    frames = inputs.astype(f32)
-    grad_out = cotangent.astype(f32)
-    branch_a = jnp.dot(att_cat, out_cat, preferred_element_type=f32) + output_bias.astype(f32)
-    middle = frames + gate_a * branch_a
-    unit_f, rstd_f = normalize(middle)
-    normed_f = (unit_f * (1.0 + scale_f) + shift_f).astype(bf16)
-    hidden_pre = jnp.dot(normed_f, expand_cat, preferred_element_type=f32) + expand_bias_cat
-    hidden_full, gelu_pull = jax.vjp(lambda v: jax.nn.gelu(v, approximate=True), hidden_pre)
-    hidden = hidden_full.astype(bf16)
-    branch_f = jnp.dot(hidden, contract_cat, preferred_element_type=f32) + contract_bias.astype(f32)
-    layer_output = (middle + gate_f * branch_f).astype(bf16)
-    row_gate_f = jnp.sum(grad_out * branch_f, axis=0)
-    grad_branch_f = (gate_f * grad_out).astype(bf16)
-    bias_down = jnp.sum(grad_branch_f.astype(f32), axis=0)
-    grad_hidden = jnp.einsum("fd,hd->fh", grad_branch_f, contract_cat, preferred_element_type=f32)
-    grad_pre = gelu_pull(grad_hidden)[0].astype(bf16)
+    vectors = [v.astype(f32).reshape(1, width) for v in (gate_a, shift_f, scale_f, gate_f, output_bias, contract_bias)]
+    far_att = [attended_here[g][r - 1] for r in range(1, n) for g in range(groups)]
+    layer_output, grad_middle, normed_f, hidden, grad_pre, grad_branch_f, grad_branch_a, att_cat, sums, bias_up, *grad_att = feed_forward(
+        place(0), attended, far_att, inputs, cotangent, vectors, [b.astype(f32).reshape(1, hidden_here) for b in expand_bias_all], out_all, expand_all, contract_all)
+    proj_all, att_cat = lax.optimization_barrier((proj_all, att_cat))
+    proj_w = [weight_proj] + [proj_all[:, (r - 1) * rows_here:r * rows_here].reshape(width, 3 * inner) for r in range(1, n)]
     contract_part = jnp.einsum("fh,fd->hd", hidden, grad_branch_f, preferred_element_type=f32)
     expand_part = jnp.einsum("fd,fh->dh", normed_f, grad_pre, preferred_element_type=f32)
-    bias_up = jnp.sum(grad_pre.astype(f32), axis=0)
-    grad_normed_f = jnp.einsum("fh,dh->fd", grad_pre, expand_cat, preferred_element_type=f32)
-
-    def norm_back(g, unit, rstd, scale):
-        u = g * (1.0 + scale)
-        return rstd * (u - jnp.mean(u, axis=-1, keepdims=True) - unit * jnp.mean(u * unit, axis=-1, keepdims=True))
-
-    grad_middle = grad_out + norm_back(grad_normed_f, unit_f, rstd_f, scale_f)
-    row_shift_f = jnp.sum(grad_normed_f, axis=0)
-    row_scale_f = jnp.sum(grad_normed_f * unit_f, axis=0)
-    row_gate_a = jnp.sum(grad_middle * branch_a, axis=0)
-    grad_branch_a = (gate_a * grad_middle).astype(bf16)
-    bias_out = jnp.sum(grad_branch_a.astype(f32), axis=0)
-    grad_att = jnp.einsum("fd,id->fi", grad_branch_a, out_cat, preferred_element_type=f32).astype(bf16)
     output_part = jnp.einsum("fi,fd->id", att_cat, grad_branch_a, preferred_element_type=f32)
+    bias_out, bias_down, row_gate_a, row_shift_f, row_scale_f, row_gate_f = (sums[k] for k in range(6))
+    bias_up = bias_up[0].reshape(n, hidden_here)
 
     def slots(part):
         return part.astype(bf16).reshape(ndp, part.size // (ndp * width), width)
@@ -509,12 +629,12 @@
             contract_part[r * hidden_here:(r + 1) * hidden_here])], axis=1)
     reduced = lax.psum_scatter(sent, "dp", scatter_dimension=0, tiled=False)
     tall = reduced.shape[0] // n
+    grads_in = [[move(grad_att[r * groups + g], -r) for r in range(n)] for g in range(groups)]
     flat, flat_far, wgrads, bias_sums = [], [[] for _ in range(1, n)], None, []
     for g in range(groups):
         whole = jnp.zeros((seq, 128), bf16)
         for r in range(n):
-            piece = move(grad_att[:, r * inner + g * 128:r * inner + (g + 1) * 128], -r)
-            whole = lax.dynamic_update_slice_in_dim(whole, piece, source[r] * frames_here, 0)
+            whole = lax.dynamic_update_slice_in_dim(whole, grads_in[g][r], source[r] * frames_here, 0)
         back = attend_bwd(tab, qkv, fq, fk, attended[g], whole, log_mass[g], cosine, sine, g, 1)
         flat.append(back)
         parts = [lax.dynamic_slice_in_dim(back, source[r] * frames_here, frames_here, 1) for r in range(1, n)]
@@ -526,18 +646,20 @@
             flat_far[r - 1].append(move(parts[r - 1], r))
         wgrads, b = weight_grad(normed_t, back, g, groups, wgrads)
         wgrads, tab = lax.optimization_barrier((wgrads, tab))
+        if g + 2 < groups:
+            grads_in[g + 2], tab = lax.optimization_barrier((grads_in[g + 2], tab))
+        if g == max(groups - 3, 0):
+            reduced, tab = lax.optimization_barrier((reduced, tab))
+            shares = [reduced[:tall]] + [move(reduced[r * tall:(r + 1) * tall], -r) for r in range(1, n)]
         if g == max(groups - 2, 0):
-            reduced, tab = lax.optimization_barrier((reduced, tab))
-            own_grads = reduced[:tall].astype(f32)
-            for r in range(1, n):
-                own_grads = own_grads + move(reduced[r * tall:(r + 1) * tall], -r).astype(f32)
-            own_grads, tab = lax.optimization_barrier((own_grads.astype(bf16), tab))
+            shares, tab = lax.optimization_barrier((shares, tab))
+            own_grads = sum(p.astype(f32) for p in shares).astype(bf16)
+            own_grads, tab = lax.optimization_barrier((own_grads, tab))
             own_grads = lax.all_gather(own_grads, "dp", axis=0)
         bias_sums.append(b[0].reshape(3, 128))
 
     wgrads, own_grads = lax.optimization_barrier((wgrads, own_grads))
     proj_own = lax.psum_scatter(wgrads.reshape(ndp, width // ndp, 3 * inner), "dp", scatter_dimension=0, tiled=False)
-    grad_projection = unpack(lax.all_gather(proj_own, "dp", axis=0, tiled=True))
     at, grads = 0, {}
     for name, w in shards[:3]:
         grads[name] = own_grads[:, at:at + heights[name]].astype(f32).reshape(w.shape)
@@ -545,28 +667,41 @@
     grad_output, grad_expand, grad_contract = grads["out"], grads["expand"], grads["contract"]
     bias_proj_grad = jnp.stack(bias_sums, axis=1).reshape(3 * inner)
 
-    grad_inputs, row_sums = input_grad(place(0), flat, [p for far in flat_far for p in far], inputs, grad_middle, scale_a, proj_cat)
-    row_shift_a, row_scale_a = row_sums[0], row_sums[1]
-
-    early = jnp.concatenate([bias_proj_grad, bias_out, bias_down, bias_up, row_shift_a, row_scale_a, row_gate_a, row_shift_f, row_scale_f, row_gate_f])
-    table = lax.all_gather(early, ("dp", "head"), axis=0)
-    table = table.reshape(ndp, n, early.shape[0])
+    grad_inputs, row_sums = input_grad(place(0), flat, [p for far in flat_far for p in far], inputs, grad_middle, scale_a, proj_w)
+    row_mods = jnp.concatenate([row_sums[0], row_sums[1], row_gate_a, row_shift_f, row_scale_f, row_gate_f])
+
+    def for_head(r):
+        own_mods = lax.dynamic_slice_in_dim(row_mods, owner[r] * local_mod, local_mod, 0)
+        return jnp.concatenate([bias_out, bias_down, bias_up[r], own_mods])
+
+    here = sum(move(for_head(r), -r) for r in range(n))
+    own_mods = here[None, 2 * width + hidden_here:]
+    small = jnp.concatenate([bias_proj_grad, here])
+    length = -(-small.shape[0] // (3 * inner)) * 3 * inner
+    small = jnp.pad(small, (0, length - small.shape[0]))
+    terms = []
+    for _ in range(3):
+        terms.append(lax.reduce_precision(small, 8, 7))
+        small = small - terms[-1]
+    terms = jnp.stack(terms).astype(bf16).reshape(-1, 3 * inner)
+    terms = jnp.pad(terms, ((0, -terms.shape[0] % 16), (0, 0)))
+    gathered = lax.all_gather(jnp.concatenate([proj_own, terms], axis=0), "dp", axis=0)
+    grad_projection = unpack(gathered, rows_here)
+    table = gathered[:, rows_here:].reshape(ndp, -1)[:, :3 * length].astype(f32).reshape(ndp, 3, length)
+    table = table[:, 0] + (table[:, 1] + table[:, 2])
+    totals = jnp.sum(table, axis=0)
     base = 3 * inner
-    own_col = lax.dynamic_index_in_dim(table, me, 1, keepdims=False)
-    grad_projection_bias = jnp.sum(own_col[:, :base], axis=0).reshape(3, inner)
-    both = jnp.sum(table[:, :, base:base + 2 * width], axis=(0, 1))
-    grad_output_bias, grad_contract_bias = both[:width], both[width:]
-    base = base + 2 * width
-    up = jnp.sum(table[:, :, base:base + n * hidden_here], axis=0).reshape(n, n, hidden_here)
-    grad_expand_bias = sum(
-        lax.dynamic_slice(up, (source[r], r, 0), (1, 1, hidden_here)).reshape(hidden_here) for r in range(n)
-    )
-    base = base + n * hidden_here
-    grad_mod = jnp.sum(lax.dynamic_slice_in_dim(table[:, :, base:], me * local_mod, local_mod, 2), axis=1)
+    grad_projection_bias = totals[:base].reshape(3, inner)
+    grad_output_bias, grad_contract_bias = totals[base:base + width], totals[base + width:base + 2 * width]
+    base += 2 * width
+    grad_expand_bias = totals[base:base + hidden_here]
+    base += hidden_here
+    grad_mod = table[:, base:base + local_mod]
     grad_mod_weight = jnp.dot(silu_all.T, grad_mod, precision=lax.Precision.HIGHEST)
-    grad_mod_bias = jnp.sum(grad_mod, axis=0)
-    own_row = lax.dynamic_slice_in_dim(grad_mod, mine, 1, 0)
-    grad_silu = lax.psum(jnp.sum(modulator_weight.astype(f32) * own_row, axis=1), "head")[None, :]
+    grad_mod_bias = totals[base:base + local_mod]
+    own_row = own_mods
+    grad_silu = jnp.sum(modulator_weight.astype(f32) * own_row, axis=1)
+    grad_silu = sum(move(grad_silu, r) for r in range(n))[None, :]
     _, silu_pull = jax.vjp(jax.nn.silu, embeds)
     grad_embed = silu_pull(grad_silu)[0]
     return (

time: 856 us -> 727 us (0.85)
  matrix products: 129 us -> 35.5 us
  local copies, waits for them, and re-layouts: 115 us -> 63 us
  waiting for transfers between devices: 158 us -> 203 us
  other arithmetic: 41.3 us -> 27.1 us
  Pallas kernels: 363 us -> 353 us
    dot_general x6 -> x0, matrix products: 90.5 us -> none  [the longest x1 31.1 us: on_device(): jnp.einsum('fd,hd->fh', grad_branch_f, contract_cat, preferred_element_ty...]
    reduce_scatter x1, waiting for transfers between devices: 0.01 us -> 59.2 us  [on_device(): reduced = lax.psum_scatter(sent, 'dp', scatter_dimension=0, tiled=False)]
    pallas_call x2 -> x3, Pallas kernels: 28.1 us -> 82.1 us  [the longest x1 52.9 us: feed_forward(): pl.pallas_call(functools.partial(middle_kernel, n, groups), grid_spec=plt...]
    ppermute x16 -> x19, waiting for transfers between devices: 91 us -> 48.4 us  [relative(): lax.ppermute(x, axis, [(i, (i + r) % size) for i in range(size)])]
    reduce_scatter x1, waiting for transfers between devices: 0.02 us -> 41.8 us  [on_device(): lax.psum_scatter(wgrads.reshape(ndp, width // ndp, 3 * inner), 'dp', scat...]
    pallas_call x4, Pallas kernels: 123 us -> 85.4 us  [attend_fwd(): pl.pallas_call(fwd_kernel, grid_spec=pltpu.PrefetchScalarGridSpec(num_sca...]
    all_gather x2, waiting for transfers between devices: 67.1 us -> 37 us  [the longest x1 32.9 us: on_device(): lax.all_gather(jnp.concatenate([proj_own, terms], axis=0), 'dp', axis=0)]
    pallas_call x4, Pallas kernels: 153 us -> 126 us  [attend_bwd(): pl.pallas_call(bwd_kernel, grid_spec=pltpu.PrefetchScalarGridSpec(num_sca...]
  transfers between devices with their start and end apart: 22 -> 25, of which waited for: 8 -> 9; matrix products, arithmetic and copies ran while one was open for 15% -> 12% of each run, Pallas kernels for 40% -> 46%
where the time goes in v4:
time: 727 us; the launch traced here: 719 us
  Pallas kernels  353 us (49%)
  waiting for transfers between devices  203 us (28%)
  local copies, waits for them, and re-layouts  63 us (9%)
  matrix products  35.5 us (5%)
  other arithmetic  27.1 us (4%)
  starting transfers between devices  22.6 us (3%)
  between operations  15.1 us (2%)
    pallas_call x4, Pallas kernels, attend_bwd(): pl.pallas_call(bwd_kernel, grid_spec=pltpu.PrefetchScalarGridSpec(num_sca...  126 us
    pallas_call x4, Pallas kernels, attend_fwd(): pl.pallas_call(fwd_kernel, grid_spec=pltpu.PrefetchScalarGridSpec(num_sca...  85.4 us
    reduce_scatter x1, waiting for transfers between devices, on_device(): reduced = lax.psum_scatter(sent, 'dp', scatter_dimension=0, tiled=False)  59.2 us
    pallas_call x1, Pallas kernels, feed_forward(): pl.pallas_call(functools.partial(middle_kernel, n, groups), grid_spec=plt...  52.9 us
    ppermute x19, waiting for transfers between devices, relative(): lax.ppermute(x, axis, [(i, (i + r) % size) for i in range(size)])  48.4 us
    reduce_scatter x1, waiting for transfers between devices, on_device(): lax.psum_scatter(wgrads.reshape(ndp, width // ndp, 3 * inner), 'dp', scat...  41.8 us
    pallas_call x4, Pallas kernels, weight_grad(): pl.pallas_call(wgrad_kernel, grid=(seq // step,), in_specs=[pl.BlockSpec(...  35.4 us
    all_gather x1, waiting for transfers between devices, on_device(): lax.all_gather(jnp.concatenate([proj_own, terms], axis=0), 'dp', axis=0)  32.9 us
  transfers between devices with their start and end apart: 25, of which 9 were waited for; matrix products, arithmetic and copies ran while one was open for 12% of the time, Pallas kernels for 46%

profile of v4, /device:TPU:0, one launch (start us, length us, event | category | flops | bytes accessed | tf_op | source)
XLA Modules:
  0.0 718.9 jit_solution(7580984858719559192)
XLA Ops:
  7.3 3.7 fusion.24
  11.0 3.0 collective-permute-start
  17.7 1.5 fusion.6
  20.0 1.6 copy.93.sin_ref
  21.7 1.6 copy.92.cos_ref
  23.4 3.2 copy.87
  26.5 2.9 copy.91.w_ref.rest_0_
  32.1 11.7 %project.2 = (bf16[3,3072,512]{2,1,0:T(8,128)(2,1)}, bf16[1024,3072]{1,0:T(8,128)(2,1)}) custom-call(s32[1]{0:T(128)} %bitcast.base, bf16[1536,1024]{1,0:T(8,128)(2,1)} %x_ref.3, f32[1,1024]{1,0:T(1,128)} %get-tuple-element.256.scale_ref, f32[1,1024]{1,0:T(1,128)} %get-tuple-element.255.shift_ref, bf16[1024,1536]{1,0:T(8,128)(2,1)} %copy.91.w_ref.rest_0_, ...), custom_call_target="tpu_custom_call" | custom-call | flops 4831838208 | bytes 11010048 | tf_op jit(solution)/shard_map/project/pallas_call | solution.py:317
  43.9 2.3 select_convert_fusion
  46.1 41.4 %collective-permute-done.1.x_ref = bf16[1536,1024]{1,0:T(8,128)(2,1)} collective-permute-done((bf16[1536,1024]{1,0:T(8,128)(2,1)}, bf16[1536,1024]{1,0:T(8,128)(2,1)}, u32[]{:S(2)}, u32[]{:S(2)}) %collective-permute-start.1) | collective-permute-done | bytes 3145760 | tf_op jit(solution)/shard_map/ppermute | solution.py:509
  87.5 11.7 %project.3 = (bf16[3,3072,512]{2,1,0:T(8,128)(2,1)}, bf16[1024,3072]{1,0:T(8,128)(2,1)}) custom-call(s32[1]{0:T(128)} %bitcast.7.base, bf16[1536,1024]{1,0:T(8,128)(2,1)} %collective-permute-done.1.x_ref, f32[1,1024]{1,0:T(1,128)} %get-tuple-element.256.scale_ref, ...), custom_call_target="tpu_custom_call", output_to_operand_aliasing={{0}: (8, {}), {1}: (9, {})} | custom-call | flops 4831838208 | bytes 11010048 | tf_op jit(solution)/shard_map/project/pallas_call | solution.py:317
  99.5 1.7 collective-permute-start.3
  101.2 21.5 %attend_fwd.4 = (bf16[3072,128]{1,0:T(8,128)(2,1)}, f32[1,8,3072]{2,1,0:T(8,128)}) custom-call(s32[36]{0:T(128)} %pad_add_fusion.tab, bf16[3,3072,512]{2,1,0:T(8,128)(2,1)} %get-tuple-element.123.q_ref.k_ref.v_ref, bf16[3,3072,512]{2,1,0:T(8,128)(2,1)} %get-tuple-element.123.q_ref.k_ref.v_ref, bf16[3,3072,512]{2,1,0:T(8,128)(2,1)} %get-tuple-element.123.q_ref.k_ref.v_ref, ...), custom_call_target="tpu_custom_call" | custom-call | flops 28991029248 | bytes 3145728 | tf_op jit(solution)/shard_map/attend_fwd/pallas_call | solution.py:177
  126.9 21.3 %attend_fwd.5 = (bf16[3072,128]{1,0:T(8,128)(2,1)}, f32[1,8,3072]{2,1,0:T(8,128)}) custom-call(s32[36]{0:T(128)} %pad_add_fusion.tab, bf16[3,3072,512]{2,1,0:T(8,128)(2,1)} %get-tuple-element.123.q_ref.k_ref.v_ref, bf16[3,3072,512]{2,1,0:T(8,128)(2,1)} %get-tuple-element.123.q_ref.k_ref.v_ref, bf16[3,3072,512]{2,1,0:T(8,128)(2,1)} %get-tuple-element.123.q_ref.k_ref.v_ref, ...), custom_call_target="tpu_custom_call" | custom-call | flops 28991029248 | bytes 3145728 | tf_op jit(solution)/shard_map/attend_fwd/pallas_call | solution.py:177
  149.2 1.8 collective-permute-start.4
  151.0 21.3 %attend_fwd.6 = (bf16[3072,128]{1,0:T(8,128)(2,1)}, f32[1,8,3072]{2,1,0:T(8,128)}) custom-call(s32[36]{0:T(128)} %pad_add_fusion.tab, bf16[3,3072,512]{2,1,0:T(8,128)(2,1)} %get-tuple-element.123.q_ref.k_ref.v_ref, bf16[3,3072,512]{2,1,0:T(8,128)(2,1)} %get-tuple-element.123.q_ref.k_ref.v_ref, bf16[3,3072,512]{2,1,0:T(8,128)(2,1)} %get-tuple-element.123.q_ref.k_ref.v_ref, ...), custom_call_target="tpu_custom_call" | custom-call | flops 28991029248 | bytes 3145728 | tf_op jit(solution)/shard_map/attend_fwd/pallas_call | solution.py:177
  173.8 21.3 %attend_fwd.7 = (bf16[3072,128]{1,0:T(8,128)(2,1)}, f32[1,8,3072]{2,1,0:T(8,128)}) custom-call(s32[36]{0:T(128)} %pad_add_fusion.tab, bf16[3,3072,512]{2,1,0:T(8,128)(2,1)} %get-tuple-element.123.q_ref.k_ref.v_ref, bf16[3,3072,512]{2,1,0:T(8,128)(2,1)} %get-tuple-element.123.q_ref.k_ref.v_ref, bf16[3,3072,512]{2,1,0:T(8,128)(2,1)} %get-tuple-element.123.q_ref.k_ref.v_ref, ...), custom_call_target="tpu_custom_call" | custom-call | flops 28991029248 | bytes 3145728 | tf_op jit(solution)/shard_map/attend_fwd/pallas_call | solution.py:177
  196.1 1.8 collective-permute-start.7
  199.2 2.3 slice.156
  202.9 5.0 fusion.35
  208.6 52.9 %feed_forward.1 = (bf16[1536,1024]{1,0:T(8,128)(2,1)}, f32[1536,1024]{1,0:T(8,128)}, bf16[1536,1024]{1,0:T(8,128)(2,1)}, bf16[1536,2048]{1,0:T(8,128)(2,1)}, bf1...) custom-call(s32[1]{0:T(128)} %bitcast.base, ...), custom_call_target="tpu_custom_call" | custom-call | flops 32212254720 | bytes 37748736 | tf_op jit(solution)/shard_map/feed_forward/pallas_call | solution.py:494
  261.5 10.0 %convolution_convert_fusion.1 = bf16[1024,2048]{1,0:T(8,128)(2,1)S(1)} fusion(bf16[1536,1024]{1,0:T(8,128)(2,1)} %get-tuple-element.167, bf16[1536,2048]{1,0:T(8,128)(2,1)} %get-tuple-element.168), kind=kOutput, calls=%fused_computation.2 | convolution fusion | flops 6444548096 | bytes 13631488 | tf_op jit(solution)/shard_map/fd,fh->dh/dot_general | solution.py:617
  271.6 1.8 fusion.38
  273.3 1.8 copy-done.31
  275.1 7.4 %convolution_convert_fusion = bf16[2048,1024]{1,0:T(8,128)(2,1)S(1)} fusion(bf16[1536,2048]{1,0:T(8,128)(2,1)S(1)} %copy-done.31, bf16[1536,1024]{1,0:T(8,128)(2,1)S(1)} %copy-done.32), kind=kOutput, calls=%fused_computation.1 | convolution fusion | flops 6444548096 | bytes 13631488 | tf_op jit(solution)/shard_map/fh,fd->hd/dot_general | solution.py:616
  282.5 2.4 fusion.37
  284.9 4.1 all-gather.11.cloned.1.call-done
  289.0 6.3 convolution_convert_fusion.2
  297.3 1.5 constant_dynamic-update-slice_fusion.4
  298.8 1.5 constant_dynamic-update-slice_fusion.3
  301.4 1.6 constant_dynamic-update-slice_fusion.1
  303.0 1.5 constant_dynamic-update-slice_fusion
  305.4 1.5 collective-permute-start.8
  307.5 1.5 collective-permute-start.10
  309.9 3.4 collective-permute-done.8
  314.2 31.5 %attend_bwd.4.g_ref.rest_2_ = bf16[3,3072,128]{2,1,0:T(8,128)(2,1)} custom-call(s32[36]{0:T(128)} %pad_add_fusion.tab, bf16[3,3072,512]{2,1,0:T(8,128)(2,1)} %get-tuple-element.123.q_ref.k_ref.v_ref, bf16[3,3072,512]{2,1,0:T(8,128)(2,1)} %get-tuple-element.123.q_ref.k_ref.v_ref, bf16[3,3072,512]{2,1,0:T(8,128)(2,1)} %get-tuple-element.123.q_ref.k_ref.v_ref, ...), custom_call_target="tpu_custom_call" | custom-call | flops 38654705664 | bytes 6291456 | tf_op jit(solution)/shard_map/attend_bwd/pallas_call | solution.py:269
  345.7 1.4 constant_dynamic-slice_fusion.3
  347.0 1.5 collective-permute-start.12
  348.6 9.2 %weight_grad.4 = (bf16[1024,1536]{1,0:T(8,128)(2,1)}, f32[8,384]{1,0:T(8,128)}) custom-call(bf16[1024,3072]{1,0:T(8,128)(2,1)} %get-tuple-element.157.nt_ref, bf16[3,3072,128]{2,1,0:T(8,128)(2,1)} %attend_bwd.4.g_ref.rest_2_), custom_call_target="tpu_custom_call" | custom-call | flops 2415919104 | bytes 8650752 | tf_op jit(solution)/shard_map/weight_grad/pallas_call | solution.py:351
  358.7 32.3 %attend_bwd.5.g_ref.rest_3_ = bf16[3,3072,128]{2,1,0:T(8,128)(2,1)} custom-call(s32[36]{0:T(128)} %pad_add_fusion.tab, bf16[3,3072,512]{2,1,0:T(8,128)(2,1)} %get-tuple-element.123.q_ref.k_ref.v_ref, bf16[3,3072,512]{2,1,0:T(8,128)(2,1)} %get-tuple-element.123.q_ref.k_ref.v_ref, bf16[3,3072,512]{2,1,0:T(8,128)(2,1)} %get-tuple-element.123.q_ref.k_ref.v_ref, ...), custom_call_target="tpu_custom_call" | custom-call | flops 38654705664 | bytes 6291456 | tf_op jit(solution)/shard_map/attend_bwd/pallas_call | solution.py:269
  391.2 1.4 constant_dynamic-slice_fusion.2
  392.7 8.9 %weight_grad.5 = (bf16[1024,1536]{1,0:T(8,128)(2,1)}, f32[8,384]{1,0:T(8,128)}) custom-call(bf16[1024,3072]{1,0:T(8,128)(2,1)} %get-tuple-element.157.nt_ref, bf16[3,3072,128]{2,1,0:T(8,128)(2,1)} %attend_bwd.5.g_ref.rest_3_, bf16[1024,1536]{1,0:T(8,128)(2,1)} %get-tuple-element.175.rest_0_), custom_call_target="tpu_custom_call", output_to_operand_aliasing={{0}: (2, {})} | custom-call | flops 2415919104 | bytes 8650752 | tf_op jit(solution)/shard_map/weight_grad/pallas_call | solution.py:351
  402.0 59.2 %reduce-scatter.3.cloned.1.call-done = bf16[1,320,1024]{2,1,0:T(8,128)(2,1)} async-done(((bf16[16,320,1024]{2,1,0:T(8,128)(2,1)}), bf16[1,320,1024]{2,1,0:T(8,128)(2,1)}) %reduce-scatter.3.cloned.1.call-update) | async-done | bytes 655376 | tf_op jit(solution)/shard_map/reduce_scatter | solution.py:630
  462.3 1.5 collective-permute-start.13
  463.8 31.2 %attend_bwd.6.g_ref.rest_4_ = bf16[3,3072,128]{2,1,0:T(8,128)(2,1)} custom-call(s32[36]{0:T(128)} %pad_add_fusion.tab, bf16[3,3072,512]{2,1,0:T(8,128)(2,1)} %get-tuple-element.123.q_ref.k_ref.v_ref, bf16[3,3072,512]{2,1,0:T(8,128)(2,1)} %get-tuple-element.123.q_ref.k_ref.v_ref, bf16[3,3072,512]{2,1,0:T(8,128)(2,1)} %get-tuple-element.123.q_ref.k_ref.v_ref, ...), custom_call_target="tpu_custom_call" | custom-call | flops 38654705664 | bytes 6291456 | tf_op jit(solution)/shard_map/attend_bwd/pallas_call | solution.py:269
  496.4 8.8 %weight_grad.6 = (bf16[1024,1536]{1,0:T(8,128)(2,1)}, f32[8,384]{1,0:T(8,128)}) custom-call(bf16[1024,3072]{1,0:T(8,128)(2,1)} %get-tuple-element.157.nt_ref, bf16[3,3072,128]{2,1,0:T(8,128)(2,1)} %attend_bwd.6.g_ref.rest_4_, bf16[1024,1536]{1,0:T(8,128)(2,1)} %get-tuple-element.186.rest_0_), custom_call_target="tpu_custom_call", output_to_operand_aliasing={{0}: (2, {})} | custom-call | flops 2415919104 | bytes 8650752 | tf_op jit(solution)/shard_map/weight_grad/pallas_call | solution.py:351
  505.1 1.8 add_convert_fusion
  508.1 31.2 %attend_bwd.7.rest_5_.g_ref = bf16[3,3072,128]{2,1,0:T(8,128)(2,1)} custom-call(s32[36]{0:T(128)} %pad_add_fusion.tab, bf16[3,3072,512]{2,1,0:T(8,128)(2,1)} %get-tuple-element.123.q_ref.k_ref.v_ref, bf16[3,3072,512]{2,1,0:T(8,128)(2,1)} %get-tuple-element.123.q_ref.k_ref.v_ref, bf16[3,3072,512]{2,1,0:T(8,128)(2,1)} %get-tuple-element.123.q_ref.k_ref.v_ref, ...), custom_call_target="tpu_custom_call" | custom-call | flops 38654705664 | bytes 6291456 | tf_op jit(solution)/shard_map/attend_bwd/pallas_call | solution.py:269
  539.3 1.5 constant_dynamic-slice_fusion
  542.2 8.6 %weight_grad.7 = (bf16[1024,1536]{1,0:T(8,128)(2,1)}, f32[8,384]{1,0:T(8,128)}) custom-call(bf16[1024,3072]{1,0:T(8,128)(2,1)} %get-tuple-element.157.nt_ref, bf16[3,3072,128]{2,1,0:T(8,128)(2,1)} %attend_bwd.7.rest_5_.g_ref, bf16[1024,1536]{1,0:T(8,128)(2,1)} %get-tuple-element.205.rest_0_), custom_call_target="tpu_custom_call", output_to_operand_aliasing={{0}: (2, {})} | custom-call | flops 2415919104 | bytes 8650752 | tf_op jit(solution)/shard_map/weight_grad/pallas_call | solution.py:351
  550.8 16.6 %all-gather.13.cloned.1.call-done = bf16[2560,1024]{1,0:T(8,128)(2,1)} async-done(((bf16[160,1024]{1,0:T(8,128)(2,1)}), bf16[2560,1024]{1,0:T(8,128)(2,1)}) %all-gather.13.cloned.1.call-update) | async-done | bytes 5242896 | tf_op jit(solution)/shard_map/all_gather | solution.py:658
  571.2 18.7 %input_grad.1 = (f32[1536,1024]{1,0:T(8,128)}, f32[8,1024]{1,0:T(8,128)}) custom-call(s32[1]{0:T(128)} %bitcast.base, bf16[1536,1024]{1,0:T(8,128)(2,1)} %x_ref.3, f32[1536,1024]{1,0:T(8,128)} %get-tuple-element.146.gm_ref, f32[1,1024]{1,0:T(1,128)} %get-tuple-element.256.scale_ref, bf16[1024,1536]{1,0:T(8,128)(2,1)} %copy.91.w_ref.rest_0_, ...), custom_call_target="tpu_custom_call" | custom-call | flops 9663676416 | bytes 25165824 | tf_op jit(solution)/shard_map/input_grad/pallas_call | solution.py:409
  590.9 1.5 collective-permute-start.17
  592.4 2.4 collective-permute-done.17
  595.0 41.8 %reduce-scatter.5.cloned.1.call-done = bf16[1,64,1536]{2,1,0:T(8,128)(2,1)} async-done(((bf16[16,64,1536]{2,1,0:T(8,128)(2,1)}), bf16[1,64,1536]{2,1,0:T(8,128)(2,1)}) %reduce-scatter.5.cloned.1.call-update) | async-done | bytes 196624 | tf_op jit(solution)/shard_map/reduce_scatter | solution.py:662
  636.8 1.6 fusion.9
  638.5 4.3 multiply_reduce_fusion
  642.8 1.4 collective-permute-start.18
  647.2 1.6 bitcast_convert_fusion.2
  649.2 2.6 bitcast_convert_fusion
  651.9 2.6 bitcast_convert_fusion.1
  654.5 32.9 %all-gather.15.cloned.1.call-done = bf16[1280,1536]{1,0:T(8,128)(2,1)} async-done(((bf16[80,1536]{1,0:T(8,128)(2,1)}), bf16[1280,1536]{1,0:T(8,128)(2,1)}) %all-gather.15.cloned.1.call-update) | async-done | bytes 3932176 | tf_op jit(solution)/shard_map/all_gather | solution.py:688
  692.6 10.6 %unpack.1 = f32[3,1024,512]{2,1,0:T(8,128)} custom-call(bf16[16,80,1536]{2,1,0:T(8,128)(2,1)} %bitcast.101), custom_call_target="tpu_custom_call" | custom-call | tf_op jit(solution)/shard_map/unpack/pallas_call | solution.py:374
  703.8 8.1 %fusion.10 = f32[1024,3072]{1,0:T(8,128)} fusion(f32[16,7680]{1,0:T(8,128)S(1)} %bitcast.115, f32[16,1,1024]{2,1,0:T(1,128)S(1)} %slice_convert_fusion.1), kind=kOutput, calls=%fused_computation.29 | convolution fusion | flops 604061696 | bytes 12845056 | tf_op jit(solution)/shard_map/dot_general | solution.py:700
  (191 shorter events, 45.7 us)
Async XLA Ops:
  7.2 3.8 copy-start.20
  7.2 7.4 %copy-start.18 = (bf16[1024]{0:T(1024)(128)(2,1)S(1)}, bf16[1024]{0:T(1024)(128)(2,1)}, u32[]{:S(2)}) copy-start(bf16[1024]{0:T(1024)(128)(2,1)} %param.24) | copy-start | bytes 6148
  7.2 7.4 %copy-start.21 = (bf16[3,512]{1,0:T(4,128)(2,1)S(1)}, bf16[3,512]{1,0:T(4,128)(2,1)}, u32[]{:S(2)}) copy-start(bf16[3,512]{1,0:T(4,128)(2,1)} %param.20) | copy-start | bytes 9220
  7.2 12.0 %copy-start.14 = (s32[1,3072]{1,0:T(1,128)S(1)}, s32[1,3072]{1,0:T(1,128)}, u32[]{:S(2)}) copy-start(s32[1,3072]{1,0:T(1,128)} %param.16) | copy-start | bytes 36868
  7.2 190.7 %all-gather.9.cloned.1.call-start = ((), (), s32[]{:S(2)}) async-start(), calls=%async_computation.4 | async-start | bytes 6684672 | tf_op jit(solution)/shard_map/all_gather | solution.py:591
  11.0 6.6 collective-permute-start
  17.6 69.9 %collective-permute-start.1 = (bf16[1536,1024]{1,0:T(8,128)(2,1)}, bf16[1536,1024]{1,0:T(8,128)(2,1)}, u32[]{:S(2)}, u32[]{:S(2)}) collective-permute-start(bf16[1536,1024]{1,0:T(8,128)(2,1)} %x_ref.3), channel_id=1, source_target_pairs={{0,1},{1,0},{2,3},{3,2},{4,5},{5,4},{6,7},{7,6},{8,9},{9,8},{10,11... | collective-permute-start | bytes 9437192 | tf_op jit(solution)/shard_map/ppermute | solution.py:509
  32.1 11.8 %copy-start.24 = (pred[128]{0:T(512)(128)(4,1)S(1)}, pred[128]{0:T(512)(128)(4,1)}, u32[]{:S(2)}) copy-start(pred[128]{0:T(512)(128)(4,1)} %broadcast_compare_fusion) | copy-start | bytes 388
  32.1 11.7 %copy-start.25 = (s32[128]{0:T(128)S(1)}, s32[128]{0:T(128)}, u32[]{:S(2)}) copy-start(s32[128]{0:T(128)} %and_select_fusion) | copy-start | bytes 1540
  99.2 24.5 %collective-permute-start.2 = (bf16[176,1024]{1,0:T(8,128)(2,1)S(1)}, bf16[176,1024]{1,0:T(8,128)(2,1)S(1)}, u32[]{:S(2)}, u32[]{:S(2)}) collective-permute-start(bf16[176,1024]{1,0:T(8,128)(2,1)S(1)} %fusion.8), channel_id=1, source_target_pairs={{0,1},{1,0},{2,3},{3,2},{4,5},{5,4},{6,7},{7,6},{8,9},{9,8},{10,11... | collective-permute-start | bytes 1081352 | tf_op jit(solution)/shard_map/ppermute | solution.py:509
  99.5 24.2 %collective-permute-start.3 = (bf16[64,1536]{0,1:T(8,128)(2,1)S(1)}, bf16[64,1536]{0,1:T(8,128)(2,1)S(1)}, u32[]{:S(2)}, u32[]{:S(2)}) collective-permute-start(bf16[64,1536]{0,1:T(8,128)(2,1)S(1)} %constant_dynamic-slice_fusion.8), channel_id=1, source_target_pairs={{0,1},{1,0},{2,3},{3,2},{4,5},{5,4},{6,7},{7,6},{8,9},{9,8},{10,11... | collective-permute-start | bytes 589832 | tf_op jit(solution)/shard_map/ppermute | solution.py:509
  101.2 22.5 %copy-start.15 = (bf16[1,1024]{1,0:T(2,128)(2,1)S(1)}, bf16[1,1024]{1,0:T(2,128)(2,1)}, u32[]{:S(2)}) copy-start(bf16[1,1024]{1,0:T(2,128)(2,1)} %param.15) | copy-start | bytes 6148
  101.2 23.6 %copy-start.22 = (bf16[1024]{0:T(1024)(128)(2,1)S(1)}, bf16[1024]{0:T(1024)(128)(2,1)}, u32[]{:S(2)}) copy-start(bf16[1024]{0:T(1024)(128)(2,1)} %param.22) | copy-start | bytes 6148
  101.2 24.2 %copy-start.23 = (bf16[1024]{0:T(1024)(128)(2,1)S(1)}, bf16[1024]{0:T(1024)(128)(2,1)}, u32[]{:S(2)}) copy-start(bf16[1024]{0:T(1024)(128)(2,1)} %param.26) | copy-start | bytes 6148
  101.2 24.8 %copy-start.19 = (bf16[1024]{0:T(1024)(128)(2,1)S(1)}, bf16[1024]{0:T(1024)(128)(2,1)}, u32[]{:S(2)}) copy-start(bf16[1024]{0:T(1024)(128)(2,1)} %param.24) | copy-start | bytes 6148
  124.6 164.5 %all-gather.11.cloned.1.call-start = ((), (), s32[]{:S(2)}) async-start(), calls=%async_computation.5 | async-start | bytes 3342336 | tf_op jit(solution)/shard_map/all_gather | solution.py:593
  126.6 24.4 %collective-permute-start.5 = (bf16[1536,128]{1,0:T(8,128)(2,1)S(1)}, bf16[1536,128]{1,0:T(8,128)(2,1)S(1)}, u32[]{:S(2)}, u32[]{:S(2)}) collective-permute-start(bf16[1536,128]{1,0:T(8,128)(2,1)S(1)} %constant_dynamic-slice_fusion.7), channel_id=1, source_target_pairs={{0,1},{1,0},{2,3},{3,2},{4,5},{5,4},{6,7},{7,6},{8,9},{9,8},{10,11... | collective-permute-start | bytes 1179656 | tf_op jit(solution)/shard_map/ppermute | solution.py:509
  149.2 24.5 %collective-permute-start.4 = (bf16[1536,128]{1,0:T(8,128)(2,1)S(1)}, bf16[1536,128]{1,0:T(8,128)(2,1)S(1)}, u32[]{:S(2)}, u32[]{:S(2)}) collective-permute-start(bf16[1536,128]{1,0:T(8,128)(2,1)S(1)} %constant_dynamic-slice_fusion.6), channel_id=1, source_target_pairs={{0,1},{1,0},{2,3},{3,2},{4,5},{5,4},{6,7},{7,6},{8,9},{9,8},{10,11... | collective-permute-start | bytes 1179656 | tf_op jit(solution)/shard_map/ppermute | solution.py:509
  151.0 21.3 %copy-start.27 = (bf16[1536,128]{1,0:T(8,128)(2,1)}, bf16[1536,128]{1,0:T(8,128)(2,1)S(1)}, u32[]{:S(2)}) copy-start(bf16[1536,128]{1,0:T(8,128)(2,1)S(1)} %collective-permute-done.5.refs_20_) | copy-start | bytes 1179652
  173.4 24.5 %collective-permute-start.6 = (bf16[1536,128]{1,0:T(8,128)(2,1)S(1)}, bf16[1536,128]{1,0:T(8,128)(2,1)S(1)}, u32[]{:S(2)}, u32[]{:S(2)}) collective-permute-start(bf16[1536,128]{1,0:T(8,128)(2,1)S(1)} %constant_dynamic-slice_fusion.5), channel_id=1, source_target_pairs={{0,1},{1,0},{2,3},{3,2},{4,5},{5,4},{6,7},{7,6},{8,9},{9,8},{10,11... | collective-permute-start | bytes 1179656 | tf_op jit(solution)/shard_map/ppermute | solution.py:509
  173.8 21.3 %copy-start.28 = (bf16[1536,128]{1,0:T(8,128)(2,1)}, bf16[1536,128]{1,0:T(8,128)(2,1)S(1)}, u32[]{:S(2)}) copy-start(bf16[1536,128]{1,0:T(8,128)(2,1)S(1)} %collective-permute-done.4.refs_21_) | copy-start | bytes 1179652
  196.1 11.7 %collective-permute-start.7 = (bf16[1536,128]{1,0:T(8,128)(2,1)S(1)}, bf16[1536,128]{1,0:T(8,128)(2,1)S(1)}, u32[]{:S(2)}, u32[]{:S(2)}) collective-permute-start(bf16[1536,128]{1,0:T(8,128)(2,1)S(1)} %constant_dynamic-slice_fusion.4), channel_id=1, source_target_pairs={{0,1},{1,0},{2,3},{3,2},{4,5},{5,4},{6,7},{7,6},{8,9},{9,8},{10,11... | collective-permute-start | bytes 1179656 | tf_op jit(solution)/shard_map/ppermute | solution.py:509
  197.9 9.9 %copy-start.29 = (bf16[1536,128]{1,0:T(8,128)(2,1)}, bf16[1536,128]{1,0:T(8,128)(2,1)S(1)}, u32[]{:S(2)}) copy-start(bf16[1536,128]{1,0:T(8,128)(2,1)S(1)} %collective-permute-done.6.refs_22_) | copy-start | bytes 1179652
  202.4 258.8 %reduce-scatter.3.cloned.1.call-start = ((), (), s32[]{:S(2)}) async-start(), calls=%async_computation.2 | async-start | bytes 11141120 | tf_op jit(solution)/shard_map/reduce_scatter | solution.py:630
  207.8 0.8 copy-start.30
  261.5 11.8 %copy-start.32 = (bf16[1536,1024]{1,0:T(8,128)(2,1)S(1)}, bf16[1536,1024]{1,0:T(8,128)(2,1)}, u32[]{:S(2)}) copy-start(bf16[1536,1024]{1,0:T(8,128)(2,1)} %get-tuple-element.170) | copy-start | bytes 9437188
  271.5 3.6 copy-start.31
  295.4 2.0 copy-start.1
  295.6 3.3 copy-start.2
  300.3 2.6 copy-start
  304.4 1.0 copy-start.26
  304.5 5.2 copy-start.11
  304.5 5.3 copy-start.10
  304.5 263.0 %all-gather.13.cloned.1.call-start = ((), (), s32[]{:S(2)}) async-start(), calls=%async_computation.6 | async-start | bytes 5570560 | tf_op jit(solution)/shard_map/all_gather | solution.py:658
  305.4 7.8 %collective-permute-start.8 = (bf16[1536,128]{1,0:T(8,128)(2,1)S(1)}, bf16[1536,128]{1,0:T(8,128)(2,1)S(1)}, u32[]{:S(2)}, u32[]{:S(2)}) collective-permute-start(bf16[1536,128]{1,0:T(8,128)(2,1)S(1)} %copy-done.26), channel_id=1, source_target_pairs={{0,1},{1,0},{2,3},{3,2},{4,5},{5,4},{6,7},{7,6},{8,9},{9,8},{10,11... | collective-permute-start | bytes 1179656 | tf_op jit(solution)/shard_map/ppermute | solution.py:509
  306.9 50.8 %collective-permute-start.9 = (bf16[1536,128]{1,0:T(8,128)(2,1)}, bf16[1536,128]{1,0:T(8,128)(2,1)S(1)}, u32[]{:S(2)}, u32[]{:S(2)}) collective-permute-start(bf16[1536,128]{1,0:T(8,128)(2,1)} %get-tuple-element.156), channel_id=1, source_target_pairs={{0,1},{1,0},{2,3},{3,2},{4,5},{5,4},{6,7},{7,6},{8,9},{9,8},{10,11... | collective-permute-start | bytes 1179656 | tf_op jit(solution)/shard_map/ppermute | solution.py:509
  307.5 50.3 %collective-permute-start.10 = (bf16[1536,128]{1,0:T(8,128)(2,1)}, bf16[1536,128]{1,0:T(8,128)(2,1)S(1)}, u32[]{:S(2)}, u32[]{:S(2)}) collective-permute-start(bf16[1536,128]{1,0:T(8,128)(2,1)} %get-tuple-element.163), channel_id=1, source_target_pairs={{0,1},{1,0},{2,3},{3,2},{4,5},{5,4},{6,7},{7,6},{8,9},{9,8},{10,11... | collective-permute-start | bytes 1179656 | tf_op jit(solution)/shard_map/ppermute | solution.py:509
  308.9 92.6 %collective-permute-start.11 = (bf16[1536,128]{1,0:T(8,128)(2,1)}, bf16[1536,128]{1,0:T(8,128)(2,1)S(1)}, u32[]{:S(2)}, u32[]{:S(2)}) collective-permute-start(bf16[1536,128]{1,0:T(8,128)(2,1)} %get-tuple-element.172), channel_id=1, source_target_pairs={{0,1},{1,0},{2,3},{3,2},{4,5},{5,4},{6,7},{7,6},{8,9},{9,8},{10,11... | collective-permute-start | bytes 1179656 | tf_op jit(solution)/shard_map/ppermute | solution.py:509
  313.3 0.9 copy-start.6
  347.0 45.6 %collective-permute-start.12 = (bf16[3,1536,128]{2,1,0:T(8,128)(2,1)S(1)}, bf16[3,1536,128]{2,1,0:T(8,128)(2,1)}, u32[]{:S(2)}, u32[]{:S(2)}) collective-permute-start(bf16[3,1536,128]{2,1,0:T(8,128)(2,1)S(1)} %constant_dynamic-slice_fusion.3), channel_id=1, source_target_pairs={{0,1},{1,0},{2,3},{3,2},{4,5},{5,4},{6,7},{7,6},{8,9},{9,8},{10,11... | collective-permute-start | bytes 3538952 | tf_op jit(solution)/shard_map/ppermute | solution.py:509
  357.7 0.7 copy-start.12
  357.8 0.9 copy-start.5
  358.7 32.4 %copy-start.9 = (bf16[1536,128]{1,0:T(8,128)(2,1)S(1)}, bf16[1536,128]{1,0:T(8,128)(2,1)}, u32[]{:S(2)}) copy-start(bf16[1536,128]{1,0:T(8,128)(2,1)} %get-tuple-element.180) | copy-start | bytes 1179652
  391.1 1.5 copy-start.13
  392.7 8.9 %copy-start.7 = (bf16[3072,128]{1,0:T(8,128)(2,1)}, bf16[3072,128]{1,0:T(8,128)(2,1)S(1)}, u32[]{:S(2)}) copy-start(bf16[3072,128]{1,0:T(8,128)(2,1)S(1)} %constant_dynamic-update-slice_fusion.9.do_ref) | copy-start | bytes 2359300
  401.6 94.8 %collective-permute-start.14 = (bf16[3,1536,128]{2,1,0:T(8,128)(2,1)S(1)}, bf16[3,1536,128]{2,1,0:T(8,128)(2,1)}, u32[]{:S(2)}, u32[]{:S(2)}) collective-permute-start(bf16[3,1536,128]{2,1,0:T(8,128)(2,1)S(1)} %constant_dynamic-slice_fusion.2), channel_id=1, source_target_pairs={{0,1},{1,0},{2,3},{3,2},{4,5},{5,4},{6,7},{7,6},{8,9},{9,8},{10,11... | collective-permute-start | bytes 3538952 | tf_op jit(solution)/shard_map/ppermute | solution.py:509
  462.3 42.8 %collective-permute-start.13 = (bf16[160,1024]{1,0:T(8,128)(2,1)S(1)}, bf16[160,1024]{1,0:T(8,128)(2,1)}, u32[]{:S(2)}, u32[]{:S(2)}) collective-permute-start(bf16[160,1024]{1,0:T(8,128)(2,1)S(1)} %get-tuple-element.235), channel_id=1, source_target_pairs={{0,1},{1,0},{2,3},{3,2},{4,5},{5,4},{6,7},{7,6},{8,9},{9,8},{10,11... | collective-permute-start | bytes 983048 | tf_op jit(solution)/shard_map/ppermute | solution.py:509
  496.3 10.8 %copy-start.8 = (bf16[1536,128]{1,0:T(8,128)(2,1)S(1)}, bf16[1536,128]{1,0:T(8,128)(2,1)}, u32[]{:S(2)}) copy-start(bf16[1536,128]{1,0:T(8,128)(2,1)} %get-tuple-element.193) | copy-start | bytes 1179652
  507.0 129.8 %reduce-scatter.5.cloned.1.call-start = ((), (), s32[]{:S(2)}) async-start(), calls=%async_computation.3 | async-start | bytes 3342336 | tf_op jit(solution)/shard_map/reduce_scatter | solution.py:662
  507.3 0.9 copy-start.4
  507.3 34.9 %copy-start.17 = (f32[8,1024]{1,0:T(8,128)S(1)}, f32[8,1024]{1,0:T(8,128)}, u32[]{:S(2)}) copy-start(f32[8,1024]{1,0:T(8,128)} %get-tuple-element.201) | copy-start | bytes 98308
  507.3 33.6 %collective-permute-start.15 = (bf16[3,1536,128]{2,1,0:T(8,128)(2,1)S(1)}, bf16[3,1536,128]{2,1,0:T(8,128)(2,1)}, u32[]{:S(2)}, u32[]{:S(2)}) collective-permute-start(bf16[3,1536,128]{2,1,0:T(8,128)(2,1)S(1)} %constant_dynamic-slice_fusion.1), channel_id=1, source_target_pairs={{0,1},{1,0},{2,3},{3,2},{4,5},{5,4},{6,7},{7,6},{8,9},{9,8},{10,11... | collective-permute-start | bytes 3538952 | tf_op jit(solution)/shard_map/ppermute | solution.py:509
  540.9 30.4 %collective-permute-start.16 = (bf16[3,1536,128]{2,1,0:T(8,128)(2,1)S(1)}, bf16[3,1536,128]{2,1,0:T(8,128)(2,1)}, u32[]{:S(2)}, u32[]{:S(2)}) collective-permute-start(bf16[3,1536,128]{2,1,0:T(8,128)(2,1)S(1)} %constant_dynamic-slice_fusion), channel_id=1, source_target_pairs={{0,1},{1,0},{2,3},{3,2},{4,5},{5,4},{6,7},{7,6},{8,9},{9,8},{10,11... | collective-permute-start | bytes 3538952 | tf_op jit(solution)/shard_map/ppermute | solution.py:509
  567.5 119.9 %all-gather.15.cloned.1.call-start = ((), (), s32[]{:S(2)}) async-start(), calls=%async_computation.7 | async-start | bytes 4177920 | tf_op jit(solution)/shard_map/all_gather | solution.py:688
  590.9 3.9 collective-permute-start.17
  638.5 8.0 %copy-start.16 = (bf16[1,1024]{1,0:T(2,128)(2,1)S(1)}, bf16[1,1024]{1,0:T(2,128)(2,1)}, u32[]{:S(2)}) copy-start(bf16[1,1024]{1,0:T(2,128)(2,1)} %param.15) | copy-start | bytes 6148
  638.5 8.6 %copy-start.3 = (bf16[2560,1024]{1,0:T(8,128)(2,1)S(1)}, bf16[2560,1024]{1,0:T(8,128)(2,1)}, u32[]{:S(2)}) copy-start(bf16[2560,1024]{1,0:T(8,128)(2,1)} %all-gather.13.cloned.1.call-done) | copy-start | bytes 15728644
  642.8 3.7 collective-permute-start.18
Sparse Core Ops, SparseCore 0:
  124.7 72.1 all-gather.8
  202.5 86.4 all-gather.10
  304.6 156.5 reduce-scatter.2
  507.1 60.3 all-gather.12
  571.7 65.0 reduce-scatter.4
  639.5 47.8 all-gather.14

commit v5 on v4

--- a/solution.py
+++ b/solution.py
@@ -431,22 +431,29 @@
     at += 4 * n
     pieces = refs[at:at + n * groups]
     at += n * groups
-    lo_ref, gm_ref, nf_ref, hid_ref, gp_ref, gbf_ref, gba_ref, att_ref, rows_ref, up_ref = refs[at:at + 10]
-    ga = refs[at + 10:]
+    lo_ref, gm_ref, kept_ref, rows_ref, up_ref = refs[at:at + 5]
+    ga = refs[at + 5:]
     inner, hid = groups * 128, cw[0].shape[0]
+    width = lo_ref.shape[1]
+    wide = n * hid // width
+
+    def keep(slot, start, value):
+        slot, start = slot + start // width, start % width
+        kept_ref[slot, :, start:start + value.shape[1]] = value
+
     gate_a, gate_f, scale_f = gate_a_ref[...], gate_f_ref[...], scale_ref[...]
     branch = ob_ref[...]
     for r in range(n):
         att = jnp.concatenate([p[...] for p in pieces[r * groups:(r + 1) * groups]], axis=1)
-        att_ref[:, r * inner:(r + 1) * inner] = att
+        keep(3, r * inner, att)
         branch = branch + mm(att, ow[r][...], NN)
     middle = x_ref[...].astype(f32) + gate_a * branch
     unit, rstd = normalize(middle)
     nf = (unit * (1.0 + scale_f) + shift_ref[...]).astype(bf16)
-    nf_ref[...] = nf
+    keep(0, 0, nf)
     cot = cot_ref[...].astype(f32)
     gbf = (gate_f * cot).astype(bf16)
-    gbf_ref[...] = gbf
+    keep(1, 0, gbf)
     low = cb_ref[...]
     gn = jnp.zeros(branch.shape, f32)
     @pl.when(pl.program_id(0) == 0)
@@ -460,11 +467,11 @@
         turn_over = jnp.tanh(ROOT * pre * (1.0 + CUBE * square))
         share = 0.5 + 0.5 * turn_over
         hidden = (pre * share).astype(bf16)
-        hid_ref[:, cols] = hidden
+        keep(4, r * hid, hidden)
         low = low + mm(hidden, cw[r][...], NN)
         slope = share + pre * (1.0 - turn_over * turn_over) * (0.5 * ROOT + 1.5 * ROOT * CUBE * square)
         gp = (mm(gbf, cw[r][...], NT) * slope).astype(bf16)
-        gp_ref[:, cols] = gp
+        keep(4 + wide, r * hid, gp)
         up_ref[0:1, cols] += jnp.sum(gp.astype(f32), axis=0, keepdims=True)
         gn = gn + mm(gp, ew[r][...], NT)
     lo_ref[...] = (middle + gate_f * low).astype(bf16)
@@ -472,7 +479,7 @@
     gm = cot + rstd * (u - jnp.mean(u, axis=-1, keepdims=True) - unit * jnp.mean(u * unit, axis=-1, keepdims=True))
     gm_ref[...] = gm
     gba = (gate_a * gm).astype(bf16)
-    gba_ref[...] = gba
+    keep(2, 0, gba)
     for r in range(n):
         back = mm(gba, ow[r][...], NT).astype(bf16)
         for g in range(groups):
@@ -490,6 +497,7 @@
     const = lambda a: pl.BlockSpec(a.shape, lambda i, s: (0, 0))
     shape = lambda cols, kind=jnp.bfloat16: jax.ShapeDtypeStruct((frames, cols), kind)
     sums = lambda cols: pl.BlockSpec((8, cols), lambda i, s: (0, 0))
+    slots = 4 + 2 * (n * hid // width)
     consts = list(vectors) + list(expand_bias) + list(out_w) + list(expand_w) + list(contract_w)
     return pl.pallas_call(
         functools.partial(middle_kernel, n, groups),
@@ -497,13 +505,51 @@
             num_scalar_prefetch=1, grid=(frames // step,),
             in_specs=[row, row] + [const(c) for c in consts]
             + [pl.BlockSpec((step, 128), lambda i, s: (s[0] + i, 0))] * groups + [wide(128)] * len(others),
-            out_specs=[row, row, row, wide(n * hid), wide(n * hid), row, row, wide(n * groups * 128), sums(width), sums(n * hid)] + [wide(128)] * (n * groups)),
-        out_shape=[shape(width), shape(width, jnp.float32), shape(width), shape(n * hid), shape(n * hid), shape(width), shape(width), shape(n * groups * 128),
+            out_specs=[row, row, pl.BlockSpec((slots, step, width), lambda i, s: (0, i, 0)), sums(width), sums(n * hid)] + [wide(128)] * (n * groups)),
+        out_shape=[shape(width), shape(width, jnp.float32), jax.ShapeDtypeStruct((slots, frames, width), jnp.bfloat16),
                    jax.ShapeDtypeStruct((8, width), jnp.float32), jax.ShapeDtypeStruct((8, n * hid), jnp.float32)] + [shape(128)] * (n * groups),
         compiler_params=pltpu.CompilerParams(vmem_limit_bytes=63 << 20),
         cost_estimate=pl.CostEstimate(flops=4 * frames * width * n * (groups * 128 + 2 * hid), bytes_accessed=24 * frames * width, transcendentals=frames * n * hid),
         name="feed_forward",
     )(base * (frames // step), x, cot, *consts, *own, *others)
+
+def stack_kernel(n, l_ref, r_ref, o_ref, acc):
+    j, k = pl.program_id(0), pl.program_id(1)
+    part = mm(l_ref[0], r_ref[0], (((0,), (0,)), ((), ())))
+    @pl.when(k == 0)
+    def _():
+        acc[...] = part
+    @pl.when(k > 0)
+    def _():
+        acc[...] += part
+    done = k == pl.num_programs(1) - 1
+    parts, rows, width = o_ref.shape
+    @pl.when(jnp.logical_and(done, j < 2 * n))
+    def _():
+        o_ref[...] = acc[...].astype(jnp.bfloat16).reshape(parts, rows, width)
+    @pl.when(jnp.logical_and(done, j == 2 * n))
+    def _():
+        tall, high = width // n, rows // n
+        for r in range(n):
+            o_ref[:, r * high:(r + 1) * high, :] = acc[r * tall:(r + 1) * tall, :].astype(jnp.bfloat16).reshape(parts, high, width)
+
+def stacked_grads(kept, n, parts):
+    slots, frames, width = kept.shape
+    step = math.gcd(512, frames)
+    rows = width // parts
+    left = lambda j, k: (jnp.where(j == 2 * n, 3, jnp.where(j % 2 == 0, 0, 4 + j // 2)), k, 0)
+    right = lambda j, k: (jnp.where(j == 2 * n, 2, jnp.where(j % 2 == 0, 4 + n + j // 2, 1)), k, 0)
+    return pl.pallas_call(
+        functools.partial(stack_kernel, n),
+        grid=(2 * n + 1, frames // step),
+        in_specs=[pl.BlockSpec((1, step, width), left), pl.BlockSpec((1, step, width), right)],
+        out_specs=pl.BlockSpec((parts, rows, width), lambda j, k: (0, j, 0)),
+        out_shape=jax.ShapeDtypeStruct((parts, (2 * n + 1) * rows, width), jnp.bfloat16),
+        scratch_shapes=[pltpu.VMEM((width, width), jnp.float32)],
+        compiler_params=pltpu.CompilerParams(vmem_limit_bytes=60 << 20),
+        cost_estimate=pl.CostEstimate(flops=2 * (2 * n + 1) * frames * width * width, bytes_accessed=8 * n * frames * width, transcendentals=0),
+        name="stacked_grads",
+    )(kept, kept)
 
 def relative(axis, size):
     return lambda x, r: x if r % size == 0 else lax.ppermute(x, axis, [(i, (i + r) % size) for i in range(size)])
@@ -552,7 +598,7 @@
     ahead, _, seg, freqs, weight_proj = lax.optimization_barrier((inputs, far_mod, segment_ids[0], freqs, projection_weight))
     elsewhere = [move(ahead, r) for r in range(1, n)]
 
-    shards = [("out", output_weight), ("expand", expand_weight), ("contract", contract_weight)]
+    shards = [("expand", expand_weight), ("contract", contract_weight), ("out", output_weight)]
     heights = {name: w.size // (ndp * width) for name, w in shards}
     cut = [lax.dynamic_slice_in_dim(w, mine * (w.shape[0] // ndp), w.shape[0] // ndp, 0).reshape(heights[name], width) for name, w in shards]
     bias_rows = jnp.pad(expand_bias[None, :], ((0, 15), (0, width - hidden_here)))
@@ -609,27 +655,34 @@
 
     vectors = [v.astype(f32).reshape(1, width) for v in (gate_a, shift_f, scale_f, gate_f, output_bias, contract_bias)]
     far_att = [attended_here[g][r - 1] for r in range(1, n) for g in range(groups)]
-    layer_output, grad_middle, normed_f, hidden, grad_pre, grad_branch_f, grad_branch_a, att_cat, sums, bias_up, *grad_att = feed_forward(
+    layer_output, grad_middle, kept, sums, bias_up, *grad_att = feed_forward(
         place(0), attended, far_att, inputs, cotangent, vectors, [b.astype(f32).reshape(1, hidden_here) for b in expand_bias_all], out_all, expand_all, contract_all)
-    proj_all, att_cat = lax.optimization_barrier((proj_all, att_cat))
+    proj_all, kept = lax.optimization_barrier((proj_all, kept))
     proj_w = [weight_proj] + [proj_all[:, (r - 1) * rows_here:r * rows_here].reshape(width, 3 * inner) for r in range(1, n)]
-    contract_part = jnp.einsum("fh,fd->hd", hidden, grad_branch_f, preferred_element_type=f32)
-    expand_part = jnp.einsum("fd,fh->dh", normed_f, grad_pre, preferred_element_type=f32)
-    output_part = jnp.einsum("fi,fd->id", att_cat, grad_branch_a, preferred_element_type=f32)
     bias_out, bias_down, row_gate_a, row_shift_f, row_scale_f, row_gate_f = (sums[k] for k in range(6))
     bias_up = bias_up[0].reshape(n, hidden_here)
 
-    def slots(part):
-        return part.astype(bf16).reshape(ndp, part.size // (ndp * width), width)
-
-    sent = jnp.concatenate([
-        slots(p) for r in range(n) for p in (
-            output_part[r * inner:(r + 1) * inner],
-            expand_part[:, r * hidden_here:(r + 1) * hidden_here],
-            contract_part[r * hidden_here:(r + 1) * hidden_here])], axis=1)
+    grads_in = [[move(grad_att[r * groups + g], -r) for r in range(n)] for g in range(groups)]
+    if hidden_here == width and n * inner == width and (width // ndp) % (16 * n) == 0:
+        sent = stacked_grads(kept, n, ndp)
+    else:
+        slots = lambda part: part.astype(bf16).reshape(ndp, part.size // (ndp * width), width)
+        side = lambda at, count: jnp.concatenate([kept[at + k] for k in range(count)], axis=1)
+        wide = n * hidden_here // width
+        expand_part = jnp.einsum("fd,fh->dh", kept[0], side(4 + wide, wide), preferred_element_type=f32)
+        contract_part = jnp.einsum("fh,fd->hd", side(4, wide), kept[1], preferred_element_type=f32)
+        output_part = jnp.einsum("fi,fd->id", kept[3], kept[2], preferred_element_type=f32)
+        cols = lambda r: slice(r * hidden_here, (r + 1) * hidden_here)
+        sent = [slots(p) for r in range(n) for p in (expand_part[:, cols(r)], contract_part[cols(r)])]
+        sent = jnp.concatenate(sent + [slots(output_part[r * inner:(r + 1) * inner]) for r in range(n)], axis=1)
+    sent, grads_in[0] = lax.optimization_barrier((sent, grads_in[0]))
     reduced = lax.psum_scatter(sent, "dp", scatter_dimension=0, tiled=False)
-    tall = reduced.shape[0] // n
-    grads_in = [[move(grad_att[r * groups + g], -r) for r in range(n)] for g in range(groups)]
+    tall = heights["expand"] + heights["contract"]
+
+    def share(r):
+        last = n * tall + r * heights["out"]
+        return jnp.concatenate([reduced[r * tall:(r + 1) * tall], reduced[last:last + heights["out"]]], axis=0)
+
     flat, flat_far, wgrads, bias_sums = [], [[] for _ in range(1, n)], None, []
     for g in range(groups):
         whole = jnp.zeros((seq, 128), bf16)
@@ -644,13 +697,13 @@
             if arrived:
                 flat_far[r - 1][-1] = arrived[r - 1]
             flat_far[r - 1].append(move(parts[r - 1], r))
+        if g == max(groups - 2, 0):
+            reduced, back = lax.optimization_barrier((reduced, back))
+            shares = [share(0)] + [move(share(r), -r) for r in range(1, n)]
         wgrads, b = weight_grad(normed_t, back, g, groups, wgrads)
         wgrads, tab = lax.optimization_barrier((wgrads, tab))
         if g + 2 < groups:
             grads_in[g + 2], tab = lax.optimization_barrier((grads_in[g + 2], tab))
-        if g == max(groups - 3, 0):
-            reduced, tab = lax.optimization_barrier((reduced, tab))
-            shares = [reduced[:tall]] + [move(reduced[r * tall:(r + 1) * tall], -r) for r in range(1, n)]
         if g == max(groups - 2, 0):
             shares, tab = lax.optimization_barrier((shares, tab))
             own_grads = sum(p.astype(f32) for p in shares).astype(bf16)

time: 727 us -> 717 us (0.986)
  Pallas kernels: 353 us -> 380 us
  matrix products: 35.5 us -> 11.8 us
  local copies, waits for them, and re-layouts: 63 us -> 47.3 us
    reduce_scatter x1, waiting for transfers between devices: 59.2 us -> 16.8 us  [on_device(): reduced = lax.psum_scatter(sent, 'dp', scatter_dimension=0, tiled=False)]
    pallas_call x0 -> x1, Pallas kernels: none -> 32.1 us  [stacked_grads(): pl.pallas_call(functools.partial(stack_kernel, n), grid=(2 * n + 1, frame...]
    all_gather x1, waiting for transfers between devices: 0.01 us -> 25.6 us  [on_device(): lax.all_gather(jnp.concatenate(moved + [embed_rows], axis=0), 'dp', axis=0)]
    all_gather x1, waiting for transfers between devices: 16.6 us -> 40.8 us  [on_device(): own_grads = lax.all_gather(own_grads, 'dp', axis=0)]
    dot_general x3 -> x0, matrix products: 23.7 us -> none  [the longest x1 10 us: on_device(): jnp.einsum('fd,fh->dh', normed_f, grad_pre, preferred_element_type=f32)]
    unnamed x79 -> x64, local copies, waits for them, and re-layouts: 14.1 us -> 3.6 us
  transfers between devices with their start and end apart: 25 -> 25, of which waited for: 9 -> 9; matrix products, arithmetic and copies ran while one was open for 12% -> 8% of each run, Pallas kernels for 46% -> 50%
where the time goes in v5:
time: 717 us; the launch traced here: 712 us
  Pallas kernels  380 us (53%)
  waiting for transfers between devices  207 us (29%)
  local copies, waits for them, and re-layouts  47.3 us (7%)
  other arithmetic  26.2 us (4%)
  starting transfers between devices  23.3 us (3%)
  between operations  15.2 us (2%)
  matrix products  11.8 us (2%)
    pallas_call x4, Pallas kernels, attend_bwd(): pl.pallas_call(bwd_kernel, grid_spec=pltpu.PrefetchScalarGridSpec(num_sca...  123 us
    pallas_call x4, Pallas kernels, attend_fwd(): pl.pallas_call(fwd_kernel, grid_spec=pltpu.PrefetchScalarGridSpec(num_sca...  84.3 us
    pallas_call x1, Pallas kernels, feed_forward(): pl.pallas_call(functools.partial(middle_kernel, n, groups), grid_spec=plt...  53 us
    ppermute x19, waiting for transfers between devices, relative(): lax.ppermute(x, axis, [(i, (i + r) % size) for i in range(size)])  49.2 us
    reduce_scatter x1, waiting for transfers between devices, on_device(): lax.psum_scatter(wgrads.reshape(ndp, width // ndp, 3 * inner), 'dp', scat...  41.6 us
    all_gather x1, waiting for transfers between devices, on_device(): own_grads = lax.all_gather(own_grads, 'dp', axis=0)  40.8 us
    pallas_call x4, Pallas kernels, weight_grad(): pl.pallas_call(wgrad_kernel, grid=(seq // step,), in_specs=[pl.BlockSpec(...  35.2 us
    all_gather x1, waiting for transfers between devices, on_device(): lax.all_gather(jnp.concatenate([proj_own, terms], axis=0), 'dp', axis=0)  33.1 us
  transfers between devices with their start and end apart: 25, of which 9 were waited for; matrix products, arithmetic and copies ran while one was open for 8% of the time, Pallas kernels for 50%

profile of v5, /device:TPU:0, one launch (start us, length us, event | category | flops | bytes accessed | tf_op | source)
XLA Modules:
  0.0 711.5 jit_solution(6534900005775727382)
XLA Ops:
  7.3 3.7 fusion.24
  11.0 3.0 collective-permute-start
  17.7 1.5 fusion.6
  20.0 1.6 copy.93.sin_ref
  21.7 1.6 copy.92.cos_ref
  23.4 3.2 copy.87
  26.5 2.9 copy.91.w_ref.rest_0_
  32.1 11.7 %project.2 = (bf16[3,3072,512]{2,1,0:T(8,128)(2,1)}, bf16[1024,3072]{1,0:T(8,128)(2,1)}) custom-call(s32[1]{0:T(128)} %bitcast.base, bf16[1536,1024]{1,0:T(8,128)(2,1)} %x_ref.3, f32[1,1024]{1,0:T(1,128)} %get-tuple-element.248.scale_ref, f32[1,1024]{1,0:T(1,128)} %get-tuple-element.247.shift_ref, bf16[1024,1536]{1,0:T(8,128)(2,1)} %copy.91.w_ref.rest_0_, ...), custom_call_target="tpu_custom_call" | custom-call | flops 4831838208 | bytes 11010048 | tf_op jit(solution)/shard_map/project/pallas_call | solution.py:317
  43.8 2.3 select_convert_fusion
  46.1 41.4 %collective-permute-done.1.x_ref = bf16[1536,1024]{1,0:T(8,128)(2,1)} collective-permute-done((bf16[1536,1024]{1,0:T(8,128)(2,1)}, bf16[1536,1024]{1,0:T(8,128)(2,1)}, u32[]{:S(2)}, u32[]{:S(2)}) %collective-permute-start.1) | collective-permute-done | bytes 3145760 | tf_op jit(solution)/shard_map/ppermute | solution.py:555
  87.5 11.7 %project.3 = (bf16[3,3072,512]{2,1,0:T(8,128)(2,1)}, bf16[1024,3072]{1,0:T(8,128)(2,1)}) custom-call(s32[1]{0:T(128)} %bitcast.7.base, bf16[1536,1024]{1,0:T(8,128)(2,1)} %collective-permute-done.1.x_ref, f32[1,1024]{1,0:T(1,128)} %get-tuple-element.248.scale_ref, ...), custom_call_target="tpu_custom_call", output_to_operand_aliasing={{0}: (8, {}), {1}: (9, {})} | custom-call | flops 4831838208 | bytes 11010048 | tf_op jit(solution)/shard_map/project/pallas_call | solution.py:317
  99.5 1.7 collective-permute-start.3
  101.2 21.1 %attend_fwd.4 = (bf16[3072,128]{1,0:T(8,128)(2,1)}, f32[1,8,3072]{2,1,0:T(8,128)}) custom-call(s32[36]{0:T(128)} %pad_add_fusion.tab, bf16[3,3072,512]{2,1,0:T(8,128)(2,1)} %get-tuple-element.121.q_ref.k_ref.v_ref, bf16[3,3072,512]{2,1,0:T(8,128)(2,1)} %get-tuple-element.121.q_ref.k_ref.v_ref, bf16[3,3072,512]{2,1,0:T(8,128)(2,1)} %get-tuple-element.121.q_ref.k_ref.v_ref, ...), custom_call_target="tpu_custom_call" | custom-call | flops 28991029248 | bytes 3145728 | tf_op jit(solution)/shard_map/attend_fwd/pallas_call | solution.py:177
  126.6 20.9 %attend_fwd.5 = (bf16[3072,128]{1,0:T(8,128)(2,1)}, f32[1,8,3072]{2,1,0:T(8,128)}) custom-call(s32[36]{0:T(128)} %pad_add_fusion.tab, bf16[3,3072,512]{2,1,0:T(8,128)(2,1)} %get-tuple-element.121.q_ref.k_ref.v_ref, bf16[3,3072,512]{2,1,0:T(8,128)(2,1)} %get-tuple-element.121.q_ref.k_ref.v_ref, bf16[3,3072,512]{2,1,0:T(8,128)(2,1)} %get-tuple-element.121.q_ref.k_ref.v_ref, ...), custom_call_target="tpu_custom_call" | custom-call | flops 28991029248 | bytes 3145728 | tf_op jit(solution)/shard_map/attend_fwd/pallas_call | solution.py:177
  148.5 1.8 collective-permute-start.4
  150.3 21.0 %attend_fwd.6 = (bf16[3072,128]{1,0:T(8,128)(2,1)}, f32[1,8,3072]{2,1,0:T(8,128)}) custom-call(s32[36]{0:T(128)} %pad_add_fusion.tab, bf16[3,3072,512]{2,1,0:T(8,128)(2,1)} %get-tuple-element.121.q_ref.k_ref.v_ref, bf16[3,3072,512]{2,1,0:T(8,128)(2,1)} %get-tuple-element.121.q_ref.k_ref.v_ref, bf16[3,3072,512]{2,1,0:T(8,128)(2,1)} %get-tuple-element.121.q_ref.k_ref.v_ref, ...), custom_call_target="tpu_custom_call" | custom-call | flops 28991029248 | bytes 3145728 | tf_op jit(solution)/shard_map/attend_fwd/pallas_call | solution.py:177
  171.3 1.0 constant_dynamic-slice_fusion.5
  172.7 25.6 %all-gather.9.cloned.1.call-done = bf16[3072,1024]{1,0:T(8,128)(2,1)} async-done(((bf16[192,1024]{1,0:T(8,128)(2,1)}), bf16[3072,1024]{1,0:T(8,128)(2,1)}) %all-gather.9.cloned.1.call-update) | async-done | bytes 6291472 | tf_op jit(solution)/shard_map/all_gather | solution.py:637
  199.2 21.3 %attend_fwd.7 = (bf16[3072,128]{1,0:T(8,128)(2,1)}, f32[1,8,3072]{2,1,0:T(8,128)}) custom-call(s32[36]{0:T(128)} %pad_add_fusion.tab, bf16[3,3072,512]{2,1,0:T(8,128)(2,1)} %get-tuple-element.121.q_ref.k_ref.v_ref, bf16[3,3072,512]{2,1,0:T(8,128)(2,1)} %get-tuple-element.121.q_ref.k_ref.v_ref, bf16[3,3072,512]{2,1,0:T(8,128)(2,1)} %get-tuple-element.121.q_ref.k_ref.v_ref, ...), custom_call_target="tpu_custom_call" | custom-call | flops 28991029248 | bytes 3145728 | tf_op jit(solution)/shard_map/attend_fwd/pallas_call | solution.py:177
  220.5 1.0 constant_dynamic-slice_fusion.4
  221.5 1.6 collective-permute-start.7
  223.1 1.3 bitcast_convert_fusion.3.refs_9_
  224.4 2.3 slice.138
  226.7 5.0 fusion.35
  232.4 53.0 %feed_forward.1 = (bf16[1536,1024]{1,0:T(8,128)(2,1)}, f32[1536,1024]{1,0:T(8,128)}, bf16[8,1536,1024]{2,1,0:T(8,128)(2,1)}, f32[8,1024]{1,0:T(8,128)}, f32[8,20...) custom-call(s32[1]{0:T(128)} %bitcast.base, ...), custom_call_target="tpu_custom_call" | custom-call | flops 32212254720 | bytes 37748736 | tf_op jit(solution)/shard_map/feed_forward/pallas_call | solution.py:502
  286.0 32.1 %stacked_grads.1 = bf16[16,320,1024]{2,1,0:T(8,128)(2,1)} custom-call(bf16[8,1536,1024]{2,1,0:T(8,128)(2,1)} %get-tuple-element.150.l_ref.r_ref, bf16[8,1536,1024]{2,1,0:T(8,128)(2,1)} %get-tuple-element.150.l_ref.r_ref), custom_call_target="tpu_custom_call" | custom-call | flops 16106127360 | bytes 25165824 | tf_op jit(solution)/shard_map/stacked_grads/pallas_call | solution.py:542
  318.2 1.6 collective-permute-start.10
  320.3 1.5 collective-permute-start.11
  322.0 4.3 collective-permute-done.10
  327.5 30.9 %attend_bwd.4.g_ref.rest_2_ = bf16[3,3072,128]{2,1,0:T(8,128)(2,1)} custom-call(s32[36]{0:T(128)} %pad_add_fusion.tab, bf16[3,3072,512]{2,1,0:T(8,128)(2,1)} %get-tuple-element.121.q_ref.k_ref.v_ref, bf16[3,3072,512]{2,1,0:T(8,128)(2,1)} %get-tuple-element.121.q_ref.k_ref.v_ref, bf16[3,3072,512]{2,1,0:T(8,128)(2,1)} %get-tuple-element.121.q_ref.k_ref.v_ref, ...), custom_call_target="tpu_custom_call" | custom-call | flops 38654705664 | bytes 6291456 | tf_op jit(solution)/shard_map/attend_bwd/pallas_call | solution.py:269
  358.3 1.5 constant_dynamic-slice_fusion.3
  359.8 1.6 collective-permute-start.12
  361.4 8.9 %weight_grad.4 = (bf16[1024,1536]{1,0:T(8,128)(2,1)}, f32[8,384]{1,0:T(8,128)}) custom-call(bf16[1024,3072]{1,0:T(8,128)(2,1)} %get-tuple-element.158.nt_ref, bf16[3,3072,128]{2,1,0:T(8,128)(2,1)} %attend_bwd.4.g_ref.rest_2_), custom_call_target="tpu_custom_call" | custom-call | flops 2415919104 | bytes 8650752 | tf_op jit(solution)/shard_map/weight_grad/pallas_call | solution.py:351
  371.1 30.8 %attend_bwd.5.g_ref.rest_3_ = bf16[3,3072,128]{2,1,0:T(8,128)(2,1)} custom-call(s32[36]{0:T(128)} %pad_add_fusion.tab, bf16[3,3072,512]{2,1,0:T(8,128)(2,1)} %get-tuple-element.121.q_ref.k_ref.v_ref, bf16[3,3072,512]{2,1,0:T(8,128)(2,1)} %get-tuple-element.121.q_ref.k_ref.v_ref, bf16[3,3072,512]{2,1,0:T(8,128)(2,1)} %get-tuple-element.121.q_ref.k_ref.v_ref, ...), custom_call_target="tpu_custom_call" | custom-call | flops 38654705664 | bytes 6291456 | tf_op jit(solution)/shard_map/attend_bwd/pallas_call | solution.py:269
  402.1 1.4 constant_dynamic-slice_fusion.2
  403.6 8.9 %weight_grad.5 = (bf16[1024,1536]{1,0:T(8,128)(2,1)}, f32[8,384]{1,0:T(8,128)}) custom-call(bf16[1024,3072]{1,0:T(8,128)(2,1)} %get-tuple-element.158.nt_ref, bf16[3,3072,128]{2,1,0:T(8,128)(2,1)} %attend_bwd.5.g_ref.rest_3_, bf16[1024,1536]{1,0:T(8,128)(2,1)} %get-tuple-element.170.rest_0_), custom_call_target="tpu_custom_call", output_to_operand_aliasing={{0}: (2, {})} | custom-call | flops 2415919104 | bytes 8650752 | tf_op jit(solution)/shard_map/weight_grad/pallas_call | solution.py:351
  413.2 30.8 %attend_bwd.6.g_ref.rest_4_ = bf16[3,3072,128]{2,1,0:T(8,128)(2,1)} custom-call(s32[36]{0:T(128)} %pad_add_fusion.tab, bf16[3,3072,512]{2,1,0:T(8,128)(2,1)} %get-tuple-element.121.q_ref.k_ref.v_ref, bf16[3,3072,512]{2,1,0:T(8,128)(2,1)} %get-tuple-element.121.q_ref.k_ref.v_ref, bf16[3,3072,512]{2,1,0:T(8,128)(2,1)} %get-tuple-element.121.q_ref.k_ref.v_ref, ...), custom_call_target="tpu_custom_call" | custom-call | flops 38654705664 | bytes 6291456 | tf_op jit(solution)/shard_map/attend_bwd/pallas_call | solution.py:269
  444.0 1.3 constant_dynamic-slice_fusion.1
  445.4 16.8 %reduce-scatter.3.cloned.1.call-done = bf16[1,320,1024]{2,1,0:T(8,128)(2,1)} async-done(((bf16[16,320,1024]{2,1,0:T(8,128)(2,1)}), bf16[1,320,1024]{2,1,0:T(8,128)(2,1)}) %reduce-scatter.3.cloned.1.call-update) | async-done | bytes 655376 | tf_op jit(solution)/shard_map/reduce_scatter | solution.py:679
  463.1 1.1 fusion.37
  464.2 1.5 collective-permute-start.14
  465.7 8.8 %weight_grad.6 = (bf16[1024,1536]{1,0:T(8,128)(2,1)}, f32[8,384]{1,0:T(8,128)}) custom-call(bf16[1024,3072]{1,0:T(8,128)(2,1)} %get-tuple-element.158.nt_ref, bf16[3,3072,128]{2,1,0:T(8,128)(2,1)} %attend_bwd.6.g_ref.rest_4_, bf16[1024,1536]{1,0:T(8,128)(2,1)} %get-tuple-element.182.rest_0_), custom_call_target="tpu_custom_call", output_to_operand_aliasing={{0}: (2, {})} | custom-call | flops 2415919104 | bytes 8650752 | tf_op jit(solution)/shard_map/weight_grad/pallas_call | solution.py:351
  475.7 1.8 collective-permute-start.15
  477.5 30.6 %attend_bwd.7.rest_5_.g_ref = bf16[3,3072,128]{2,1,0:T(8,128)(2,1)} custom-call(s32[36]{0:T(128)} %pad_add_fusion.tab, bf16[3,3072,512]{2,1,0:T(8,128)(2,1)} %get-tuple-element.121.q_ref.k_ref.v_ref, bf16[3,3072,512]{2,1,0:T(8,128)(2,1)} %get-tuple-element.121.q_ref.k_ref.v_ref, bf16[3,3072,512]{2,1,0:T(8,128)(2,1)} %get-tuple-element.121.q_ref.k_ref.v_ref, ...), custom_call_target="tpu_custom_call" | custom-call | flops 38654705664 | bytes 6291456 | tf_op jit(solution)/shard_map/attend_bwd/pallas_call | solution.py:269
  508.1 1.4 constant_dynamic-slice_fusion
  510.3 8.7 %weight_grad.7 = (bf16[1024,1536]{1,0:T(8,128)(2,1)}, f32[8,384]{1,0:T(8,128)}) custom-call(bf16[1024,3072]{1,0:T(8,128)(2,1)} %get-tuple-element.158.nt_ref, bf16[3,3072,128]{2,1,0:T(8,128)(2,1)} %attend_bwd.7.rest_5_.g_ref, bf16[1024,1536]{1,0:T(8,128)(2,1)} %get-tuple-element.201.rest_0_), custom_call_target="tpu_custom_call", output_to_operand_aliasing={{0}: (2, {})} | custom-call | flops 2415919104 | bytes 8650752 | tf_op jit(solution)/shard_map/weight_grad/pallas_call | solution.py:351
  519.0 40.8 %all-gather.13.cloned.1.call-done = bf16[2560,1024]{1,0:T(8,128)(2,1)} async-done(((bf16[160,1024]{1,0:T(8,128)(2,1)}), bf16[2560,1024]{1,0:T(8,128)(2,1)}) %all-gather.13.cloned.1.call-update) | async-done | bytes 5242896 | tf_op jit(solution)/shard_map/all_gather | solution.py:711
  563.6 18.7 %input_grad.1 = (f32[1536,1024]{1,0:T(8,128)}, f32[8,1024]{1,0:T(8,128)}) custom-call(s32[1]{0:T(128)} %bitcast.base, bf16[1536,1024]{1,0:T(8,128)(2,1)} %x_ref.3, f32[1536,1024]{1,0:T(8,128)} %get-tuple-element.144.gm_ref, f32[1,1024]{1,0:T(1,128)} %get-tuple-element.248.scale_ref, bf16[1024,1536]{1,0:T(8,128)(2,1)} %copy.91.w_ref.rest_0_, ...), custom_call_target="tpu_custom_call" | custom-call | flops 9663676416 | bytes 25165824 | tf_op jit(solution)/shard_map/input_grad/pallas_call | solution.py:409
  583.2 1.5 collective-permute-start.17
  584.7 2.3 collective-permute-done.17
  587.4 41.6 %reduce-scatter.5.cloned.1.call-done = bf16[1,64,1536]{2,1,0:T(8,128)(2,1)} async-done(((bf16[16,64,1536]{2,1,0:T(8,128)(2,1)}), bf16[1,64,1536]{2,1,0:T(8,128)(2,1)}) %reduce-scatter.5.cloned.1.call-update) | async-done | bytes 196624 | tf_op jit(solution)/shard_map/reduce_scatter | solution.py:715
  629.0 1.6 fusion.9
  630.7 4.3 multiply_reduce_fusion
  635.0 1.5 collective-permute-start.18
  637.5 1.2 collective-permute-done.18
  639.4 1.6 bitcast_convert_fusion.2
  641.4 2.6 bitcast_convert_fusion
  644.1 2.6 bitcast_convert_fusion.1
  646.7 33.1 %all-gather.15.cloned.1.call-done = bf16[1280,1536]{1,0:T(8,128)(2,1)} async-done(((bf16[80,1536]{1,0:T(8,128)(2,1)}), bf16[1280,1536]{1,0:T(8,128)(2,1)}) %all-gather.15.cloned.1.call-update) | async-done | bytes 3932176 | tf_op jit(solution)/shard_map/all_gather | solution.py:741
  679.8 1.2 slice.179
  681.5 1.2 reshape.335
  682.7 1.1 fusion.31
  685.0 10.6 %unpack.1 = f32[3,1024,512]{2,1,0:T(8,128)} custom-call(bf16[16,80,1536]{2,1,0:T(8,128)(2,1)} %bitcast.85), custom_call_target="tpu_custom_call" | custom-call | tf_op jit(solution)/shard_map/unpack/pallas_call | solution.py:374
  696.2 8.1 %fusion.10 = f32[1024,3072]{1,0:T(8,128)} fusion(f32[16,7680]{1,0:T(8,128)S(1)} %bitcast.97, f32[16,1,1024]{2,1,0:T(1,128)S(1)} %slice_convert_fusion.1), kind=kOutput, calls=%fused_computation.28 | convolution fusion | flops 604061696 | bytes 12845056 | tf_op jit(solution)/shard_map/dot_general | solution.py:753
  (173 shorter events, 31.2 us)
Async XLA Ops:
  7.2 3.8 copy-start.17
  7.2 7.4 %copy-start.15 = (bf16[1024]{0:T(1024)(128)(2,1)S(1)}, bf16[1024]{0:T(1024)(128)(2,1)}, u32[]{:S(2)}) copy-start(bf16[1024]{0:T(1024)(128)(2,1)} %param.24) | copy-start | bytes 6148
  7.2 7.4 %copy-start.18 = (bf16[3,512]{1,0:T(4,128)(2,1)S(1)}, bf16[3,512]{1,0:T(4,128)(2,1)}, u32[]{:S(2)}) copy-start(bf16[3,512]{1,0:T(4,128)(2,1)} %param.20) | copy-start | bytes 9220
  7.2 12.0 %copy-start.11 = (s32[1,3072]{1,0:T(1,128)S(1)}, s32[1,3072]{1,0:T(1,128)}, u32[]{:S(2)}) copy-start(s32[1,3072]{1,0:T(1,128)} %param.16) | copy-start | bytes 36868
  7.2 191.0 %all-gather.9.cloned.1.call-start = ((), (), s32[]{:S(2)}) async-start(), calls=%async_computation.4 | async-start | bytes 6684672 | tf_op jit(solution)/shard_map/all_gather | solution.py:637
  11.0 6.6 collective-permute-start
  17.6 69.9 %collective-permute-start.1 = (bf16[1536,1024]{1,0:T(8,128)(2,1)}, bf16[1536,1024]{1,0:T(8,128)(2,1)}, u32[]{:S(2)}, u32[]{:S(2)}) collective-permute-start(bf16[1536,1024]{1,0:T(8,128)(2,1)} %x_ref.3), channel_id=1, source_target_pairs={{0,1},{1,0},{2,3},{3,2},{4,5},{5,4},{6,7},{7,6},{8,9},{9,8},{10,11... | collective-permute-start | bytes 9437192 | tf_op jit(solution)/shard_map/ppermute | solution.py:555
  32.1 11.8 %copy-start.21 = (pred[128]{0:T(512)(128)(4,1)S(1)}, pred[128]{0:T(512)(128)(4,1)}, u32[]{:S(2)}) copy-start(pred[128]{0:T(512)(128)(4,1)} %broadcast_compare_fusion) | copy-start | bytes 388
  32.1 11.7 %copy-start.22 = (s32[128]{0:T(128)S(1)}, s32[128]{0:T(128)}, u32[]{:S(2)}) copy-start(s32[128]{0:T(128)} %and_select_fusion) | copy-start | bytes 1540
  99.2 24.2 %collective-permute-start.2 = (bf16[176,1024]{1,0:T(8,128)(2,1)S(1)}, bf16[176,1024]{1,0:T(8,128)(2,1)S(1)}, u32[]{:S(2)}, u32[]{:S(2)}) collective-permute-start(bf16[176,1024]{1,0:T(8,128)(2,1)S(1)} %fusion.8), channel_id=1, source_target_pairs={{0,1},{1,0},{2,3},{3,2},{4,5},{5,4},{6,7},{7,6},{8,9},{9,8},{10,11... | collective-permute-start | bytes 1081352 | tf_op jit(solution)/shard_map/ppermute | solution.py:555
  99.5 23.9 %collective-permute-start.3 = (bf16[64,1536]{0,1:T(8,128)(2,1)S(1)}, bf16[64,1536]{0,1:T(8,128)(2,1)S(1)}, u32[]{:S(2)}, u32[]{:S(2)}) collective-permute-start(bf16[64,1536]{0,1:T(8,128)(2,1)S(1)} %constant_dynamic-slice_fusion.8), channel_id=1, source_target_pairs={{0,1},{1,0},{2,3},{3,2},{4,5},{5,4},{6,7},{7,6},{8,9},{9,8},{10,11... | collective-permute-start | bytes 589832 | tf_op jit(solution)/shard_map/ppermute | solution.py:555
  101.2 22.2 %copy-start.12 = (bf16[1,1024]{1,0:T(2,128)(2,1)S(1)}, bf16[1,1024]{1,0:T(2,128)(2,1)}, u32[]{:S(2)}) copy-start(bf16[1,1024]{1,0:T(2,128)(2,1)} %param.15) | copy-start | bytes 6148
  101.2 23.2 %copy-start.19 = (bf16[1024]{0:T(1024)(128)(2,1)S(1)}, bf16[1024]{0:T(1024)(128)(2,1)}, u32[]{:S(2)}) copy-start(bf16[1024]{0:T(1024)(128)(2,1)} %param.22) | copy-start | bytes 6148
  101.2 23.8 %copy-start.20 = (bf16[1024]{0:T(1024)(128)(2,1)S(1)}, bf16[1024]{0:T(1024)(128)(2,1)}, u32[]{:S(2)}) copy-start(bf16[1024]{0:T(1024)(128)(2,1)} %param.26) | copy-start | bytes 6148
  101.2 24.4 %copy-start.16 = (bf16[1024]{0:T(1024)(128)(2,1)S(1)}, bf16[1024]{0:T(1024)(128)(2,1)}, u32[]{:S(2)}) copy-start(bf16[1024]{0:T(1024)(128)(2,1)} %param.24) | copy-start | bytes 6148
  124.2 161.8 %all-gather.11.cloned.1.call-start = ((), (), s32[]{:S(2)}) async-start(), calls=%async_computation.5 | async-start | bytes 3342336 | tf_op jit(solution)/shard_map/all_gather | solution.py:639
  126.3 24.0 %collective-permute-start.5 = (bf16[1536,128]{1,0:T(8,128)(2,1)S(1)}, bf16[1536,128]{1,0:T(8,128)(2,1)S(1)}, u32[]{:S(2)}, u32[]{:S(2)}) collective-permute-start(bf16[1536,128]{1,0:T(8,128)(2,1)S(1)} %constant_dynamic-slice_fusion.7), channel_id=1, source_target_pairs={{0,1},{1,0},{2,3},{3,2},{4,5},{5,4},{6,7},{7,6},{8,9},{9,8},{10,11... | collective-permute-start | bytes 1179656 | tf_op jit(solution)/shard_map/ppermute | solution.py:555
  148.5 24.2 %collective-permute-start.4 = (bf16[1536,128]{1,0:T(8,128)(2,1)S(1)}, bf16[1536,128]{1,0:T(8,128)(2,1)S(1)}, u32[]{:S(2)}, u32[]{:S(2)}) collective-permute-start(bf16[1536,128]{1,0:T(8,128)(2,1)S(1)} %constant_dynamic-slice_fusion.6), channel_id=1, source_target_pairs={{0,1},{1,0},{2,3},{3,2},{4,5},{5,4},{6,7},{7,6},{8,9},{9,8},{10,11... | collective-permute-start | bytes 1179656 | tf_op jit(solution)/shard_map/ppermute | solution.py:555
  150.3 21.0 %copy-start.24 = (bf16[1536,128]{1,0:T(8,128)(2,1)}, bf16[1536,128]{1,0:T(8,128)(2,1)S(1)}, u32[]{:S(2)}) copy-start(bf16[1536,128]{1,0:T(8,128)(2,1)S(1)} %collective-permute-done.5.refs_20_) | copy-start | bytes 1179652
  172.3 50.8 %collective-permute-start.6 = (bf16[1536,128]{1,0:T(8,128)(2,1)S(1)}, bf16[1536,128]{1,0:T(8,128)(2,1)S(1)}, u32[]{:S(2)}, u32[]{:S(2)}) collective-permute-start(bf16[1536,128]{1,0:T(8,128)(2,1)S(1)} %constant_dynamic-slice_fusion.5), channel_id=1, source_target_pairs={{0,1},{1,0},{2,3},{3,2},{4,5},{5,4},{6,7},{7,6},{8,9},{9,8},{10,11... | collective-permute-start | bytes 1179656 | tf_op jit(solution)/shard_map/ppermute | solution.py:555
  172.6 47.8 %copy-start.25 = (bf16[1536,128]{1,0:T(8,128)(2,1)}, bf16[1536,128]{1,0:T(8,128)(2,1)S(1)}, u32[]{:S(2)}) copy-start(bf16[1536,128]{1,0:T(8,128)(2,1)S(1)} %collective-permute-done.4.refs_21_) | copy-start | bytes 1179652
  199.1 263.1 %reduce-scatter.3.cloned.1.call-start = ((), (), s32[]{:S(2)}) async-start(), calls=%async_computation.2 | async-start | bytes 11141120 | tf_op jit(solution)/shard_map/reduce_scatter | solution.py:679
  221.5 10.2 %collective-permute-start.7 = (bf16[1536,128]{1,0:T(8,128)(2,1)S(1)}, bf16[1536,128]{1,0:T(8,128)(2,1)S(1)}, u32[]{:S(2)}, u32[]{:S(2)}) collective-permute-start(bf16[1536,128]{1,0:T(8,128)(2,1)S(1)} %constant_dynamic-slice_fusion.4), channel_id=1, source_target_pairs={{0,1},{1,0},{2,3},{3,2},{4,5},{5,4},{6,7},{7,6},{8,9},{9,8},{10,11... | collective-permute-start | bytes 1179656 | tf_op jit(solution)/shard_map/ppermute | solution.py:555
  223.1 8.6 %copy-start.26 = (bf16[1536,128]{1,0:T(8,128)(2,1)}, bf16[1536,128]{1,0:T(8,128)(2,1)S(1)}, u32[]{:S(2)}) copy-start(bf16[1536,128]{1,0:T(8,128)(2,1)S(1)} %collective-permute-done.6.refs_22_) | copy-start | bytes 1179652
  231.7 0.8 copy-start.27
  285.4 32.7 %collective-permute-start.8 = (bf16[1536,128]{1,0:T(8,128)(2,1)}, bf16[1536,128]{1,0:T(8,128)(2,1)S(1)}, u32[]{:S(2)}, u32[]{:S(2)}) collective-permute-start(bf16[1536,128]{1,0:T(8,128)(2,1)} %get-tuple-element.152), channel_id=1, source_target_pairs={{0,1},{1,0},{2,3},{3,2},{4,5},{5,4},{6,7},{7,6},{8,9},{9,8},{10,11... | collective-permute-start | bytes 1179656 | tf_op jit(solution)/shard_map/ppermute | solution.py:555
  318.1 3.8 copy-start.8
  318.1 8.3 %copy-start.7 = (bf16[1536,128]{1,0:T(8,128)(2,1)S(1)}, bf16[1536,128]{1,0:T(8,128)(2,1)}, u32[]{:S(2)}) copy-start(bf16[1536,128]{1,0:T(8,128)(2,1)} %get-tuple-element.153) | copy-start | bytes 1179652
  318.1 241.7 %all-gather.13.cloned.1.call-start = ((), (), s32[]{:S(2)}) async-start(), calls=%async_computation.6 | async-start | bytes 5570560 | tf_op jit(solution)/shard_map/all_gather | solution.py:711
  318.2 8.1 %collective-permute-start.10 = (bf16[1536,128]{1,0:T(8,128)(2,1)}, bf16[1536,128]{1,0:T(8,128)(2,1)S(1)}, u32[]{:S(2)}, u32[]{:S(2)}) collective-permute-start(bf16[1536,128]{1,0:T(8,128)(2,1)} %get-tuple-element.164), channel_id=1, source_target_pairs={{0,1},{1,0},{2,3},{3,2},{4,5},{5,4},{6,7},{7,6},{8,9},{9,8},{10,11... | collective-permute-start | bytes 1179656 | tf_op jit(solution)/shard_map/ppermute | solution.py:555
  319.8 50.6 %collective-permute-start.9 = (bf16[1536,128]{1,0:T(8,128)(2,1)}, bf16[1536,128]{1,0:T(8,128)(2,1)S(1)}, u32[]{:S(2)}, u32[]{:S(2)}) collective-permute-start(bf16[1536,128]{1,0:T(8,128)(2,1)} %get-tuple-element.157), channel_id=1, source_target_pairs={{0,1},{1,0},{2,3},{3,2},{4,5},{5,4},{6,7},{7,6},{8,9},{9,8},{10,11... | collective-permute-start | bytes 1179656 | tf_op jit(solution)/shard_map/ppermute | solution.py:555
  320.3 92.2 %collective-permute-start.11 = (bf16[1536,128]{1,0:T(8,128)(2,1)}, bf16[1536,128]{1,0:T(8,128)(2,1)S(1)}, u32[]{:S(2)}, u32[]{:S(2)}) collective-permute-start(bf16[1536,128]{1,0:T(8,128)(2,1)} %get-tuple-element.167), channel_id=1, source_target_pairs={{0,1},{1,0},{2,3},{3,2},{4,5},{5,4},{6,7},{7,6},{8,9},{9,8},{10,11... | collective-permute-start | bytes 1179656 | tf_op jit(solution)/shard_map/ppermute | solution.py:555
  326.3 32.0 %copy-start.2 = (bf16[3072,128]{1,0:T(8,128)(2,1)}, bf16[3072,128]{1,0:T(8,128)(2,1)S(1)}, u32[]{:S(2)}) copy-start(bf16[3072,128]{1,0:T(8,128)(2,1)S(1)} %constant_dynamic-update-slice_fusion.4.do_ref) | copy-start | bytes 2359300
  326.6 0.9 copy-start.3
  359.8 43.8 %collective-permute-start.12 = (bf16[3,1536,128]{2,1,0:T(8,128)(2,1)S(1)}, bf16[3,1536,128]{2,1,0:T(8,128)(2,1)}, u32[]{:S(2)}, u32[]{:S(2)}) collective-permute-start(bf16[3,1536,128]{2,1,0:T(8,128)(2,1)S(1)} %constant_dynamic-slice_fusion.3), channel_id=1, source_target_pairs={{0,1},{1,0},{2,3},{3,2},{4,5},{5,4},{6,7},{7,6},{8,9},{9,8},{10,11... | collective-permute-start | bytes 3538952 | tf_op jit(solution)/shard_map/ppermute | solution.py:555
  370.4 0.7 copy-start.9
  371.1 30.9 %copy-start.6 = (bf16[1536,128]{1,0:T(8,128)(2,1)S(1)}, bf16[1536,128]{1,0:T(8,128)(2,1)}, u32[]{:S(2)}) copy-start(bf16[1536,128]{1,0:T(8,128)(2,1)} %get-tuple-element.174) | copy-start | bytes 1179652
  402.0 1.5 copy-start.10
  403.6 8.9 %copy-start.4 = (bf16[3072,128]{1,0:T(8,128)(2,1)}, bf16[3072,128]{1,0:T(8,128)(2,1)S(1)}, u32[]{:S(2)}) copy-start(bf16[3072,128]{1,0:T(8,128)(2,1)S(1)} %constant_dynamic-update-slice_fusion.2.do_ref) | copy-start | bytes 2359300
  412.5 32.9 %collective-permute-start.13 = (bf16[3,1536,128]{2,1,0:T(8,128)(2,1)S(1)}, bf16[3,1536,128]{2,1,0:T(8,128)(2,1)}, u32[]{:S(2)}, u32[]{:S(2)}) collective-permute-start(bf16[3,1536,128]{2,1,0:T(8,128)(2,1)S(1)} %constant_dynamic-slice_fusion.2), channel_id=1, source_target_pairs={{0,1},{1,0},{2,3},{3,2},{4,5},{5,4},{6,7},{7,6},{8,9},{9,8},{10,11... | collective-permute-start | bytes 3538952 | tf_op jit(solution)/shard_map/ppermute | solution.py:555
  464.2 10.3 %collective-permute-start.14 = (bf16[160,1024]{1,0:T(8,128)(2,1)S(1)}, bf16[160,1024]{1,0:T(8,128)(2,1)S(1)}, u32[]{:S(2)}, u32[]{:S(2)}) collective-permute-start(bf16[160,1024]{1,0:T(8,128)(2,1)S(1)} %pad_maximum_fusion.1), channel_id=1, source_target_pairs={{0,1},{1,0},{2,3},{3,2},{4,5},{5,4},{6,7},{7,6},{8,9},{9,8},{10,11... | collective-permute-start | bytes 983048 | tf_op jit(solution)/shard_map/ppermute | solution.py:555
  474.5 1.1 copy-start.5
  475.4 153.6 %reduce-scatter.5.cloned.1.call-start = ((), (), s32[]{:S(2)}) async-start(), calls=%async_computation.3 | async-start | bytes 3342336 | tf_op jit(solution)/shard_map/reduce_scatter | solution.py:715
  475.7 1.8 copy-start.1
  475.7 33.8 %collective-permute-start.15 = (bf16[3,1536,128]{2,1,0:T(8,128)(2,1)S(1)}, bf16[3,1536,128]{2,1,0:T(8,128)(2,1)S(1)}, u32[]{:S(2)}, u32[]{:S(2)}) collective-permute-start(bf16[3,1536,128]{2,1,0:T(8,128)(2,1)S(1)} %constant_dynamic-slice_fusion.1), channel_id=1, source_target_pairs={{0,1},{1,0},{2,3},{3,2},{4,5},{5,4},{6,7},{7,6},{8,9},{9,8},{10,11... | collective-permute-start | bytes 3538952 | tf_op jit(solution)/shard_map/ppermute | solution.py:555
  508.1 2.2 copy-start.14
  509.5 9.5 %copy-start.23 = (bf16[3,1536,128]{2,1,0:T(8,128)(2,1)}, bf16[3,1536,128]{2,1,0:T(8,128)(2,1)S(1)}, u32[]{:S(2)}) copy-start(bf16[3,1536,128]{2,1,0:T(8,128)(2,1)S(1)} %collective-permute-done.15.rest_8_) | copy-start | bytes 3538948
  509.5 54.1 %collective-permute-start.16 = (bf16[3,1536,128]{2,1,0:T(8,128)(2,1)S(1)}, bf16[3,1536,128]{2,1,0:T(8,128)(2,1)}, u32[]{:S(2)}, u32[]{:S(2)}) collective-permute-start(bf16[3,1536,128]{2,1,0:T(8,128)(2,1)S(1)} %constant_dynamic-slice_fusion), channel_id=1, source_target_pairs={{0,1},{1,0},{2,3},{3,2},{4,5},{5,4},{6,7},{7,6},{8,9},{9,8},{10,11... | collective-permute-start | bytes 3538952 | tf_op jit(solution)/shard_map/ppermute | solution.py:555
  559.8 119.9 %all-gather.15.cloned.1.call-start = ((), (), s32[]{:S(2)}) async-start(), calls=%async_computation.7 | async-start | bytes 4177920 | tf_op jit(solution)/shard_map/all_gather | solution.py:741
  583.2 3.9 collective-permute-start.17
  630.7 8.0 %copy-start.13 = (bf16[1,1024]{1,0:T(2,128)(2,1)S(1)}, bf16[1,1024]{1,0:T(2,128)(2,1)}, u32[]{:S(2)}) copy-start(bf16[1,1024]{1,0:T(2,128)(2,1)} %param.15) | copy-start | bytes 6148
  630.7 8.6 %copy-start = (bf16[2560,1024]{1,0:T(8,128)(2,1)S(1)}, bf16[2560,1024]{1,0:T(8,128)(2,1)}, u32[]{:S(2)}) copy-start(bf16[2560,1024]{1,0:T(8,128)(2,1)} %all-gather.13.cloned.1.call-done) | copy-start | bytes 15728644
  635.0 3.7 collective-permute-start.18
Sparse Core Ops, SparseCore 0:
  124.3 73.8 all-gather.8
  200.5 56.4 all-gather.10
  318.3 143.8 reduce-scatter.2
  475.5 84.2 all-gather.12
  564.0 64.9 reduce-scatter.4
  631.7 48.0 all-gather.14

commit v6 on v5

--- a/solution.py
+++ b/solution.py
@@ -192,8 +192,11 @@
     lane = lax.broadcasted_iota(jnp.int32, g.shape, 1) % HDIM
     return g * cos + jnp.where(lane < HDIM // 2, pltpu.roll(u, 96, 1), -pltpu.roll(u, 32, 1))
 
-def bwd_kernel(tab, q_ref, k_ref, v_ref, fq_ref, fk_ref, o_ref, do_ref, lse_ref, cos_ref, sin_ref, g_ref, ka, kb, ks, vs, dk, dv):
+def bwd_kernel(tab, q_ref, k_ref, v_ref, fq_ref, fk_ref, o_ref, do_ref, lse_ref, cos_ref, sin_ref, nt_ref, *rest):
+    g_ref, w_ref, b_ref, ka, kb, ks, vs, dk, dv, nt, acc, sem = rest[-12:]
     seq = q_ref.shape[1]
+    bring = pltpu.make_async_copy(nt_ref, nt, sem)
+    bring.start()
     nq = seq // QB
     lowm = low_half(QB)
     @pl.when(pl.program_id(0) == 0)
@@ -260,24 +263,40 @@
         return 0
     lax.fori_loop(0, nq, finish, 0)
 
-def attend_bwd(tab, qkv, fq, fk, o, do, lse, cos, sin, first=0, pairs=None):
+    bring.wait()
+    acc[...] = jnp.zeros_like(acc)
+    step = math.gcd(1024, seq)
+    def weigh(i, total):
+        rows = pl.ds(pl.multiple_of(i * step, step), step)
+        g = jnp.concatenate([g_ref[0, rows, :], g_ref[1, rows, :], g_ref[2, rows, :]], axis=1)
+        acc[...] += mm(nt[:, rows], g, NN)
+        return total + jnp.sum(g.astype(jnp.float32), axis=0, keepdims=True)
+    total = lax.fori_loop(0, seq // step, weigh, jnp.zeros((1, 384), jnp.float32))
+    b_ref[...] = jnp.broadcast_to(total, b_ref.shape)
+    w_ref[...] = acc[...].astype(jnp.bfloat16)
+
+def attend_bwd(tab, qkv, fq, fk, o, do, lse, cos, sin, nt, index, groups, before=None):
     _, seq, inner = qkv.shape
-    pairs = pairs or inner // 128
-    part = lambda t: pl.BlockSpec((1, seq, 128), lambda p, tab: (t, 0, first + p))
+    width = nt.shape[0]
+    part = lambda t: pl.BlockSpec((1, seq, 128), lambda p, tab: (t, 0, index))
     whole = pl.BlockSpec((seq, 128), lambda p, tab: (0, 0))
-    cols = pl.BlockSpec((seq, 128), lambda p, tab: (0, p))
+    outside = pl.BlockSpec(memory_space=pl.ANY)
+    kept = () if before is None else (before,)
     return pl.pallas_call(
         bwd_kernel,
         grid_spec=pltpu.PrefetchScalarGridSpec(
-            num_scalar_prefetch=1, grid=(pairs,),
-            in_specs=[part(0), part(1), part(2), whole, whole, cols, cols, pl.BlockSpec((1, 8, seq), lambda p, tab: (p, 0, 0)), whole, whole],
-            out_specs=pl.BlockSpec((3, seq, 128), lambda p, tab: (0, 0, p)),
-            scratch_shapes=[pltpu.VMEM((seq + CK, 128), jnp.bfloat16)] * 4 + [pltpu.VMEM((seq + CK, 128), jnp.float32)] * 2),
-        out_shape=jax.ShapeDtypeStruct((3, seq, pairs * 128), jnp.bfloat16),
+            num_scalar_prefetch=1, grid=(1,),
+            in_specs=[part(0), part(1), part(2), whole, whole, whole, whole, pl.BlockSpec((1, 8, seq), lambda p, tab: (0, 0, 0)), whole, whole, outside]
+            + [outside] * len(kept),
+            out_specs=[pl.BlockSpec((3, seq, 128), lambda p, tab: (0, 0, 0)), pl.BlockSpec((width, 384), lambda p, tab: (0, index)), pl.BlockSpec((8, 384), lambda p, tab: (0, 0))],
+            scratch_shapes=[pltpu.VMEM((seq + CK, 128), jnp.bfloat16)] * 4 + [pltpu.VMEM((seq + CK, 128), jnp.float32)] * 2
+            + [pltpu.VMEM((width, seq), jnp.bfloat16), pltpu.VMEM((width, 384), jnp.float32), pltpu.SemaphoreType.DMA]),
+        out_shape=[jax.ShapeDtypeStruct((3, seq, 128), jnp.bfloat16), jax.ShapeDtypeStruct((width, 384 * groups), jnp.bfloat16), jax.ShapeDtypeStruct((8, 384), jnp.float32)],
+        input_output_aliases={12: 1} if kept else {},
         compiler_params=pltpu.CompilerParams(vmem_limit_bytes=60 << 20),
-        cost_estimate=pl.CostEstimate(flops=4096 * pairs * seq * seq, bytes_accessed=16 * pairs * seq * 128, transcendentals=0),
+        cost_estimate=pl.CostEstimate(flops=4096 * seq * seq, bytes_accessed=16 * seq * 128 + 2 * width * seq, transcendentals=0),
         name="attend_bwd",
-    )(tab, qkv, qkv, qkv, fq, fk, o, do, lse, cos, sin)
+    )(tab, qkv, qkv, qkv, fq, fk, o, do, lse, cos, sin, nt, *kept)
 
 def normalize(x):
     mean = jnp.mean(x, axis=-1, keepdims=True)
@@ -327,59 +346,35 @@
         name="project",
     )(base * (frames // step), x, scale, shift, w, b, cos, sin, *(before or ()))
 
-def wgrad_kernel(nt_ref, g_ref, *rest):
-    w_ref, b_ref, acc = rest[-3:]
-    i = pl.program_id(0)
-    g = jnp.concatenate([g_ref[0], g_ref[1], g_ref[2]], axis=1)
-    part = mm(nt_ref[...], g, NN)
-    sums = jnp.broadcast_to(jnp.sum(g.astype(jnp.float32), axis=0, keepdims=True), b_ref.shape)
-    @pl.when(i == 0)
-    def _():
-        acc[...] = part
-        b_ref[...] = sums
-    @pl.when(i > 0)
-    def _():
-        acc[...] += part
-        b_ref[...] += sums
-    @pl.when(i == pl.num_programs(0) - 1)
-    def _():
-        w_ref[...] = acc[...].astype(jnp.bfloat16)
-
-def weight_grad(nt, g, index, groups, before=None):
-    width, seq = nt.shape
-    step = math.gcd(512, seq)
-    return pl.pallas_call(
-        wgrad_kernel,
-        grid=(seq // step,),
-        in_specs=[pl.BlockSpec((width, step), lambda i: (0, i)), pl.BlockSpec((3, step, 128), lambda i: (0, i, 0))]
-        + ([] if before is None else [pl.BlockSpec(memory_space=pl.ANY)]),
-        out_specs=[pl.BlockSpec((width, 384), lambda i: (0, index)), pl.BlockSpec((8, 384), lambda i: (0, 0))],
-        out_shape=[jax.ShapeDtypeStruct((width, 384 * groups), jnp.bfloat16), jax.ShapeDtypeStruct((8, 384), jnp.float32)],
-        scratch_shapes=[pltpu.VMEM((width, 384), jnp.float32)],
-        input_output_aliases={} if before is None else {2: 0},
-        compiler_params=pltpu.CompilerParams(vmem_limit_bytes=60 << 20),
-        cost_estimate=pl.CostEstimate(flops=2 * seq * width * 384, bytes_accessed=2 * seq * (width + 384), transcendentals=0),
-        name="weight_grad",
-    )(nt, g, *(() if before is None else (before,)))
-
-def unpack_kernel(g_ref, o_ref):
-    rows = o_ref.shape[1]
-    for t in range(3):
-        for g in range(o_ref.shape[2] // 128):
-            at = g * 384 + t * 128
-            o_ref[t, :, g * 128:(g + 1) * 128] = g_ref[0, :rows, at:at + 128].astype(jnp.float32)
-
-def unpack(g, rows):
+def cut_up(a, cols):
+    return jnp.concatenate([a[:, c:c + cols] for c in range(0, a.shape[1], cols)], axis=0)
+
+def unpack_kernel(heights, g_ref, *outs):
+    cols = g_ref.shape[2]
+    at = 0
+    for out, high in zip(outs, heights):
+        for c in range(0, out.shape[1], cols):
+            out[:, c:c + cols] = g_ref[0, at:at + high, :].astype(jnp.float32)
+            at += high
+    proj = outs[-1]
+    rows = proj.shape[1]
+    for g in range(proj.shape[2] // 128):
+        for t in range(3):
+            block, lane = divmod(g * 384 + t * 128, cols)
+            start = at + block * rows
+            proj[t, :, g * 128:(g + 1) * 128] = g_ref[0, start:start + rows, lane:lane + 128].astype(jnp.float32)
+
+def unpack(g, heights, width, rows, inner):
     parts, tall, cols = g.shape
     return pl.pallas_call(
-        unpack_kernel,
+        functools.partial(unpack_kernel, heights),
         grid=(parts,),
         in_specs=[pl.BlockSpec((1, tall, cols), lambda i: (i, 0, 0))],
-        out_specs=pl.BlockSpec((3, rows, cols // 3), lambda i: (0, i, 0)),
-        out_shape=jax.ShapeDtypeStruct((3, parts * rows, cols // 3), jnp.float32),
+        out_specs=[pl.BlockSpec((None, h, width), lambda i: (i, 0, 0)) for h in heights] + [pl.BlockSpec((3, rows, inner), lambda i: (0, i, 0))],
+        out_shape=[jax.ShapeDtypeStruct((parts, h, width), jnp.float32) for h in heights] + [jax.ShapeDtypeStruct((3, parts * rows, inner), jnp.float32)],
         compiler_params=pltpu.CompilerParams(vmem_limit_bytes=60 << 20),
         name="unpack",
-    )(g).transpose(1, 0, 2)
+    )(g)
 
 def side_by_side(pieces):
     return jnp.concatenate([p[t] for t in range(3) for p in pieces], axis=1)
@@ -630,16 +625,14 @@
         attended.append(o)
         log_mass.append(lse)
         halves = [lax.dynamic_slice_in_dim(o, source[r] * frames_here, frames_here, 0) for r in range(1, n)]
-        halves, tab = lax.optimization_barrier((halves, tab))
+        halves, tab, attended_here[-1:] = lax.optimization_barrier((halves, tab, attended_here[-1:]))
         attended_here.append([move(halves[r - 1], r) for r in range(1, n)])
         if g == 0:
             moved, moved_proj, tab = lax.optimization_barrier((moved, moved_proj, tab))
             packed = lax.all_gather(jnp.concatenate(moved + [embed_rows], axis=0), "dp", axis=0)
-            proj_rows, _ = lax.optimization_barrier((jnp.concatenate(moved_proj, axis=0), packed))
-            proj_all = lax.all_gather(proj_rows, "dp", axis=0)
-        else:
-            attended_here[g - 1], tab = lax.optimization_barrier((attended_here[g - 1], tab))
-    packed, _ = lax.optimization_barrier((packed, log_mass[-1]))
+    packed, attended_here[:-1], _ = lax.optimization_barrier((packed, attended_here[:-1], log_mass[-1]))
+    proj_rows, _ = lax.optimization_barrier((jnp.concatenate(moved_proj, axis=0), packed))
+    proj_all = lax.all_gather(proj_rows, "dp", axis=0)
 
     whole_w = {name: [w] for name, w in shards}
     expand_bias_all = [expand_bias]
@@ -688,36 +681,27 @@
         whole = jnp.zeros((seq, 128), bf16)
         for r in range(n):
             whole = lax.dynamic_update_slice_in_dim(whole, grads_in[g][r], source[r] * frames_here, 0)
-        back = attend_bwd(tab, qkv, fq, fk, attended[g], whole, log_mass[g], cosine, sine, g, 1)
+        back, wgrads, b = attend_bwd(tab, qkv, fq, fk, attended[g], whole, log_mass[g], cosine, sine, normed_t, g, groups, wgrads)
         flat.append(back)
         parts = [lax.dynamic_slice_in_dim(back, source[r] * frames_here, frames_here, 1) for r in range(1, n)]
         arrived = [far[-1] for far in flat_far if far]
-        parts, arrived, back = lax.optimization_barrier((parts, arrived, back))
+        if g == 0 and groups > 1:
+            grads_in[1], parts = lax.optimization_barrier((grads_in[1], parts))
+        parts, arrived, wgrads = lax.optimization_barrier((parts, arrived, wgrads))
         for r in range(1, n):
             if arrived:
                 flat_far[r - 1][-1] = arrived[r - 1]
             flat_far[r - 1].append(move(parts[r - 1], r))
-        if g == max(groups - 2, 0):
-            reduced, back = lax.optimization_barrier((reduced, back))
-            shares = [share(0)] + [move(share(r), -r) for r in range(1, n)]
-        wgrads, b = weight_grad(normed_t, back, g, groups, wgrads)
         wgrads, tab = lax.optimization_barrier((wgrads, tab))
         if g + 2 < groups:
             grads_in[g + 2], tab = lax.optimization_barrier((grads_in[g + 2], tab))
         if g == max(groups - 2, 0):
-            shares, tab = lax.optimization_barrier((shares, tab))
-            own_grads = sum(p.astype(f32) for p in shares).astype(bf16)
-            own_grads, tab = lax.optimization_barrier((own_grads, tab))
-            own_grads = lax.all_gather(own_grads, "dp", axis=0)
+            reduced, tab = lax.optimization_barrier((reduced, tab))
+            shares = [share(0)] + [move(share(r), -r) for r in range(1, n)]
         bias_sums.append(b[0].reshape(3, 128))
 
-    wgrads, own_grads = lax.optimization_barrier((wgrads, own_grads))
-    proj_own = lax.psum_scatter(wgrads.reshape(ndp, width // ndp, 3 * inner), "dp", scatter_dimension=0, tiled=False)
-    at, grads = 0, {}
-    for name, w in shards[:3]:
-        grads[name] = own_grads[:, at:at + heights[name]].astype(f32).reshape(w.shape)
-        at += heights[name]
-    grad_output, grad_expand, grad_contract = grads["out"], grads["expand"], grads["contract"]
+    proj_own = lax.psum_scatter(wgrads.reshape(ndp, rows_here, 3 * inner), "dp", scatter_dimension=0, tiled=False)
+    own_grads = sum(p.astype(f32) for p in shares).astype(bf16)
     bias_proj_grad = jnp.stack(bias_sums, axis=1).reshape(3 * inner)
 
     grad_inputs, row_sums = input_grad(place(0), flat, [p for far in flat_far for p in far], inputs, grad_middle, scale_a, proj_w)
@@ -730,17 +714,27 @@
     here = sum(move(for_head(r), -r) for r in range(n))
     own_mods = here[None, 2 * width + hidden_here:]
     small = jnp.concatenate([bias_proj_grad, here])
-    length = -(-small.shape[0] // (3 * inner)) * 3 * inner
+    cols = math.gcd(3 * inner, width)
+    length = -(-small.shape[0] // cols) * cols
     small = jnp.pad(small, (0, length - small.shape[0]))
     terms = []
     for _ in range(3):
         terms.append(lax.reduce_precision(small, 8, 7))
         small = small - terms[-1]
-    terms = jnp.stack(terms).astype(bf16).reshape(-1, 3 * inner)
+    terms = jnp.stack(terms).astype(bf16).reshape(-1, cols)
     terms = jnp.pad(terms, ((0, -terms.shape[0] % 16), (0, 0)))
-    gathered = lax.all_gather(jnp.concatenate([proj_own, terms], axis=0), "dp", axis=0)
-    grad_projection = unpack(gathered, rows_here)
-    table = gathered[:, rows_here:].reshape(ndp, -1)[:, :3 * length].astype(f32).reshape(ndp, 3, length)
+    at, split = 0, []
+    for name, w in shards:
+        split.append(cut_up(own_grads[at:at + heights[name]], cols))
+        at += heights[name]
+    split = jnp.concatenate(split, axis=0)
+    own_part = jnp.concatenate([split, cut_up(proj_own, cols), terms], axis=0)
+    gathered = lax.all_gather(own_part, "dp", axis=0)
+    *grads, grad_projection = unpack(gathered, tuple(heights[name] for name, _ in shards), width, rows_here, inner)
+    grad_expand, grad_contract, grad_output = (v.reshape(w.shape) for v, (_, w) in zip(grads, shards))
+    grad_projection = grad_projection.transpose(1, 0, 2)
+    above = own_part.shape[0] - terms.shape[0]
+    table = gathered[:, above:].reshape(ndp, -1)[:, :3 * length].astype(f32).reshape(ndp, 3, length)
     table = table[:, 0] + (table[:, 1] + table[:, 2])
     totals = jnp.sum(table, axis=0)
     base = 3 * inner

time: 717 us -> 722 us (level)
  Pallas kernels: 380 us -> 435 us
  waiting for transfers between devices: 207 us -> 158 us
  other arithmetic: 26.2 us -> 18.6 us
    pallas_call x4, Pallas kernels: 84.3 us -> 130 us  [attend_fwd(): pl.pallas_call(fwd_kernel, grid_spec=pltpu.PrefetchScalarGridSpec(num_sca...]
    pallas_call x4, Pallas kernels: 123 us -> 163 us  [attend_bwd(): pl.pallas_call(bwd_kernel, grid_spec=pltpu.PrefetchScalarGridSpec(num_sca...]
    pallas_call x5 -> x1, Pallas kernels: 45.8 us -> 14 us  [unpack(): pl.pallas_call(functools.partial(unpack_kernel, heights), grid=(parts,),...]
    all_gather x1, waiting for transfers between devices: 25.6 us -> 0.02 us  [on_device(): lax.all_gather(jnp.concatenate(moved + [embed_rows], axis=0), 'dp', axis=0)]
    reduce_scatter x1, waiting for transfers between devices: 41.6 us -> 22.4 us  [on_device(): lax.psum_scatter(wgrads.reshape(ndp, rows_here, 3 * inner), 'dp', scatter...]
    reduce_scatter x1, waiting for transfers between devices: 16.8 us -> 0.01 us  [on_device(): reduced = lax.psum_scatter(sent, 'dp', scatter_dimension=0, tiled=False)]
    ppermute x19, waiting for transfers between devices: 49.2 us -> 65.3 us  [relative(): lax.ppermute(x, axis, [(i, (i + r) % size) for i in range(size)])]
    all_gather x2 -> x1, waiting for transfers between devices: 73.9 us -> 69.8 us  [on_device(): gathered = lax.all_gather(own_part, 'dp', axis=0)]
  transfers between devices with their start and end apart: 25 -> 24, of which waited for: 9 -> 7; matrix products, arithmetic and copies ran while one was open for 8% -> 8% of each run, Pallas kernels for 50% -> 58%
where the time goes in v6:
time: 722 us; the launch traced here: 710 us
  Pallas kernels  435 us (60%)
  waiting for transfers between devices  158 us (22%)
  local copies, waits for them, and re-layouts  52.2 us (7%)
  starting transfers between devices  19.5 us (3%)
  other arithmetic  18.6 us (3%)
  between operations  15.2 us (2%)
  matrix products  11.8 us (2%)
    pallas_call x4, Pallas kernels, attend_bwd(): pl.pallas_call(bwd_kernel, grid_spec=pltpu.PrefetchScalarGridSpec(num_sca...  163 us
    pallas_call x4, Pallas kernels, attend_fwd(): pl.pallas_call(fwd_kernel, grid_spec=pltpu.PrefetchScalarGridSpec(num_sca...  130 us
    all_gather x1, waiting for transfers between devices, on_device(): gathered = lax.all_gather(own_part, 'dp', axis=0)  69.8 us
    ppermute x19, waiting for transfers between devices, relative(): lax.ppermute(x, axis, [(i, (i + r) % size) for i in range(size)])  65.3 us
    pallas_call x1, Pallas kernels, feed_forward(): pl.pallas_call(functools.partial(middle_kernel, n, groups), grid_spec=plt...  53 us
    pallas_call x1, Pallas kernels, stacked_grads(): pl.pallas_call(functools.partial(stack_kernel, n), grid=(2 * n + 1, frame...  32.1 us
    pallas_call x2, Pallas kernels, project(): pl.pallas_call(qkv_kernel, grid_spec=pltpu.PrefetchScalarGridSpec(num_sca...  23.4 us
    reduce_scatter x1, waiting for transfers between devices, on_device(): lax.psum_scatter(wgrads.reshape(ndp, rows_here, 3 * inner), 'dp', scatter...  22.4 us
  transfers between devices with their start and end apart: 24, of which 7 were waited for; matrix products, arithmetic and copies ran while one was open for 8% of the time, Pallas kernels for 58%

profile of v6, /device:TPU:0, one launch (start us, length us, event | category | flops | bytes accessed | tf_op | source)
XLA Modules:
  0.0 709.9 jit_solution(13849801768008551495)
XLA Ops:
  7.3 3.7 fusion.22
  11.0 3.0 collective-permute-start
  14.7 0.9 constant_dynamic-slice_fusion.9
  15.5 1.0 constant_dynamic-slice_fusion.10
  17.7 1.5 fusion.5
  20.0 1.6 copy.93.sin_ref
  21.7 1.6 copy.92.cos_ref
  23.4 3.2 copy.87
  26.5 2.9 copy.91.w_ref.rest_0_
  29.5 0.9 slice_reduce_fusion.1
  32.2 11.7 %project.2 = (bf16[3,3072,512]{2,1,0:T(8,128)(2,1)}, bf16[1024,3072]{1,0:T(8,128)(2,1)}) custom-call(s32[1]{0:T(128)} %bitcast.base, bf16[1536,1024]{1,0:T(8,128)(2,1)} %x_ref.3, f32[1,1024]{1,0:T(1,128)} %get-tuple-element.254.scale_ref, f32[1,1024]{1,0:T(1,128)} %get-tuple-element.253.shift_ref, bf16[1024,1536]{1,0:T(8,128)(2,1)} %copy.91.w_ref.rest_0_, ...), custom_call_target="tpu_custom_call" | custom-call | flops 4831838208 | bytes 11010048 | tf_op jit(solution)/shard_map/project/pallas_call | solution.py:336
  43.9 2.3 select_convert_fusion
  46.2 41.4 %collective-permute-done.1.x_ref = bf16[1536,1024]{1,0:T(8,128)(2,1)} collective-permute-done((bf16[1536,1024]{1,0:T(8,128)(2,1)}, bf16[1536,1024]{1,0:T(8,128)(2,1)}, u32[]{:S(2)}, u32[]{:S(2)}) %collective-permute-start.1) | collective-permute-done | bytes 3145760 | tf_op jit(solution)/shard_map/ppermute | solution.py:550
  87.5 11.7 %project.3 = (bf16[3,3072,512]{2,1,0:T(8,128)(2,1)}, bf16[1024,3072]{1,0:T(8,128)(2,1)}) custom-call(s32[1]{0:T(128)} %bitcast.7.base, bf16[1536,1024]{1,0:T(8,128)(2,1)} %collective-permute-done.1.x_ref, f32[1,1024]{1,0:T(1,128)} %get-tuple-element.254.scale_ref, ...), custom_call_target="tpu_custom_call", output_to_operand_aliasing={{0}: (8, {}), {1}: (9, {})} | custom-call | flops 4831838208 | bytes 11010048 | tf_op jit(solution)/shard_map/project/pallas_call | solution.py:336
  99.5 1.7 collective-permute-start.3
  101.2 32.7 %attend_fwd.4 = (bf16[3072,128]{1,0:T(8,128)(2,1)}, f32[1,8,3072]{2,1,0:T(8,128)}) custom-call(s32[36]{0:T(128)} %pad_add_fusion.tab, bf16[3,3072,512]{2,1,0:T(8,128)(2,1)} %get-tuple-element.125.q_ref.k_ref.v_ref, bf16[3,3072,512]{2,1,0:T(8,128)(2,1)} %get-tuple-element.125.q_ref.k_ref.v_ref, bf16[3,3072,512]{2,1,0:T(8,128)(2,1)} %get-tuple-element.125.q_ref.k_ref.v_ref, ...), custom_call_target="tpu_custom_call" | custom-call | flops 28991029248 | bytes 3145728 | tf_op jit(solution)/shard_map/attend_fwd/pallas_call | solution.py:177
  133.9 1.0 constant_dynamic-slice_fusion.7
  136.1 32.5 %attend_fwd.5 = (bf16[3072,128]{1,0:T(8,128)(2,1)}, f32[1,8,3072]{2,1,0:T(8,128)}) custom-call(s32[36]{0:T(128)} %pad_add_fusion.tab, bf16[3,3072,512]{2,1,0:T(8,128)(2,1)} %get-tuple-element.125.q_ref.k_ref.v_ref, bf16[3,3072,512]{2,1,0:T(8,128)(2,1)} %get-tuple-element.125.q_ref.k_ref.v_ref, bf16[3,3072,512]{2,1,0:T(8,128)(2,1)} %get-tuple-element.125.q_ref.k_ref.v_ref, ...), custom_call_target="tpu_custom_call" | custom-call | flops 28991029248 | bytes 3145728 | tf_op jit(solution)/shard_map/attend_fwd/pallas_call | solution.py:177
  168.7 1.0 constant_dynamic-slice_fusion.6
  169.8 32.6 %attend_fwd.6 = (bf16[3072,128]{1,0:T(8,128)(2,1)}, f32[1,8,3072]{2,1,0:T(8,128)}) custom-call(s32[36]{0:T(128)} %pad_add_fusion.tab, bf16[3,3072,512]{2,1,0:T(8,128)(2,1)} %get-tuple-element.125.q_ref.k_ref.v_ref, bf16[3,3072,512]{2,1,0:T(8,128)(2,1)} %get-tuple-element.125.q_ref.k_ref.v_ref, bf16[3,3072,512]{2,1,0:T(8,128)(2,1)} %get-tuple-element.125.q_ref.k_ref.v_ref, ...), custom_call_target="tpu_custom_call" | custom-call | flops 28991029248 | bytes 3145728 | tf_op jit(solution)/shard_map/attend_fwd/pallas_call | solution.py:177
  202.4 1.0 constant_dynamic-slice_fusion.5
  203.6 32.6 %attend_fwd.7 = (bf16[3072,128]{1,0:T(8,128)(2,1)}, f32[1,8,3072]{2,1,0:T(8,128)}) custom-call(s32[36]{0:T(128)} %pad_add_fusion.tab, bf16[3,3072,512]{2,1,0:T(8,128)(2,1)} %get-tuple-element.125.q_ref.k_ref.v_ref, bf16[3,3072,512]{2,1,0:T(8,128)(2,1)} %get-tuple-element.125.q_ref.k_ref.v_ref, bf16[3,3072,512]{2,1,0:T(8,128)(2,1)} %get-tuple-element.125.q_ref.k_ref.v_ref, ...), custom_call_target="tpu_custom_call" | custom-call | flops 28991029248 | bytes 3145728 | tf_op jit(solution)/shard_map/attend_fwd/pallas_call | solution.py:177
  236.2 1.0 constant_dynamic-slice_fusion.4
  240.4 1.3 bitcast_convert_fusion.refs_9_
  241.7 2.3 slice.165
  244.0 5.0 fusion.33
  250.2 53.0 %feed_forward.1 = (bf16[1536,1024]{1,0:T(8,128)(2,1)}, f32[1536,1024]{1,0:T(8,128)}, bf16[8,1536,1024]{2,1,0:T(8,128)(2,1)}, f32[8,1024]{1,0:T(8,128)}, f32[8,20...) custom-call(s32[1]{0:T(128)} %bitcast.base, ...), custom_call_target="tpu_custom_call" | custom-call | flops 32212254720 | bytes 37748736 | tf_op jit(solution)/shard_map/feed_forward/pallas_call | solution.py:497
  303.2 1.6 collective-permute-start.8
  304.9 32.1 %stacked_grads.1 = bf16[16,320,1024]{2,1,0:T(8,128)(2,1)} custom-call(bf16[8,1536,1024]{2,1,0:T(8,128)(2,1)} %get-tuple-element.154.l_ref.r_ref, bf16[8,1536,1024]{2,1,0:T(8,128)(2,1)} %get-tuple-element.154.l_ref.r_ref), custom_call_target="tpu_custom_call" | custom-call | flops 16106127360 | bytes 25165824 | tf_op jit(solution)/shard_map/stacked_grads/pallas_call | solution.py:537
  338.4 1.6 collective-permute-start.10
  340.5 1.4 fusion.36
  342.7 0.9 copy-done.1
  343.6 41.5 %attend_bwd.4 = (bf16[3,3072,128]{2,1,0:T(8,128)(2,1)}, bf16[1024,1536]{1,0:T(8,128)(2,1)}, f32[8,384]{1,0:T(8,128)}) custom-call(s32[36]{0:T(128)} %pad_add_fusion.tab, bf16[3,3072,512]{2,1,0:T(8,128)(2,1)} %get-tuple-element.125.q_ref.k_ref.v_ref, bf16[3,3072,512]{2,1,0:T(8,128)(2,1)} %get-tuple-element.125.q_ref.k_ref.v_ref, ...), custom_call_target="tpu_custom_call" | custom-call | flops 38654705664 | bytes 12582912 | tf_op jit(solution)/shard_map/attend_bwd/pallas_call | solution.py:285
  385.1 1.4 constant_dynamic-slice_fusion.3
  386.5 1.6 collective-permute-start.12
  388.4 0.9 copy-done.2
  389.3 40.6 %attend_bwd.5 = (bf16[3,3072,128]{2,1,0:T(8,128)(2,1)}, bf16[1024,1536]{1,0:T(8,128)(2,1)}, f32[8,384]{1,0:T(8,128)}) custom-call(s32[36]{0:T(128)} %pad_add_fusion.tab, bf16[3,3072,512]{2,1,0:T(8,128)(2,1)} %get-tuple-element.125.q_ref.k_ref.v_ref, bf16[3,3072,512]{2,1,0:T(8,128)(2,1)} %get-tuple-element.125.q_ref.k_ref.v_ref, ...), custom_call_target="tpu_custom_call", output_to_operand_aliasing={{1}: (12, {})} | custom-call | flops 38654705664 | bytes 12582912 | tf_op jit(solution)/shard_map/attend_bwd/pallas_call | solution.py:285
  430.1 1.2 slice_reduce_fusion.5
  432.6 40.7 %attend_bwd.6 = (bf16[3,3072,128]{2,1,0:T(8,128)(2,1)}, bf16[1024,1536]{1,0:T(8,128)(2,1)}, f32[8,384]{1,0:T(8,128)}) custom-call(s32[36]{0:T(128)} %pad_add_fusion.tab, bf16[3,3072,512]{2,1,0:T(8,128)(2,1)} %get-tuple-element.125.q_ref.k_ref.v_ref, bf16[3,3072,512]{2,1,0:T(8,128)(2,1)} %get-tuple-element.125.q_ref.k_ref.v_ref, ...), custom_call_target="tpu_custom_call", output_to_operand_aliasing={{1}: (12, {})} | custom-call | flops 38654705664 | bytes 12582912 | tf_op jit(solution)/shard_map/attend_bwd/pallas_call | solution.py:285
  473.4 0.9 slice_reduce_fusion.3
  474.4 1.1 constant_dynamic-update-slice_fusion.1.do_ref
  475.6 1.6 collective-permute-start.14
  477.3 0.9 fusion.35
  478.2 1.1 fusion.34
  480.4 40.4 %attend_bwd.7 = (bf16[3,3072,128]{2,1,0:T(8,128)(2,1)}, bf16[1024,1536]{1,0:T(8,128)(2,1)}, f32[8,384]{1,0:T(8,128)}) custom-call(s32[36]{0:T(128)} %pad_add_fusion.tab, bf16[3,3072,512]{2,1,0:T(8,128)(2,1)} %get-tuple-element.125.q_ref.k_ref.v_ref, bf16[3,3072,512]{2,1,0:T(8,128)(2,1)} %get-tuple-element.125.q_ref.k_ref.v_ref, ...), custom_call_target="tpu_custom_call", output_to_operand_aliasing={{1}: (12, {})} | custom-call | flops 38654705664 | bytes 12582912 | tf_op jit(solution)/shard_map/attend_bwd/pallas_call | solution.py:285
  521.5 1.4 constant_dynamic-slice_fusion
  523.0 1.6 collective-permute-start.15
  524.6 1.1 add_convert_fusion
  525.8 20.1 %collective-permute-done.15.rest_9_ = bf16[3,1536,128]{2,1,0:T(8,128)(2,1)S(1)} collective-permute-done((bf16[3,1536,128]{2,1,0:T(8,128)(2,1)S(1)}, bf16[3,1536,128]{2,1,0:T(8,128)(2,1)S(1)}, u32[]{:S(2)}, u32[]{:S(2)}) %collective-permute-start.15) | collective-permute-done | bytes 1179680 | tf_op jit(solution)/shard_map/ppermute | solution.py:550
  545.8 1.0 copy-done.32
  546.9 18.9 %input_grad.1 = (f32[1536,1024]{1,0:T(8,128)}, f32[8,1024]{1,0:T(8,128)}) custom-call(s32[1]{0:T(128)} %bitcast.base, bf16[1536,1024]{1,0:T(8,128)(2,1)} %x_ref.3, f32[1536,1024]{1,0:T(8,128)} %get-tuple-element.148.gm_ref, f32[1,1024]{1,0:T(1,128)} %get-tuple-element.254.scale_ref, bf16[1024,1536]{1,0:T(8,128)(2,1)} %copy.91.w_ref.rest_0_, ...), custom_call_target="tpu_custom_call" | custom-call | flops 9663676416 | bytes 25165824 | tf_op jit(solution)/shard_map/input_grad/pallas_call | solution.py:404
  566.8 1.6 collective-permute-start.16
  568.4 2.3 collective-permute-done.16
  571.0 22.4 %reduce-scatter.5.cloned.1.call-done = bf16[1,64,1536]{2,1,0:T(8,128)(2,1)} async-done(((bf16[16,64,1536]{2,1,0:T(8,128)(2,1)}), bf16[1,64,1536]{2,1,0:T(8,128)(2,1)}) %reduce-scatter.5.cloned.1.call-update) | async-done | bytes 196624 | tf_op jit(solution)/shard_map/reduce_scatter | solution.py:703
  596.8 4.1 multiply_reduce_fusion
  601.0 1.5 collective-permute-start.17
  602.5 1.0 slice_convert_fusion.1
  603.5 1.1 collective-permute-done.17
  605.2 69.8 %all-gather.11.cloned.1.call-done = bf16[8960,512]{1,0:T(8,128)(2,1)} async-done(((bf16[560,512]{1,0:T(8,128)(2,1)}), bf16[8960,512]{1,0:T(8,128)(2,1)}) %all-gather.11.cloned.1.call-update) | async-done | bytes 9175056 | tf_op jit(solution)/shard_map/all_gather | solution.py:732
  675.1 1.2 slice.221
  676.8 1.2 reshape.323
  678.0 1.1 fusion.29
  680.3 14.0 %unpack.1 = (f32[16,64,1024]{2,1,0:T(8,128)}, f32[16,64,1024]{2,1,0:T(8,128)}, f32[16,32,1024]{2,1,0:T(8,128)}, f32[3,1024,512]{2,1,0:T(8,128)}) custom-call(bf16[16,560,512]{2,1,0:T(8,128)(2,1)} %bitcast.74), custom_call_target="tpu_custom_call" | custom-call | tf_op jit(solution)/shard_map/unpack/pallas_call | solution.py:369
  694.9 8.1 %fusion.8 = f32[1024,3072]{1,0:T(8,128)} fusion(f32[16,7680]{1,0:T(8,128)S(1)} %bitcast.87, f32[16,1,1024]{2,1,0:T(1,128)S(1)} %slice_convert_fusion.1), kind=kOutput, calls=%fused_computation.21 | convolution fusion | flops 604061696 | bytes 12845056 | tf_op jit(solution)/shard_map/dot_general | solution.py:747
  (191 shorter events, 24.8 us)
Async XLA Ops:
  7.2 3.8 copy-start.26
  7.2 7.4 %copy-start.24 = (bf16[1024]{0:T(1024)(128)(2,1)S(1)}, bf16[1024]{0:T(1024)(128)(2,1)}, u32[]{:S(2)}) copy-start(bf16[1024]{0:T(1024)(128)(2,1)} %param.24) | copy-start | bytes 6148
  7.2 7.4 %copy-start.27 = (bf16[3,512]{1,0:T(4,128)(2,1)S(1)}, bf16[3,512]{1,0:T(4,128)(2,1)}, u32[]{:S(2)}) copy-start(bf16[3,512]{1,0:T(4,128)(2,1)} %param.20) | copy-start | bytes 9220
  7.2 12.0 %copy-start.12 = (s32[1,3072]{1,0:T(1,128)S(1)}, s32[1,3072]{1,0:T(1,128)}, u32[]{:S(2)}) copy-start(s32[1,3072]{1,0:T(1,128)} %param.16) | copy-start | bytes 36868
  7.2 230.0 %all-gather.7.cloned.1.call-start = ((), (), s32[]{:S(2)}) async-start(), calls=%async_computation.4 | async-start | bytes 6684672 | tf_op jit(solution)/shard_map/all_gather | solution.py:632
  11.0 6.6 collective-permute-start
  17.6 69.9 %collective-permute-start.1 = (bf16[1536,1024]{1,0:T(8,128)(2,1)}, bf16[1536,1024]{1,0:T(8,128)(2,1)}, u32[]{:S(2)}, u32[]{:S(2)}) collective-permute-start(bf16[1536,1024]{1,0:T(8,128)(2,1)} %x_ref.3), channel_id=1, source_target_pairs={{0,1},{1,0},{2,3},{3,2},{4,5},{5,4},{6,7},{7,6},{8,9},{9,8},{10,11... | collective-permute-start | bytes 9437192 | tf_op jit(solution)/shard_map/ppermute | solution.py:550
  32.1 11.8 %copy-start.30 = (pred[128]{0:T(512)(128)(4,1)S(1)}, pred[128]{0:T(512)(128)(4,1)}, u32[]{:S(2)}) copy-start(pred[128]{0:T(512)(128)(4,1)} %broadcast_compare_fusion) | copy-start | bytes 388
  32.1 11.7 %copy-start.31 = (s32[128]{0:T(128)S(1)}, s32[128]{0:T(128)}, u32[]{:S(2)}) copy-start(s32[128]{0:T(128)} %and_select_fusion) | copy-start | bytes 1540
  99.2 35.8 %collective-permute-start.2 = (bf16[176,1024]{1,0:T(8,128)(2,1)S(1)}, bf16[176,1024]{1,0:T(8,128)(2,1)S(1)}, u32[]{:S(2)}, u32[]{:S(2)}) collective-permute-start(bf16[176,1024]{1,0:T(8,128)(2,1)S(1)} %fusion.7), channel_id=1, source_target_pairs={{0,1},{1,0},{2,3},{3,2},{4,5},{5,4},{6,7},{7,6},{8,9},{9,8},{10,11... | collective-permute-start | bytes 1081352 | tf_op jit(solution)/shard_map/ppermute | solution.py:550
  99.5 35.5 %collective-permute-start.3 = (bf16[64,1536]{0,1:T(8,128)(2,1)S(1)}, bf16[64,1536]{0,1:T(8,128)(2,1)S(1)}, u32[]{:S(2)}, u32[]{:S(2)}) collective-permute-start(bf16[64,1536]{0,1:T(8,128)(2,1)S(1)} %constant_dynamic-slice_fusion.8), channel_id=1, source_target_pairs={{0,1},{1,0},{2,3},{3,2},{4,5},{5,4},{6,7},{7,6},{8,9},{9,8},{10,11... | collective-permute-start | bytes 589832 | tf_op jit(solution)/shard_map/ppermute | solution.py:550
  101.2 33.8 %copy-start.13 = (bf16[1,1024]{1,0:T(2,128)(2,1)S(1)}, bf16[1,1024]{1,0:T(2,128)(2,1)}, u32[]{:S(2)}) copy-start(bf16[1,1024]{1,0:T(2,128)(2,1)} %param.15) | copy-start | bytes 6148
  135.8 169.1 %all-gather.9.cloned.1.call-start = ((), (), s32[]{:S(2)}) async-start(), calls=%async_computation.5 | async-start | bytes 3342336 | tf_op jit(solution)/shard_map/all_gather | solution.py:635
  136.1 33.6 %collective-permute-start.4 = (bf16[1536,128]{1,0:T(8,128)(2,1)S(1)}, bf16[1536,128]{1,0:T(8,128)(2,1)S(1)}, u32[]{:S(2)}, u32[]{:S(2)}) collective-permute-start(bf16[1536,128]{1,0:T(8,128)(2,1)S(1)} %constant_dynamic-slice_fusion.7), channel_id=1, source_target_pairs={{0,1},{1,0},{2,3},{3,2},{4,5},{5,4},{6,7},{7,6},{8,9},{9,8},{10,11... | collective-permute-start | bytes 1179656 | tf_op jit(solution)/shard_map/ppermute | solution.py:550
  169.7 32.7 %copy-start.35 = (bf16[1536,128]{1,0:T(8,128)(2,1)}, bf16[1536,128]{1,0:T(8,128)(2,1)S(1)}, u32[]{:S(2)}) copy-start(bf16[1536,128]{1,0:T(8,128)(2,1)S(1)} %collective-permute-done.4.refs_20_) | copy-start | bytes 1179652
  169.7 33.8 %collective-permute-start.5 = (bf16[1536,128]{1,0:T(8,128)(2,1)S(1)}, bf16[1536,128]{1,0:T(8,128)(2,1)S(1)}, u32[]{:S(2)}, u32[]{:S(2)}) collective-permute-start(bf16[1536,128]{1,0:T(8,128)(2,1)S(1)} %constant_dynamic-slice_fusion.6), channel_id=1, source_target_pairs={{0,1},{1,0},{2,3},{3,2},{4,5},{5,4},{6,7},{7,6},{8,9},{9,8},{10,11... | collective-permute-start | bytes 1179656 | tf_op jit(solution)/shard_map/ppermute | solution.py:550
  203.4 35.1 %copy-start.28 = (bf16[1024]{0:T(1024)(128)(2,1)S(1)}, bf16[1024]{0:T(1024)(128)(2,1)}, u32[]{:S(2)}) copy-start(bf16[1024]{0:T(1024)(128)(2,1)} %param.22) | copy-start | bytes 6148
  203.5 35.7 %copy-start.29 = (bf16[1024]{0:T(1024)(128)(2,1)S(1)}, bf16[1024]{0:T(1024)(128)(2,1)}, u32[]{:S(2)}) copy-start(bf16[1024]{0:T(1024)(128)(2,1)} %param.26) | copy-start | bytes 6148
  203.5 36.3 %copy-start.25 = (bf16[1024]{0:T(1024)(128)(2,1)S(1)}, bf16[1024]{0:T(1024)(128)(2,1)}, u32[]{:S(2)}) copy-start(bf16[1024]{0:T(1024)(128)(2,1)} %param.24) | copy-start | bytes 6148
  203.5 32.7 %copy-start.36 = (bf16[1536,128]{1,0:T(8,128)(2,1)}, bf16[1536,128]{1,0:T(8,128)(2,1)S(1)}, u32[]{:S(2)}) copy-start(bf16[1536,128]{1,0:T(8,128)(2,1)S(1)} %collective-permute-done.5.refs_21_) | copy-start | bytes 1179652
  203.5 33.7 %collective-permute-start.6 = (bf16[1536,128]{1,0:T(8,128)(2,1)S(1)}, bf16[1536,128]{1,0:T(8,128)(2,1)S(1)}, u32[]{:S(2)}, u32[]{:S(2)}) collective-permute-start(bf16[1536,128]{1,0:T(8,128)(2,1)S(1)} %constant_dynamic-slice_fusion.5), channel_id=1, source_target_pairs={{0,1},{1,0},{2,3},{3,2},{4,5},{5,4},{6,7},{7,6},{8,9},{9,8},{10,11... | collective-permute-start | bytes 1179656 | tf_op jit(solution)/shard_map/ppermute | solution.py:550
  237.2 11.8 %copy-start.37 = (bf16[1536,128]{1,0:T(8,128)(2,1)}, bf16[1536,128]{1,0:T(8,128)(2,1)S(1)}, u32[]{:S(2)}) copy-start(bf16[1536,128]{1,0:T(8,128)(2,1)S(1)} %collective-permute-done.6.refs_22_) | copy-start | bytes 1179652
  238.1 239.2 %reduce-scatter.3.cloned.1.call-start = ((), (), s32[]{:S(2)}) async-start(), calls=%async_computation.2 | async-start | bytes 11141120 | tf_op jit(solution)/shard_map/reduce_scatter | solution.py:672
  240.4 9.1 %collective-permute-start.7 = (bf16[1536,128]{1,0:T(8,128)(2,1)S(1)}, bf16[1536,128]{1,0:T(8,128)(2,1)S(1)}, u32[]{:S(2)}, u32[]{:S(2)}) collective-permute-start(bf16[1536,128]{1,0:T(8,128)(2,1)S(1)} %constant_dynamic-slice_fusion.4), channel_id=1, source_target_pairs={{0,1},{1,0},{2,3},{3,2},{4,5},{5,4},{6,7},{7,6},{8,9},{9,8},{10,11... | collective-permute-start | bytes 1179656 | tf_op jit(solution)/shard_map/ppermute | solution.py:550
  249.5 0.7 copy-start.38
  303.2 33.8 %collective-permute-start.8 = (bf16[1536,128]{1,0:T(8,128)(2,1)}, bf16[1536,128]{1,0:T(8,128)(2,1)S(1)}, u32[]{:S(2)}, u32[]{:S(2)}) collective-permute-start(bf16[1536,128]{1,0:T(8,128)(2,1)} %get-tuple-element.156), channel_id=1, source_target_pairs={{0,1},{1,0},{2,3},{3,2},{4,5},{5,4},{6,7},{7,6},{8,9},{9,8},{10,11... | collective-permute-start | bytes 1179656 | tf_op jit(solution)/shard_map/ppermute | solution.py:550
  337.0 1.0 copy-start.33
  337.0 1.5 copy-start.34
  337.0 4.9 copy-start.17
  337.0 5.6 copy-start.11
  337.0 256.4 %reduce-scatter.5.cloned.1.call-start = ((), (), s32[]{:S(2)}) async-start(), calls=%async_computation.3 | async-start | bytes 3342336 | tf_op jit(solution)/shard_map/reduce_scatter | solution.py:703
  338.0 48.5 %collective-permute-start.9 = (bf16[1536,128]{1,0:T(8,128)(2,1)S(1)}, bf16[1536,128]{1,0:T(8,128)(2,1)S(1)}, u32[]{:S(2)}, u32[]{:S(2)}) collective-permute-start(bf16[1536,128]{1,0:T(8,128)(2,1)S(1)} %copy-done.33), channel_id=1, source_target_pairs={{0,1},{1,0},{2,3},{3,2},{4,5},{5,4},{6,7},{7,6},{8,9},{9,8},{10,11... | collective-permute-start | bytes 1179656 | tf_op jit(solution)/shard_map/ppermute | solution.py:550
  338.4 48.1 %collective-permute-start.10 = (bf16[1536,128]{1,0:T(8,128)(2,1)S(1)}, bf16[1536,128]{1,0:T(8,128)(2,1)S(1)}, u32[]{:S(2)}, u32[]{:S(2)}) collective-permute-start(bf16[1536,128]{1,0:T(8,128)(2,1)S(1)} %copy-done.34), channel_id=1, source_target_pairs={{0,1},{1,0},{2,3},{3,2},{4,5},{5,4},{6,7},{7,6},{8,9},{9,8},{10,11... | collective-permute-start | bytes 1179656 | tf_op jit(solution)/shard_map/ppermute | solution.py:550
  340.0 92.1 %collective-permute-start.11 = (bf16[1536,128]{1,0:T(8,128)(2,1)}, bf16[1536,128]{1,0:T(8,128)(2,1)S(1)}, u32[]{:S(2)}, u32[]{:S(2)}) collective-permute-start(bf16[1536,128]{1,0:T(8,128)(2,1)} %get-tuple-element.177), channel_id=1, source_target_pairs={{0,1},{1,0},{2,3},{3,2},{4,5},{5,4},{6,7},{7,6},{8,9},{9,8},{10,11... | collective-permute-start | bytes 1179656 | tf_op jit(solution)/shard_map/ppermute | solution.py:550
  342.7 0.9 copy-start.1
  385.1 3.2 copy-start.9
  386.5 45.6 %collective-permute-start.12 = (bf16[3,1536,128]{2,1,0:T(8,128)(2,1)S(1)}, bf16[3,1536,128]{2,1,0:T(8,128)(2,1)}, u32[]{:S(2)}, u32[]{:S(2)}) collective-permute-start(bf16[3,1536,128]{2,1,0:T(8,128)(2,1)S(1)} %constant_dynamic-slice_fusion.3), channel_id=1, source_target_pairs={{0,1},{1,0},{2,3},{3,2},{4,5},{5,4},{6,7},{7,6},{8,9},{9,8},{10,11... | collective-permute-start | bytes 3538952 | tf_op jit(solution)/shard_map/ppermute | solution.py:550
  388.4 0.9 copy-start.2
  389.3 40.7 %copy-start.8 = (bf16[1536,128]{1,0:T(8,128)(2,1)S(1)}, bf16[1536,128]{1,0:T(8,128)(2,1)}, u32[]{:S(2)}) copy-start(bf16[1536,128]{1,0:T(8,128)(2,1)} %get-tuple-element.183) | copy-start | bytes 1179652
  429.9 2.2 copy-start.5
  430.1 2.5 copy-start.3
  432.1 41.2 %copy-start.10 = (bf16[1536,128]{1,0:T(8,128)(2,1)}, bf16[1536,128]{1,0:T(8,128)(2,1)S(1)}, u32[]{:S(2)}) copy-start(bf16[1536,128]{1,0:T(8,128)(2,1)S(1)} %collective-permute-done.11) | copy-start | bytes 1179652
  432.1 43.5 %collective-permute-start.13 = (bf16[3,1536,128]{2,1,0:T(8,128)(2,1)S(1)}, bf16[3,1536,128]{2,1,0:T(8,128)(2,1)}, u32[]{:S(2)}, u32[]{:S(2)}) collective-permute-start(bf16[3,1536,128]{2,1,0:T(8,128)(2,1)S(1)} %constant_dynamic-slice_fusion.2), channel_id=1, source_target_pairs={{0,1},{1,0},{2,3},{3,2},{4,5},{5,4},{6,7},{7,6},{8,9},{9,8},{10,11... | collective-permute-start | bytes 3538952 | tf_op jit(solution)/shard_map/ppermute | solution.py:550
  432.6 41.7 %copy-start.7 = (bf16[1536,128]{1,0:T(8,128)(2,1)S(1)}, bf16[1536,128]{1,0:T(8,128)(2,1)}, u32[]{:S(2)}) copy-start(bf16[1536,128]{1,0:T(8,128)(2,1)} %get-tuple-element.194) | copy-start | bytes 1179652
  473.4 2.1 copy-start.6
  475.5 4.9 copy-start
  475.6 47.3 %collective-permute-start.14 = (bf16[3,1536,128]{2,1,0:T(8,128)(2,1)S(1)}, bf16[3,1536,128]{2,1,0:T(8,128)(2,1)}, u32[]{:S(2)}, u32[]{:S(2)}) collective-permute-start(bf16[3,1536,128]{2,1,0:T(8,128)(2,1)S(1)} %constant_dynamic-slice_fusion.1), channel_id=1, source_target_pairs={{0,1},{1,0},{2,3},{3,2},{4,5},{5,4},{6,7},{7,6},{8,9},{9,8},{10,11... | collective-permute-start | bytes 3538952 | tf_op jit(solution)/shard_map/ppermute | solution.py:550
  480.0 44.7 %collective-permute-start.18 = (bf16[160,1024]{1,0:T(8,128)(2,1)}, bf16[160,1024]{1,0:T(8,128)(2,1)}, u32[]{:S(2)}, u32[]{:S(2)}) collective-permute-start(bf16[160,1024]{1,0:T(8,128)(2,1)} %pad_maximum_fusion), channel_id=1, source_target_pairs={{0,1},{1,0},{2,3},{3,2},{4,5},{5,4},{6,7},{7,6},{8,9},{9,8},{10,11... | collective-permute-start | bytes 983048 | tf_op jit(solution)/shard_map/ppermute | solution.py:550
  522.9 152.1 %all-gather.11.cloned.1.call-start = ((), (), s32[]{:S(2)}) async-start(), calls=%async_computation.6 | async-start | bytes 9748480 | tf_op jit(solution)/shard_map/all_gather | solution.py:732
  523.0 22.8 %collective-permute-start.15 = (bf16[3,1536,128]{2,1,0:T(8,128)(2,1)S(1)}, bf16[3,1536,128]{2,1,0:T(8,128)(2,1)S(1)}, u32[]{:S(2)}, u32[]{:S(2)}) collective-permute-start(bf16[3,1536,128]{2,1,0:T(8,128)(2,1)S(1)} %constant_dynamic-slice_fusion), channel_id=1, source_target_pairs={{0,1},{1,0},{2,3},{3,2},{4,5},{5,4},{6,7},{7,6},{8,9},{9,8},{10,11... | collective-permute-start | bytes 3538952 | tf_op jit(solution)/shard_map/ppermute | solution.py:550
  545.8 1.0 copy-start.32
  546.8 19.8 %copy-start.21 = (f32[1,1024]{1,0:T(1,128)S(1)}, f32[1,1024]{1,0:T(1,128)}, u32[]{:S(2)}) copy-start(f32[1,1024]{1,0:T(1,128)} %get-tuple-element.243) | copy-start | bytes 12292
  546.8 19.9 %copy-start.20 = (f32[1,1024]{1,0:T(1,128)S(1)}, f32[1,1024]{1,0:T(1,128)}, u32[]{:S(2)}) copy-start(f32[1,1024]{1,0:T(1,128)} %get-tuple-element.242) | copy-start | bytes 12292
  546.8 19.9 %copy-start.19 = (f32[1,1024]{1,0:T(1,128)S(1)}, f32[1,1024]{1,0:T(1,128)}, u32[]{:S(2)}) copy-start(f32[1,1024]{1,0:T(1,128)} %get-tuple-element.241) | copy-start | bytes 12292
  546.8 19.9 %copy-start.18 = (f32[1,1024]{1,0:T(1,128)S(1)}, f32[1,1024]{1,0:T(1,128)}, u32[]{:S(2)}) copy-start(f32[1,1024]{1,0:T(1,128)} %get-tuple-element.240) | copy-start | bytes 12292
  546.8 19.9 %copy-start.15 = (f32[1,1024]{1,0:T(1,128)S(1)}, f32[1,1024]{1,0:T(1,128)}, u32[]{:S(2)}) copy-start(f32[1,1024]{1,0:T(1,128)} %get-tuple-element.244) | copy-start | bytes 12292
  546.9 19.9 %copy-start.16 = (f32[1,1024]{1,0:T(1,128)S(1)}, f32[1,1024]{1,0:T(1,128)}, u32[]{:S(2)}) copy-start(f32[1,1024]{1,0:T(1,128)} %get-tuple-element.245) | copy-start | bytes 12292
  546.9 19.9 %copy-start.23 = (f32[1,1024]{1,0:T(1,128)S(1)}, f32[1,1024]{1,0:T(1,128)}, u32[]{:S(2)}) copy-start(f32[1,1024]{1,0:T(1,128)} %get-tuple-element.236) | copy-start | bytes 12292
  546.9 23.8 %copy-start.22 = (f32[1,1024]{1,0:T(1,128)S(1)}, f32[1,1024]{1,0:T(1,128)}, u32[]{:S(2)}) copy-start(f32[1,1024]{1,0:T(1,128)} %get-tuple-element.235) | copy-start | bytes 12292
  566.8 3.9 collective-permute-start.16
  596.0 0.8 copy-start.4
  596.8 7.8 %copy-start.14 = (bf16[1,1024]{1,0:T(2,128)(2,1)S(1)}, bf16[1,1024]{1,0:T(2,128)(2,1)}, u32[]{:S(2)}) copy-start(bf16[1,1024]{1,0:T(2,128)(2,1)} %param.15) | copy-start | bytes 6148
  601.0 3.7 collective-permute-start.17
Sparse Core Ops, SparseCore 0:
  135.9 60.4 all-gather.6
  238.2 45.6 all-gather.8
  337.2 119.6 reduce-scatter.2
  523.0 70.3 reduce-scatter.4
  596.9 78.0 all-gather.10

commit v7 on v6

--- a/solution.py
+++ b/solution.py
@@ -328,7 +328,7 @@
 def project(base, seq, x, scale, shift, w, b, cos, sin, before=None):
     frames, width = x.shape
     inner = w.shape[1] // 3
-    step = math.gcd(256, frames)
+    step = math.gcd(512, frames)
     row = pl.BlockSpec((step, width), lambda i, s: (i, 0))
     table = pl.BlockSpec((step, 128), lambda i, s: (s[0] + i, 0))
     const = lambda a: pl.BlockSpec(a.shape, lambda i, s: (0, 0))
@@ -346,35 +346,27 @@
         name="project",
     )(base * (frames // step), x, scale, shift, w, b, cos, sin, *(before or ()))
 
-def cut_up(a, cols):
-    return jnp.concatenate([a[:, c:c + cols] for c in range(0, a.shape[1], cols)], axis=0)
-
-def unpack_kernel(heights, g_ref, *outs):
-    cols = g_ref.shape[2]
-    at = 0
-    for out, high in zip(outs, heights):
-        for c in range(0, out.shape[1], cols):
-            out[:, c:c + cols] = g_ref[0, at:at + high, :].astype(jnp.float32)
-            at += high
-    proj = outs[-1]
-    rows = proj.shape[1]
-    for g in range(proj.shape[2] // 128):
+def unpack_kernel(g_ref, o_ref):
+    parts = g_ref.shape[0]
+    rows = o_ref.shape[1] // parts
+    for p in range(parts):
         for t in range(3):
-            block, lane = divmod(g * 384 + t * 128, cols)
-            start = at + block * rows
-            proj[t, :, g * 128:(g + 1) * 128] = g_ref[0, start:start + rows, lane:lane + 128].astype(jnp.float32)
-
-def unpack(g, heights, width, rows, inner):
+            for g in range(o_ref.shape[2] // 128):
+                at = g * 384 + t * 128
+                o_ref[t, p * rows:(p + 1) * rows, g * 128:(g + 1) * 128] = g_ref[p, :rows, at:at + 128].astype(jnp.float32)
+
+def unpack(g, rows):
     parts, tall, cols = g.shape
+    many = math.gcd(4, parts)
     return pl.pallas_call(
-        functools.partial(unpack_kernel, heights),
-        grid=(parts,),
-        in_specs=[pl.BlockSpec((1, tall, cols), lambda i: (i, 0, 0))],
-        out_specs=[pl.BlockSpec((None, h, width), lambda i: (i, 0, 0)) for h in heights] + [pl.BlockSpec((3, rows, inner), lambda i: (0, i, 0))],
-        out_shape=[jax.ShapeDtypeStruct((parts, h, width), jnp.float32) for h in heights] + [jax.ShapeDtypeStruct((3, parts * rows, inner), jnp.float32)],
+        unpack_kernel,
+        grid=(parts // many,),
+        in_specs=[pl.BlockSpec((many, tall, cols), lambda i: (i, 0, 0))],
+        out_specs=pl.BlockSpec((3, many * rows, cols // 3), lambda i: (0, i, 0)),
+        out_shape=jax.ShapeDtypeStruct((3, parts * rows, cols // 3), jnp.float32),
         compiler_params=pltpu.CompilerParams(vmem_limit_bytes=60 << 20),
         name="unpack",
-    )(g)
+    )(g).transpose(1, 0, 2)
 
 def side_by_side(pieces):
     return jnp.concatenate([p[t] for t in range(3) for p in pieces], axis=1)
@@ -485,7 +477,7 @@
 def feed_forward(base, own, others, x, cot, vectors, expand_bias, out_w, expand_w, contract_w):
     frames, width = x.shape
     n, groups = len(out_w), len(own)
-    step = math.gcd(256, frames)
+    step = math.gcd(384, frames)
     hid = contract_w[0].shape[0]
     row = pl.BlockSpec((step, width), lambda i, s: (i, 0))
     wide = lambda cols: pl.BlockSpec((step, cols), lambda i, s: (i, 0))
@@ -530,7 +522,7 @@
 
 def stacked_grads(kept, n, parts):
     slots, frames, width = kept.shape
-    step = math.gcd(512, frames)
+    step = math.gcd(1536, frames)
     rows = width // parts
     left = lambda j, k: (jnp.where(j == 2 * n, 3, jnp.where(j % 2 == 0, 0, 4 + j // 2)), k, 0)
     right = lambda j, k: (jnp.where(j == 2 * n, 2, jnp.where(j % 2 == 0, 4 + n + j // 2, 1)), k, 0)
@@ -688,6 +680,13 @@
         if g == 0 and groups > 1:
             grads_in[1], parts = lax.optimization_barrier((grads_in[1], parts))
         parts, arrived, wgrads = lax.optimization_barrier((parts, arrived, wgrads))
+        if g == max(groups - 2, 0):
+            reduced, wgrads = lax.optimization_barrier((reduced, wgrads))
+            own_grads = share(0).astype(f32)
+            for r in range(1, n):
+                own_grads = own_grads + move(share(r), -r).astype(f32)
+            own_grads, parts, tab = lax.optimization_barrier((own_grads.astype(bf16), parts, tab))
+            whole_grads = lax.all_gather(own_grads, "dp", axis=0)
         for r in range(1, n):
             if arrived:
                 flat_far[r - 1][-1] = arrived[r - 1]
@@ -695,13 +694,15 @@
         wgrads, tab = lax.optimization_barrier((wgrads, tab))
         if g + 2 < groups:
             grads_in[g + 2], tab = lax.optimization_barrier((grads_in[g + 2], tab))
-        if g == max(groups - 2, 0):
-            reduced, tab = lax.optimization_barrier((reduced, tab))
-            shares = [share(0)] + [move(share(r), -r) for r in range(1, n)]
         bias_sums.append(b[0].reshape(3, 128))
 
+    wgrads, whole_grads = lax.optimization_barrier((wgrads, whole_grads))
     proj_own = lax.psum_scatter(wgrads.reshape(ndp, rows_here, 3 * inner), "dp", scatter_dimension=0, tiled=False)
-    own_grads = sum(p.astype(f32) for p in shares).astype(bf16)
+    at, grads = 0, {}
+    for name, w in shards:
+        grads[name] = whole_grads[:, at:at + heights[name]].astype(f32).reshape(w.shape)
+        at += heights[name]
+    grad_output, grad_expand, grad_contract = grads["out"], grads["expand"], grads["contract"]
     bias_proj_grad = jnp.stack(bias_sums, axis=1).reshape(3 * inner)
 
     grad_inputs, row_sums = input_grad(place(0), flat, [p for far in flat_far for p in far], inputs, grad_middle, scale_a, proj_w)
@@ -714,7 +715,7 @@
     here = sum(move(for_head(r), -r) for r in range(n))
     own_mods = here[None, 2 * width + hidden_here:]
     small = jnp.concatenate([bias_proj_grad, here])
-    cols = math.gcd(3 * inner, width)
+    cols = 3 * inner
     length = -(-small.shape[0] // cols) * cols
     small = jnp.pad(small, (0, length - small.shape[0]))
     terms = []
@@ -723,17 +724,9 @@
         small = small - terms[-1]
     terms = jnp.stack(terms).astype(bf16).reshape(-1, cols)
     terms = jnp.pad(terms, ((0, -terms.shape[0] % 16), (0, 0)))
-    at, split = 0, []
-    for name, w in shards:
-        split.append(cut_up(own_grads[at:at + heights[name]], cols))
-        at += heights[name]
-    split = jnp.concatenate(split, axis=0)
-    own_part = jnp.concatenate([split, cut_up(proj_own, cols), terms], axis=0)
-    gathered = lax.all_gather(own_part, "dp", axis=0)
-    *grads, grad_projection = unpack(gathered, tuple(heights[name] for name, _ in shards), width, rows_here, inner)
-    grad_expand, grad_contract, grad_output = (v.reshape(w.shape) for v, (_, w) in zip(grads, shards))
-    grad_projection = grad_projection.transpose(1, 0, 2)
-    above = own_part.shape[0] - terms.shape[0]
+    gathered = lax.all_gather(jnp.concatenate([proj_own, terms], axis=0), "dp", axis=0)
+    grad_projection = unpack(gathered, rows_here)
+    above = rows_here
     table = gathered[:, above:].reshape(ndp, -1)[:, :3 * length].astype(f32).reshape(ndp, 3, length)
     table = table[:, 0] + (table[:, 1] + table[:, 2])
     totals = jnp.sum(table, axis=0)

time: 722 us -> 687 us (0.952)
  Pallas kernels: 435 us -> 405 us
  waiting for transfers between devices: 158 us -> 150 us
  other arithmetic: 18.6 us -> 26.1 us
    reduce_scatter x1, waiting for transfers between devices: 22.4 us -> 41.5 us  [on_device(): lax.psum_scatter(wgrads.reshape(ndp, rows_here, 3 * inner), 'dp', scatter...]
    ppermute x19, waiting for transfers between devices: 65.3 us -> 50.9 us  [relative(): lax.ppermute(x, axis, [(i, (i + r) % size) for i in range(size)])]
    all_gather x1 -> x2, waiting for transfers between devices: 69.8 us -> 57.6 us  [the longest x1 32.9 us: on_device(): lax.all_gather(jnp.concatenate([proj_own, terms], axis=0), 'dp', axis=0)]
    pallas_call x1, Pallas kernels: 32.1 us -> 22.7 us  [stacked_grads(): pl.pallas_call(functools.partial(stack_kernel, n), grid=(2 * n + 1, frame...]
    pallas_call x1, Pallas kernels: 14 us -> 5.27 us  [unpack(): pl.pallas_call(unpack_kernel, grid=(parts // many,), in_specs=[pl.BlockSp...]
  transfers between devices with their start and end apart: 24 -> 25, of which waited for: 7 -> 7; matrix products, arithmetic and copies ran while one was open for 8% -> 9% of each run, Pallas kernels for 58% -> 57%
where the time goes in v7:
time: 687 us; the launch traced here: 678 us
  Pallas kernels  405 us (59%)
  waiting for transfers between devices  150 us (22%)
  local copies, waits for them, and re-layouts  48.7 us (7%)
  other arithmetic  26.1 us (4%)
  starting transfers between devices  20.5 us (3%)
  between operations  15.4 us (2%)
  matrix products  11.8 us (2%)
    pallas_call x4, Pallas kernels, attend_bwd(): pl.pallas_call(bwd_kernel, grid_spec=pltpu.PrefetchScalarGridSpec(num_sca...  158 us
    pallas_call x4, Pallas kernels, attend_fwd(): pl.pallas_call(fwd_kernel, grid_spec=pltpu.PrefetchScalarGridSpec(num_sca...  126 us
    pallas_call x1, Pallas kernels, feed_forward(): pl.pallas_call(functools.partial(middle_kernel, n, groups), grid_spec=plt...  51.7 us
    ppermute x19, waiting for transfers between devices, relative(): lax.ppermute(x, axis, [(i, (i + r) % size) for i in range(size)])  50.9 us
    reduce_scatter x1, waiting for transfers between devices, on_device(): lax.psum_scatter(wgrads.reshape(ndp, rows_here, 3 * inner), 'dp', scatter...  41.5 us
    all_gather x1, waiting for transfers between devices, on_device(): lax.all_gather(jnp.concatenate([proj_own, terms], axis=0), 'dp', axis=0)  32.9 us
    all_gather x1, waiting for transfers between devices, on_device(): whole_grads = lax.all_gather(own_grads, 'dp', axis=0)  24.7 us
    pallas_call x1, Pallas kernels, stacked_grads(): pl.pallas_call(functools.partial(stack_kernel, n), grid=(2 * n + 1, frame...  22.7 us
  transfers between devices with their start and end apart: 25, of which 7 were waited for; matrix products, arithmetic and copies ran while one was open for 9% of the time, Pallas kernels for 57%

profile of v7, /device:TPU:0, one launch (start us, length us, event | category | flops | bytes accessed | tf_op | source)
XLA Modules:
  0.0 677.6 jit_solution(14918699470685812614)
XLA Ops:
  7.3 3.7 fusion.24
  11.0 3.0 collective-permute-start
  15.5 1.0 constant_dynamic-slice_fusion.10
  17.7 1.5 fusion.6
  20.0 1.6 copy.93.sin_ref
  21.7 1.6 copy.92.cos_ref
  23.4 3.2 copy.87
  26.5 2.9 copy.91.w_ref.rest_0_
  29.5 0.9 slice_reduce_fusion.1
  32.1 11.0 %project.2 = (bf16[3,3072,512]{2,1,0:T(8,128)(2,1)}, bf16[1024,3072]{1,0:T(8,128)(2,1)}) custom-call(s32[1]{0:T(128)} %bitcast.10.base, bf16[1536,1024]{1,0:T(8,128)(2,1)} %x_ref.3, f32[1,1024]{1,0:T(1,128)} %get-tuple-element.258.scale_ref, f32[1,1024]{1,0:T(1,128)} %get-tuple-element.257.shift_ref, bf16[1024,1536]{1,0:T(8,128)(2,1)} %copy.91.w_ref.rest_0_, ...), custom_call_target="tpu_custom_call" | custom-call | flops 4831838208 | bytes 11010048 | tf_op jit(solution)/shard_map/project/pallas_call | solution.py:336
  43.1 2.3 select_convert_fusion
  45.4 42.2 %collective-permute-done.1.x_ref = bf16[1536,1024]{1,0:T(8,128)(2,1)} collective-permute-done((bf16[1536,1024]{1,0:T(8,128)(2,1)}, bf16[1536,1024]{1,0:T(8,128)(2,1)}, u32[]{:S(2)}, u32[]{:S(2)}) %collective-permute-start.1) | collective-permute-done | bytes 3145760 | tf_op jit(solution)/shard_map/ppermute | solution.py:542
  87.5 11.0 %project.3 = (bf16[3,3072,512]{2,1,0:T(8,128)(2,1)}, bf16[1024,3072]{1,0:T(8,128)(2,1)}) custom-call(s32[1]{0:T(128)} %bitcast.7.base, bf16[1536,1024]{1,0:T(8,128)(2,1)} %collective-permute-done.1.x_ref, f32[1,1024]{1,0:T(1,128)} %get-tuple-element.258.scale_ref, ...), custom_call_target="tpu_custom_call", output_to_operand_aliasing={{0}: (8, {}), {1}: (9, {})} | custom-call | flops 4831838208 | bytes 11010048 | tf_op jit(solution)/shard_map/project/pallas_call | solution.py:336
  98.8 1.7 collective-permute-start.3
  100.5 31.8 %attend_fwd.4 = (bf16[3072,128]{1,0:T(8,128)(2,1)}, f32[1,8,3072]{2,1,0:T(8,128)}) custom-call(s32[36]{0:T(128)} %pad_add_fusion.tab, bf16[3,3072,512]{2,1,0:T(8,128)(2,1)} %get-tuple-element.126.q_ref.k_ref.v_ref, bf16[3,3072,512]{2,1,0:T(8,128)(2,1)} %get-tuple-element.126.q_ref.k_ref.v_ref, bf16[3,3072,512]{2,1,0:T(8,128)(2,1)} %get-tuple-element.126.q_ref.k_ref.v_ref, ...), custom_call_target="tpu_custom_call" | custom-call | flops 28991029248 | bytes 3145728 | tf_op jit(solution)/shard_map/attend_fwd/pallas_call | solution.py:177
  132.3 1.0 constant_dynamic-slice_fusion.7
  134.3 31.4 %attend_fwd.5 = (bf16[3072,128]{1,0:T(8,128)(2,1)}, f32[1,8,3072]{2,1,0:T(8,128)}) custom-call(s32[36]{0:T(128)} %pad_add_fusion.tab, bf16[3,3072,512]{2,1,0:T(8,128)(2,1)} %get-tuple-element.126.q_ref.k_ref.v_ref, bf16[3,3072,512]{2,1,0:T(8,128)(2,1)} %get-tuple-element.126.q_ref.k_ref.v_ref, bf16[3,3072,512]{2,1,0:T(8,128)(2,1)} %get-tuple-element.126.q_ref.k_ref.v_ref, ...), custom_call_target="tpu_custom_call" | custom-call | flops 28991029248 | bytes 3145728 | tf_op jit(solution)/shard_map/attend_fwd/pallas_call | solution.py:177
  165.7 1.0 constant_dynamic-slice_fusion.6
  166.8 31.5 %attend_fwd.6 = (bf16[3072,128]{1,0:T(8,128)(2,1)}, f32[1,8,3072]{2,1,0:T(8,128)}) custom-call(s32[36]{0:T(128)} %pad_add_fusion.tab, bf16[3,3072,512]{2,1,0:T(8,128)(2,1)} %get-tuple-element.126.q_ref.k_ref.v_ref, bf16[3,3072,512]{2,1,0:T(8,128)(2,1)} %get-tuple-element.126.q_ref.k_ref.v_ref, bf16[3,3072,512]{2,1,0:T(8,128)(2,1)} %get-tuple-element.126.q_ref.k_ref.v_ref, ...), custom_call_target="tpu_custom_call" | custom-call | flops 28991029248 | bytes 3145728 | tf_op jit(solution)/shard_map/attend_fwd/pallas_call | solution.py:177
  198.3 1.0 constant_dynamic-slice_fusion.5
  199.5 31.4 %attend_fwd.7 = (bf16[3072,128]{1,0:T(8,128)(2,1)}, f32[1,8,3072]{2,1,0:T(8,128)}) custom-call(s32[36]{0:T(128)} %pad_add_fusion.tab, bf16[3,3072,512]{2,1,0:T(8,128)(2,1)} %get-tuple-element.126.q_ref.k_ref.v_ref, bf16[3,3072,512]{2,1,0:T(8,128)(2,1)} %get-tuple-element.126.q_ref.k_ref.v_ref, bf16[3,3072,512]{2,1,0:T(8,128)(2,1)} %get-tuple-element.126.q_ref.k_ref.v_ref, ...), custom_call_target="tpu_custom_call" | custom-call | flops 28991029248 | bytes 3145728 | tf_op jit(solution)/shard_map/attend_fwd/pallas_call | solution.py:177
  230.9 1.0 constant_dynamic-slice_fusion.4
  235.1 1.3 bitcast_convert_fusion.3.refs_9_
  236.5 2.3 slice.138
  238.7 4.9 fusion.35
  244.5 51.7 %feed_forward.1 = (bf16[1536,1024]{1,0:T(8,128)(2,1)}, f32[1536,1024]{1,0:T(8,128)}, bf16[8,1536,1024]{2,1,0:T(8,128)(2,1)}, f32[8,1024]{1,0:T(8,128)}, f32[8,20...) custom-call(s32[1]{0:T(128)} %bitcast.base, ...), custom_call_target="tpu_custom_call" | custom-call | flops 32212254720 | bytes 37748736 | tf_op jit(solution)/shard_map/feed_forward/pallas_call | solution.py:489
  296.2 2.1 collective-permute-start.8
  298.2 22.7 %stacked_grads.1 = bf16[16,320,1024]{2,1,0:T(8,128)(2,1)} custom-call(bf16[8,1536,1024]{2,1,0:T(8,128)(2,1)} %get-tuple-element.155.l_ref.r_ref, bf16[8,1536,1024]{2,1,0:T(8,128)(2,1)} %get-tuple-element.155.l_ref.r_ref), custom_call_target="tpu_custom_call" | custom-call | flops 16106127360 | bytes 25165824 | tf_op jit(solution)/shard_map/stacked_grads/pallas_call | solution.py:529
  321.1 0.9 copy-done.22
  322.1 1.9 collective-permute-start.10
  325.3 39.4 %attend_bwd.4 = (bf16[3,3072,128]{2,1,0:T(8,128)(2,1)}, bf16[1024,1536]{1,0:T(8,128)(2,1)}, f32[8,384]{1,0:T(8,128)}) custom-call(s32[36]{0:T(128)} %pad_add_fusion.tab, bf16[3,3072,512]{2,1,0:T(8,128)(2,1)} %get-tuple-element.126.q_ref.k_ref.v_ref, bf16[3,3072,512]{2,1,0:T(8,128)(2,1)} %get-tuple-element.126.q_ref.k_ref.v_ref, ...), custom_call_target="tpu_custom_call" | custom-call | flops 38654705664 | bytes 12582912 | tf_op jit(solution)/shard_map/attend_bwd/pallas_call | solution.py:285
  364.7 1.4 constant_dynamic-slice_fusion.3
  366.1 2.0 collective-permute-start.12
  369.2 39.6 %attend_bwd.5 = (bf16[3,3072,128]{2,1,0:T(8,128)(2,1)}, bf16[1024,1536]{1,0:T(8,128)(2,1)}, f32[8,384]{1,0:T(8,128)}) custom-call(s32[36]{0:T(128)} %pad_add_fusion.tab, bf16[3,3072,512]{2,1,0:T(8,128)(2,1)} %get-tuple-element.126.q_ref.k_ref.v_ref, bf16[3,3072,512]{2,1,0:T(8,128)(2,1)} %get-tuple-element.126.q_ref.k_ref.v_ref, ...), custom_call_target="tpu_custom_call", output_to_operand_aliasing={{1}: (12, {})} | custom-call | flops 38654705664 | bytes 12582912 | tf_op jit(solution)/shard_map/attend_bwd/pallas_call | solution.py:285
  409.1 1.7 copy-done.5
  411.0 39.8 %attend_bwd.6 = (bf16[3,3072,128]{2,1,0:T(8,128)(2,1)}, bf16[1024,1536]{1,0:T(8,128)(2,1)}, f32[8,384]{1,0:T(8,128)}) custom-call(s32[36]{0:T(128)} %pad_add_fusion.tab, bf16[3,3072,512]{2,1,0:T(8,128)(2,1)} %get-tuple-element.126.q_ref.k_ref.v_ref, bf16[3,3072,512]{2,1,0:T(8,128)(2,1)} %get-tuple-element.126.q_ref.k_ref.v_ref, ...), custom_call_target="tpu_custom_call", output_to_operand_aliasing={{1}: (12, {})} | custom-call | flops 38654705664 | bytes 12582912 | tf_op jit(solution)/shard_map/attend_bwd/pallas_call | solution.py:285
  450.8 1.4 constant_dynamic-slice_fusion.1
  452.2 0.9 fusion.38
  453.2 1.1 fusion.37
  454.3 2.0 collective-permute-start.14
  456.3 5.1 collective-permute-done.14
  462.6 2.0 collective-permute-start.15
  464.6 39.4 %attend_bwd.7 = (bf16[3,3072,128]{2,1,0:T(8,128)(2,1)}, bf16[1024,1536]{1,0:T(8,128)(2,1)}, f32[8,384]{1,0:T(8,128)}) custom-call(s32[36]{0:T(128)} %pad_add_fusion.tab, bf16[3,3072,512]{2,1,0:T(8,128)(2,1)} %get-tuple-element.126.q_ref.k_ref.v_ref, bf16[3,3072,512]{2,1,0:T(8,128)(2,1)} %get-tuple-element.126.q_ref.k_ref.v_ref, ...), custom_call_target="tpu_custom_call", output_to_operand_aliasing={{1}: (12, {})} | custom-call | flops 38654705664 | bytes 12582912 | tf_op jit(solution)/shard_map/attend_bwd/pallas_call | solution.py:285
  504.0 1.4 constant_dynamic-slice_fusion
  505.4 1.2 collective-permute-start.16
  506.6 24.7 %all-gather.13.cloned.1.call-done = bf16[2560,1024]{1,0:T(8,128)(2,1)} async-done(((bf16[160,1024]{1,0:T(8,128)(2,1)}), bf16[2560,1024]{1,0:T(8,128)(2,1)}) %all-gather.13.cloned.1.call-update) | async-done | bytes 5242896 | tf_op jit(solution)/shard_map/all_gather | solution.py:689
  535.0 18.9 %input_grad.1 = (f32[1536,1024]{1,0:T(8,128)}, f32[8,1024]{1,0:T(8,128)}) custom-call(s32[1]{0:T(128)} %bitcast.16.base, bf16[1536,1024]{1,0:T(8,128)(2,1)} %x_ref.3, f32[1536,1024]{1,0:T(8,128)} %get-tuple-element.149.gm_ref, f32[1,1024]{1,0:T(1,128)} %get-tuple-element.258.scale_ref, bf16[1024,1536]{1,0:T(8,128)(2,1)} %copy.91.w_ref.rest_0_, ...), custom_call_target="tpu_custom_call" | custom-call | flops 9663676416 | bytes 25165824 | tf_op jit(solution)/shard_map/input_grad/pallas_call | solution.py:396
  554.9 1.5 collective-permute-start.17
  556.4 2.3 collective-permute-done.17
  559.0 41.5 %reduce-scatter.5.cloned.1.call-done = bf16[1,64,1536]{2,1,0:T(8,128)(2,1)} async-done(((bf16[16,64,1536]{2,1,0:T(8,128)(2,1)}), bf16[1,64,1536]{2,1,0:T(8,128)(2,1)}) %reduce-scatter.5.cloned.1.call-update) | async-done | bytes 196624 | tf_op jit(solution)/shard_map/reduce_scatter | solution.py:700
  600.5 1.6 fusion.9
  602.2 4.3 multiply_reduce_fusion
  606.5 1.4 collective-permute-start.18
  607.9 1.0 slice_convert_fusion.1
  608.9 1.3 collective-permute-done.18
  610.9 1.6 bitcast_convert_fusion.2
  613.0 2.6 bitcast_convert_fusion
  615.6 2.6 bitcast_convert_fusion.1
  618.2 32.9 %all-gather.15.cloned.1.call-done = bf16[1280,1536]{1,0:T(8,128)(2,1)} async-done(((bf16[80,1536]{1,0:T(8,128)(2,1)}), bf16[1280,1536]{1,0:T(8,128)(2,1)}) %all-gather.15.cloned.1.call-update) | async-done | bytes 3932176 | tf_op jit(solution)/shard_map/all_gather | solution.py:727
  651.1 1.2 slice.179
  652.9 1.2 reshape.339
  654.1 1.1 fusion.31
  656.4 5.3 unpack.1
  662.3 8.1 %fusion.10 = f32[1024,3072]{1,0:T(8,128)} fusion(f32[16,7680]{1,0:T(8,128)S(1)} %bitcast.99, f32[16,1,1024]{2,1,0:T(1,128)S(1)} %slice_convert_fusion.1), kind=kOutput, calls=%fused_computation.27 | convolution fusion | flops 604061696 | bytes 12845056 | tf_op jit(solution)/shard_map/dot_general | solution.py:740
  (168 shorter events, 23.2 us)
Async XLA Ops:
  7.2 3.8 copy-start.16
  7.2 7.4 %copy-start.14 = (bf16[1024]{0:T(1024)(128)(2,1)S(1)}, bf16[1024]{0:T(1024)(128)(2,1)}, u32[]{:S(2)}) copy-start(bf16[1024]{0:T(1024)(128)(2,1)} %param.24) | copy-start | bytes 6148
  7.2 7.4 %copy-start.17 = (bf16[3,512]{1,0:T(4,128)(2,1)S(1)}, bf16[3,512]{1,0:T(4,128)(2,1)}, u32[]{:S(2)}) copy-start(bf16[3,512]{1,0:T(4,128)(2,1)} %param.20) | copy-start | bytes 9220
  7.2 12.0 %copy-start.10 = (s32[1,3072]{1,0:T(1,128)S(1)}, s32[1,3072]{1,0:T(1,128)}, u32[]{:S(2)}) copy-start(s32[1,3072]{1,0:T(1,128)} %param.16) | copy-start | bytes 36868
  7.2 224.8 %all-gather.9.cloned.1.call-start = ((), (), s32[]{:S(2)}) async-start(), calls=%async_computation.4 | async-start | bytes 6684672 | tf_op jit(solution)/shard_map/all_gather | solution.py:624
  11.0 6.6 collective-permute-start
  17.6 69.9 %collective-permute-start.1 = (bf16[1536,1024]{1,0:T(8,128)(2,1)}, bf16[1536,1024]{1,0:T(8,128)(2,1)}, u32[]{:S(2)}, u32[]{:S(2)}) collective-permute-start(bf16[1536,1024]{1,0:T(8,128)(2,1)} %x_ref.3), channel_id=1, source_target_pairs={{0,1},{1,0},{2,3},{3,2},{4,5},{5,4},{6,7},{7,6},{8,9},{9,8},{10,11... | collective-permute-start | bytes 9437192 | tf_op jit(solution)/shard_map/ppermute | solution.py:542
  32.0 11.0 %copy-start.20 = (pred[128]{0:T(512)(128)(4,1)S(1)}, pred[128]{0:T(512)(128)(4,1)}, u32[]{:S(2)}) copy-start(pred[128]{0:T(512)(128)(4,1)} %broadcast_compare_fusion) | copy-start | bytes 388
  32.0 11.0 %copy-start.21 = (s32[128]{0:T(128)S(1)}, s32[128]{0:T(128)}, u32[]{:S(2)}) copy-start(s32[128]{0:T(128)} %and_select_fusion) | copy-start | bytes 1540
  98.5 34.9 %collective-permute-start.2 = (bf16[176,1024]{1,0:T(8,128)(2,1)S(1)}, bf16[176,1024]{1,0:T(8,128)(2,1)S(1)}, u32[]{:S(2)}, u32[]{:S(2)}) collective-permute-start(bf16[176,1024]{1,0:T(8,128)(2,1)S(1)} %fusion.8), channel_id=1, source_target_pairs={{0,1},{1,0},{2,3},{3,2},{4,5},{5,4},{6,7},{7,6},{8,9},{9,8},{10,11... | collective-permute-start | bytes 1081352 | tf_op jit(solution)/shard_map/ppermute | solution.py:542
  98.8 34.6 %collective-permute-start.3 = (bf16[64,1536]{0,1:T(8,128)(2,1)S(1)}, bf16[64,1536]{0,1:T(8,128)(2,1)S(1)}, u32[]{:S(2)}, u32[]{:S(2)}) collective-permute-start(bf16[64,1536]{0,1:T(8,128)(2,1)S(1)} %constant_dynamic-slice_fusion.8), channel_id=1, source_target_pairs={{0,1},{1,0},{2,3},{3,2},{4,5},{5,4},{6,7},{7,6},{8,9},{9,8},{10,11... | collective-permute-start | bytes 589832 | tf_op jit(solution)/shard_map/ppermute | solution.py:542
  100.5 32.9 %copy-start.11 = (bf16[1,1024]{1,0:T(2,128)(2,1)S(1)}, bf16[1,1024]{1,0:T(2,128)(2,1)}, u32[]{:S(2)}) copy-start(bf16[1,1024]{1,0:T(2,128)(2,1)} %param.15) | copy-start | bytes 6148
  134.2 164.1 %all-gather.11.cloned.1.call-start = ((), (), s32[]{:S(2)}) async-start(), calls=%async_computation.5 | async-start | bytes 3342336 | tf_op jit(solution)/shard_map/all_gather | solution.py:627
  134.2 32.5 %collective-permute-start.4 = (bf16[1536,128]{1,0:T(8,128)(2,1)S(1)}, bf16[1536,128]{1,0:T(8,128)(2,1)S(1)}, u32[]{:S(2)}, u32[]{:S(2)}) collective-permute-start(bf16[1536,128]{1,0:T(8,128)(2,1)S(1)} %constant_dynamic-slice_fusion.7), channel_id=1, source_target_pairs={{0,1},{1,0},{2,3},{3,2},{4,5},{5,4},{6,7},{7,6},{8,9},{9,8},{10,11... | collective-permute-start | bytes 1179656 | tf_op jit(solution)/shard_map/ppermute | solution.py:542
  166.8 31.6 %copy-start.24 = (bf16[1536,128]{1,0:T(8,128)(2,1)}, bf16[1536,128]{1,0:T(8,128)(2,1)S(1)}, u32[]{:S(2)}) copy-start(bf16[1536,128]{1,0:T(8,128)(2,1)S(1)} %collective-permute-done.4.refs_20_) | copy-start | bytes 1179652
  166.8 32.6 %collective-permute-start.5 = (bf16[1536,128]{1,0:T(8,128)(2,1)S(1)}, bf16[1536,128]{1,0:T(8,128)(2,1)S(1)}, u32[]{:S(2)}, u32[]{:S(2)}) collective-permute-start(bf16[1536,128]{1,0:T(8,128)(2,1)S(1)} %constant_dynamic-slice_fusion.6), channel_id=1, source_target_pairs={{0,1},{1,0},{2,3},{3,2},{4,5},{5,4},{6,7},{7,6},{8,9},{9,8},{10,11... | collective-permute-start | bytes 1179656 | tf_op jit(solution)/shard_map/ppermute | solution.py:542
  199.3 34.0 %copy-start.18 = (bf16[1024]{0:T(1024)(128)(2,1)S(1)}, bf16[1024]{0:T(1024)(128)(2,1)}, u32[]{:S(2)}) copy-start(bf16[1024]{0:T(1024)(128)(2,1)} %param.22) | copy-start | bytes 6148
  199.4 34.6 %copy-start.19 = (bf16[1024]{0:T(1024)(128)(2,1)S(1)}, bf16[1024]{0:T(1024)(128)(2,1)}, u32[]{:S(2)}) copy-start(bf16[1024]{0:T(1024)(128)(2,1)} %param.26) | copy-start | bytes 6148
  199.4 35.2 %copy-start.15 = (bf16[1024]{0:T(1024)(128)(2,1)S(1)}, bf16[1024]{0:T(1024)(128)(2,1)}, u32[]{:S(2)}) copy-start(bf16[1024]{0:T(1024)(128)(2,1)} %param.24) | copy-start | bytes 6148
  199.4 31.5 %copy-start.25 = (bf16[1536,128]{1,0:T(8,128)(2,1)}, bf16[1536,128]{1,0:T(8,128)(2,1)S(1)}, u32[]{:S(2)}) copy-start(bf16[1536,128]{1,0:T(8,128)(2,1)S(1)} %collective-permute-done.5.refs_21_) | copy-start | bytes 1179652
  199.4 32.6 %collective-permute-start.6 = (bf16[1536,128]{1,0:T(8,128)(2,1)S(1)}, bf16[1536,128]{1,0:T(8,128)(2,1)S(1)}, u32[]{:S(2)}, u32[]{:S(2)}) collective-permute-start(bf16[1536,128]{1,0:T(8,128)(2,1)S(1)} %constant_dynamic-slice_fusion.5), channel_id=1, source_target_pairs={{0,1},{1,0},{2,3},{3,2},{4,5},{5,4},{6,7},{7,6},{8,9},{9,8},{10,11... | collective-permute-start | bytes 1179656 | tf_op jit(solution)/shard_map/ppermute | solution.py:542
  232.0 11.7 %copy-start.26 = (bf16[1536,128]{1,0:T(8,128)(2,1)}, bf16[1536,128]{1,0:T(8,128)(2,1)S(1)}, u32[]{:S(2)}) copy-start(bf16[1536,128]{1,0:T(8,128)(2,1)S(1)} %collective-permute-done.6.refs_22_) | copy-start | bytes 1179652
  232.9 219.3 %reduce-scatter.3.cloned.1.call-start = ((), (), s32[]{:S(2)}) async-start(), calls=%async_computation.2 | async-start | bytes 11141120 | tf_op jit(solution)/shard_map/reduce_scatter | solution.py:664
  235.1 8.6 %collective-permute-start.7 = (bf16[1536,128]{1,0:T(8,128)(2,1)S(1)}, bf16[1536,128]{1,0:T(8,128)(2,1)S(1)}, u32[]{:S(2)}, u32[]{:S(2)}) collective-permute-start(bf16[1536,128]{1,0:T(8,128)(2,1)S(1)} %constant_dynamic-slice_fusion.4), channel_id=1, source_target_pairs={{0,1},{1,0},{2,3},{3,2},{4,5},{5,4},{6,7},{7,6},{8,9},{9,8},{10,11... | collective-permute-start | bytes 1179656 | tf_op jit(solution)/shard_map/ppermute | solution.py:542
  243.7 0.8 copy-start.27
  296.2 24.8 %collective-permute-start.8 = (bf16[1536,128]{1,0:T(8,128)(2,1)}, bf16[1536,128]{1,0:T(8,128)(2,1)S(1)}, u32[]{:S(2)}, u32[]{:S(2)}) collective-permute-start(bf16[1536,128]{1,0:T(8,128)(2,1)} %get-tuple-element.157), channel_id=1, source_target_pairs={{0,1},{1,0},{2,3},{3,2},{4,5},{5,4},{6,7},{7,6},{8,9},{9,8},{10,11... | collective-permute-start | bytes 1179656 | tf_op jit(solution)/shard_map/ppermute | solution.py:542
  321.0 1.0 copy-start.22
  321.0 1.1 copy-start.23
  321.0 3.2 copy-start.9
  321.0 210.2 %all-gather.13.cloned.1.call-start = ((), (), s32[]{:S(2)}) async-start(), calls=%async_computation.6 | async-start | bytes 5570560 | tf_op jit(solution)/shard_map/all_gather | solution.py:689
  322.0 44.1 %collective-permute-start.9 = (bf16[1536,128]{1,0:T(8,128)(2,1)S(1)}, bf16[1536,128]{1,0:T(8,128)(2,1)S(1)}, u32[]{:S(2)}, u32[]{:S(2)}) collective-permute-start(bf16[1536,128]{1,0:T(8,128)(2,1)S(1)} %copy-done.22), channel_id=1, source_target_pairs={{0,1},{1,0},{2,3},{3,2},{4,5},{5,4},{6,7},{7,6},{8,9},{9,8},{10,11... | collective-permute-start | bytes 1179656 | tf_op jit(solution)/shard_map/ppermute | solution.py:542
  322.1 44.0 %collective-permute-start.10 = (bf16[1536,128]{1,0:T(8,128)(2,1)S(1)}, bf16[1536,128]{1,0:T(8,128)(2,1)S(1)}, u32[]{:S(2)}, u32[]{:S(2)}) collective-permute-start(bf16[1536,128]{1,0:T(8,128)(2,1)S(1)} %copy-done.23), channel_id=1, source_target_pairs={{0,1},{1,0},{2,3},{3,2},{4,5},{5,4},{6,7},{7,6},{8,9},{9,8},{10,11... | collective-permute-start | bytes 1179656 | tf_op jit(solution)/shard_map/ppermute | solution.py:542
  324.0 86.8 %collective-permute-start.11 = (bf16[1536,128]{1,0:T(8,128)(2,1)}, bf16[1536,128]{1,0:T(8,128)(2,1)S(1)}, u32[]{:S(2)}, u32[]{:S(2)}) collective-permute-start(bf16[1536,128]{1,0:T(8,128)(2,1)} %get-tuple-element.178), channel_id=1, source_target_pairs={{0,1},{1,0},{2,3},{3,2},{4,5},{5,4},{6,7},{7,6},{8,9},{9,8},{10,11... | collective-permute-start | bytes 1179656 | tf_op jit(solution)/shard_map/ppermute | solution.py:542
  324.4 0.9 copy-start.2
  364.7 3.5 copy-start.8
  366.1 44.7 %collective-permute-start.12 = (bf16[3,1536,128]{2,1,0:T(8,128)(2,1)S(1)}, bf16[3,1536,128]{2,1,0:T(8,128)(2,1)}, u32[]{:S(2)}, u32[]{:S(2)}) collective-permute-start(bf16[3,1536,128]{2,1,0:T(8,128)(2,1)S(1)} %constant_dynamic-slice_fusion.3), channel_id=1, source_target_pairs={{0,1},{1,0},{2,3},{3,2},{4,5},{5,4},{6,7},{7,6},{8,9},{9,8},{10,11... | collective-permute-start | bytes 3538952 | tf_op jit(solution)/shard_map/ppermute | solution.py:542
  368.3 0.9 copy-start.3
  369.2 39.7 %copy-start.7 = (bf16[1536,128]{1,0:T(8,128)(2,1)S(1)}, bf16[1536,128]{1,0:T(8,128)(2,1)}, u32[]{:S(2)}) copy-start(bf16[1536,128]{1,0:T(8,128)(2,1)} %get-tuple-element.184) | copy-start | bytes 1179652
  408.8 1.9 copy-start.5
  409.1 1.9 copy-start.4
  410.9 41.3 %collective-permute-start.13 = (bf16[3,1536,128]{2,1,0:T(8,128)(2,1)S(1)}, bf16[3,1536,128]{2,1,0:T(8,128)(2,1)}, u32[]{:S(2)}, u32[]{:S(2)}) collective-permute-start(bf16[3,1536,128]{2,1,0:T(8,128)(2,1)S(1)} %constant_dynamic-slice_fusion.2), channel_id=1, source_target_pairs={{0,1},{1,0},{2,3},{3,2},{4,5},{5,4},{6,7},{7,6},{8,9},{9,8},{10,11... | collective-permute-start | bytes 3538952 | tf_op jit(solution)/shard_map/ppermute | solution.py:542
  452.2 10.2 %copy-start.6 = (bf16[1536,128]{1,0:T(8,128)(2,1)S(1)}, bf16[1536,128]{1,0:T(8,128)(2,1)}, u32[]{:S(2)}) copy-start(bf16[1536,128]{1,0:T(8,128)(2,1)} %get-tuple-element.198) | copy-start | bytes 1179652
  454.3 7.1 %collective-permute-start.14 = (bf16[160,1024]{1,0:T(8,128)(2,1)S(1)}, bf16[160,1024]{1,0:T(8,128)(2,1)S(1)}, u32[]{:S(2)}, u32[]{:S(2)}) collective-permute-start(bf16[160,1024]{1,0:T(8,128)(2,1)S(1)} %pad_maximum_fusion), channel_id=1, source_target_pairs={{0,1},{1,0},{2,3},{3,2},{4,5},{5,4},{6,7},{7,6},{8,9},{9,8},{10,11... | collective-permute-start | bytes 983048 | tf_op jit(solution)/shard_map/ppermute | solution.py:542
  462.3 138.3 %reduce-scatter.5.cloned.1.call-start = ((), (), s32[]{:S(2)}) async-start(), calls=%async_computation.3 | async-start | bytes 3342336 | tf_op jit(solution)/shard_map/reduce_scatter | solution.py:700
  462.6 2.0 copy-start.1
  462.6 42.8 %collective-permute-start.15 = (bf16[3,1536,128]{2,1,0:T(8,128)(2,1)S(1)}, bf16[3,1536,128]{2,1,0:T(8,128)(2,1)}, u32[]{:S(2)}, u32[]{:S(2)}) collective-permute-start(bf16[3,1536,128]{2,1,0:T(8,128)(2,1)S(1)} %constant_dynamic-slice_fusion.1), channel_id=1, source_target_pairs={{0,1},{1,0},{2,3},{3,2},{4,5},{5,4},{6,7},{7,6},{8,9},{9,8},{10,11... | collective-permute-start | bytes 3538952 | tf_op jit(solution)/shard_map/ppermute | solution.py:542
  504.0 2.6 copy-start.13
  505.4 29.6 %collective-permute-start.16 = (bf16[3,1536,128]{2,1,0:T(8,128)(2,1)S(1)}, bf16[3,1536,128]{2,1,0:T(8,128)(2,1)}, u32[]{:S(2)}, u32[]{:S(2)}) collective-permute-start(bf16[3,1536,128]{2,1,0:T(8,128)(2,1)S(1)} %constant_dynamic-slice_fusion), channel_id=1, source_target_pairs={{0,1},{1,0},{2,3},{3,2},{4,5},{5,4},{6,7},{7,6},{8,9},{9,8},{10,11... | collective-permute-start | bytes 3538952 | tf_op jit(solution)/shard_map/ppermute | solution.py:542
  531.3 119.9 %all-gather.15.cloned.1.call-start = ((), (), s32[]{:S(2)}) async-start(), calls=%async_computation.7 | async-start | bytes 4177920 | tf_op jit(solution)/shard_map/all_gather | solution.py:727
  554.9 3.9 collective-permute-start.17
  602.2 8.0 %copy-start.12 = (bf16[1,1024]{1,0:T(2,128)(2,1)S(1)}, bf16[1,1024]{1,0:T(2,128)(2,1)}, u32[]{:S(2)}) copy-start(bf16[1,1024]{1,0:T(2,128)(2,1)} %param.15) | copy-start | bytes 6148
  602.2 8.6 %copy-start = (bf16[2560,1024]{1,0:T(8,128)(2,1)S(1)}, bf16[2560,1024]{1,0:T(8,128)(2,1)}, u32[]{:S(2)}) copy-start(bf16[2560,1024]{1,0:T(8,128)(2,1)} %all-gather.13.cloned.1.call-done) | copy-start | bytes 15728644
  606.5 3.7 collective-permute-start.18
Sparse Core Ops, SparseCore 0:
  134.3 62.0 all-gather.8
  233.0 51.2 all-gather.10
  321.1 124.7 reduce-scatter.2
  462.4 68.8 all-gather.12
  535.5 65.0 reduce-scatter.4
  603.2 47.8 all-gather.14
